TPU v7x, 32 devices: a whole 2x2x4 slice. The times are simulated.
32 devices in a mesh: dp: 4 (over y, x), expert: 4 (over z), tensor: 2 (over core).
Axes of the slice: x: 2, y: 2, z: 4, core: 2. Of those that a mesh axis runs over, the one named last changes fastest.
Arguments:
- tokens: bfloat16 [4096, 2048], P(('dp', 'expert'), 'tensor'), may hold values from -6 to 6
- norm_attn: float32 [2048], P('tensor'), may hold values from 0.5 to 1.5
- norm_mlp: float32 [2048], P('tensor'), may hold values from 0.5 to 1.5
- w_kv: float32 [2048, 2, 2048], P(('dp', 'expert'), None, 'tensor'), may hold values from -0.125 to 0.125
- router_attn: float32 [2048, 8], replicated, may hold values from -0.125 to 0.125
- router_mlp: float32 [2048, 8], replicated, may hold values from -0.125 to 0.125
- w_query: float32 [8, 2048, 2048], P('expert', 'dp', 'tensor'), may hold values from -0.125 to 0.125
- w_output: float32 [8, 2048, 2048], P('expert', 'tensor', 'dp'), may hold values from -0.5 to 0.5
- w_gateup: float32 [8, 2048, 2, 5632], P('expert', 'dp', None, 'tensor'), may hold values from -0.125 to 0.125
- w_down: float32 [8, 5632, 2048], P('expert', 'tensor', 'dp'), may hold values from -0.078125 to 0.078125
- segments: int32 [4096], P(('dp', 'expert')), may hold values from 0 to 127, never falling along the last dimension, each value on 1 to 1024 neighbouring positions
- att_routes: int32 [4096, 2], P(('dp', 'expert')), may hold values from 0 to 7, all different within a row; in each aligned block of 256 rows (0 to 255, 256 to 511, ...) at most 96 rows name the same one
- mlp_routes: int32 [4096, 2], P(('dp', 'expert')), may hold values from 0 to 7, all different within a row; in each aligned block of 256 rows (0 to 255, 256 to 511, ...) at most 96 rows name the same one
- cotangent: bfloat16 [4096, 2048], P(('dp', 'expert'), 'tensor'), may hold values from -6 to 6
Outputs:
- out: bfloat16 [4096, 2048], P(('dp', 'expert'), 'tensor')
- grad_tokens: float32 [4096, 2048], P(('dp', 'expert'), 'tensor')
- grad_norm_attn: float32 [2048], P('tensor')
- grad_norm_mlp: float32 [2048], P('tensor')
- grad_w_kv: float32 [2048, 2, 2048], P(('dp', 'expert'), None, 'tensor')
- grad_router_attn: float32 [2048, 8], replicated
- grad_router_mlp: float32 [2048, 8], replicated
- grad_w_query: float32 [8, 2048, 2048], P('expert', 'dp', 'tensor')
- grad_w_output: float32 [8, 2048, 2048], P('expert', 'tensor', 'dp')
- grad_w_gateup: float32 [8, 2048, 2, 5632], P('expert', 'dp', None, 'tensor')
- grad_w_down: float32 [8, 5632, 2048], P('expert', 'tensor', 'dp')
Inputs may be any that keep to these rules, and one draw needn't show every extreme that they name: `segments`: document numbers never fall along the tokens; a document holds 1 to 1024 tokens and one holds exactly 1024; a document may continue across the end of a sequence, but attention never does. `att_routes`: each token names 2 different experts; the 256 tokens of one device name no expert more than 96 times, and on some device some expert exactly 96 times. `mlp_routes`: each token names 2 different experts; the 256 tokens of one device name no expert more than 96 times, and on some device some expert exactly 96 times.
All inputs are finite; a program needn't handle non-finite values.
Results may differ from a plain program's by a relative error of at most 0.018.
Values may be sent and summed in bfloat16 or wider, within the bound.
No kernel may reach another device: no remote copies, remote signals or barrier semaphores. Data moves between devices by JAX's collectives and lax.ppermute only.
A program may use at most 384 MiB of HBM per device.

v0:
```python
import math

import jax
import jax.numpy as jnp
from jax import lax
from jax.sharding import PartitionSpec as P

HD = 128


EPSILON = 1e-06
MASKED = -1000000000.0


def rope_angle(positions, head_dim):
    half_dim = head_dim // 2
    frequency = jnp.exp(
        jnp.arange(half_dim, dtype=jnp.float32) * (-2.0 * math.log(10000.0) / head_dim)
    )
    return positions.astype(jnp.float32)[:, None] * frequency[None, :]


def rotate(values, angles):
    half_dim = values.shape[-1] // 2
    cosine = jnp.cos(angles)[..., None, :]
    sine_part = jnp.sin(angles)[..., None, :]
    first_half = values[..., :half_dim]
    second = values[..., half_dim:]
    return jnp.concatenate(
        [first_half * cosine - second * sine_part, second * cosine + first_half * sine_part], -1
    )


def slot_tables(routes, experts, capacity):
    flat_routes = routes.reshape(-1)
    one_hot = (flat_routes[:, None] == jnp.arange(experts, dtype=jnp.int32)[None, :]).astype(
        jnp.int32
    )
    slot_rank = jnp.sum((jnp.cumsum(one_hot, 0) - one_hot) * one_hot, 1)
    slot_index = flat_routes * capacity + slot_rank
    slot_table = (
        jnp.zeros((experts * capacity,), jnp.int32)
        .at[slot_index]
        .set(jnp.arange(flat_routes.shape[0], dtype=jnp.int32) + 1)
    )
    return (slot_index, slot_table)


def pack_rows(source_rows, slot_table, per_row):
    live_slot = slot_table > 0
    row_index = jnp.maximum(slot_table - 1, 0) // per_row
    gathered = jnp.take(source_rows, row_index, axis=0)
    return jnp.where(live_slot[:, None], gathered, jnp.zeros((), source_rows.dtype))


def block_size(row_count):
    return max(
        (divisor for divisor in range(1, min(row_count, 512) + 1) if row_count % divisor == 0)
    )


def row_total(values):
    return lax.psum(values, "tensor")


def full_columns(values):
    return lax.all_gather(values, "tensor", axis=1, tiled=True)


def column_share(values):
    return lax.psum_scatter(values, "tensor", scatter_dimension=1, tiled=True)


def to_owner(values):
    return lax.all_to_all(values, "expert", split_axis=0, concat_axis=0, tiled=True)


def to_home(values):
    return lax.all_to_all(values, "expert", split_axis=0, concat_axis=0, tiled=True)


def normalize(residual, gain_vector, full_width):
    row_scale = lax.rsqrt(
        row_total(jnp.sum(residual * residual, 1, keepdims=True)) / full_width + EPSILON
    )
    return (residual * row_scale * gain_vector, row_scale)


def normalize_back(residual, gain_vector, row_scale, grad_normed, full_width):
    inner_sum = row_total(jnp.sum(grad_normed * gain_vector * residual, 1, keepdims=True))
    grad_residual = (
        row_scale * gain_vector * grad_normed
        - residual * (row_scale * row_scale * row_scale) * inner_sum / full_width
    )
    grad_gain = jnp.sum(grad_normed * residual * row_scale, 0)
    return (grad_residual, grad_gain)


def route_gates(full_rows, router, routes):
    logits = jnp.dot(full_rows, router.astype(jnp.bfloat16), preferred_element_type=jnp.float32)
    chosen = jnp.take_along_axis(logits, routes, axis=1)
    return jax.nn.softmax(chosen, axis=1)


def gates_back(gates, grad_gates, routes, experts):
    grad_chosen = gates * (grad_gates - jnp.sum(gates * grad_gates, 1, keepdims=True))
    picks = (routes[:, :, None] == jnp.arange(experts, dtype=jnp.int32)[None, None, :]).astype(
        jnp.float32
    )
    return jnp.sum(grad_chosen[:, :, None] * picks, 1).astype(jnp.bfloat16)


def owner_slots(routes_seq, experts, capacity, groups, local_count, group_index):
    top_count = routes_seq.shape[1]
    per_source = routes_seq.reshape(groups, -1, top_count)
    tables = jax.vmap(lambda routes: slot_tables(routes, experts, capacity)[1])(per_source)
    tables = lax.dynamic_slice_in_dim(
        tables.reshape(groups, experts, capacity), group_index * local_count, local_count, 1
    )
    source_base = (jnp.arange(groups, dtype=jnp.int32) * per_source.shape[1])[:, None, None]
    return (source_base + jnp.maximum(tables - 1, 0) // top_count).reshape(-1)


def masked_scores(query_block, pos_block, seg_block, key_rows, seq_seg, score_scale):
    key_pos = jnp.arange(key_rows.shape[0], dtype=jnp.int32)
    raw_scores = (
        jnp.einsum("qhd,khd->hqk", query_block, key_rows, preferred_element_type=jnp.float32)
        * score_scale
    )
    allowed = (seg_block[:, None] == seq_seg[None, :]) & (pos_block[:, None] >= key_pos[None, :])
    return jnp.where(allowed[None], raw_scores, MASKED)


def attend_forward(query_rows, row_pos, row_seg, key_rows, value_rows, seq_seg):
    row_count, head_count, head_dim = query_rows.shape
    block_rows = block_size(row_count)
    score_scale = 1.0 / math.sqrt(head_dim)

    def one_block(pieces):
        query_block, pos_block, seg_block = pieces
        scores = masked_scores(query_block, pos_block, seg_block, key_rows, seq_seg, score_scale)
        row_peak = jnp.max(scores, -1, keepdims=True)
        row_exp = jnp.exp(scores - row_peak)
        row_mass = jnp.sum(row_exp, -1, keepdims=True)
        softmax_rows = (row_exp / row_mass).astype(jnp.bfloat16)
        mixed_rows = jnp.einsum(
            "hqk,khd->qhd", softmax_rows, value_rows, preferred_element_type=jnp.float32
        )
        return (mixed_rows.astype(jnp.bfloat16), (row_peak + jnp.log(row_mass))[..., 0])

    mixed_rows, log_mass = lax.map(
        one_block,
        (
            query_rows.reshape(-1, block_rows, head_count, head_dim),
            row_pos.reshape(-1, block_rows),
            row_seg.reshape(-1, block_rows),
        ),
    )
    return (mixed_rows.reshape(row_count, head_count, head_dim), log_mass)


def attend_backward(
    query_rows, row_pos, row_seg, key_rows, value_rows, seq_seg, log_mass, grad_mixed
):
    row_count, head_count, head_dim = query_rows.shape
    block_rows = block_size(row_count)
    score_scale = 1.0 / math.sqrt(head_dim)

    def one_block(carried, pieces):
        grad_keys, grad_values = carried
        query_block, pos_block, seg_block, mass_block, grad_block = pieces
        scores = masked_scores(query_block, pos_block, seg_block, key_rows, seq_seg, score_scale)
        softmax_rows = jnp.exp(scores - mass_block[..., None])
        grad_soft = jnp.einsum(
            "qhd,khd->hqk", grad_block, value_rows, preferred_element_type=jnp.float32
        )
        inner_sum = jnp.sum(softmax_rows * grad_soft, -1, keepdims=True)
        grad_scores = (softmax_rows * (grad_soft - inner_sum)).astype(jnp.bfloat16)
        grad_query = (
            jnp.einsum("hqk,khd->qhd", grad_scores, key_rows, preferred_element_type=jnp.float32)
            * score_scale
        )
        grad_keys = (
            grad_keys
            + jnp.einsum(
                "hqk,qhd->khd", grad_scores, query_block, preferred_element_type=jnp.float32
            )
            * score_scale
        )
        grad_values = grad_values + jnp.einsum(
            "hqk,qhd->khd",
            softmax_rows.astype(jnp.bfloat16),
            grad_block,
            preferred_element_type=jnp.float32,
        )
        return ((grad_keys, grad_values), grad_query)

    zero_keys = jnp.zeros(key_rows.shape, jnp.float32)
    pieces = (
        query_rows.reshape(-1, block_rows, head_count, head_dim),
        row_pos.reshape(-1, block_rows),
        row_seg.reshape(-1, block_rows),
        log_mass,
        grad_mixed.reshape(-1, block_rows, head_count, head_dim),
    )
    (grad_keys, grad_values), grad_query = lax.scan(one_block, (zero_keys, zero_keys), pieces)
    return (grad_query.reshape(row_count, head_count, head_dim), grad_keys, grad_values)


def shards(
    tokens,
    norm_attn,
    norm_mlp,
    w_kv,
    router_attn,
    router_mlp,
    w_query,
    w_output,
    w_gateup,
    w_down,
    segments,
    att_routes,
    mlp_routes,
    cotangent,
):
    token_count, width_part = tokens.shape
    parts = lax.axis_size("tensor")
    groups = lax.axis_size("expert")
    full_width = width_part * parts
    top_count = att_routes.shape[1]
    experts_att = router_attn.shape[1]
    experts_mlp = router_mlp.shape[1]
    local_att = w_query.shape[0]
    local_mlp = w_gateup.shape[0]
    capacity = 3 * token_count // 8
    head_dim = HD
    heads_part = w_query.shape[2] // head_dim
    group_index = lax.axis_index("expert")
    part_index = lax.axis_index("tensor")
    local_query = w_query.astype(jnp.bfloat16)
    local_output = w_output.astype(jnp.bfloat16)
    local_gateup = w_gateup.astype(jnp.bfloat16)
    local_down = w_down.astype(jnp.bfloat16)
    whole_query, whole_output, whole_gateup, whole_down = (
        lax.all_gather(local_query, "dp", axis=1, tiled=True),
        lax.all_gather(local_output, "dp", axis=2, tiled=True),
        lax.all_gather(local_gateup, "dp", axis=1, tiled=True),
        lax.all_gather(local_down, "dp", axis=2, tiled=True),
    )
    kv_full = lax.all_gather(w_kv.astype(jnp.bfloat16), ("dp", "expert"), axis=0, tiled=True)
    seq_seg, seq_att_routes, seq_mlp_routes = (
        lax.all_gather(segments, "expert", axis=0, tiled=True),
        lax.all_gather(att_routes, "expert", axis=0, tiled=True),
        lax.all_gather(mlp_routes, "expert", axis=0, tiled=True),
    )
    residual = tokens.astype(jnp.float32)
    normed_a, scale_a = normalize(residual, norm_attn, full_width)
    rows_a = full_columns(normed_a.astype(jnp.bfloat16))
    kv_raw = jnp.einsum("td,dgf->tgf", rows_a, kv_full, preferred_element_type=jnp.float32)
    positions = group_index * token_count + jnp.arange(token_count, dtype=jnp.int32)
    angles = rope_angle(positions, head_dim)
    key_rows = rotate(kv_raw[:, 0].reshape(token_count, heads_part, head_dim), angles).astype(
        jnp.bfloat16
    )
    value_rows = kv_raw[:, 1].reshape(token_count, heads_part, head_dim).astype(jnp.bfloat16)
    seq_keys, seq_values = (
        lax.all_gather(key_rows, "expert", axis=0, tiled=True),
        lax.all_gather(value_rows, "expert", axis=0, tiled=True),
    )
    gates_a = route_gates(rows_a, router_attn, att_routes)
    index_a, table_a = slot_tables(att_routes, experts_att, capacity)
    held_a = to_owner(
        pack_rows(rows_a, table_a, top_count).reshape(experts_att, capacity, full_width)
    ).reshape(groups, local_att, capacity, full_width)
    pos_a = owner_slots(seq_att_routes, experts_att, capacity, groups, local_att, group_index)
    owner_rows = groups * local_att * capacity
    angle_rows = rope_angle(pos_a, head_dim)
    query_raw = jnp.einsum(
        "slcd,ldf->slcf", held_a, whole_query, preferred_element_type=jnp.float32
    )
    query_rows = rotate(query_raw.reshape(owner_rows, heads_part, head_dim), angle_rows).astype(
        jnp.bfloat16
    )
    seg_rows = jnp.take(seq_seg, pos_a)
    mixed_rows, log_mass = attend_forward(
        query_rows, pos_a, seg_rows, seq_keys, seq_values, seq_seg
    )
    mixed_owner = mixed_rows.reshape(groups, local_att, capacity, heads_part * head_dim)
    branch_a = jnp.einsum(
        "slcf,lfd->slcd", mixed_owner, whole_output, preferred_element_type=jnp.float32
    )
    back_a = column_share(branch_a.reshape(owner_rows, full_width)).astype(jnp.bfloat16)
    home_a = to_home(back_a.reshape(experts_att, capacity, width_part))
    taken_a = jnp.take(home_a.reshape(experts_att * capacity, width_part), index_a, axis=0).reshape(
        token_count, top_count, width_part
    )
    middle = residual + jnp.sum(gates_a[:, :, None] * taken_a.astype(jnp.float32), 1)
    normed_b, scale_b = normalize(middle, norm_mlp, full_width)
    rows_b = full_columns(normed_b.astype(jnp.bfloat16))
    gates_b = route_gates(rows_b, router_mlp, mlp_routes)
    index_b, table_b = slot_tables(mlp_routes, experts_mlp, capacity)
    held_b = to_owner(
        pack_rows(rows_b, table_b, top_count).reshape(experts_mlp, capacity, full_width)
    ).reshape(groups, local_mlp, capacity, full_width)
    gate_up = jnp.einsum(
        "slcd,ldgf->slcgf", held_b, whole_gateup, preferred_element_type=jnp.float32
    )
    gate_part = gate_up[:, :, :, 0]
    up_part = gate_up[:, :, :, 1]
    sigmoid_gate = jax.nn.sigmoid(gate_part)
    silu_gate = gate_part * sigmoid_gate
    hidden = (silu_gate * up_part).astype(jnp.bfloat16)
    branch_b = jnp.einsum("slcf,lfd->slcd", hidden, whole_down, preferred_element_type=jnp.float32)
    back_b = column_share(branch_b.reshape(-1, full_width)).astype(jnp.bfloat16)
    home_b = to_home(back_b.reshape(experts_mlp, capacity, width_part))
    taken_b = jnp.take(home_b.reshape(experts_mlp * capacity, width_part), index_b, axis=0).reshape(
        token_count, top_count, width_part
    )
    output = middle + jnp.sum(gates_b[:, :, None] * taken_b.astype(jnp.float32), 1)
    whole_query, whole_output, whole_gateup, whole_down = (
        lax.all_gather(local_query, "dp", axis=1, tiled=True),
        lax.all_gather(local_output, "dp", axis=2, tiled=True),
        lax.all_gather(local_gateup, "dp", axis=1, tiled=True),
        lax.all_gather(local_down, "dp", axis=2, tiled=True),
    )
    grad_out = cotangent.astype(jnp.float32)
    grad_gates_b = row_total(jnp.sum(grad_out[:, None, :] * taken_b.astype(jnp.float32), 2))
    grad_logit_b = gates_back(gates_b, grad_gates_b, mlp_routes, experts_mlp)
    grad_taken_b = (
        (gates_b[:, :, None] * grad_out[:, None, :])
        .astype(jnp.bfloat16)
        .reshape(token_count * top_count, width_part)
    )
    sent_grad_b = to_owner(
        pack_rows(grad_taken_b, table_b, 1).reshape(experts_mlp, capacity, width_part)
    )
    held_grad_b = full_columns(sent_grad_b.reshape(-1, width_part)).reshape(
        groups, local_mlp, capacity, full_width
    )
    grad_hidden = jnp.einsum(
        "slcd,lfd->slcf", held_grad_b, whole_down, preferred_element_type=jnp.float32
    )
    grad_wdown = jnp.einsum(
        "slcf,slcd->lfd", hidden, held_grad_b, preferred_element_type=jnp.float32
    )
    grad_gate = grad_hidden * up_part * sigmoid_gate * (1.0 + gate_part * (1.0 - sigmoid_gate))
    grad_up = grad_hidden * silu_gate
    grad_both = jnp.stack([grad_gate, grad_up], 3).astype(jnp.bfloat16)
    grad_wgateup = jnp.einsum(
        "slcd,slcgf->ldgf", held_b, grad_both, preferred_element_type=jnp.float32
    )
    grad_rows_b = jnp.einsum(
        "slcgf,ldgf->slcd", grad_both, whole_gateup, preferred_element_type=jnp.float32
    )
    back_grad_b = column_share(grad_rows_b.reshape(-1, full_width)).astype(jnp.bfloat16)
    home_grad_b = to_home(back_grad_b.reshape(experts_mlp, capacity, width_part))
    copies_b = jnp.take(
        home_grad_b.reshape(experts_mlp * capacity, width_part), index_b, axis=0
    ).reshape(token_count, top_count, width_part)
    router_mlp_part = lax.dynamic_slice_in_dim(
        router_mlp, part_index * width_part, width_part, 0
    ).astype(jnp.bfloat16)
    grad_normed_b = jnp.sum(copies_b.astype(jnp.float32), 1) + jnp.dot(
        grad_logit_b, router_mlp_part.T, preferred_element_type=jnp.float32
    )
    grad_router_b = jnp.einsum(
        "td,te->de", rows_b, grad_logit_b, preferred_element_type=jnp.float32
    )
    grad_mid_norm, grad_gain_b = normalize_back(
        middle, norm_mlp, scale_b, grad_normed_b, full_width
    )
    grad_middle = grad_out + grad_mid_norm
    grad_gates_a = row_total(jnp.sum(grad_middle[:, None, :] * taken_a.astype(jnp.float32), 2))
    grad_logit_a = gates_back(gates_a, grad_gates_a, att_routes, experts_att)
    grad_taken_a = (
        (gates_a[:, :, None] * grad_middle[:, None, :])
        .astype(jnp.bfloat16)
        .reshape(token_count * top_count, width_part)
    )
    sent_grad_a = to_owner(
        pack_rows(grad_taken_a, table_a, 1).reshape(experts_att, capacity, width_part)
    )
    held_grad_a = full_columns(sent_grad_a.reshape(-1, width_part)).reshape(
        groups, local_att, capacity, full_width
    )
    grad_mixed = jnp.einsum(
        "slcd,lfd->slcf", held_grad_a, whole_output, preferred_element_type=jnp.float32
    ).astype(jnp.bfloat16)
    grad_woutput = jnp.einsum(
        "slcf,slcd->lfd", mixed_owner, held_grad_a, preferred_element_type=jnp.float32
    )
    grad_query_rot, grad_keys_seq, grad_values_seq = attend_backward(
        query_rows,
        pos_a,
        seg_rows,
        seq_keys,
        seq_values,
        seq_seg,
        log_mass,
        grad_mixed.reshape(owner_rows, heads_part, head_dim),
    )
    grad_query_raw = (
        rotate(grad_query_rot, -angle_rows)
        .astype(jnp.bfloat16)
        .reshape(groups, local_att, capacity, heads_part * head_dim)
    )
    grad_wquery = jnp.einsum(
        "slcd,slcf->ldf", held_a, grad_query_raw, preferred_element_type=jnp.float32
    )
    grad_rows_a = jnp.einsum(
        "slcf,ldf->slcd", grad_query_raw, whole_query, preferred_element_type=jnp.float32
    )
    back_grad_a = column_share(grad_rows_a.reshape(-1, full_width)).astype(jnp.bfloat16)
    grad_keys, grad_values = (
        lax.psum_scatter(
            grad_keys_seq.astype(jnp.bfloat16), "expert", scatter_dimension=0, tiled=True
        ).astype(jnp.float32),
        lax.psum_scatter(
            grad_values_seq.astype(jnp.bfloat16), "expert", scatter_dimension=0, tiled=True
        ).astype(jnp.float32),
    )
    grad_kv = (
        jnp.stack([rotate(grad_keys, -angles), grad_values], 1)
        .astype(jnp.bfloat16)
        .reshape(token_count, 2, heads_part * head_dim)
    )
    grad_wkv = jnp.einsum("td,tgf->dgf", rows_a, grad_kv, preferred_element_type=jnp.float32)
    grad_rows_kv = column_share(
        jnp.einsum("tgf,dgf->td", grad_kv, kv_full, preferred_element_type=jnp.float32)
    )
    home_grad_a = to_home(back_grad_a.reshape(experts_att, capacity, width_part))
    copies_a = jnp.take(
        home_grad_a.reshape(experts_att * capacity, width_part), index_a, axis=0
    ).reshape(token_count, top_count, width_part)
    router_attn_part = lax.dynamic_slice_in_dim(
        router_attn, part_index * width_part, width_part, 0
    ).astype(jnp.bfloat16)
    grad_normed_a = (
        grad_rows_kv
        + jnp.sum(copies_a.astype(jnp.float32), 1)
        + jnp.dot(grad_logit_a, router_attn_part.T, preferred_element_type=jnp.float32)
    )
    grad_router_a = jnp.einsum(
        "td,te->de", rows_a, grad_logit_a, preferred_element_type=jnp.float32
    )
    grad_in_norm, grad_gain_a = normalize_back(
        residual, norm_attn, scale_a, grad_normed_a, full_width
    )
    grad_tokens = grad_middle + grad_in_norm
    small_sums = lax.psum(
        (grad_router_a, grad_router_b, grad_gain_a, grad_gain_b), ("dp", "expert")
    )
    expert_sums = (
        lax.psum_scatter(
            grad_wquery.astype(jnp.bfloat16), "dp", scatter_dimension=1, tiled=True
        ).astype(jnp.float32),
        lax.psum_scatter(
            grad_woutput.astype(jnp.bfloat16), "dp", scatter_dimension=2, tiled=True
        ).astype(jnp.float32),
        lax.psum_scatter(
            grad_wgateup.astype(jnp.bfloat16), "dp", scatter_dimension=1, tiled=True
        ).astype(jnp.float32),
        lax.psum_scatter(
            grad_wdown.astype(jnp.bfloat16), "dp", scatter_dimension=2, tiled=True
        ).astype(jnp.float32),
    )
    grad_wkv_share = lax.psum_scatter(grad_wkv, ("dp", "expert"), scatter_dimension=0, tiled=True)
    return (
        output.astype(jnp.bfloat16),
        grad_tokens,
        small_sums[2],
        small_sums[3],
        grad_wkv_share,
        small_sums[0],
        small_sums[1],
        expert_sums[0],
        expert_sums[1],
        expert_sums[2],
        expert_sums[3],
    )


def solution(mesh):
    in_specs = (
        P(("dp", "expert"), "tensor"),
        P("tensor"),
        P("tensor"),
        P(("dp", "expert"), None, "tensor"),
        P(),
        P(),
        P("expert", "dp", "tensor"),
        P("expert", "tensor", "dp"),
        P("expert", "dp", None, "tensor"),
        P("expert", "tensor", "dp"),
        P(("dp", "expert")),
        P(("dp", "expert"), None),
        P(("dp", "expert"), None),
        P(("dp", "expert"), "tensor"),
    )
    out_specs = (
        P(("dp", "expert"), "tensor"),
        P(("dp", "expert"), "tensor"),
        P("tensor"),
        P("tensor"),
        P(("dp", "expert"), None, "tensor"),
        P(),
        P(),
        P("expert", "dp", "tensor"),
        P("expert", "tensor", "dp"),
        P("expert", "dp", None, "tensor"),
        P("expert", "tensor", "dp"),
    )
    return jax.shard_map(shards, mesh=mesh, in_specs=in_specs, out_specs=out_specs, check_vma=False)
```

profile of v0, /device:TPU:0, one launch (start us, length us, event | category | flops | bytes accessed | tf_op | source)
XLA Modules:
  0.0 2962.6 jit_solution(4308469058607301545)
XLA Ops:
  26.0 117.3 %all-gather.17.cloned.1.call-done = bf16[2048,2,1024]{2,0,1:T(8,128)(2,1)} async-done(((bf16[128,2,1024]{2,0,1:T(8,128)(2,1)}), bf16[2048,2,1024]{2,0,1:T(8,128)(2,1)}) %all-gather.17.cloned.1.call-update) | async-done | bytes 8388624 | tf_op jit(solution)/shard_map/all_gather | solution.py:250
  143.3 6.0 fusion.104
  174.9 71.6 %all_gather.44 = s32[1024,2]{0,1:T(2,128)S(1)} all-gather(s32[256,2]{0,1:T(2,128)S(1)} %copy-done.55), channel_id=1, replica_groups=mesh['dp'=4,'expert'=4,'tensor'=2] {'expert'}, dimensions={0}, use_global_device_ids=true | all-gather | bytes 10240 | tf_op jit(solution)/shard_map/all_gather | solution.py:253
  253.3 8.3 scatter_custom_fusion.2
  261.9 7.8 all-gather
  277.2 6.7 fusion.75
  296.8 28.8 all-gather.21.cloned.1.call-done
  325.7 29.3 while.27
  358.0 56.2 %all-gather.23.cloned.1.call-done = bf16[2,1024,2048]{2,1,0:T(8,128)(2,1)} async-done(((bf16[2,1024,512]{2,1,0:T(8,128)(2,1)}), bf16[2,1024,2048]{2,1,0:T(8,128)(2,1)}) %all-gather.23.cloned.1.call-update) | async-done | bytes 8388624 | tf_op jit(solution)/shard_map/all_gather | solution.py:246
  414.1 5.8 fusion.60
  423.3 14.6 reduce-scatter.13.cloned.1.call-done
  451.7 31.7 %all-to-all-done.1 = bf16[8,96,1024]{2,1,0:T(8,128)(2,1)S(1)} async-done(((bf16[8,96,1024]{2,1,0:T(8,128)(2,1)}), bf16[8,96,1024]{2,1,0:T(8,128)(2,1)S(1)}, u32[]{:S(2)}, u32[]{:S(2)}) %all-to-all-start.1) | async-done | bytes 1572896 | tf_op jit(solution)/shard_map/all_to_all | solution.py:79
  499.3 16.0 copy.338
  515.4 9.1 convert_element_type.236
  530.7 8.3 gather_fusion.5
  539.9 73.8 %all_to_all.40 = bf16[8,96,2048]{2,1,0:T(8,128)(2,1)S(1)} all-to-all(bf16[8,96,2048]{2,1,0:T(8,128)(2,1)S(1)} %bitcast.328), channel_id=1, replica_groups=mesh['dp'=4,'expert'=4,'tensor'=2] {'expert'}, dimensions={0} | all-to-all | bytes 6291456 | tf_op jit(solution)/shard_map/all_to_all | solution.py:75
  613.7 302.9 %all-gather.27.cloned.1.call-done = bf16[2,2048,2,2816]{3,1,2,0:T(8,128)(2,1)} async-done(((bf16[2,512,2,2816]{3,1,2,0:T(8,128)(2,1)}), bf16[2,2048,2,2816]{3,1,2,0:T(8,128)(2,1)}) %all-gather.27.cloned.1.call-update) | async-done | bytes 46137360 | tf_op jit(solution)/shard_map/all_gather | solution.py:247
  916.5 29.4 fusion.55
  945.9 9.4 multiply_convert_fusion.1
  955.3 173.5 %all-gather.29.cloned.1.call-done = bf16[2,2816,2048]{2,1,0:T(8,128)(2,1)} async-done(((bf16[2,2816,512]{2,1,0:T(8,128)(2,1)}), bf16[2,2816,2048]{2,1,0:T(8,128)(2,1)}) %all-gather.29.cloned.1.call-update) | async-done | bytes 23068688 | tf_op jit(solution)/shard_map/all_gather | solution.py:248
  1128.7 13.8 fusion.66
  1145.7 14.7 reduce-scatter.15.cloned.1.call-done
  1163.7 4.9 all-to-all-start.3
  1181.7 24.3 all-to-all-done.3
  1219.3 41.0 %all_to_all.41 = bf16[8,96,1024]{2,1,0:T(8,128)(2,1)} all-to-all(bf16[8,96,1024]{2,1,0:T(8,128)(2,1)S(1)} %bitcast.340), channel_id=1, replica_groups=mesh['dp'=4,'expert'=4,'tensor'=2] {'expert'}, dimensions={0} | all-to-all | bytes 3145728 | tf_op jit(solution)/shard_map/all_to_all | solution.py:75
  1260.3 11.3 all-gather.31.cloned.1.call-done
  1271.6 16.2 fusion.36
  1287.8 14.0 fusion.59
  1301.8 27.4 fusion.34
  1329.3 15.8 reduce-scatter.17.cloned.1.call-done
  1353.6 37.1 %all-to-all-done.5 = bf16[8,96,1024]{2,1,0:T(8,128)(2,1)S(1)} async-done(((bf16[8,96,1024]{2,1,0:T(8,128)(2,1)}), bf16[8,96,1024]{2,1,0:T(8,128)(2,1)S(1)}, u32[]{:S(2)}, u32[]{:S(2)}) %all-to-all-start.5) | async-done | bytes 1572896 | tf_op jit(solution)/shard_map/all_to_all | solution.py:79
  1400.7 5.2 reduce_sum.229
  1432.0 40.8 %all_to_all.42 = bf16[8,96,1024]{2,1,0:T(8,128)(2,1)} all-to-all(bf16[8,96,1024]{2,1,0:T(8,128)(2,1)S(1)} %bitcast.341), channel_id=1, replica_groups=mesh['dp'=4,'expert'=4,'tensor'=2] {'expert'}, dimensions={0} | all-to-all | bytes 3145728 | tf_op jit(solution)/shard_map/all_to_all | solution.py:75
  1472.9 11.2 all-gather.33.cloned.1.call-done
  1484.1 7.8 fusion.87
  1493.7 87.2 %while.28 = (s32[]{:T(128)}, f32[1024,8,128]{0,2,1:T(8,128)}, f32[1024,8,128]{0,2,1:T(8,128)}, f32[2,384,8,128]{3,2,1,0:T(8,128)}, bf16[2,384,8,128]{3,1,2,0:T(8...) while((s32[]{:T(128)}, f32[1024,8,128]{0,2,1:T(8,128)}, ...), condition=%wide.region_38.43_spmd.clone, body=%wide.region_36.42_spmd.clone.sunk | while | flops 4080530432 | bytes 285836608 | solution.py:206
  1497.8 10.4 multiply_reduce_fusion.12
  1508.2 9.6 multiply_convert_fusion.6
  1517.8 6.7 bitcast_add_fusion.5
  1525.9 5.6 bitcast_add_fusion.6
  1539.8 10.4 multiply_reduce_fusion.12
  1550.1 9.6 multiply_convert_fusion.6
  1559.7 7.9 bitcast_add_fusion.5
  1569.0 7.3 bitcast_add_fusion.6
  1593.0 6.4 fusion.63
  1602.6 27.4 reduce-scatter.21.cloned.1.call-done
  1631.3 44.7 %reduce-scatter.19.cloned.1.call-done = bf16[256,8,128]{0,2,1:T(8,128)(2,1)} async-done(((bf16[1024,8,128]{0,2,1:T(8,128)(2,1)}), bf16[256,8,128]{0,2,1:T(8,128)(2,1)}) %reduce-scatter.19.cloned.1.call-update) | async-done | bytes 524304 | tf_op jit(solution)/shard_map/reduce_scatter | solution.py:415
  1677.5 7.2 convolution_bitcast_fusion
  1684.8 9.1 bitcast_convert_fusion.3
  1695.3 8.6 bitcast_convert_fusion.2
  1704.1 19.7 bitcast_convert_fusion.1
  1725.0 8.5 fusion.102
  1733.5 31.7 %bitcast_convert_fusion = bf16[2,2048,2,2816]{3,1,2,0:T(8,128)(2,1)} fusion(bf16[4,2,96,2048,1]{3,2,1,0,4:T(8,128)(2,1)} %bitcast.322, bf16[4,2,96,1,2816]{4,2,0,1,3:T(8,128)(2,1)} %get-tuple-element.359, bf16[4,2,96,1,2816]{4,2,0,1,3:T(8,128)(2,1)} %get-tuple-element.358), kind=kOutput, calls=%fused_computation.64 | convolution fusion | flops 17744134144 | bytes 57933824 | tf_op jit(solution)/shard_map/slcd,slcgf->ldgf/dot_general | solution.py:349
  1779.6 30.7 %all-to-all-done.7 = bf16[8,96,1024]{2,1,0:T(8,128)(2,1)} async-done(((bf16[8,96,1024]{2,1,0:T(8,128)(2,1)}), bf16[8,96,1024]{2,1,0:T(8,128)(2,1)}, u32[]{:S(2)}, u32[]{:S(2)}) %all-to-all-start.7) | async-done | bytes 1572896 | tf_op jit(solution)/shard_map/all_to_all | solution.py:79
  1810.3 5.4 gather_fusion.10
  1819.5 5.1 reduce_sum.235
  1830.6 42.1 %all-reduce = (f32[1024]{0:T(1024)}, f32[1024]{0:T(1024)}) all-reduce(f32[1024]{0:T(1024)S(1)} %get-tuple-element.280, f32[1024]{0:T(1024)S(1)} %copy-done.78), channel_id=1, replica_groups=mesh['dp'=4,'expert'=4,'tensor'=2] {'dp','expert'}, use_global_device_ids=true, to_apply=%region_51.56 | all-reduce | flops 2048 | bytes 16384 | tf_op jit(solution)/shard_map/psum | solution.py:450
  1877.0 10.5 reduce-scatter.31.cloned.1.call-done
  1891.7 204.5 %reduce-scatter.35.cloned.1.call-done = bf16[2,2816,512]{2,1,0:T(8,128)(2,1)} async-done(((bf16[2,2816,2048]{2,1,0:T(8,128)(2,1)}), bf16[2,2816,512]{2,1,0:T(8,128)(2,1)}) %reduce-scatter.35.cloned.1.call-update) | async-done | bytes 5767184 | tf_op jit(solution)/shard_map/reduce_scatter | solution.py:463
  2096.2 8.9 convert_element_type.269
  2105.0 343.5 %reduce-scatter.27.cloned.1.call-done = f32[128,2,1024]{2,0,1:T(8,128)} async-done(((f32[2048,2,1024]{2,0,1:T(8,128)}), f32[128,2,1024]{2,0,1:T(8,128)}) %reduce-scatter.27.cloned.1.call-update) | async-done | bytes 1048592 | tf_op jit(solution)/shard_map/reduce_scatter | solution.py:467
  2451.5 389.3 %reduce-scatter.33.cloned.1.call-done = bf16[2,512,2,2816]{3,1,2,0:T(8,128)(2,1)} async-done(((bf16[2,2048,2,2816]{3,1,2,0:T(8,128)(2,1)}), bf16[2,512,2,2816]{3,1,2,0:T(8,128)(2,1)}) %reduce-scatter.33.cloned.1.call-update) | async-done | bytes 11534352 | tf_op jit(solution)/shard_map/reduce_scatter | solution.py:460
  2840.8 23.4 copy.224
  2864.2 88.1 %all-reduce.4.cloned.1.call-done = (f32[2048,8]{0,1:T(8,128)}, f32[2048,8]{0,1:T(8,128)}) async-done(((f32[2048,8]{0,1:T(8,128)}, f32[2048,8]{0,1:T(8,128)}), (f32[2048,8]{0,1:T(8,128)}, f32[2048,8]{0,1:T(8,128)})) %all-reduce.4.cloned.1.call-update) | async-done | bytes 131088 | tf_op jit(solution)/shard_map/psum | solution.py:450
  (511 shorter events, 300.3 us)
Async XLA Ops:
  7.2 18.9 all-gather.13.cloned.1.call-start
  14.3 129.0 %all-gather.17.cloned.1.call-start = ((), (), s32[]{:S(2)}) async-start(), calls=%async_computation.22 | async-start | bytes 8912896 | tf_op jit(solution)/shard_map/all_gather | solution.py:250
  16.6 260.6 %all-gather.15.cloned.1.call-start = ((), (), s32[]{:S(2)}) async-start(), calls=%async_computation.21 | async-start | bytes 10485760 | tf_op jit(solution)/shard_map/all_gather | solution.py:245
  20.6 276.3 %all-gather.19.cloned.1.call-start = ((), (), s32[]{:S(2)}) async-start(), calls=%async_computation.23 | async-start | bytes 2621440 | tf_op jit(solution)/shard_map/all_gather | solution.py:267
  151.5 174.2 %all-gather.21.cloned.1.call-start = ((), (), s32[]{:S(2)}) async-start(), calls=%async_computation.24 | async-start | bytes 2621440 | tf_op jit(solution)/shard_map/all_gather | solution.py:268
  151.7 11.1 copy-start.35
  155.5 97.8 %copy-start.87 = (s32[512]{0:T(512)}, s32[512]{0:T(512)S(1)}, u32[]{:S(2)}) copy-start(s32[512]{0:T(512)S(1)} %iota_add_fusion) | copy-start | bytes 6148
  166.3 110.9 %all-to-all-start = ((bf16[8,96,2048]{2,1,0:T(8,128)(2,1)}), bf16[8,96,2048]{2,1,0:T(8,128)(2,1)}, u32[]{:S(2)}, u32[]{:S(2)}) async-start(bf16[8,96,2048]{2,1,0:T(8,128)(2,1)} %bitcast.16), calls=%async_computation | async-start | bytes 6291456 | tf_op jit(solution)/shard_map/all_to_all | solution.py:75
  171.0 243.2 %all-gather.23.cloned.1.call-start = ((), (), s32[]{:S(2)}) async-start(), calls=%async_computation.25 | async-start | bytes 10485760 | tf_op jit(solution)/shard_map/all_gather | solution.py:246
  174.8 78.2 %copy-start.100 = (s32[2]{0:T(128)S(1)}, s32[2]{0:T(128)}, u32[]{:S(2)}) copy-start(s32[2]{0:T(128)} %constant.225) | copy-start | bytes 28
  174.8 78.3 %copy-start.99 = (s32[2]{0:T(128)S(1)}, s32[2]{0:T(128)}, u32[]{:S(2)}) copy-start(s32[2]{0:T(128)} %constant.228) | copy-start | bytes 28
  174.8 87.1 %copy-start.98 = (s32[256]{0:T(256)S(1)}, s32[256]{0:T(256)}, u32[]{:S(2)}) copy-start(s32[256]{0:T(256)} %param.36) | copy-start | bytes 3076
  174.8 263.0 %reduce-scatter.13.cloned.1.call-start = ((), (), s32[]{:S(2)}) async-start(), calls=%async_computation.26 | async-start | bytes 9437184 | tf_op jit(solution)/shard_map/reduce_scatter | solution.py:71
  355.0 65.0 %copy-start.2 = (s32[1024]{0:T(1024)}, s32[1024]{0:T(1024)S(1)}, u32[]{:S(2)}) copy-start(s32[1024]{0:T(1024)S(1)} %get-tuple-element.648) | copy-start | bytes 12292
  355.0 65.0 %copy-start.11 = (bf16[2,384,8,128]{3,1,2,0:T(8,128)(2,1)}, bf16[2,384,8,128]{3,1,2,0:T(8,128)(2,1)S(1)}, u32[]{:S(2)}) copy-start(bf16[2,384,8,128]{3,1,2,0:T(8,128)(2,1)S(1)} %get-tuple-element.655) | copy-start | bytes 4718596
  355.0 65.0 %copy-start.49 = (s32[2,384]{1,0:T(2,128)}, s32[2,384]{1,0:T(2,128)S(1)}, u32[]{:S(2)}) copy-start(s32[2,384]{1,0:T(2,128)S(1)} %get-tuple-element.728) | copy-start | bytes 9220
  355.0 65.0 %copy-start.51 = (s32[2,384]{1,0:T(2,128)}, s32[2,384]{1,0:T(2,128)S(1)}, u32[]{:S(2)}) copy-start(s32[2,384]{1,0:T(2,128)S(1)} %get-tuple-element.729) | copy-start | bytes 9220
  358.0 62.0 %copy-start.18 = (bf16[4,2,96,1024]{3,2,1,0:T(8,128)(2,1)}, bf16[4,2,96,1024]{3,2,1,0:T(8,128)(2,1)S(1)}, u32[]{:S(2)}) copy-start(bf16[4,2,96,1024]{3,2,1,0:T(8,128)(2,1)S(1)} %reshape_reshape.13) | copy-start | bytes 4718596
  423.2 22.8 copy-start.56
  423.2 23.0 copy-start.86
  423.2 23.1 copy-start.36
  423.2 23.3 copy-start.69
  423.2 23.3 copy-start.71
  423.2 23.3 copy-start.6
  423.2 23.3 copy-start.54
  441.1 42.3 %all-to-all-start.1 = ((bf16[8,96,1024]{2,1,0:T(8,128)(2,1)}), bf16[8,96,1024]{2,1,0:T(8,128)(2,1)S(1)}, u32[]{:S(2)}, u32[]{:S(2)}) async-start(bf16[8,96,1024]{2,1,0:T(8,128)(2,1)} %bitcast.338), calls=%async_computation.2 | async-start | bytes 3145728 | tf_op jit(solution)/shard_map/all_to_all | solution.py:79
  446.0 84.7 %all-gather.25.cloned.1.call-start = ((), (), s32[]{:S(2)}) async-start(), calls=%async_computation.27 | async-start | bytes 1572864 | tf_op jit(solution)/shard_map/all_gather | solution.py:67
  446.6 38.9 %copy-start.88 = (pred[512]{0:T(512)(128)(4,1)}, pred[512]{0:T(512)(128)(4,1)S(1)}, u32[]{:S(2)}) copy-start(pred[512]{0:T(512)(128)(4,1)S(1)} %get-tuple-element.344) | copy-start | bytes 1540
  446.6 36.8 %copy-start.76 = (s32[1024]{0:T(1024)}, s32[1024]{0:T(1024)S(1)}, u32[]{:S(2)}) copy-start(s32[1024]{0:T(1024)S(1)} %pad_clamp_fusion.4) | copy-start | bytes 12292
  450.9 34.6 %copy-start.66 = (f32[256]{0:T(256)}, f32[256]{0:T(256)S(1)}, u32[]{:S(2)}) copy-start(f32[256]{0:T(256)S(1)} %get-tuple-element.342) | copy-start | bytes 3076
  451.6 33.9 %copy-start.72 = (f32[256]{0:T(256)}, f32[256]{0:T(256)S(1)}, u32[]{:S(2)}) copy-start(f32[256]{0:T(256)S(1)} %fusion.110) | copy-start | bytes 3076
  451.7 38.9 %copy-start.44 = (f32[256,2]{1,0:T(8,128)}, f32[256,2]{1,0:T(8,128)S(1)}, u32[]{:S(2)}) copy-start(f32[256,2]{1,0:T(8,128)S(1)} %fusion.109) | copy-start | bytes 6148
  495.2 20.1 copy-start.16
  498.3 17.0 copy-start.79
  499.3 417.3 %all-gather.27.cloned.1.call-start = ((), (), s32[]{:S(2)}) async-start(), calls=%async_computation.28 | async-start | bytes 57671680 | tf_op jit(solution)/shard_map/all_gather | solution.py:247
  515.3 613.4 %all-gather.29.cloned.1.call-start = ((), (), s32[]{:S(2)}) async-start(), calls=%async_computation.29 | async-start | bytes 28835840 | tf_op jit(solution)/shard_map/all_gather | solution.py:248
  524.5 635.9 %reduce-scatter.15.cloned.1.call-start = ((), (), s32[]{:S(2)}) async-start(), calls=%async_computation.30 | async-start | bytes 9437184 | tf_op jit(solution)/shard_map/reduce_scatter | solution.py:71
  613.7 332.2 %copy-start.13 = (bf16[8,96,2048]{2,1,0:T(8,128)(2,1)}, bf16[8,96,2048]{2,1,0:T(8,128)(2,1)S(1)}, u32[]{:S(2)}) copy-start(bf16[8,96,2048]{2,1,0:T(8,128)(2,1)S(1)} %all_to_all.40) | copy-start | bytes 9437188
  1163.7 42.3 %all-to-all-start.3 = ((bf16[8,96,1024]{2,1,0:T(8,128)(2,1)}), bf16[8,96,1024]{2,1,0:T(8,128)(2,1)S(1)}, u32[]{:S(2)}, u32[]{:S(2)}) async-start(bf16[8,96,1024]{2,1,0:T(8,128)(2,1)} %bitcast.337), calls=%async_computation.5 | async-start | bytes 3145728 | tf_op jit(solution)/shard_map/all_to_all | solution.py:79
  1168.5 103.1 %all-gather.31.cloned.1.call-start = ((), (), s32[]{:S(2)}) async-start(), calls=%async_computation.31 | async-start | bytes 4718592 | tf_op jit(solution)/shard_map/all_gather | solution.py:67
  1260.3 84.8 %reduce-scatter.17.cloned.1.call-start = ((), (), s32[]{:S(2)}) async-start(), calls=%async_computation.32 | async-start | bytes 9437184 | tf_op jit(solution)/shard_map/reduce_scatter | solution.py:71
  1329.2 23.9 copy-start.63
  1329.2 24.0 copy-start.45
  1329.3 24.1 copy-start.93
  1348.3 42.3 %all-to-all-start.5 = ((bf16[8,96,1024]{2,1,0:T(8,128)(2,1)}), bf16[8,96,1024]{2,1,0:T(8,128)(2,1)S(1)}, u32[]{:S(2)}, u32[]{:S(2)}) async-start(bf16[8,96,1024]{2,1,0:T(8,128)(2,1)} %bitcast.63), calls=%async_computation.8 | async-start | bytes 3145728 | tf_op jit(solution)/shard_map/all_to_all | solution.py:79
  1353.2 130.9 %all-gather.33.cloned.1.call-start = ((), (), s32[]{:S(2)}) async-start(), calls=%async_computation.33 | async-start | bytes 4718592 | tf_op jit(solution)/shard_map/all_gather | solution.py:67
  1353.6 52.3 %copy-start.60 = (bf16[256,8]{0,1:T(8,128)(2,1)}, bf16[256,8]{0,1:T(8,128)(2,1)S(1)}, u32[]{:S(2)}) copy-start(bf16[256,8]{0,1:T(8,128)(2,1)S(1)} %select_reduce_fusion.1) | copy-start | bytes 12292
  1400.7 10.9 copy-start.31
  1472.8 157.2 %reduce-scatter.21.cloned.1.call-start = ((), (), s32[]{:S(2)}) async-start(), calls=%async_computation.35 | async-start | bytes 2621440 | tf_op jit(solution)/shard_map/reduce_scatter | solution.py:418
  1497.2 11.0 copy-start
  1539.1 11.0 copy-start
  1584.8 91.1 %reduce-scatter.19.cloned.1.call-start = ((), (), s32[]{:S(2)}) async-start(), calls=%async_computation.34 | async-start | bytes 2621440 | tf_op jit(solution)/shard_map/reduce_scatter | solution.py:415
  1588.9 176.4 %reduce-scatter.25.cloned.1.call-start = ((), (), s32[]{:S(2)}) async-start(), calls=%async_computation.37 | async-start | bytes 9437184 | tf_op jit(solution)/shard_map/reduce_scatter | solution.py:71
  1602.6 74.5 %copy-start.46 = (f32[256,64]{0,1:T(8,128)S(1)}, f32[256,64]{0,1:T(8,128)}, u32[]{:S(2)}) copy-start(f32[256,64]{0,1:T(8,128)} %get-tuple-element.386) | copy-start | bytes 196612
  1602.6 74.5 %copy-start.47 = (f32[256,64]{0,1:T(8,128)S(1)}, f32[256,64]{0,1:T(8,128)}, u32[]{:S(2)}) copy-start(f32[256,64]{0,1:T(8,128)} %get-tuple-element.388) | copy-start | bytes 196612
  1602.6 222.0 %reduce-scatter.23.cloned.1.call-start = ((), (), s32[]{:S(2)}) async-start(), calls=%async_computation.36 | async-start | bytes 3145728 | tf_op jit(solution)/shard_map/reduce_scatter | solution.py:71
  1684.7 187.9 %reduce-scatter.29.cloned.1.call-start = ((), (), s32[]{:S(2)}) async-start(), calls=%async_computation.39 | async-start | bytes 10485760 | tf_op jit(solution)/shard_map/reduce_scatter | solution.py:454
  1694.0 193.5 %reduce-scatter.31.cloned.1.call-start = ((), (), s32[]{:S(2)}) async-start(), calls=%async_computation.40 | async-start | bytes 10485760 | tf_op jit(solution)/shard_map/reduce_scatter | solution.py:457
  1704.0 392.2 %reduce-scatter.35.cloned.1.call-start = ((), (), s32[]{:S(2)}) async-start(), calls=%async_computation.42 | async-start | bytes 28835840 | tf_op jit(solution)/shard_map/reduce_scatter | solution.py:463
  1723.8 724.8 %reduce-scatter.27.cloned.1.call-start = ((), (), s32[]{:S(2)}) async-start(), calls=%async_computation.38 | async-start | bytes 17825792 | tf_op jit(solution)/shard_map/reduce_scatter | solution.py:467
  1733.5 1107.4 %reduce-scatter.33.cloned.1.call-start = ((), (), s32[]{:S(2)}) async-start(), calls=%async_computation.41 | async-start | bytes 57671680 | tf_op jit(solution)/shard_map/reduce_scatter | solution.py:460
  1768.7 41.6 %copy-start.77 = (s32[1024]{0:T(1024)S(1)}, s32[1024]{0:T(1024)}, u32[]{:S(2)}) copy-start(s32[1024]{0:T(1024)} %copy-done.76) | copy-start | bytes 12292
  1768.7 41.6 %all-to-all-start.7 = ((bf16[8,96,1024]{2,1,0:T(8,128)(2,1)}), bf16[8,96,1024]{2,1,0:T(8,128)(2,1)}, u32[]{:S(2)}, u32[]{:S(2)}) async-start(bf16[8,96,1024]{2,1,0:T(8,128)(2,1)} %bitcast.339), calls=%async_computation.14 | async-start | bytes 3145728 | tf_op jit(solution)/shard_map/all_to_all | solution.py:79
  1773.3 1179.0 %all-reduce.4.cloned.1.call-start = ((), (), s32[]{:S(2)}) async-start(), calls=%async_computation.43 | async-start | bytes 262144 | tf_op jit(solution)/shard_map/psum | solution.py:450
  (75 other events, 385.9 us)
Sparse Core Ops, SparseCore 0:
  14.4 11.6 all-gather.12
  29.4 113.8 all-gather.16
  145.7 85.7 all-gather.14
  233.6 46.0 all-gather.18
  281.1 44.5 all-gather.20
  327.9 86.1 all-gather.22
  423.3 14.4 reduce-scatter.12
  499.4 8.0 all-gather.24
  515.4 401.0 all-gather.26
  918.4 210.3 all-gather.28
  1145.9 14.4 reduce-scatter.14
  1260.4 11.1 all-gather.30
  1329.4 15.6 reduce-scatter.16
  1472.9 11.1 all-gather.32
  1584.9 45.0 reduce-scatter.20
  1632.7 43.1 reduce-scatter.18
  1678.2 13.7 reduce-scatter.24
  1694.7 10.8 reduce-scatter.22
  1709.4 87.5 reduce-scatter.28
  1800.0 87.4 reduce-scatter.30
  1891.5 204.6 reduce-scatter.34
  2098.5 350.0 reduce-scatter.26
  2451.7 389.1 reduce-scatter.32
  2847.7 104.5 all-reduce.3
where the time goes:
time: 2970 us; the launch traced here: 2960 us
  waiting for transfers between devices  1980 us (67%)
  blocking collectives  294 us (10%)
  matrix products  288 us (10%)
  other arithmetic  181 us (6%)
  local copies, waits for them, and re-layouts  174 us (6%)
    reduce_scatter x1, waiting for transfers between devices, shards(): lax.psum_scatter(grad_wgateup.astype(jnp.bfloat16), 'dp', scatter_dimensi...  389 us
    reduce_scatter x1, waiting for transfers between devices, shards(): lax.psum_scatter(grad_wkv, ('dp', 'expert'), scatter_dimension=0, tiled=T...  344 us
    all_gather x1, waiting for transfers between devices, shards(): lax.all_gather(local_gateup, 'dp', axis=1, tiled=True)  303 us
    reduce_scatter x1, waiting for transfers between devices, shards(): lax.psum_scatter(grad_wdown.astype(jnp.bfloat16), 'dp', scatter_dimension...  204 us
    all_gather x1, waiting for transfers between devices, shards(): lax.all_gather(local_down, 'dp', axis=2, tiled=True)  173 us
    all_to_all x3, blocking collectives, to_owner(): lax.all_to_all(values, 'expert', split_axis=0, concat_axis=0, tiled=True)  155 us
    all_to_all x4, waiting for transfers between devices, to_home(): lax.all_to_all(values, 'expert', split_axis=0, concat_axis=0, tiled=True)  124 us
    all_gather x1, waiting for transfers between devices, shards(): lax.all_gather(w_kv.astype(jnp.bfloat16), ('dp', 'expert'), axis=0, tiled...  117 us
  transfers between devices with their start and end apart: 29, of which 22 were waited for; matrix products, arithmetic and copies ran while one was open for 13% of the time, Pallas kernels for 0%

commit v1 on v0

v1 whole, which is shorter than its diff:
```python
import math

import jax
import jax.numpy as jnp
from jax import lax
from jax.sharding import PartitionSpec as P

HD = 128
EPSILON = 1e-06
MASKED = -1000000000.0
F32 = jnp.float32
BF16 = jnp.bfloat16


def dot(lhs, rhs):
    return jnp.dot(lhs, rhs, preferred_element_type=F32)


def ein(spec, lhs, rhs):
    return jnp.einsum(spec, lhs, rhs, preferred_element_type=F32)


def rope_angle(positions):
    half_dim = HD // 2
    frequency = jnp.exp(
        jnp.arange(half_dim, dtype=F32) * (-2.0 * math.log(10000.0) / HD)
    )
    return positions.astype(F32)[:, None] * frequency[None, :]


def rotate(values, cosine, sine):
    half_dim = values.shape[-1] // 2
    cosine = cosine[..., None, :]
    sine = sine[..., None, :]
    first = values[..., :half_dim]
    second = values[..., half_dim:]
    return jnp.concatenate([first * cosine - second * sine, second * cosine + first * sine], -1)


def block_size(row_count):
    return max(d for d in range(1, min(row_count, 512) + 1) if row_count % d == 0)


def swap(values):
    return lax.ppermute(values, "tensor", [(0, 1), (1, 0)])


def a2a(values, axis):
    return lax.all_to_all(values, axis, split_axis=0, concat_axis=0, tiled=True)


def total_over(values, axis):
    count = lax.axis_size(axis)
    step = 1
    while step < count:
        values = values + lax.ppermute(values, axis, [(i, i ^ step) for i in range(count)])
        step *= 2
    return values


def core_sum(values):
    return values + swap(values)


def both_halves(values, core):
    other = swap(values)
    first = jnp.where(core == 0, values, other)
    second = jnp.where(core == 0, other, values)
    return jnp.concatenate([first, second], -1)


def one_hot_slots(routes, experts, capacity):
    token_count = routes.shape[1]
    member = (routes[:, None, :, 0] == experts[None, :, None]) | (
        routes[:, None, :, 1] == experts[None, :, None]
    )
    tokens = jnp.arange(token_count, dtype=jnp.int32)
    upper = (tokens[:, None] < tokens[None, :]).astype(BF16)
    rank = dot(member.astype(BF16), upper).astype(jnp.int32)
    slots = jnp.arange(capacity, dtype=jnp.int32)
    return member[:, :, None, :] & (rank[:, :, None, :] == slots[None, None, :, None])


def masked_scores(query_block, pos_block, seg_block, key_rows, seq_seg, score_scale):
    key_pos = jnp.arange(key_rows.shape[0], dtype=jnp.int32)
    raw = ein("qhd,khd->hqk", query_block, key_rows) * score_scale
    allowed = (seg_block[:, None] == seq_seg[None, :]) & (pos_block[:, None] >= key_pos[None, :])
    return jnp.where(allowed[None], raw, MASKED)


def attend_forward(query_rows, row_pos, row_seg, key_rows, value_rows, seq_seg):
    row_count, head_count, head_dim = query_rows.shape
    block_rows = block_size(row_count)
    score_scale = 1.0 / math.sqrt(head_dim)

    def one_block(pieces):
        query_block, pos_block, seg_block = pieces
        scores = masked_scores(query_block, pos_block, seg_block, key_rows, seq_seg, score_scale)
        row_peak = jnp.max(scores, -1, keepdims=True)
        row_exp = jnp.exp(scores - row_peak)
        row_mass = jnp.sum(row_exp, -1, keepdims=True)
        softmax_rows = (row_exp / row_mass).astype(BF16)
        mixed = ein("hqk,khd->qhd", softmax_rows, value_rows)
        return (mixed.astype(BF16), (row_peak + jnp.log(row_mass))[..., 0])

    mixed, log_mass = lax.map(
        one_block,
        (
            query_rows.reshape(-1, block_rows, head_count, head_dim),
            row_pos.reshape(-1, block_rows),
            row_seg.reshape(-1, block_rows),
        ),
    )
    return (mixed.reshape(row_count, head_count, head_dim), log_mass)


def attend_backward(
    query_rows, row_pos, row_seg, key_rows, value_rows, seq_seg, log_mass, grad_mixed
):
    row_count, head_count, head_dim = query_rows.shape
    block_rows = block_size(row_count)
    score_scale = 1.0 / math.sqrt(head_dim)

    def one_block(carried, pieces):
        grad_keys, grad_values = carried
        query_block, pos_block, seg_block, mass_block, grad_block = pieces
        scores = masked_scores(query_block, pos_block, seg_block, key_rows, seq_seg, score_scale)
        softmax_rows = jnp.exp(scores - mass_block[..., None])
        grad_soft = ein("qhd,khd->hqk", grad_block, value_rows)
        inner_sum = jnp.sum(softmax_rows * grad_soft, -1, keepdims=True)
        grad_scores = (softmax_rows * (grad_soft - inner_sum)).astype(BF16)
        grad_query = ein("hqk,khd->qhd", grad_scores, key_rows) * score_scale
        grad_keys = grad_keys + ein("hqk,qhd->khd", grad_scores, query_block) * score_scale
        grad_values = grad_values + ein("hqk,qhd->khd", softmax_rows.astype(BF16), grad_block)
        return ((grad_keys, grad_values), grad_query)

    zero_keys = jnp.zeros(key_rows.shape, F32)
    pieces = (
        query_rows.reshape(-1, block_rows, head_count, head_dim),
        row_pos.reshape(-1, block_rows),
        row_seg.reshape(-1, block_rows),
        log_mass,
        grad_mixed.reshape(-1, block_rows, head_count, head_dim),
    )
    (grad_keys, grad_values), grad_query = lax.scan(one_block, (zero_keys, zero_keys), pieces)
    return (grad_query.reshape(row_count, head_count, head_dim), grad_keys, grad_values)


def shards(
    tokens,
    norm_attn,
    norm_mlp,
    w_kv,
    router_attn,
    router_mlp,
    w_query,
    w_output,
    w_gateup,
    w_down,
    segments,
    att_routes,
    mlp_routes,
    cotangent,
):
    count, width = tokens.shape
    full_width = 2 * width
    planes = lax.axis_size("expert")
    columns = lax.axis_size("dp")
    plane = lax.axis_index("expert")
    column = lax.axis_index("dp")
    core = lax.axis_index("tensor")
    n_att = router_attn.shape[1]
    n_mlp = router_mlp.shape[1]
    local_att = w_query.shape[0]
    local_mlp = w_gateup.shape[0]
    ff_parts = columns // local_mlp
    depth = w_gateup.shape[1]
    ff_core = w_gateup.shape[3]
    ff = ff_core // ff_parts
    cap = 3 * count // 8
    seq = planes * count
    feats = w_query.shape[2]
    heads = feats // HD
    kv_part = feats // planes
    part_heads = kv_part // HD
    mlp_expert = plane * local_mlp + column % local_mlp

    ints = jnp.stack(
        [segments, att_routes[:, 0], att_routes[:, 1], mlp_routes[:, 0], mlp_routes[:, 1]]
        + [segments] * 3,
        0,
    )
    all_ints = lax.all_gather(ints, ("dp", "expert"), axis=0, tiled=False).reshape(
        columns, planes, 8, count
    )
    seq_ints = lax.dynamic_index_in_dim(all_ints, column, 0, keepdims=False)
    seq_seg = seq_ints[:, 0].reshape(seq)
    seq_att = jnp.stack([seq_ints[:, 1], seq_ints[:, 2]], -1)
    every_mlp = jnp.stack([all_ints[:, :, 3], all_ints[:, :, 4]], -1).reshape(-1, count, 2)

    seq_tokens = lax.all_gather(tokens, "expert", axis=0, tiled=True)
    residual = tokens.astype(F32)

    def rms_scale(values):
        return lax.rsqrt(
            core_sum(jnp.sum(values * values, 1, keepdims=True)) / full_width + EPSILON
        )

    scale_a = rms_scale(residual)
    rows_a_half = (residual * scale_a * norm_attn).astype(BF16)
    seq_res = seq_tokens.astype(F32)
    seq_scale = rms_scale(seq_res)
    seq_a_half = (seq_res * seq_scale * norm_attn).astype(BF16)
    seq_a = both_halves(seq_a_half, core)

    kv_local = (
        w_kv.astype(BF16).reshape(w_kv.shape[0], 2, planes, kv_part).transpose(2, 0, 1, 3)
    )
    kv_local = a2a(kv_local, "expert")
    w_kv_part = lax.all_gather(kv_local, "dp", axis=0, tiled=True).reshape(
        full_width, 2 * kv_part
    )
    kv_raw = dot(seq_a, w_kv_part)
    angles = rope_angle(jnp.arange(seq, dtype=jnp.int32))
    cos_seq, sin_seq = jnp.cos(angles), jnp.sin(angles)
    key_part = rotate(kv_raw[:, :kv_part].reshape(seq, part_heads, HD), cos_seq, sin_seq)
    kv_part_rows = jnp.stack(
        [key_part.astype(BF16), kv_raw[:, kv_part:].reshape(seq, part_heads, HD).astype(BF16)], 0
    )
    kv_rows = lax.all_gather(kv_part_rows, "expert", axis=2, tiled=True)
    key_rows, value_rows = kv_rows[0], kv_rows[1]

    whole_query = lax.all_gather(w_query.astype(BF16), "dp", axis=1, tiled=True)
    whole_output = lax.all_gather(w_output.astype(BF16), "dp", axis=2, tiled=True)

    gu_send = (
        w_gateup.reshape(local_mlp, depth, 2, ff_parts, ff)
        .transpose(3, 0, 1, 2, 4)
        .astype(BF16)
        .reshape(columns, depth, 2 * ff)
    )
    w_gu = a2a(gu_send, "dp").reshape(full_width, 2 * ff)
    down_send = (
        w_down.reshape(local_mlp, ff_parts, ff, depth)
        .transpose(1, 0, 2, 3)
        .astype(BF16)
        .reshape(columns, ff, depth)
    )
    w_dn = a2a(down_send, "dp")

    own_att = jnp.arange(local_att, dtype=jnp.int32) + plane * local_att
    att_slots = one_hot_slots(seq_att, own_att, cap)
    home_att = one_hot_slots(att_routes[None], jnp.arange(n_att, dtype=jnp.int32), cap)[0]
    home_mlp = one_hot_slots(mlp_routes[None], jnp.arange(n_mlp, dtype=jnp.int32), cap)[0]
    mlp_slots = one_hot_slots(every_mlp, mlp_expert[None], cap)[:, 0]
    other_expert = jnp.sum(every_mlp, -1) - mlp_expert
    row_other = jnp.sum(jnp.where(mlp_slots, other_expert[:, None, :], 0), -1).reshape(-1)

    def by_choice(home, routes):
        experts = home.shape[0]
        named = routes.T[:, None, :] == jnp.arange(experts, dtype=jnp.int32)[None, :, None]
        picks = home[None] & named[:, :, None, :]
        return picks.astype(BF16).reshape(2, experts * cap, count)

    pick_att = by_choice(home_att, att_routes)
    pick_mlp = by_choice(home_mlp, mlp_routes)
    flat_att = home_att.astype(BF16).reshape(n_att * cap, count)
    flat_mlp = home_mlp.astype(BF16).reshape(n_mlp * cap, count)
    seq_pos = jnp.arange(seq, dtype=jnp.int32).reshape(planes, 1, 1, count)
    row_pos = jnp.sum(jnp.where(att_slots, seq_pos, 0), -1).reshape(-1)
    row_seg = jnp.sum(
        jnp.where(att_slots, seq_seg.reshape(planes, 1, 1, count), 0), -1
    ).reshape(-1)
    att_rows = planes * local_att * cap

    def to_expert(rows_half):
        held = a2a(rows_half.reshape(planes, local_mlp * cap, width), "expert")
        held = held.reshape(planes, local_mlp, cap, width).transpose(1, 0, 2, 3)
        sent = jnp.broadcast_to(
            held[None], (ff_parts, local_mlp, planes, cap, width)
        ).reshape(columns, planes * cap, width)
        return both_halves(a2a(sent, "dp").reshape(-1, width), core)

    grad_rows_out = to_expert(dot(flat_mlp, cotangent).astype(BF16))
    grad_hidden_raw = ein("rsd,sfd->rf", grad_rows_out.reshape(-1, columns, depth), w_dn)

    def gates_of(half_rows, router, routes):
        part = lax.dynamic_slice_in_dim(router, core * width, width, 0).astype(BF16)
        logits = core_sum(ein("de,td->et", part, half_rows))
        experts = router.shape[1]
        named = (
            routes.T[:, None, :] == jnp.arange(experts, dtype=jnp.int32)[None, :, None]
        ).astype(F32)
        chosen = jnp.sum(named * logits[None], 1)
        return jax.nn.softmax(chosen, axis=0), named, part

    gates_a, named_a, router_a = gates_of(rows_a_half, router_attn, att_routes)
    held_a = ein(
        "slct,std->lscd", att_slots.astype(BF16), seq_a.reshape(planes, count, full_width)
    ).astype(BF16)
    held_a = held_a.reshape(local_att, planes * cap, full_width)
    pos_rows = row_pos.reshape(planes, local_att, cap).transpose(1, 0, 2).reshape(-1)
    seg_rows = row_seg.reshape(planes, local_att, cap).transpose(1, 0, 2).reshape(-1)
    angle_rows = rope_angle(pos_rows)
    cos_rows, sin_rows = jnp.cos(angle_rows), jnp.sin(angle_rows)
    query_raw = ein("lrd,ldf->lrf", held_a, whole_query)
    query_rows = rotate(query_raw.reshape(att_rows, heads, HD), cos_rows, sin_rows).astype(BF16)
    mixed_rows, log_mass = attend_forward(
        query_rows, pos_rows, seg_rows, key_rows, value_rows, seq_seg
    )
    mixed_owner = mixed_rows.reshape(local_att, planes * cap, feats)

    def halves(values, axis):
        mine = lax.dynamic_slice_in_dim(values, core * width, width, axis)
        theirs = lax.dynamic_slice_in_dim(values, (1 - core) * width, width, axis)
        return mine, theirs

    def att_home(rows):
        sent = rows.astype(BF16).reshape(local_att, planes, cap, width).transpose(1, 0, 2, 3)
        return a2a(sent.reshape(planes, local_att * cap, width), "expert").reshape(-1, width)

    out_mine, out_theirs = halves(whole_output, 2)
    given = swap(ein("lrf,lfd->lrd", mixed_owner, out_theirs).astype(BF16))
    branch_a = ein("lrf,lfd->lrd", mixed_owner, out_mine) + given.astype(F32)
    home_a = att_home(branch_a)
    taken_a = ein("jst,sd->jtd", pick_att, home_a)
    middle = residual + jnp.sum(gates_a[:, :, None] * taken_a, 0)

    scale_b = rms_scale(middle)
    rows_b_half = (middle * scale_b * norm_mlp).astype(BF16)
    gates_b, named_b, router_b = gates_of(rows_b_half, router_mlp, mlp_routes)
    held_b = to_expert(dot(flat_mlp, rows_b_half).astype(BF16))
    gate_up = dot(held_b, w_gu)
    row_logits = dot(held_b, router_mlp.astype(BF16))
    expert_ids = jnp.arange(n_mlp, dtype=jnp.int32)[None, :]
    own_logit = jnp.sum(jnp.where(expert_ids == mlp_expert, row_logits, 0.0), 1, keepdims=True)
    other_logit = jnp.sum(
        jnp.where(expert_ids == row_other[:, None], row_logits, 0.0), 1, keepdims=True
    )
    row_gate = jax.nn.sigmoid(own_logit - other_logit)
    gate_part = gate_up[:, :ff]
    up_part = gate_up[:, ff:]
    sig = jax.nn.sigmoid(gate_part)
    silu = gate_part * sig
    hidden32 = silu * up_part
    hidden = hidden32.astype(BF16)
    hidden_gated = (hidden32 * row_gate).astype(BF16)
    row_dgate = jnp.sum(hidden32 * grad_hidden_raw, 1)
    grad_hidden = grad_hidden_raw * row_gate
    grad_gate = (grad_hidden * up_part * sig * (1.0 + gate_part * (1.0 - sig))).astype(BF16)
    grad_up = (grad_hidden * silu).astype(BF16)
    grad_both = jnp.concatenate([grad_gate, grad_up], 1)

    def mlp_home(rows):
        tail = rows.shape[1:]
        got = a2a(rows.reshape((columns, planes * cap) + tail), "dp")
        got = got.reshape((ff_parts, local_mlp, planes, cap) + tail).astype(F32)
        summed = jnp.sum(got, 0).swapaxes(0, 1).astype(rows.dtype)
        back = a2a(summed.reshape((planes, local_mlp * cap) + tail), "expert")
        return back.reshape((n_mlp * cap,) + tail)

    dgate_home = mlp_home(core_sum(row_dgate))
    gu_mine, gu_theirs = halves(w_gu, 0)
    given = swap(ein("rf,df->rd", grad_both, gu_theirs).astype(BF16))
    copies = (ein("rf,df->rd", grad_both, gu_mine) + given.astype(F32)).astype(BF16)
    home_db = mlp_home(copies)

    def gates_back(gates, grad_gates, named):
        chosen = gates * (grad_gates - jnp.sum(gates * grad_gates, 0, keepdims=True))
        return jnp.sum(chosen[:, None, :] * named, 0).astype(BF16)

    grad_gates_b = jnp.sum(pick_mlp.astype(F32) * dgate_home[None, :, None], 1)
    grad_logit_b = gates_back(gates_b, grad_gates_b, named_b)
    grad_normed_b = ein("st,sd->td", flat_mlp, home_db) + ein("et,de->td", grad_logit_b, router_b)
    grad_router_b = ein("et,td->ed", grad_logit_b, rows_b_half)

    def normalize_back(values, gain, row_scale, grad_normed):
        inner = core_sum(jnp.sum(grad_normed * gain * values, 1, keepdims=True))
        grad_values = (
            row_scale * gain * grad_normed
            - values * (row_scale * row_scale * row_scale) * inner / full_width
        )
        return grad_values, jnp.sum(grad_normed * values * row_scale, 0)

    grad_out = cotangent.astype(F32)
    grad_mid_norm, grad_gain_b = normalize_back(middle, norm_mlp, scale_b, grad_normed_b)
    grad_middle = grad_out + grad_mid_norm

    grad_gates_a = core_sum(jnp.sum(grad_middle[None] * taken_a, 2))
    grad_logit_a = gates_back(gates_a, grad_gates_a, named_a)
    grad_taken_a = (gates_a[:, :, None] * grad_middle[None]).astype(BF16)
    sent_a = ein("jst,jtd->sd", pick_att, grad_taken_a).astype(BF16)
    held_grad_a = both_halves(
        a2a(sent_a.reshape(planes, local_att * cap, width), "expert").reshape(-1, width), core
    )
    held_grad_a = (
        held_grad_a.reshape(planes, local_att, cap, full_width)
        .transpose(1, 0, 2, 3)
        .reshape(local_att, planes * cap, full_width)
    )
    grad_mixed = ein("lrd,lfd->lrf", held_grad_a, whole_output).astype(BF16)
    grad_query_rot, grad_keys, grad_values = attend_backward(
        query_rows,
        pos_rows,
        seg_rows,
        key_rows,
        value_rows,
        seq_seg,
        log_mass,
        grad_mixed.reshape(att_rows, heads, HD),
    )
    grad_query_raw = (
        rotate(grad_query_rot, cos_rows, -sin_rows)
        .astype(BF16)
        .reshape(local_att, planes * cap, feats)
    )
    grad_kv_seq = jnp.stack([grad_keys, grad_values], 0).astype(BF16)
    grad_kv_part = lax.psum_scatter(
        grad_kv_seq, "expert", scatter_dimension=2, tiled=True
    ).astype(F32)
    grad_kv = jnp.concatenate(
        [
            rotate(grad_kv_part[0], cos_seq, -sin_seq).reshape(seq, kv_part),
            grad_kv_part[1].reshape(seq, kv_part),
        ],
        1,
    ).astype(BF16)
    query_mine, query_theirs = halves(whole_query, 1)
    kv_mine, kv_theirs = halves(w_kv_part, 0)

    def grad_seq(query_half, kv_half):
        rows = ein("lrf,ldf->lrd", grad_query_raw, query_half).astype(BF16)
        spread = ein(
            "slct,lscd->std",
            att_slots.astype(BF16),
            rows.reshape(local_att, planes, cap, width),
        )
        return spread.reshape(seq, width) + ein("tf,df->td", grad_kv, kv_half)

    given = swap(grad_seq(query_theirs, kv_theirs).astype(BF16))
    grad_seq_a = (grad_seq(query_mine, kv_mine) + given.astype(F32)).astype(BF16)
    grad_rows_a = lax.psum_scatter(
        grad_seq_a, "expert", scatter_dimension=0, tiled=True
    ).astype(F32)
    grad_normed_a = grad_rows_a + ein("et,de->td", grad_logit_a, router_a)
    grad_router_a = ein("et,td->ed", grad_logit_a, rows_a_half)
    grad_in_norm, grad_gain_a = normalize_back(residual, norm_attn, scale_a, grad_normed_a)
    grad_tokens = grad_middle + grad_in_norm

    grad_gu = ein("rd,rf->df", held_b, grad_both).astype(BF16)
    got_gu = a2a(grad_gu.reshape(columns, depth, 2 * ff), "dp")
    grad_wgateup = (
        got_gu.reshape(ff_parts, local_mlp, depth, 2, ff)
        .transpose(1, 2, 3, 0, 4)
        .astype(F32)
        .reshape(w_gateup.shape)
    )
    grad_dn = ein(
        "rf,rsd->sfd", hidden_gated, grad_rows_out.reshape(-1, columns, depth)
    ).astype(BF16)
    got_dn = a2a(grad_dn, "dp")
    grad_wdown = (
        got_dn.reshape(ff_parts, local_mlp, ff, depth)
        .transpose(1, 0, 2, 3)
        .astype(F32)
        .reshape(w_down.shape)
    )
    grad_woutput = lax.psum_scatter(
        ein("lrf,lrd->lfd", mixed_owner, held_grad_a).astype(BF16),
        "dp",
        scatter_dimension=2,
        tiled=True,
    ).astype(F32)
    grad_wquery = lax.psum_scatter(
        ein("lrd,lrf->ldf", held_a, grad_query_raw).astype(BF16),
        "dp",
        scatter_dimension=1,
        tiled=True,
    ).astype(F32)
    grad_kv_w = lax.psum_scatter(
        ein("td,tf->df", seq_a, grad_kv).astype(BF16), "dp", scatter_dimension=0, tiled=True
    )
    grad_kv_w = a2a(grad_kv_w.reshape(planes, w_kv.shape[0], 2, kv_part), "expert")
    grad_wkv = grad_kv_w.transpose(1, 2, 0, 3).astype(F32).reshape(w_kv.shape)

    dn_lo = w_dn.reshape(2, columns // 2, ff, depth)
    dn_mine = lax.dynamic_index_in_dim(dn_lo, core, 0, keepdims=False)
    dn_theirs = lax.dynamic_index_in_dim(dn_lo, 1 - core, 0, keepdims=False)
    rows_total = held_b.shape[0]

    def branch_half(weights):
        return ein("rf,sfd->rsd", hidden, weights).reshape(rows_total, width)

    given = swap(branch_half(dn_theirs).astype(BF16))
    branch_b = (branch_half(dn_mine) + given.astype(F32)).astype(BF16)
    home_b = mlp_home(branch_b)
    taken_b = ein("jst,sd->jtd", pick_mlp, home_b)
    output = middle + jnp.sum(gates_b[:, :, None] * taken_b, 0)

    small = jnp.concatenate(
        [grad_router_a, grad_router_b, grad_gain_a[None], grad_gain_b[None]], 0
    )
    small = total_over(total_over(small, "dp"), "expert")
    routers = both_halves(small[: n_att + n_mlp], core)
    return (
        output.astype(BF16),
        grad_tokens,
        small[n_att + n_mlp],
        small[n_att + n_mlp + 1],
        grad_wkv,
        routers[:n_att].T,
        routers[n_att:].T,
        grad_wquery,
        grad_woutput,
        grad_wgateup,
        grad_wdown,
    )


def solution(mesh):
    in_specs = (
        P(("dp", "expert"), "tensor"),
        P("tensor"),
        P("tensor"),
        P(("dp", "expert"), None, "tensor"),
        P(),
        P(),
        P("expert", "dp", "tensor"),
        P("expert", "tensor", "dp"),
        P("expert", "dp", None, "tensor"),
        P("expert", "tensor", "dp"),
        P(("dp", "expert")),
        P(("dp", "expert"), None),
        P(("dp", "expert"), None),
        P(("dp", "expert"), "tensor"),
    )
    out_specs = (
        P(("dp", "expert"), "tensor"),
        P(("dp", "expert"), "tensor"),
        P("tensor"),
        P("tensor"),
        P(("dp", "expert"), None, "tensor"),
        P(),
        P(),
        P("expert", "dp", "tensor"),
        P("expert", "tensor", "dp"),
        P("expert", "dp", None, "tensor"),
        P("expert", "tensor", "dp"),
    )
    return jax.shard_map(shards, mesh=mesh, in_specs=in_specs, out_specs=out_specs, check_vma=False)
```

time: 2970 us -> 1860 us (0.63)
  waiting for transfers between devices: 1980 us -> 933 us
  blocking collectives: 294 us -> 122 us
  local copies, waits for them, and re-layouts: 174 us -> 280 us
  other arithmetic: 181 us -> 119 us
  starting transfers between devices: 24.7 us -> 80.9 us
    reduce_scatter x12 -> x4, waiting for transfers between devices: 1060 us -> 0.01 us  [the longest x1 0.01 us: shards(): lax.psum_scatter(grad_seq_a, 'expert', scatter_dimension=0, tiled=True)]
    all_gather x11 -> x5, waiting for transfers between devices: 705 us -> 183 us  [the longest x1 76.4 us: shards(): whole_query = lax.all_gather(w_query.astype(BF16), 'dp', axis=1, tiled=True)]
    all_to_all x5 -> x15, waiting for transfers between devices: 124 us -> 414 us  [a2a(): return lax.all_to_all(values, axis, split_axis=0, concat_axis=0, tiled=True)]
    ppermute x0 -> x22, waiting for transfers between devices: none -> 199 us  [the longest x4 182 us: total_over(): lax.ppermute(values, axis, [(i, i ^ step) for i in range(count)])]
    unnamed x24 -> x11, waiting for transfers between devices: 0.39 us -> 137 us
    reshape x2 -> x12, local copies, waits for them, and re-layouts: 0.15 us -> 124 us  [the longest x3 97.6 us: shards(): grad_wgateup = got_gu.reshape(ff_parts, local_mlp, depth, 2, ff).transpos...]
    psum x1 -> x0, waiting for transfers between devices: 88.1 us -> none  [shards(): lax.psum((grad_router_a, grad_router_b, grad_gain_a, grad_gain_b), ('dp',...]
    all_to_all x3, blocking collectives: 155 us -> 78.2 us  [a2a(): return lax.all_to_all(values, axis, split_axis=0, concat_axis=0, tiled=True)]
  transfers between devices with their start and end apart: 29 -> 47, of which waited for: 22 -> 28; matrix products, arithmetic and copies ran while one was open for 13% -> 27% of each run, Pallas kernels for 0% -> 0%
where the time goes in v1:
time: 1860 us; the launch traced here: 1850 us
  waiting for transfers between devices  933 us (50%)
  matrix products  296 us (16%)
  local copies, waits for them, and re-layouts  280 us (15%)
  blocking collectives  122 us (7%)
  other arithmetic  119 us (6%)
  starting transfers between devices  80.9 us (4%)
    all_to_all x15, waiting for transfers between devices, a2a(): return lax.all_to_all(values, axis, split_axis=0, concat_axis=0, tiled=True)  414 us
    dot_general x45, matrix products, ein(): return jnp.einsum(spec, lhs, rhs, preferred_element_type=F32)  267 us
    ppermute x4, waiting for transfers between devices, total_over(): lax.ppermute(values, axis, [(i, i ^ step) for i in range(count)])  182 us
    unnamed x11, waiting for transfers between devices  137 us
    reshape x3, local copies, waits for them, and re-layouts, shards(): grad_wgateup = got_gu.reshape(ff_parts, local_mlp, depth, 2, ff).transpos...  97.6 us
    all_to_all x3, blocking collectives, a2a(): return lax.all_to_all(values, axis, split_axis=0, concat_axis=0, tiled=True)  78.2 us
    all_gather x1, waiting for transfers between devices, shards(): whole_query = lax.all_gather(w_query.astype(BF16), 'dp', axis=1, tiled=True)  76.4 us
    all_to_all x15, starting transfers between devices, a2a(): return lax.all_to_all(values, axis, split_axis=0, concat_axis=0, tiled=True)  69.2 us
  transfers between devices with their start and end apart: 47, of which 28 were waited for; matrix products, arithmetic and copies ran while one was open for 27% of the time, Pallas kernels for 0%

profile of v1, /device:TPU:0, one launch (start us, length us, event | category | flops | bytes accessed | tf_op | source)
XLA Modules:
  0.0 1846.8 jit_solution(4024647821339229838)
XLA Ops:
  9.5 32.0 %all_to_all.99 = bf16[4,128,2,256]{1,3,2,0:T(8,128)(2,1)S(1)} all-to-all(bf16[4,128,2,256]{1,3,2,0:T(8,128)(2,1)S(1)} %copy.413), channel_id=1, replica_groups=mesh['dp'=4,'expert'=4,'tensor'=2] {'expert'}, dimensions={0} | all-to-all | bytes 1048576 | tf_op jit(solution)/shard_map/all_to_all | solution.py:49
  42.6 21.8 %all-gather.7.cloned.1.call-done = bf16[1024,1024]{1,0:T(8,128)(2,1)} async-done(((bf16[256,1024]{1,0:T(8,128)(2,1)}), bf16[1024,1024]{1,0:T(8,128)(2,1)}) %all-gather.7.cloned.1.call-update) | async-done | bytes 2097168 | tf_op jit(solution)/shard_map/all_gather | solution.py:201
  71.7 29.6 %all-gather.11.cloned.1.call-done = bf16[16,128,2,256]{3,1,2,0:T(8,128)(2,1)} async-done(((bf16[4,128,2,256]{3,1,2,0:T(8,128)(2,1)}), bf16[16,128,2,256]{3,1,2,0:T(8,128)(2,1)}) %all-gather.11.cloned.1.call-update) | async-done | bytes 2097168 | tf_op jit(solution)/shard_map/all_gather | solution.py:220
  120.3 43.3 %all-gather = s32[128,256]{1,0:T(8,128)S(1)} all-gather(s32[8,256]{1,0:T(8,128)S(1)} %stack.28), channel_id=2, replica_groups=mesh['dp'=4,'expert'=4,'tensor'=2] {'dp','expert'}, dimensions={0}, use_global_device_ids=true | all-gather | bytes 139264 | tf_op jit(solution)/shard_map/all_gather | solution.py:193
  172.5 23.2 %all-gather.13.cloned.1.call-done = bf16[2,1024,8,128]{1,3,2,0:T(8,128)(2,1)} async-done(((bf16[2,1024,2,128]{1,3,2,0:T(8,128)(2,1)}), bf16[2,1024,8,128]{1,3,2,0:T(8,128)(2,1)}) %all-gather.13.cloned.1.call-update) | async-done | bytes 4194320 | tf_op jit(solution)/shard_map/all_gather | solution.py:230
  207.8 76.4 %all-gather.9.cloned.1.call-done = bf16[2,2048,1024]{2,1,0:T(8,128)(2,1)} async-done(((bf16[2,512,1024]{2,1,0:T(8,128)(2,1)}), bf16[2,2048,1024]{2,1,0:T(8,128)(2,1)}) %all-gather.9.cloned.1.call-update) | async-done | bytes 8388624 | tf_op jit(solution)/shard_map/all_gather | solution.py:233
  284.2 6.7 fusion.170
  310.7 31.0 %while.27 = (s32[]{:T(128)}, bf16[2,384,8,128]{1,3,2,0:T(8,128)(2,1)}, f32[2,8,384]{2,1,0:T(8,128)S(1)}, s32[2,384]{1,0:T(2,128)S(1)}, s32[4,1,256]{2,1,0:T(1,12...) while((s32[]{:T(128)}, ...), condition=%wide.region_10.11_spmd, body=%wide.region_7.10_spmd.sunk | while | flops 1649931264 | bytes 56734872 | solution.py:106
  318.3 5.4 fusion.239
  333.7 5.4 fusion.239
  341.7 32.4 %all-gather.15.cloned.1.call-done = bf16[2,1024,2048]{2,1,0:T(8,128)(2,1)} async-done(((bf16[2,1024,512]{2,1,0:T(8,128)(2,1)}), bf16[2,1024,2048]{2,1,0:T(8,128)(2,1)}) %all-gather.15.cloned.1.call-update) | async-done | bytes 8388624 | tf_op jit(solution)/shard_map/all_gather | solution.py:234
  374.1 5.6 fusion.68
  383.6 5.0 add_convert_fusion.3
  398.7 33.0 %all-to-all-done.1 = bf16[4,192,1024]{2,1,0:T(8,128)(2,1)S(1)} async-done(((bf16[4,192,1024]{2,1,0:T(8,128)(2,1)}), bf16[4,192,1024]{2,1,0:T(8,128)(2,1)S(1)}, u32[]{:S(2)}, u32[]{:S(2)}) %all-to-all-start.1) | async-done | bytes 1572896 | tf_op jit(solution)/shard_map/all_to_all | solution.py:49
  448.3 25.1 %all-to-all-done.8 = bf16[4,192,1024]{2,1,0:T(8,128)(2,1)S(1)} async-done(((bf16[4,192,1024]{2,1,0:T(8,128)(2,1)}), bf16[4,192,1024]{2,1,0:T(8,128)(2,1)S(1)}, u32[]{:S(2)}, u32[]{:S(2)}) %all-to-all-start.8) | async-done | bytes 1572896 | tf_op jit(solution)/shard_map/all_to_all | solution.py:49
  479.1 35.2 %all-to-all-done.2 = bf16[4,192,1024]{2,1,0:T(8,128)(2,1)} async-done(((bf16[4,192,1024]{2,1,0:T(8,128)(2,1)}), bf16[4,192,1024]{2,1,0:T(8,128)(2,1)}, u32[]{:S(2)}, u32[]{:S(2)}) %all-to-all-start.2) | async-done | bytes 1572896 | tf_op jit(solution)/shard_map/all_to_all | solution.py:49
  524.1 32.9 %all-to-all-done.9 = bf16[4,384,1024]{2,1,0:T(8,128)(2,1)S(1)} async-done(((bf16[4,384,1024]{2,1,0:T(8,128)(2,1)}), bf16[4,384,1024]{2,1,0:T(8,128)(2,1)S(1)}, u32[]{:S(2)}, u32[]{:S(2)}) %all-to-all-start.9) | async-done | bytes 3145760 | tf_op jit(solution)/shard_map/all_to_all | solution.py:49
  565.2 30.4 %copy.428 = bf16[2,512,2,2816]{1,3,2,0:T(8,128)(2,1)} copy(f32[2,512,2,2816]{3,2,1,0:T(2,128)} %param.26) | data formatting | bytes 34603008 | tf_op args[8]
  595.5 9.9 copy.429
  605.4 6.2 all-to-all-start.4
  619.2 5.0 convert_element_type.348
  627.4 5.4 broadcast_select_fusion.1
  632.8 104.3 %all-to-all-done.4 = bf16[4,512,2816]{1,2,0:T(8,128)(2,1)} async-done(((bf16[4,512,2816]{1,2,0:T(8,128)(2,1)}), bf16[4,512,2816]{1,2,0:T(8,128)(2,1)}, u32[]{:S(2)}, u32[]{:S(2)}) %all-to-all-start.4) | async-done | bytes 11534368 | tf_op jit(solution)/shard_map/all_to_all | solution.py:49
  737.1 5.3 all-to-all-start.5
  742.5 5.9 pad_maximum_fusion.2
  748.3 16.1 copy.430
  772.1 21.2 %fusion.67 = f32[1536,2816]{1,0:T(8,128)} fusion(bf16[2048,2816]{1,0:T(8,128)(2,1)S(1)} %bitcast.384, bf16[1536,1024]{0,1:T(8,128)(2,1)S(1)} %get-tuple-element.431, bf16[1536,1024]{0,1:T(8,128)(2,1)S(1)} %get-tuple-element.430), kind=kOutput, calls=%fused_computation.133 | convolution fusion | flops 17729323008 | bytes 35127296 | tf_op jit(solution)/shard_map/dot_general | solution.py:16
  793.2 12.9 all-to-all-done.5
  806.1 24.6 %multiply_convert_fusion.3 = (bf16[1536,1408]{1,0:T(8,128)(2,1)}, bf16[1536,1408]{1,0:T(8,128)(2,1)}, f32[1536]{0:T(1024)S(1)}, f32[1536,1408]{1,0:T(8,128)}) fusion(f32[1536,2816]{1,0:T(8,128)} %fusion.67, f32[1536]{0:T(1024)S(1)} %add_divide_fusion.1, bf16[1536,4,512]{0,2,1:T(8,128)(2,1)} %bitcast.390, bf16[4,1408,512]{2,1,0:T(8,128)(2,1)} %all-to-all-done.5), kind=kOutput, calls=%fused_computation.59 | convolution fusion | flops 8895133696 | bytes 46673920 | tf_op jit(solution)/shard_map/rsd,sfd->rf/dot_general | solution.py:20
  830.7 14.4 fusion.55
  852.7 9.9 convolution_convert_fusion.3
  863.1 5.2 collective-permute-done.11
  868.3 7.2 all_to_all.100
  879.6 14.9 add_convert_fusion
  902.8 10.0 add_convert_fusion.1
  912.8 20.7 %all-to-all-done.10 = bf16[4,384,1024]{2,1,0:T(8,128)(2,1)S(1)} async-done(((bf16[4,384,1024]{2,1,0:T(8,128)(2,1)}), bf16[4,384,1024]{2,1,0:T(8,128)(2,1)S(1)}, u32[]{:S(2)}, u32[]{:S(2)}) %all-to-all-start.10) | async-done | bytes 3145760 | tf_op jit(solution)/shard_map/all_to_all | solution.py:49
  943.2 30.6 %all-to-all-done.6 = bf16[4,384,1024]{2,1,0:T(8,128)(2,1)} async-done(((bf16[4,384,1024]{2,1,0:T(8,128)(2,1)}), bf16[4,384,1024]{2,1,0:T(8,128)(2,1)}, u32[]{:S(2)}, u32[]{:S(2)}) %all-to-all-start.6) | async-done | bytes 3145760 | tf_op jit(solution)/shard_map/all_to_all | solution.py:49
  982.8 32.0 %all-to-all-done.11 = bf16[4,192,1024]{2,1,0:T(8,128)(2,1)} async-done(((bf16[4,192,1024]{2,1,0:T(8,128)(2,1)}), bf16[4,192,1024]{2,1,0:T(8,128)(2,1)}, u32[]{:S(2)}, u32[]{:S(2)}) %all-to-all-start.11) | async-done | bytes 1572896 | tf_op jit(solution)/shard_map/all_to_all | solution.py:49
  1025.2 30.4 %all-to-all-done.7 = bf16[4,192,1024]{2,1,0:T(8,128)(2,1)} async-done(((bf16[4,192,1024]{2,1,0:T(8,128)(2,1)}), bf16[4,192,1024]{2,1,0:T(8,128)(2,1)}, u32[]{:S(2)}, u32[]{:S(2)}) %all-to-all-start.7) | async-done | bytes 1572896 | tf_op jit(solution)/shard_map/all_to_all | solution.py:49
  1060.6 39.0 %all_to_all.101 = bf16[4,192,1024]{2,1,0:T(8,128)(2,1)S(1)} all-to-all(bf16[4,192,1024]{2,1,0:T(8,128)(2,1)S(1)} %bitcast.429), channel_id=1, replica_groups=mesh['dp'=4,'expert'=4,'tensor'=2] {'expert'}, dimensions={0} | all-to-all | bytes 3145728 | tf_op jit(solution)/shard_map/all_to_all | solution.py:49
  1113.0 87.1 %while.28 = (s32[]{:T(128)}, f32[1024,8,128]{0,2,1:T(8,128)}, f32[1024,8,128]{0,2,1:T(8,128)}, f32[2,384,8,128]{3,2,1,0:T(8,128)}, bf16[2,384,8,128]{3,1,2,0:T(8...) while((s32[]{:T(128)}, f32[1024,8,128]{0,2,1:T(8,128)}, ...), condition=%wide.region_30.31_spmd.clone, body=%wide.region_28.30_spmd.clone.sunk | while | flops 4080530432 | bytes 285836608 | solution.py:145
  1116.9 10.4 multiply_reduce_fusion.11
  1127.3 9.6 multiply_convert_fusion.8
  1136.8 6.7 bitcast_add_fusion.6
  1145.0 5.6 bitcast_add_fusion.7
  1158.8 10.4 multiply_reduce_fusion.11
  1169.2 9.6 multiply_convert_fusion.8
  1178.8 7.9 bitcast_add_fusion.6
  1188.1 7.3 bitcast_add_fusion.7
  1222.8 135.8 %all-reduce.3.cloned.1.call-done = bf16[2,1024,8,128]{1,3,2,0:T(8,128)(2,1)} async-done(((bf16[2,1024,8,128]{1,3,2,0:T(8,128)(2,1)}), bf16[2,1024,8,128]{1,3,2,0:T(8,128)(2,1)}) %all-reduce.3.cloned.1.call-update) | async-done | bytes 4194320
  1371.1 5.3 convolution_convert_fusion.5
  1376.5 10.2 convolution_convert_fusion.2
  1388.0 8.6 convolution_convert_fusion.1
  1397.3 16.3 convert_bitcast_fusion.1
  1413.6 5.6 all-to-all-start.17
  1419.2 25.3 %convolution_convert_fusion = bf16[2048,2816]{1,0:T(8,128)(2,1)} fusion(bf16[1536,1408]{1,0:T(8,128)(2,1)} %get-tuple-element.427, bf16[1536,1408]{1,0:T(8,128)(2,1)} %get-tuple-element.426, bf16[1536,1024]{0,1:T(8,128)(2,1)} %copy-done.38, bf16[1536,1024]{0,1:T(8,128)(2,1)S(1)} %copy-done.37), kind=kOutput, calls=%fused_computation.52 | convolution fusion | flops 17752391680 | bytes 26476544 | tf_op jit(solution)/shard_map/rd,rf->df/dot_general | solution.py:20
  1444.5 56.7 %all-to-all-done.17 = bf16[4,1408,512]{1,2,0:T(8,128)(2,1)} async-done(((bf16[4,1408,512]{1,2,0:T(8,128)(2,1)}), bf16[4,1408,512]{1,2,0:T(8,128)(2,1)}, u32[]{:S(2)}, u32[]{:S(2)}) %all-to-all-start.17) | async-done | bytes 5767200 | tf_op jit(solution)/shard_map/all_to_all | solution.py:49
  1501.2 6.3 all-to-all-start.16
  1516.9 176.7 %collective-permute-done.17 = f32[18,1024]{1,0:T(8,128)S(1)} collective-permute-done((f32[18,1024]{1,0:T(8,128)S(1)}, f32[18,1024]{1,0:T(8,128)S(1)}, u32[]{:S(2)}, u32[]{:S(2)}) %collective-permute-start.17) | collective-permute-done | bytes 73760 | tf_op jit(solution)/shard_map/ppermute | solution.py:56
  1698.9 7.8 convert_bitcast_fusion
  1706.7 12.0 copy.457
  1718.7 25.0 %reshape.1096 = f32[2,2,512,2,1408]{4,3,2,1,0:T(2,128)} reshape(bf16[4,512,2816]{2,1,0:T(8,128)(2,1)} %all-to-all-done.16) | data formatting | bytes 34603008 | tf_op jit(solution)/shard_map/reshape | solution.py:456
  1743.6 38.9 %copy.536 = f32[2,2,512,2,1408]{4,0,3,2,1:T(2,128)} copy(f32[2,2,512,2,1408]{4,3,2,1,0:T(2,128)} %reshape.1096) | data formatting | bytes 46137344 | tf_op jit(solution)/shard_map/reshape | solution.py:456
  1782.5 33.8 %reshape.1089 = f32[2,512,2,2816]{3,2,1,0:T(2,128)} reshape(f32[2,512,2,2,1408]{4,3,2,1,0:T(2,128)} %bitcast.365) | data formatting | bytes 46137344 | tf_op jit(solution)/shard_map/reshape | solution.py:456
  (520 shorter events, 323.0 us)
Async XLA Ops:
  7.2 430.3 %copy-start = (f32[2048,8]{0,1:T(8,128)S(1)}, f32[2048,8]{0,1:T(8,128)}, u32[]{:S(2)}) copy-start(f32[2048,8]{0,1:T(8,128)} %param.22) | copy-start | bytes 196612
  7.2 57.2 %all-gather.7.cloned.1.call-start = ((), (), s32[]{:S(2)}) async-start(), calls=%async_computation.22 | async-start | bytes 2621440 | tf_op jit(solution)/shard_map/all_gather | solution.py:201
  7.9 93.3 %all-gather.11.cloned.1.call-start = ((), (), s32[]{:S(2)}) async-start(), calls=%async_computation.24 | async-start | bytes 2621440 | tf_op jit(solution)/shard_map/all_gather | solution.py:220
  9.4 58.4 %copy-start.72 = (f32[1024]{0:T(1024)S(1)}, f32[1024]{0:T(1024)}, u32[]{:S(2)}) copy-start(f32[1024]{0:T(1024)} %param.19) | copy-start | bytes 12292
  42.5 153.2 %all-gather.13.cloned.1.call-start = ((), (), s32[]{:S(2)}) async-start(), calls=%async_computation.25 | async-start | bytes 5242880 | tf_op jit(solution)/shard_map/all_gather | solution.py:230
  66.6 1.2 collective-permute-start.2
  69.7 36.0 %collective-permute-start.3 = (bf16[1024,1024]{1,0:T(8,128)(2,1)}, bf16[1024,1024]{1,0:T(8,128)(2,1)}, u32[]{:S(2)}, u32[]{:S(2)}) collective-permute-start(bf16[1024,1024]{1,0:T(8,128)(2,1)} %fusion.43), channel_id=1, source_target_pairs={{0,1},{1,0},{2,3},{3,2},{4,5},{5,4},{6,7},{7,6},{8,9},{9,8},{10,11... | collective-permute-start | bytes 6291464 | tf_op jit(solution)/shard_map/ppermute | solution.py:45
  71.7 39.5 %copy-start.39 = (f32[1024,64]{0,1:T(8,128)}, f32[1024,64]{0,1:T(8,128)S(1)}, u32[]{:S(2)}) copy-start(f32[1024,64]{0,1:T(8,128)S(1)} %get-tuple-element.465) | copy-start | bytes 786436
  112.4 171.8 %all-gather.9.cloned.1.call-start = ((), (), s32[]{:S(2)}) async-start(), calls=%async_computation.23 | async-start | bytes 10485760 | tf_op jit(solution)/shard_map/all_gather | solution.py:233
  116.4 257.7 %all-gather.15.cloned.1.call-start = ((), (), s32[]{:S(2)}) async-start(), calls=%async_computation.26 | async-start | bytes 10485760 | tf_op jit(solution)/shard_map/all_gather | solution.py:234
  120.2 46.9 %copy-start.22 = (bf16[1024,1024]{1,0:T(8,128)(2,1)S(1)}, bf16[1024,1024]{1,0:T(8,128)(2,1)}, u32[]{:S(2)}) copy-start(bf16[1024,1024]{1,0:T(8,128)(2,1)} %copy-done.21) | copy-start | bytes 6291460
  167.1 124.6 %copy-start.33 = (f32[768,64]{1,0:T(8,128)}, f32[768,64]{1,0:T(8,128)S(1)}, u32[]{:S(2)}) copy-start(f32[768,64]{1,0:T(8,128)S(1)} %get-tuple-element.468) | copy-start | bytes 589828
  341.6 38.1 %copy-start.5 = (bf16[1024,8,128]{2,0,1:T(8,128)(2,1)}, bf16[1024,8,128]{2,0,1:T(8,128)(2,1)S(1)}, u32[]{:S(2)}) copy-start(bf16[1024,8,128]{2,0,1:T(8,128)(2,1)S(1)} %get-tuple-element.715) | copy-start | bytes 6291460
  341.6 38.1 %copy-start.48 = (s32[4,1,256]{2,1,0:T(1,128)}, s32[4,1,256]{2,1,0:T(1,128)S(1)}, u32[]{:S(2)}) copy-start(s32[4,1,256]{2,1,0:T(1,128)S(1)} %get-tuple-element.775) | copy-start | bytes 12292
  379.7 3.8 collective-permute-start.4
  389.9 41.9 %all-to-all-start.1 = ((bf16[4,192,1024]{2,1,0:T(8,128)(2,1)}), bf16[4,192,1024]{2,1,0:T(8,128)(2,1)S(1)}, u32[]{:S(2)}, u32[]{:S(2)}) async-start(bf16[4,192,1024]{2,1,0:T(8,128)(2,1)} %bitcast.42), calls=%async_computation.1 | async-start | bytes 3145728 | tf_op jit(solution)/shard_map/all_to_all | solution.py:49
  394.7 42.8 %copy-start.73 = (f32[1024]{0:T(1024)S(1)}, f32[1024]{0:T(1024)}, u32[]{:S(2)}) copy-start(f32[1024]{0:T(1024)} %param.19) | copy-start | bytes 12292
  394.7 42.2 %collective-permute-start = (f32[256,1]{0,1:T(1,128)S(1)}, f32[256,1]{0,1:T(1,128)S(1)}, u32[]{:S(2)}, u32[]{:S(2)}) collective-permute-start(f32[256,1]{0,1:T(1,128)S(1)} %bitcast.478), channel_id=1, source_target_pairs={{0,1},{1,0},{2,3},{3,2},{4,5},{5,4},{6,7},{7,6},{8,9},{9,8},{10,11... | collective-permute-start | bytes 3080 | tf_op jit(solution)/shard_map/ppermute | solution.py:45
  398.7 40.3 %copy-start.78 = (pred[2,8,256]{2,1,0:T(8,128)(4,1)}, pred[2,8,256]{2,1,0:T(8,128)(4,1)S(1)}, u32[]{:S(2)}) copy-start(pred[2,8,256]{2,1,0:T(8,128)(4,1)S(1)} %iota_compare_fusion.12) | copy-start | bytes 12292
  432.9 40.4 %all-to-all-start.8 = ((bf16[4,192,1024]{2,1,0:T(8,128)(2,1)}), bf16[4,192,1024]{2,1,0:T(8,128)(2,1)S(1)}, u32[]{:S(2)}, u32[]{:S(2)}) async-start(bf16[4,192,1024]{2,1,0:T(8,128)(2,1)} %bitcast.393), calls=%async_computation.8 | async-start | bytes 3145728 | tf_op jit(solution)/shard_map/all_to_all | solution.py:49
  437.8 1.2 collective-permute-start.1
  443.8 1.2 collective-permute-start.5
  473.4 40.9 %all-to-all-start.2 = ((bf16[4,192,1024]{2,1,0:T(8,128)(2,1)}), bf16[4,192,1024]{2,1,0:T(8,128)(2,1)}, u32[]{:S(2)}, u32[]{:S(2)}) async-start(bf16[4,192,1024]{2,1,0:T(8,128)(2,1)} %bitcast.394), calls=%async_computation.2 | async-start | bytes 3145728 | tf_op jit(solution)/shard_map/all_to_all | solution.py:49
  517.7 39.3 %all-to-all-start.9 = ((bf16[4,384,1024]{2,1,0:T(8,128)(2,1)}), bf16[4,384,1024]{2,1,0:T(8,128)(2,1)S(1)}, u32[]{:S(2)}, u32[]{:S(2)}) async-start(bf16[4,384,1024]{2,1,0:T(8,128)(2,1)} %bitcast.377), calls=%async_computation.9 | async-start | bytes 6291456 | tf_op jit(solution)/shard_map/all_to_all | solution.py:49
  560.5 44.9 %all-to-all-start.3 = ((bf16[4,384,1024]{2,1,0:T(8,128)(2,1)}), bf16[4,384,1024]{2,1,0:T(8,128)(2,1)}, u32[]{:S(2)}, u32[]{:S(2)}) async-start(bf16[4,384,1024]{2,1,0:T(8,128)(2,1)} %bitcast.376), calls=%async_computation.3 | async-start | bytes 6291456 | tf_op jit(solution)/shard_map/all_to_all | solution.py:49
  605.4 131.7 %all-to-all-start.4 = ((bf16[4,512,2816]{1,2,0:T(8,128)(2,1)}), bf16[4,512,2816]{1,2,0:T(8,128)(2,1)}, u32[]{:S(2)}, u32[]{:S(2)}) async-start(bf16[4,512,2816]{1,2,0:T(8,128)(2,1)} %bitcast.366), calls=%async_computation.4 | async-start | bytes 23068672 | tf_op jit(solution)/shard_map/all_to_all | solution.py:49
  614.5 12.6 collective-permute-start.9
  617.7 146.7 %collective-permute-start.7 = (bf16[1536,1024]{0,1:T(8,128)(2,1)S(1)}, bf16[1536,1024]{0,1:T(8,128)(2,1)}, u32[]{:S(2)}, u32[]{:S(2)}) collective-permute-start(bf16[1536,1024]{0,1:T(8,128)(2,1)S(1)} %copy.426), channel_id=1, source_target_pairs={{0,1},{1,0},{2,3},{3,2},{4,5},{5,4},{6,7},{7,6},{8,9},{9,8},{10,11... | collective-permute-start | bytes 9437192 | tf_op jit(solution)/shard_map/ppermute | solution.py:45
  737.1 69.0 %all-to-all-start.5 = ((bf16[4,1408,512]{2,1,0:T(8,128)(2,1)}), bf16[4,1408,512]{2,1,0:T(8,128)(2,1)}, u32[]{:S(2)}, u32[]{:S(2)}) async-start(bf16[4,1408,512]{2,1,0:T(8,128)(2,1)} %bitcast.370), calls=%async_computation.5 | async-start | bytes 11534336 | tf_op jit(solution)/shard_map/all_to_all | solution.py:49
  768.0 38.1 %copy-start.96 = (f32[1536]{0:T(1024)}, f32[1536]{0:T(1024)S(1)}, u32[]{:S(2)}) copy-start(f32[1536]{0:T(1024)S(1)} %add_divide_fusion.1) | copy-start | bytes 18436
  845.1 34.5 %collective-permute-start.10 = (bf16[1536,1024]{1,0:T(8,128)(2,1)}, bf16[1536,1024]{1,0:T(8,128)(2,1)}, u32[]{:S(2)}, u32[]{:S(2)}) collective-permute-start(bf16[1536,1024]{1,0:T(8,128)(2,1)} %fusion.55), channel_id=1, source_target_pairs={{0,1},{1,0},{2,3},{3,2},{4,5},{5,4},{6,7},{7,6},{8,9},{9,8},{10,11... | collective-permute-start | bytes 9437192 | tf_op jit(solution)/shard_map/ppermute | solution.py:45
  862.6 40.2 %collective-permute-start.8 = (bf16[1536,1024]{1,0:T(8,128)(2,1)}, bf16[1536,1024]{1,0:T(8,128)(2,1)}, u32[]{:S(2)}, u32[]{:S(2)}) collective-permute-start(bf16[1536,1024]{1,0:T(8,128)(2,1)} %convolution_convert_fusion.3), channel_id=1, source_target_pairs={{0,1},{1,0},{2,3},{3,2},{4,5},{5,4},{6,7},{7,6},{8,9},{9,8},{10,11... | collective-permute-start | bytes 9437192 | tf_op jit(solution)/shard_map/ppermute | solution.py:45
  863.1 5.2 collective-permute-start.11
  876.3 18.2 all-to-all-start.13
  894.5 39.0 %all-to-all-start.10 = ((bf16[4,384,1024]{2,1,0:T(8,128)(2,1)}), bf16[4,384,1024]{2,1,0:T(8,128)(2,1)S(1)}, u32[]{:S(2)}, u32[]{:S(2)}) async-start(bf16[4,384,1024]{2,1,0:T(8,128)(2,1)} %bitcast.419), calls=%async_computation.10 | async-start | bytes 6291456 | tf_op jit(solution)/shard_map/all_to_all | solution.py:49
  933.5 40.3 %all-to-all-start.6 = ((bf16[4,384,1024]{2,1,0:T(8,128)(2,1)}), bf16[4,384,1024]{2,1,0:T(8,128)(2,1)}, u32[]{:S(2)}, u32[]{:S(2)}) async-start(bf16[4,384,1024]{2,1,0:T(8,128)(2,1)} %bitcast.420), calls=%async_computation.6 | async-start | bytes 6291456 | tf_op jit(solution)/shard_map/all_to_all | solution.py:49
  973.8 41.0 %all-to-all-start.11 = ((bf16[4,192,1024]{2,1,0:T(8,128)(2,1)}), bf16[4,192,1024]{2,1,0:T(8,128)(2,1)}, u32[]{:S(2)}, u32[]{:S(2)}) async-start(bf16[4,192,1024]{2,1,0:T(8,128)(2,1)} %bitcast.91), calls=%async_computation.11 | async-start | bytes 3145728 | tf_op jit(solution)/shard_map/all_to_all | solution.py:49
  981.4 38.2 %copy-start.29 = (bf16[256,1024]{1,0:T(8,128)(2,1)S(1)}, bf16[256,1024]{1,0:T(8,128)(2,1)}, u32[]{:S(2)}) copy-start(bf16[256,1024]{1,0:T(8,128)(2,1)} %copy-done.28) | copy-start | bytes 1572868
  981.4 39.4 %copy-start.47 = (pred[768,256]{1,0:T(8,128)(4,1)S(1)}, pred[768,256]{1,0:T(8,128)(4,1)}, u32[]{:S(2)}) copy-start(pred[768,256]{1,0:T(8,128)(4,1)} %get-tuple-element.469) | copy-start | bytes 589828
  981.5 39.3 %copy-start.79 = (pred[2,8,256]{2,1,0:T(8,128)(4,1)S(1)}, pred[2,8,256]{2,1,0:T(8,128)(4,1)}, u32[]{:S(2)}) copy-start(pred[2,8,256]{2,1,0:T(8,128)(4,1)} %copy-done.78) | copy-start | bytes 12292
  1014.8 40.9 %all-to-all-start.7 = ((bf16[4,192,1024]{2,1,0:T(8,128)(2,1)}), bf16[4,192,1024]{2,1,0:T(8,128)(2,1)}, u32[]{:S(2)}, u32[]{:S(2)}) async-start(bf16[4,192,1024]{2,1,0:T(8,128)(2,1)} %bitcast.76), calls=%async_computation.7 | async-start | bytes 3145728 | tf_op jit(solution)/shard_map/all_to_all | solution.py:49
  1019.2 339.4 %all-reduce.3.cloned.1.call-start = ((), (), s32[]{:S(2)}) async-start(), calls=%async_computation.31 | async-start | bytes 8388608
  1019.8 1.2 collective-permute-start.6
  1024.7 33.5 %collective-permute-start.12 = (f32[256,1]{0,1:T(1,128)S(1)}, f32[256,1]{0,1:T(1,128)S(1)}, u32[]{:S(2)}, u32[]{:S(2)}) collective-permute-start(f32[256,1]{0,1:T(1,128)S(1)} %bitcast.468), channel_id=1, source_target_pairs={{0,1},{1,0},{2,3},{3,2},{4,5},{5,4},{6,7},{7,6},{8,9},{9,8},{10,11... | collective-permute-start | bytes 3080 | tf_op jit(solution)/shard_map/ppermute | solution.py:45
  1059.5 40.1 %copy-start.17 = (f32[256,1024]{1,0:T(8,128)}, f32[256,1024]{1,0:T(8,128)S(1)}, u32[]{:S(2)}) copy-start(f32[256,1024]{1,0:T(8,128)S(1)} %get-tuple-element.452) | copy-start | bytes 3145732
  1099.5 3.4 collective-permute-start.13
  1206.2 305.1 %reduce-scatter.8.cloned.1.call-start = ((), (), s32[]{:S(2)}) async-start(), calls=%async_computation.27 | async-start | bytes 2621440 | tf_op jit(solution)/shard_map/reduce_scatter | solution.py:442
  1220.0 140.1 %copy-start.40 = (f32[1024,64]{0,1:T(8,128)S(1)}, f32[1024,64]{0,1:T(8,128)}, u32[]{:S(2)}) copy-start(f32[1024,64]{0,1:T(8,128)} %copy-done.39) | copy-start | bytes 786436
  1220.0 140.1 %copy-start.46 = (f32[1024,64]{0,1:T(8,128)S(1)}, f32[1024,64]{0,1:T(8,128)}, u32[]{:S(2)}) copy-start(f32[1024,64]{0,1:T(8,128)} %get-tuple-element.463) | copy-start | bytes 786436
  1220.0 140.3 %copy-start.26 = (bf16[64,8,16,128]{3,1,2,0:T(8,128)(2,1)S(1)}, bf16[64,8,16,128]{3,1,2,0:T(8,128)(2,1)}, u32[]{:S(2)}) copy-start(bf16[64,8,16,128]{3,1,2,0:T(8,128)(2,1)} %copy.537) | copy-start | bytes 6291460
  1362.4 4.9 collective-permute-start.14
  1370.8 144.1 %reduce-scatter.10.cloned.1.call-start = ((), (), s32[]{:S(2)}) async-start(), calls=%async_computation.28 | async-start | bytes 2621440 | tf_op jit(solution)/shard_map/reduce_scatter | solution.py:480
  1376.4 455.0 %reduce-scatter.12.cloned.1.call-start = ((), (), s32[]{:S(2)}) async-start(), calls=%async_computation.29 | async-start | bytes 10485760 | tf_op jit(solution)/shard_map/reduce_scatter | solution.py:474
  1386.7 448.8 %reduce-scatter.14.cloned.1.call-start = ((), (), s32[]{:S(2)}) async-start(), calls=%async_computation.30 | async-start | bytes 10485760 | tf_op jit(solution)/shard_map/reduce_scatter | solution.py:468
  1413.6 87.6 %all-to-all-start.17 = ((bf16[4,1408,512]{1,2,0:T(8,128)(2,1)}), bf16[4,1408,512]{1,2,0:T(8,128)(2,1)}, u32[]{:S(2)}, u32[]{:S(2)}) async-start(bf16[4,1408,512]{1,2,0:T(8,128)(2,1)} %convert_bitcast_fusion.1), calls=%async_computation.21 | async-start | bytes 11534336 | tf_op jit(solution)/shard_map/all_to_all | solution.py:49
  1501.2 193.9 %all-to-all-start.16 = ((bf16[4,512,2816]{2,1,0:T(8,128)(2,1)}), bf16[4,512,2816]{2,1,0:T(8,128)(2,1)}, u32[]{:S(2)}, u32[]{:S(2)}) async-start(bf16[4,512,2816]{2,1,0:T(8,128)(2,1)} %bitcast.385), calls=%async_computation.20 | async-start | bytes 23068672 | tf_op jit(solution)/shard_map/all_to_all | solution.py:49
  1509.7 1.2 collective-permute-start.15
  1513.0 180.6 %collective-permute-start.17 = (f32[18,1024]{1,0:T(8,128)S(1)}, f32[18,1024]{1,0:T(8,128)S(1)}, u32[]{:S(2)}, u32[]{:S(2)}) collective-permute-start(f32[18,1024]{1,0:T(8,128)S(1)} %pad_maximum_fusion.20), channel_id=1, source_target_pairs={{0,8},{8,0},{16,24},{24,16},{1,9},{9,1},{17,25},{25,17},{2,10},{10... | collective-permute-start | bytes 221192 | tf_op jit(solution)/shard_map/ppermute | solution.py:56
  1693.6 122.7 %collective-permute-start.18 = (f32[18,1024]{1,0:T(8,128)S(1)}, f32[18,1024]{1,0:T(8,128)S(1)}, u32[]{:S(2)}, u32[]{:S(2)}) collective-permute-start(f32[18,1024]{1,0:T(8,128)S(1)} %fusion.163), channel_id=1, source_target_pairs={{0,16},{8,24},{16,0},{24,8},{1,17},{9,25},{17,1},{25,9},{2,18},{10... | collective-permute-start | bytes 221192 | tf_op jit(solution)/shard_map/ppermute | solution.py:56
  1695.1 123.2 %all-to-all-start.15 = ((bf16[4,128,2,256]{3,2,1,0:T(2,128)(2,1)}), bf16[4,128,2,256]{3,2,1,0:T(2,128)(2,1)S(1)}, u32[]{:S(2)}, u32[]{:S(2)}) async-start(bf16[4,128,2,256]{3,2,1,0:T(2,128)(2,1)} %reshape.1077), calls=%async_computation.17 | async-start | bytes 1048576 | tf_op jit(solution)/shard_map/all_to_all | solution.py:49
  1816.3 3.7 collective-permute-start.16
  1816.3 5.4 collective-permute-start.19
  1821.8 7.6 collective-permute-start.20
  1829.4 1.3 collective-permute-start.21
  (98 other events, 693.7 us)
Sparse Core Ops, SparseCore 0:
  9.6 54.7 all-gather.6
  66.8 34.4 all-gather.10
  112.5 83.1 all-gather.12
  198.0 86.2 all-gather.8
  286.5 87.5 all-gather.14
  1206.3 152.1 all-reduce.2
  1371.0 42.9 reduce-scatter.7
  1417.5 77.8 reduce-scatter.9
  1498.8 205.7 reduce-scatter.11
  1707.5 84.7 reduce-scatter.13

commit v2 on v1

v2 whole, which is shorter than its diff:
```python
import functools
import math

import jax
import jax.numpy as jnp
from jax import lax
from jax.experimental import pallas as pl
from jax.experimental.pallas import tpu as pltpu
from jax.sharding import PartitionSpec as P

HD = 128
EPSILON = 1e-06
MASKED = -1000000000.0
F32 = jnp.float32
BF16 = jnp.bfloat16
LIMIT = 60 << 20
NT = (((1,), (1,)), ((), ()))
TN = (((0,), (0,)), ((), ()))


def dot(lhs, rhs):
    return jnp.dot(lhs, rhs, preferred_element_type=F32)


def ein(spec, lhs, rhs):
    return jnp.einsum(spec, lhs, rhs, preferred_element_type=F32)


def gdot(lhs, rhs, dims):
    return lax.dot_general(lhs, rhs, dims, preferred_element_type=F32)


def swap(values):
    return lax.ppermute(values, "tensor", [(0, 1), (1, 0)])


def a2a(values, axis):
    return lax.all_to_all(values, axis, split_axis=0, concat_axis=0, tiled=True)


def total_over(values, axis):
    count = lax.axis_size(axis)
    step = 1
    while step < count:
        values = values + lax.ppermute(values, axis, [(i, i ^ step) for i in range(count)])
        step *= 2
    return values


def core_sum(values):
    return values + swap(values)


def relay(values, axis):
    count = lax.axis_size(axis)
    up, down = [values], [values]
    for _ in range(count - 1):
        up.append(lax.ppermute(up[-1], axis, [(i, i + 1) for i in range(count - 1)]))
        down.append(lax.ppermute(down[-1], axis, [(i + 1, i) for i in range(count - 1)]))
    return [values] + [down[j] + up[count - j] for j in range(1, count)]


def shift(blocks, sign):
    count = lax.axis_size("expert")
    return [blocks[0]] + [
        lax.ppermute(blocks[j], "expert", [(i, (i + sign * j) % count) for i in range(count)])
        for j in range(1, count)
    ]


def cross(blocks):
    count = lax.axis_size("dp")
    return [blocks[0]] + [
        lax.ppermute(blocks[k], "dp", [(i, i ^ k) for i in range(count)]) for k in range(1, count)
    ]


def both_halves(values, core):
    other = swap(values)
    first = jnp.where(core == 0, values, other)
    second = jnp.where(core == 0, other, values)
    return jnp.concatenate([first, second], -1)


def one_hot_slots(routes, experts, capacity):
    token_count = routes.shape[2]
    member = (routes[:, None, 0] == experts[None, :, None]) | (
        routes[:, None, 1] == experts[None, :, None]
    )
    tokens = jnp.arange(token_count, dtype=jnp.int32)
    upper = (tokens[:, None] < tokens[None, :]).astype(BF16)
    rank = dot(member.astype(BF16), upper).astype(jnp.int32)
    slots = jnp.arange(capacity, dtype=jnp.int32)
    return member[:, :, None, :] & (rank[:, :, None, :] == slots[None, None, :, None])


def params(*kinds):
    return pltpu.CompilerParams(dimension_semantics=kinds, vmem_limit_bytes=LIMIT)


def pack_kernel(ff, parts, src, out):
    for part in range(parts):
        for half in range(2):
            out[part, 0, :, half * ff : (half + 1) * ff] = src[
                0, :, half, part * ff : (part + 1) * ff
            ].astype(BF16)


def pack_gateup(weights, parts):
    local, depth, _, ff_core = weights.shape
    ff = ff_core // parts
    if ff % 128:
        moved = weights.reshape(local, depth, 2, parts, ff).transpose(3, 0, 1, 2, 4)
        return moved.astype(BF16).reshape(parts, local, depth, 2 * ff)
    rows = min(depth, 128)
    return pl.pallas_call(
        functools.partial(pack_kernel, ff, parts),
        grid=(local, depth // rows),
        in_specs=[pl.BlockSpec((1, rows, 2, ff_core), lambda l, r: (l, r, 0, 0))],
        out_specs=pl.BlockSpec((parts, 1, rows, 2 * ff), lambda l, r: (0, l, r, 0)),
        out_shape=jax.ShapeDtypeStruct((parts, local, depth, 2 * ff), BF16),
        compiler_params=params("parallel", "parallel"),
        name="pack_gateup",
    )(weights)


def unpack_kernel(ff, parts, src, out):
    for part in range(parts):
        for half in range(2):
            out[0, :, half, part * ff : (part + 1) * ff] = src[
                part, 0, :, half * ff : (half + 1) * ff
            ].astype(F32)


def unpack_gateup(grads, parts):
    _, local, depth, ff2 = grads.shape
    ff = ff2 // 2
    if ff % 128:
        moved = grads.reshape(parts, local, depth, 2, ff).transpose(1, 2, 3, 0, 4)
        return moved.astype(F32).reshape(local, depth, 2, parts * ff)
    rows = min(depth, 128)
    return pl.pallas_call(
        functools.partial(unpack_kernel, ff, parts),
        grid=(local, depth // rows),
        in_specs=[pl.BlockSpec((parts, 1, rows, 2 * ff), lambda l, r: (0, l, r, 0))],
        out_specs=pl.BlockSpec((1, rows, 2, parts * ff), lambda l, r: (l, r, 0, 0)),
        out_shape=jax.ShapeDtypeStruct((local, depth, 2, parts * ff), F32),
        compiler_params=params("parallel", "parallel"),
        name="unpack_gateup",
    )(grads)


def cast_kernel(src, out):
    out[...] = src[...].reshape(out.shape).astype(out.dtype)


def pack_down(weights, parts):
    local, ff_core, depth = weights.shape
    ff = ff_core // parts
    return pl.pallas_call(
        cast_kernel,
        grid=(parts, local),
        in_specs=[pl.BlockSpec((1, ff, depth), lambda p, l: (l, p, 0))],
        out_specs=pl.BlockSpec((1, 1, ff, depth), lambda p, l: (p, l, 0, 0)),
        out_shape=jax.ShapeDtypeStruct((parts, local, ff, depth), BF16),
        compiler_params=params("parallel", "parallel"),
        name="pack_down",
    )(weights)


def unpack_down(grads):
    parts, local, ff, depth = grads.shape
    return pl.pallas_call(
        cast_kernel,
        grid=(parts, local),
        in_specs=[pl.BlockSpec((1, 1, ff, depth), lambda p, l: (p, l, 0, 0))],
        out_specs=pl.BlockSpec((1, ff, depth), lambda p, l: (l, p, 0)),
        out_shape=jax.ShapeDtypeStruct((local, parts * ff, depth), F32),
        compiler_params=params("parallel", "parallel"),
        name="unpack_down",
    )(grads)


def turn(values, cosine, sine):
    return values * cosine + pltpu.roll(values, HD // 2, 1) * sine


def att_fwd_kernel(
    place, q_in, kv, cos, sin, row_pos, row_seg, key_seg, *rest
):
    o_out, q_out = rest[-2:]
    query = turn(q_in[...], cos[...], sin[...]).astype(BF16)
    q_out[...] = query
    scores = gdot(query, kv[0, :, :HD], NT) * (1.0 / math.sqrt(HD))
    key_pos = lax.broadcasted_iota(jnp.int32, scores.shape, 1)
    allowed = (row_seg[...] == key_seg[...]) & (row_pos[...] >= key_pos)
    scores = jnp.where(allowed, scores, MASKED)
    peak = jnp.max(scores, 1, keepdims=True)
    weight = jnp.exp(scores - peak)
    mass = jnp.sum(weight, 1, keepdims=True)
    soft = (weight * (1.0 / mass)).astype(BF16)
    o_out[...] = dot(soft, kv[0, :, HD:]).astype(BF16)


def att_forward(place, q_raw, kv, cos, sin, row_pos, row_seg, key_seg, group, before):
    rows, feats = q_raw.shape
    seq, wide = kv.shape[1:]
    group_heads = wide // (2 * HD)
    block = min(256, rows)
    head = lambda h, i, place: (i, place[group] * group_heads + h)
    row = lambda h, i, place: (i, 0)
    in_specs = [
        pl.BlockSpec((block, HD), head),
        pl.BlockSpec((1, seq, 2 * HD), lambda h, i, place: (0, 0, h)),
        pl.BlockSpec((block, HD), row),
        pl.BlockSpec((block, HD), row),
        pl.BlockSpec((block, 1), row),
        pl.BlockSpec((block, 1), row),
        pl.BlockSpec((1, seq), lambda h, i, place: (0, 0)),
    ]
    operands = [place, q_raw, kv, cos, sin, row_pos, row_seg, key_seg]
    aliases = {}
    if before is not None:
        in_specs += [pl.BlockSpec(memory_space=pl.ANY)] * 2
        operands += list(before)
        aliases = {8: 0, 9: 1}
    return pl.pallas_call(
        att_fwd_kernel,
        grid_spec=pltpu.PrefetchScalarGridSpec(
            num_scalar_prefetch=1,
            grid=(group_heads, rows // block),
            in_specs=in_specs,
            out_specs=[pl.BlockSpec((block, HD), head)] * 2,
        ),
        out_shape=[jax.ShapeDtypeStruct((rows, feats), BF16)] * 2,
        input_output_aliases=aliases,
        compiler_params=params("arbitrary", "arbitrary"),
        name="attention_fwd",
    )(*operands)


def att_bwd_kernel(
    place, q_in, do_in, kv, cos, sin, key_cos, key_sin, row_pos, row_seg, key_seg,
    dq_out, dkv_out, dk_sum, dv_sum,
):
    step = pl.program_id(1)
    scale = 1.0 / math.sqrt(HD)
    query, grad_out = q_in[...], do_in[...]
    keys, values = kv[0, :, :HD], kv[0, :, HD:]
    scores = gdot(keys, query, NT) * scale
    key_pos = lax.broadcasted_iota(jnp.int32, scores.shape, 0)
    allowed = (row_seg[...] == key_seg[...]) & (row_pos[...] >= key_pos)
    scores = jnp.where(allowed, scores, MASKED)
    peak = jnp.max(scores, 0, keepdims=True)
    weight = jnp.exp(scores - peak)
    soft = weight * (1.0 / jnp.sum(weight, 0, keepdims=True))
    grad_soft = gdot(values, grad_out, NT)
    inner = jnp.sum(soft * grad_soft, 0, keepdims=True)
    grad_scores = (soft * (grad_soft - inner)).astype(BF16)
    grad_query = gdot(grad_scores, keys, TN) * scale
    dq_out[...] = turn(grad_query, cos[...], -sin[...]).astype(BF16)

    @pl.when(step == 0)
    def _():
        dk_sum[...] = jnp.zeros_like(dk_sum)
        dv_sum[...] = jnp.zeros_like(dv_sum)

    dk_sum[...] += dot(grad_scores, query)
    dv_sum[...] += dot(soft.astype(BF16), grad_out)

    @pl.when(step == pl.num_programs(1) - 1)
    def _():
        grad_keys = turn(dk_sum[...] * scale, key_cos[...], -key_sin[...])
        dkv_out[0, :, :HD] = grad_keys.astype(BF16)
        dkv_out[0, :, HD:] = dv_sum[...].astype(BF16)


def att_backward(
    place, query, grad_mixed, kv, cos, sin, key_cos, key_sin, row_pos, row_seg, key_seg
):
    rows, feats = query.shape
    planes, seq, wide = kv.shape
    group_heads = wide // (2 * HD)
    block = min(256, rows)
    group = lambda h: h // group_heads
    inner = lambda h: lax.rem(h, group_heads)
    head = lambda h, i, place: (i, place[group(h)] * group_heads + inner(h))
    row = lambda h, i, place: (i, 0)
    lane = lambda h, i, place: (0, i)
    whole = lambda h, i, place: (0, 0)
    return pl.pallas_call(
        att_bwd_kernel,
        grid_spec=pltpu.PrefetchScalarGridSpec(
            num_scalar_prefetch=1,
            grid=(planes * group_heads, rows // block),
            in_specs=[
                pl.BlockSpec((block, HD), head),
                pl.BlockSpec((block, HD), head),
                pl.BlockSpec((1, seq, 2 * HD), lambda h, i, place: (group(h), 0, inner(h))),
                pl.BlockSpec((block, HD), row),
                pl.BlockSpec((block, HD), row),
                pl.BlockSpec((seq, HD), whole),
                pl.BlockSpec((seq, HD), whole),
                pl.BlockSpec((1, block), lane),
                pl.BlockSpec((1, block), lane),
                pl.BlockSpec((seq, 1), whole),
            ],
            out_specs=[
                pl.BlockSpec((block, HD), head),
                pl.BlockSpec(
                    (1, seq, 2 * HD), lambda h, i, place: (place[group(h)], 0, inner(h))
                ),
            ],
            scratch_shapes=[pltpu.VMEM((seq, HD), F32)] * 2,
        ),
        out_shape=[
            jax.ShapeDtypeStruct((rows, feats), BF16),
            jax.ShapeDtypeStruct((planes, seq, wide), BF16),
        ],
        compiler_params=params("arbitrary", "arbitrary"),
        name="attention_bwd",
    )(place, query, grad_mixed, kv, cos, sin, key_cos, key_sin, row_pos, row_seg, key_seg)


def raw_kernel(core, g_own, g_other, w_dn, out):
    columns = w_dn.shape[0]
    half, depth = columns // 2, w_dn.shape[2]
    total = jnp.zeros(out.shape, F32)
    for i in range(half):
        part = slice(i * depth, (i + 1) * depth)
        total += gdot(g_own[:, part], w_dn[core[0] * half + i], NT)
        total += gdot(g_other[:, part], w_dn[(1 - core[0]) * half + i], NT)
    out[...] = total


def hidden_raw(core, g_own, g_other, w_dn):
    rows, width = g_own.shape
    columns, ff, depth = w_dn.shape
    block = 256
    return pl.pallas_call(
        raw_kernel,
        grid_spec=pltpu.PrefetchScalarGridSpec(
            num_scalar_prefetch=1,
            grid=(rows // block,),
            in_specs=[
                pl.BlockSpec((block, width), lambda i, c: (i, 0)),
                pl.BlockSpec((block, width), lambda i, c: (i, 0)),
                pl.BlockSpec(
                    (columns, ff, depth), lambda i, c: (0, 0, 0), pipeline_mode=pl.Buffered(1)
                ),
            ],
            out_specs=pl.BlockSpec((block, ff), lambda i, c: (i, 0)),
        ),
        out_shape=jax.ShapeDtypeStruct((rows, ff), F32),
        compiler_params=params("arbitrary"),
        name="hidden_raw",
    )(core, g_own, g_other, w_dn)


def ff_kernel(place, x_own, x_other, w_gu, raw, router, other, hid, hid_gated, duw, dgate):
    core, expert = place[0], place[1]
    width = x_own.shape[1]
    ff = raw.shape[1]
    mine = pl.ds(pl.multiple_of(core * width, width), width)
    theirs = pl.ds(pl.multiple_of((1 - core) * width, width), width)

    def product(weights):
        return dot(x_own[...], weights[mine, :]) + dot(x_other[...], weights[theirs, :])

    logits = product(router)
    lanes = lax.broadcasted_iota(jnp.int32, logits.shape, 1)
    own_logit = jnp.sum(jnp.where(lanes == expert, logits, 0.0), 1, keepdims=True)
    other_logit = jnp.sum(jnp.where(lanes == other[...], logits, 0.0), 1, keepdims=True)
    gate = jax.nn.sigmoid(own_logit - other_logit)
    both = product(w_gu)
    gate_part, up_part = both[:, :ff], both[:, ff:]
    sig = 1.0 / (1.0 + jnp.exp(-gate_part))
    silu = gate_part * sig
    hidden = silu * up_part
    hid[...] = hidden.astype(BF16)
    hid_gated[...] = (hidden * gate).astype(BF16)
    dgate[...] = jnp.sum(hidden * raw[...], 1, keepdims=True)
    grad_hidden = raw[...] * gate
    duw[:, :ff] = (grad_hidden * up_part * (sig * (1.0 + gate_part * (1.0 - sig)))).astype(BF16)
    duw[:, ff:] = (grad_hidden * silu).astype(BF16)


def feed_forward(place, x_own, x_other, w_gu, raw, router, other):
    rows, width = x_own.shape
    ff = raw.shape[1]
    block = 256
    row = lambda i, c: (i, 0)
    whole = lambda i, c: (0, 0)
    return pl.pallas_call(
        ff_kernel,
        grid_spec=pltpu.PrefetchScalarGridSpec(
            num_scalar_prefetch=1,
            grid=(rows // block,),
            in_specs=[
                pl.BlockSpec((block, width), row),
                pl.BlockSpec((block, width), row),
                pl.BlockSpec(w_gu.shape, whole, pipeline_mode=pl.Buffered(1)),
                pl.BlockSpec((block, ff), row),
                pl.BlockSpec(router.shape, whole, pipeline_mode=pl.Buffered(1)),
                pl.BlockSpec((block, 1), row),
            ],
            out_specs=[
                pl.BlockSpec((block, ff), row),
                pl.BlockSpec((block, ff), row),
                pl.BlockSpec((block, 2 * ff), row),
                pl.BlockSpec((block, 1), row),
            ],
        ),
        out_shape=[
            jax.ShapeDtypeStruct((rows, ff), BF16),
            jax.ShapeDtypeStruct((rows, ff), BF16),
            jax.ShapeDtypeStruct((rows, 2 * ff), BF16),
            jax.ShapeDtypeStruct((rows, 1), F32),
        ],
        compiler_params=params("arbitrary"),
        name="feed_forward",
    )(place, x_own, x_other, w_gu, raw, router, other)


def rows_kernel(transposed, which, lhs, weights, *rest):
    out = rest[-1]
    if transposed:
        total = gdot(lhs[...], weights[...], NT)
    else:
        total = jnp.concatenate(
            [dot(lhs[...], weights[i]) for i in range(weights.shape[0])], 1
        )
    if len(rest) > 1:
        total = total + rest[0][...].astype(F32)
    out[...] = total.astype(BF16)


def rows_half(which, lhs, weights, width, add=None):
    rows, inner = lhs.shape
    transposed = weights.ndim == 2
    block = 256
    row = lambda i, c: (i, 0)
    if transposed:
        w_spec = pl.BlockSpec(
            (width, inner), lambda i, c: (c[0], 0), pipeline_mode=pl.Buffered(1)
        )
    else:
        w_spec = pl.BlockSpec(
            (weights.shape[0] // 2,) + weights.shape[1:],
            lambda i, c: (c[0], 0, 0),
            pipeline_mode=pl.Buffered(1),
        )
    in_specs = [pl.BlockSpec((block, inner), row), w_spec]
    operands = [which, lhs, weights]
    if add is not None:
        in_specs.append(pl.BlockSpec((block, width), row))
        operands.append(add)
    return pl.pallas_call(
        functools.partial(rows_kernel, transposed),
        grid_spec=pltpu.PrefetchScalarGridSpec(
            num_scalar_prefetch=1,
            grid=(rows // block,),
            in_specs=in_specs,
            out_specs=pl.BlockSpec((block, width), row),
        ),
        out_shape=jax.ShapeDtypeStruct((rows, width), BF16),
        compiler_params=params("arbitrary"),
        name="rows_half",
    )(*operands)


def shards(
    tokens,
    norm_attn,
    norm_mlp,
    w_kv,
    router_attn,
    router_mlp,
    w_query,
    w_output,
    w_gateup,
    w_down,
    segments,
    att_routes,
    mlp_routes,
    cotangent,
):
    count, width = tokens.shape
    full_width = 2 * width
    planes = lax.axis_size("expert")
    columns = lax.axis_size("dp")
    plane = lax.axis_index("expert")
    column = lax.axis_index("dp")
    core = lax.axis_index("tensor")
    n_att = router_attn.shape[1]
    n_mlp = router_mlp.shape[1]
    local_att = w_query.shape[0]
    local_mlp = w_gateup.shape[0]
    ff_parts = columns // local_mlp
    depth = w_gateup.shape[1]
    ff = w_gateup.shape[3] // ff_parts
    cap = 3 * count // 8
    seq = planes * count
    feats = w_query.shape[2]
    kv_part = feats // planes
    part_heads = kv_part // HD
    own_local = column % local_mlp
    mlp_expert = plane * local_mlp + own_local
    steps = jnp.arange(planes, dtype=jnp.int32)
    source_planes = (plane + steps) % planes
    target_planes = (plane - steps + planes) % planes
    near_local = own_local ^ jnp.arange(local_mlp, dtype=jnp.int32)
    core_at = core.astype(jnp.int32)[None]
    other_at = 1 - core_at

    def absolute(blocks):
        twice = jnp.concatenate([blocks, blocks], 0)
        return lax.dynamic_slice_in_dim(twice, (planes - plane) % planes, planes, 0)

    def relative(blocks):
        twice = jnp.concatenate([blocks, blocks], 0)
        return lax.dynamic_slice_in_dim(twice, plane, planes, 0)

    kv_send = w_kv.astype(BF16).reshape(w_kv.shape[0], 2, planes, part_heads, HD)
    kv_send = a2a(kv_send.transpose(2, 0, 3, 1, 4), "expert")
    w_kv_part = lax.all_gather(kv_send, "dp", axis=0, tiled=True).reshape(
        full_width, 2 * kv_part
    )
    whole_query = lax.all_gather(w_query.astype(BF16), "dp", axis=1, tiled=True)
    whole_output = lax.all_gather(w_output.astype(BF16), "dp", axis=2, tiled=True)
    down_send = pack_down(w_down, ff_parts).reshape(columns, ff, depth)
    w_dn = a2a(down_send, "dp")
    gu_send = pack_gateup(w_gateup, ff_parts).reshape(columns, depth, 2 * ff)
    w_gu = a2a(gu_send, "dp").reshape(full_width, 2 * ff)

    ints = jnp.concatenate(
        [
            segments[None],
            att_routes.T,
            mlp_routes.T,
            jnp.zeros((3, count), jnp.int32),
        ],
        0,
    )
    near_ints = jnp.stack(relay(ints, "expert"), 0)[None]
    step = 1
    while step < columns:
        pairs = [(i, i ^ step) for i in range(columns)]
        near_ints = jnp.concatenate([near_ints, lax.ppermute(near_ints, "dp", pairs)], 0)
        step *= 2

    residual = tokens.astype(F32)
    seq_res = jnp.concatenate(relay(tokens, "expert"), 0).astype(F32)

    def rms_scale(values):
        return lax.rsqrt(
            core_sum(jnp.sum(values * values, 1, keepdims=True)) / full_width + EPSILON
        )

    seq_scale = rms_scale(seq_res)
    seq_a_half = (seq_res * seq_scale * norm_attn).astype(BF16)
    scale_a = seq_scale[:count]
    rows_a_half = seq_a_half[:count]
    seq_a = both_halves(seq_a_half, core)

    def angles_of(positions):
        frequency = jnp.exp(
            jnp.arange(HD // 2, dtype=F32) * (-2.0 * math.log(10000.0) / HD)
        )
        angle = positions.astype(F32)[:, None] * frequency[None, :]
        cosine, sine = jnp.cos(angle), jnp.sin(angle)
        return jnp.concatenate([cosine, cosine], 1), jnp.concatenate([-sine, sine], 1)

    seq_pos = jnp.arange(seq, dtype=jnp.int32)
    cos_seq, sin_seq = angles_of(seq_pos)
    near_pos = source_planes[:, None] * count + jnp.arange(count, dtype=jnp.int32)[None]
    cos_near, sin_near = angles_of(near_pos.reshape(-1))
    kv_raw = dot(seq_a, w_kv_part).reshape(seq, part_heads, 2, HD)
    keys = kv_raw[:, :, 0]
    turned = jnp.concatenate([keys[..., HD // 2 :], keys[..., : HD // 2]], -1)
    keys = keys * cos_near[:, None] + turned * sin_near[:, None]
    kv_mine = jnp.stack([keys.astype(BF16), kv_raw[:, :, 1].astype(BF16)], 2)
    kv_mine = absolute(kv_mine.reshape(planes, count, 2 * kv_part)).reshape(seq, 2 * kv_part)
    kv_near = relay(kv_mine, "expert")

    seq_ints = near_ints[0]
    own_att = jnp.arange(local_att, dtype=jnp.int32) + plane * local_att
    att_ids = (target_planes[:, None] * local_att + jnp.arange(local_att)[None]).reshape(-1)
    mlp_ids = (target_planes[:, None] * local_mlp + near_local[None]).reshape(-1)
    att_slots = one_hot_slots(seq_ints[:, 1:3], own_att, cap)
    home_att = one_hot_slots(ints[None, 1:3], att_ids, cap)[0]
    home_mlp = one_hot_slots(ints[None, 3:5], mlp_ids, cap)[0]
    every_mlp = near_ints[:, :, 3:5].reshape(-1, 2, count)
    mlp_slots = one_hot_slots(every_mlp, mlp_expert[None], cap)[:, 0]
    other_expert = jnp.sum(every_mlp, 1) - mlp_expert
    row_other = jnp.sum(jnp.where(mlp_slots, other_expert[:, None, :], 0), -1).reshape(-1, 1)

    def by_choice(home, routes, ids):
        named = routes[:, None, :] == ids[None, :, None]
        picks = home[None] & named[:, :, None, :]
        return picks.astype(BF16).reshape(2, -1, count)

    pick_att = by_choice(home_att, ints[1:3], att_ids)
    pick_mlp = by_choice(home_mlp, ints[3:5], mlp_ids)
    flat_mlp = home_mlp.astype(BF16).reshape(n_mlp * cap, count)
    spread = att_slots.astype(BF16)
    row_pos = jnp.sum(
        jnp.where(att_slots, near_pos[:, None, None, :], 0), -1
    ).transpose(1, 0, 2).reshape(-1)
    row_seg = jnp.sum(
        jnp.where(att_slots, seq_ints[:, 0][:, None, None, :], 0), -1
    ).transpose(1, 0, 2).reshape(-1)
    seq_seg = absolute(seq_ints[:, 0]).reshape(seq)
    att_rows = planes * local_att * cap

    def to_expert(rows_half):
        held = shift(list(rows_half.reshape(planes, local_mlp, cap, width)), -1)
        held = jnp.stack(held, 1)
        sent = [held[k % local_mlp].reshape(planes * cap, width) for k in range(columns)]
        own = jnp.concatenate(cross(sent), 0)
        return own, swap(own)

    g_own, g_other = to_expert(dot(flat_mlp, cotangent).astype(BF16))
    raw = hidden_raw(core_at, g_own, g_other, w_dn)

    def gates_of(half_rows, router, routes):
        part = lax.dynamic_slice_in_dim(router, core * width, width, 0).astype(BF16)
        logits = core_sum(ein("de,td->et", part, half_rows))
        experts = router.shape[1]
        named = (
            routes[:, None, :] == jnp.arange(experts, dtype=jnp.int32)[None, :, None]
        ).astype(F32)
        chosen = jnp.sum(named * logits[None], 1)
        return jax.nn.softmax(chosen, axis=0), named, part

    gates_a, named_a, router_a = gates_of(rows_a_half, router_attn, ints[1:3])
    held_a = ein("slct,std->lscd", spread, seq_a.reshape(planes, count, full_width)).astype(BF16)
    held_a = held_a.reshape(local_att, planes * cap, full_width)
    cos_rows, sin_rows = angles_of(row_pos)
    query_raw = ein("lrd,ldf->lrf", held_a, whole_query).reshape(att_rows, feats)
    before = None
    order = [0, planes // 2] + [j for j in range(1, planes) if j != planes // 2]
    for j in order:
        before = att_forward(
            source_planes, query_raw, kv_near[j][None], cos_rows, sin_rows,
            row_pos[:, None], row_seg[:, None], seq_seg[None], j, before,
        )
    mixed_rows, query_rows = before
    mixed_owner = mixed_rows.reshape(local_att, planes * cap, feats)

    def halves(values, axis):
        mine = lax.dynamic_slice_in_dim(values, core * width, width, axis)
        theirs = lax.dynamic_slice_in_dim(values, (1 - core) * width, width, axis)
        return mine, theirs

    out_mine, out_theirs = halves(whole_output, 2)
    given = swap(ein("lrf,lfd->lrd", mixed_owner, out_theirs).astype(BF16))
    branch_a = ein("lrf,lfd->lrd", mixed_owner, out_mine) + given.astype(F32)
    branch_a = branch_a.astype(BF16).reshape(local_att, planes, cap, width)
    home_a = jnp.concatenate(
        shift([branch_a[:, j].reshape(local_att * cap, width) for j in range(planes)], 1), 0
    )
    taken_a = ein("jst,sd->jtd", pick_att, home_a)
    middle = residual + jnp.sum(gates_a[:, :, None] * taken_a, 0)

    scale_b = rms_scale(middle)
    rows_b_half = (middle * scale_b * norm_mlp).astype(BF16)
    gates_b, named_b, router_b = gates_of(rows_b_half, router_mlp, ints[3:5])
    x_own, x_other = to_expert(dot(flat_mlp, rows_b_half).astype(BF16))
    router_wide = jnp.pad(router_mlp.astype(BF16), ((0, 0), (0, HD - n_mlp)))
    place = jnp.stack([core, mlp_expert]).astype(jnp.int32)
    hidden, hidden_gated, grad_both, row_dgate = feed_forward(
        place, x_own, x_other, w_gu, raw, router_wide, row_other
    )

    def mlp_home(rows):
        tail = rows.shape[1:]
        got = cross(list(rows.reshape((columns, planes, cap) + tail)))
        sums = []
        for near in range(local_mlp):
            parts = [got[k].astype(F32) for k in range(near, columns, local_mlp)]
            sums.append(functools.reduce(jnp.add, parts).astype(rows.dtype))
        back = shift(
            [jnp.concatenate([part[j] for part in sums], 0) for j in range(planes)], 1
        )
        return jnp.concatenate(back, 0)

    dgate_home = mlp_home(core_sum(row_dgate[:, 0]))
    given = swap(rows_half(other_at, grad_both, w_gu, width))
    home_db = mlp_home(rows_half(core_at, grad_both, w_gu, width, given))

    def gates_back(gates, grad_gates, named):
        chosen = gates * (grad_gates - jnp.sum(gates * grad_gates, 0, keepdims=True))
        return jnp.sum(chosen[:, None, :] * named, 0).astype(BF16)

    grad_gates_b = jnp.sum(pick_mlp.astype(F32) * dgate_home[None, :, None], 1)
    grad_logit_b = gates_back(gates_b, grad_gates_b, named_b)
    grad_normed_b = ein("st,sd->td", flat_mlp, home_db) + ein("et,de->td", grad_logit_b, router_b)
    grad_router_b = ein("et,td->ed", grad_logit_b, rows_b_half)

    def normalize_back(values, gain, row_scale, grad_normed):
        inner = core_sum(jnp.sum(grad_normed * gain * values, 1, keepdims=True))
        grad_values = (
            row_scale * gain * grad_normed
            - values * (row_scale * row_scale * row_scale) * inner / full_width
        )
        return grad_values, jnp.sum(grad_normed * values * row_scale, 0)

    grad_out = cotangent.astype(F32)
    grad_mid_norm, grad_gain_b = normalize_back(middle, norm_mlp, scale_b, grad_normed_b)
    grad_middle = grad_out + grad_mid_norm

    grad_gates_a = core_sum(jnp.sum(grad_middle[None] * taken_a, 2))
    grad_logit_a = gates_back(gates_a, grad_gates_a, named_a)
    grad_taken_a = (gates_a[:, :, None] * grad_middle[None]).astype(BF16)
    sent_a = ein("jst,jtd->sd", pick_att, grad_taken_a).astype(BF16)
    got_a = shift(list(sent_a.reshape(planes, local_att, cap, width)), -1)
    held_grad_a = both_halves(
        jnp.stack(got_a, 1).reshape(local_att, planes * cap, width), core
    )
    grad_mixed = ein("lrd,lfd->lrf", held_grad_a, whole_output).astype(BF16)
    grad_query, grad_kv_seq = att_backward(
        source_planes, query_rows, grad_mixed.reshape(att_rows, feats),
        jnp.stack(kv_near, 0), cos_rows, sin_rows, cos_seq, sin_seq,
        row_pos[None], row_seg[None], seq_seg[:, None],
    )
    grad_query = grad_query.reshape(local_att, planes * cap, feats)
    grad_kv = lax.psum_scatter(grad_kv_seq, "expert", scatter_dimension=0, tiled=True)
    grad_kv = relative(grad_kv.reshape(planes, count, 2 * kv_part)).reshape(seq, 2 * kv_part)
    query_mine, query_theirs = halves(whole_query, 1)
    kvw_mine, kvw_theirs = halves(w_kv_part, 0)

    def grad_seq(query_half, kv_half):
        rows = ein("lrf,ldf->lrd", grad_query, query_half).astype(BF16)
        rows = ein("slct,lscd->std", spread, rows.reshape(local_att, planes, cap, width))
        return rows.reshape(seq, width) + ein("tf,df->td", grad_kv, kv_half)

    given = swap(grad_seq(query_theirs, kvw_theirs).astype(BF16))
    grad_seq_a = (grad_seq(query_mine, kvw_mine) + given.astype(F32)).astype(BF16)
    back_a = shift(list(grad_seq_a.reshape(planes, count, width)), 1)
    grad_rows_a = functools.reduce(jnp.add, [part.astype(F32) for part in back_a])
    grad_normed_a = grad_rows_a + ein("et,de->td", grad_logit_a, router_a)
    grad_router_a = ein("et,td->ed", grad_logit_a, rows_a_half)
    grad_in_norm, grad_gain_a = normalize_back(residual, norm_attn, scale_a, grad_normed_a)
    grad_tokens = grad_middle + grad_in_norm

    def absolute_halves(own, other):
        first = jnp.where(core == 0, own, other)
        second = jnp.where(core == 0, other, own)
        return jnp.concatenate([first, second], -1)

    x_rows = absolute_halves(x_own, x_other)
    g_rows = absolute_halves(g_own, g_other)
    grad_gu = ein("rd,rf->df", x_rows, grad_both).astype(BF16)
    got_gu = a2a(grad_gu.reshape(columns, depth, 2 * ff), "dp")
    grad_wgateup = unpack_gateup(got_gu.reshape(ff_parts, local_mlp, depth, 2 * ff), ff_parts)
    grad_dn = ein("rf,rsd->sfd", hidden_gated, g_rows.reshape(-1, columns, depth)).astype(BF16)
    got_dn = a2a(grad_dn, "dp")
    grad_wdown = unpack_down(got_dn.reshape(ff_parts, local_mlp, ff, depth))
    grad_woutput = lax.psum_scatter(
        ein("lrf,lrd->lfd", mixed_owner, held_grad_a).astype(BF16),
        "dp",
        scatter_dimension=2,
        tiled=True,
    ).astype(F32)
    grad_wquery = lax.psum_scatter(
        ein("lrd,lrf->ldf", held_a, grad_query).astype(BF16),
        "dp",
        scatter_dimension=1,
        tiled=True,
    ).astype(F32)
    grad_kv_w = lax.psum_scatter(
        ein("td,tf->df", seq_a, grad_kv).astype(BF16), "dp", scatter_dimension=0, tiled=True
    )
    grad_kv_w = a2a(
        grad_kv_w.reshape(planes, w_kv.shape[0], part_heads, 2, HD), "expert"
    )
    grad_wkv = grad_kv_w.transpose(1, 3, 0, 2, 4).astype(F32).reshape(w_kv.shape)

    given = swap(rows_half(other_at, hidden, w_dn, width))
    home_b = mlp_home(rows_half(core_at, hidden, w_dn, width, given))
    taken_b = ein("jst,sd->jtd", pick_mlp, home_b)
    output = middle + jnp.sum(gates_b[:, :, None] * taken_b, 0)

    small = jnp.concatenate(
        [grad_router_a, grad_router_b, grad_gain_a[None], grad_gain_b[None]], 0
    )
    small = total_over(total_over(small, "dp"), "expert")
    routers = both_halves(small[: n_att + n_mlp], core)
    return (
        output.astype(BF16),
        grad_tokens,
        small[n_att + n_mlp],
        small[n_att + n_mlp + 1],
        grad_wkv,
        routers[:n_att].T,
        routers[n_att:].T,
        grad_wquery,
        grad_woutput,
        grad_wgateup,
        grad_wdown,
    )


def solution(mesh):
    in_specs = (
        P(("dp", "expert"), "tensor"),
        P("tensor"),
        P("tensor"),
        P(("dp", "expert"), None, "tensor"),
        P(),
        P(),
        P("expert", "dp", "tensor"),
        P("expert", "tensor", "dp"),
        P("expert", "dp", None, "tensor"),
        P("expert", "tensor", "dp"),
        P(("dp", "expert")),
        P(("dp", "expert"), None),
        P(("dp", "expert"), None),
        P(("dp", "expert"), "tensor"),
    )
    out_specs = (
        P(("dp", "expert"), "tensor"),
        P(("dp", "expert"), "tensor"),
        P("tensor"),
        P("tensor"),
        P(("dp", "expert"), None, "tensor"),
        P(),
        P(),
        P("expert", "dp", "tensor"),
        P("expert", "tensor", "dp"),
        P("expert", "dp", None, "tensor"),
        P("expert", "tensor", "dp"),
    )
    return jax.shard_map(shards, mesh=mesh, in_specs=in_specs, out_specs=out_specs, check_vma=False)
```

time: 1860 us -> 1410 us (0.76)
  waiting for transfers between devices: 933 us -> 673 us
  Pallas kernels: 0 us -> 235 us
  local copies, waits for them, and re-layouts: 280 us -> 61.6 us
  matrix products: 296 us -> 123 us
  blocking collectives: 122 us -> 20.6 us
  starting transfers between devices: 80.9 us -> 172 us
  other arithmetic: 119 us -> 93.1 us
    ppermute x0 -> x59, waiting for transfers between devices: none -> 349 us  [the longest x24 145 us: shift(): lax.ppermute(blocks[j], 'expert', [(i, (i + sign * j) % count) for i in r...]
    all_to_all x15 -> x5, waiting for transfers between devices: 414 us -> 80.9 us  [a2a(): return lax.all_to_all(values, axis, split_axis=0, concat_axis=0, tiled=True)]
    pallas_call x0 -> x15, Pallas kernels: none -> 235 us  [the longest x1 50.2 us: att_backward(): pl.pallas_call(att_bwd_kernel, grid_spec=pltpu.PrefetchScalarGridSpec(num...]
    dot_general x45 -> x26, matrix products: 267 us -> 119 us  [ein(): return jnp.einsum(spec, lhs, rhs, preferred_element_type=F32)]
    unnamed x11 -> x7, waiting for transfers between devices: 137 us -> 0.11 us
    ppermute x0 -> x59, starting transfers between devices: none -> 134 us  [the longest x24 55.1 us: shift(): lax.ppermute(blocks[j], 'expert', [(i, (i + sign * j) % count) for i in r...]
    reshape x12 -> x8, local copies, waits for them, and re-layouts: 124 us -> 18.6 us  [the longest x1 8.7 us: shards(): g_rows.reshape(-1, columns, depth)]
    reduce_scatter x2, waiting for transfers between devices: 0.01 us -> 82.5 us  [the longest x1 82.5 us: shards(): lax.psum_scatter(grad_kv_seq, 'expert', scatter_dimension=0, tiled=True)]
  transfers between devices with their start and end apart: 47 -> 92, of which waited for: 28 -> 43; matrix products, arithmetic and copies ran while one was open for 27% -> 17% of each run, Pallas kernels for 0% -> 10%
where the time goes in v2:
time: 1410 us; the launch traced here: 1390 us
  waiting for transfers between devices  673 us (48%)
  Pallas kernels  235 us (17%)
  starting transfers between devices  172 us (12%)
  matrix products  123 us (9%)
  other arithmetic  93.1 us (7%)
  local copies, waits for them, and re-layouts  61.6 us (4%)
  blocking collectives  20.6 us (1%)
  between operations  16.7 us (1%)
    ppermute x24, waiting for transfers between devices, shift(): lax.ppermute(blocks[j], 'expert', [(i, (i + sign * j) % count) for i in r...  145 us
    ppermute x15, waiting for transfers between devices, cross(): lax.ppermute(blocks[k], 'dp', [(i, i ^ k) for i in range(count)])  144 us
    dot_general x26, matrix products, ein(): return jnp.einsum(spec, lhs, rhs, preferred_element_type=F32)  119 us
    ppermute x4, waiting for transfers between devices, total_over(): lax.ppermute(values, axis, [(i, i ^ step) for i in range(count)])  118 us
    reduce_scatter x1, waiting for transfers between devices, shards(): lax.psum_scatter(grad_kv_seq, 'expert', scatter_dimension=0, tiled=True)  82.5 us
    all_to_all x5, waiting for transfers between devices, a2a(): return lax.all_to_all(values, axis, split_axis=0, concat_axis=0, tiled=True)  80.9 us
    ppermute x24, starting transfers between devices, shift(): lax.ppermute(blocks[j], 'expert', [(i, (i + sign * j) % count) for i in r...  55.1 us
    ppermute x9, waiting for transfers between devices, relay(): lax.ppermute(down[-1], axis, [(i + 1, i) for i in range(count - 1)])  54.6 us
  transfers between devices with their start and end apart: 92, of which 43 were waited for; matrix products, arithmetic and copies ran while one was open for 17% of the time, Pallas kernels for 10%

profile of v2, /device:TPU:0, one launch (start us, length us, event | category | flops | bytes accessed | tf_op | source)
XLA Modules:
  0.0 1394.5 jit_solution(4531490180520743846)
XLA Ops:
  9.1 20.6 %all_to_all.30 = bf16[4,128,2,2,128]{4,2,3,1,0:T(2,128)(2,1)S(1)} all-to-all(bf16[4,128,2,2,128]{4,2,3,1,0:T(2,128)(2,1)S(1)} %copy.282), channel_id=1, replica_groups=mesh['dp'=4,'expert'=4,'tensor'=2] {'expert'}, dimensions={0} | all-to-all | bytes 1048576 | tf_op jit(solution)/shard_map/all_to_all | solution.py:38
  44.5 8.4 collective-permute-done
  58.8 7.5 collective-permute-done.4
  67.6 5.3 collective-permute-start.3
  78.9 7.0 pack_down.1
  85.9 5.2 all-to-all-start.2
  98.3 5.0 fusion.87
  131.7 5.6 collective-permute-start.18
  143.3 14.1 %collective-permute-done.14 = s32[8,256]{1,0:T(8,128)S(1)} collective-permute-done((s32[8,256]{1,0:T(8,128)S(1)}, s32[8,256]{1,0:T(8,128)S(1)}, u32[]{:S(2)}, u32[]{:S(2)}) %collective-permute-start.14) | collective-permute-done | bytes 8224 | tf_op jit(solution)/shard_map/ppermute | solution.py:59
  160.2 6.0 collective-permute-start.19
  170.3 15.1 %collective-permute-done.16 = bf16[1024,512]{1,0:T(8,128)(2,1)} collective-permute-done((bf16[1024,512]{1,0:T(8,128)(2,1)}, bf16[1024,512]{1,0:T(8,128)(2,1)}, u32[]{:S(2)}, u32[]{:S(2)}) %collective-permute-start.16) | collective-permute-done | bytes 1048608 | tf_op jit(solution)/shard_map/ppermute | solution.py:59
  189.3 4.6 collective-permute-start.20
  201.1 9.6 collective-permute-done.17
  216.8 9.6 fusion.146
  226.4 8.8 attention_fwd.4
  235.2 8.8 attention_fwd.5
  244.0 8.8 attention_fwd.6
  252.9 8.9 attention_fwd.7
  261.8 37.6 %all-gather.8.cloned.1.call-done = bf16[2,1024,2048]{2,1,0:T(8,128)(2,1)} async-done(((bf16[2,1024,512]{2,1,0:T(8,128)(2,1)}), bf16[2,1024,2048]{2,1,0:T(8,128)(2,1)}) %all-gather.8.cloned.1.call-update) | async-done | bytes 8388624 | tf_op jit(solution)/shard_map/all_gather | solution.py:530
  299.3 5.7 fusion.23
  311.7 25.8 %pack_gateup.1 = bf16[2,2,512,2816]{3,2,1,0:T(8,128)(2,1)} custom-call(f32[2,512,2,2816]{3,2,1,0:T(2,128)} %src.2), custom_call_target="tpu_custom_call" | custom-call | tf_op jit(solution)/shard_map/pack_gateup/pallas_call | solution.py:116
  337.5 6.3 all-to-all-start.1
  354.6 9.2 collective-permute-done.24
  367.5 21.9 %collective-permute-done.23 = bf16[192,1024]{1,0:T(8,128)(2,1)} collective-permute-done((bf16[192,1024]{1,0:T(8,128)(2,1)}, bf16[192,1024]{1,0:T(8,128)(2,1)}, u32[]{:S(2)}, u32[]{:S(2)}) %collective-permute-start.23) | collective-permute-done | bytes 393248 | tf_op jit(solution)/shard_map/ppermute | solution.py:66
  397.0 7.7 collective-permute-start.29
  416.0 11.3 collective-permute-done.28
  434.3 54.6 %collective-permute-done.39 = bf16[384,1024]{1,0:T(8,128)(2,1)S(1)} collective-permute-done((bf16[384,1024]{1,0:T(8,128)(2,1)S(1)}, bf16[384,1024]{1,0:T(8,128)(2,1)S(1)}, u32[]{:S(2)}, u32[]{:S(2)}) %collective-permute-start.39) | collective-permute-done | bytes 786464 | tf_op jit(solution)/shard_map/ppermute | solution.py:74
  489.5 16.3 %collective-permute-done.38 = bf16[384,1024]{1,0:T(8,128)(2,1)S(1)} collective-permute-done((bf16[384,1024]{1,0:T(8,128)(2,1)S(1)}, bf16[384,1024]{1,0:T(8,128)(2,1)S(1)}, u32[]{:S(2)}, u32[]{:S(2)}) %collective-permute-start.38) | collective-permute-done | bytes 786464 | tf_op jit(solution)/shard_map/ppermute | solution.py:74
  508.0 14.7 %collective-permute-done.32 = bf16[384,1024]{1,0:T(8,128)(2,1)S(1)} collective-permute-done((bf16[384,1024]{1,0:T(8,128)(2,1)S(1)}, bf16[384,1024]{1,0:T(8,128)(2,1)S(1)}, u32[]{:S(2)}, u32[]{:S(2)}) %collective-permute-start.32) | collective-permute-done | bytes 786464 | tf_op jit(solution)/shard_map/ppermute | solution.py:74
  522.7 14.8 %collective-permute-done.31 = bf16[384,1024]{1,0:T(8,128)(2,1)S(1)} collective-permute-done((bf16[384,1024]{1,0:T(8,128)(2,1)S(1)}, bf16[384,1024]{1,0:T(8,128)(2,1)S(1)}, u32[]{:S(2)}, u32[]{:S(2)}) %collective-permute-start.31) | collective-permute-done | bytes 786464 | tf_op jit(solution)/shard_map/ppermute | solution.py:74
  552.4 15.1 %hidden_raw.1.raw = f32[1536,1408]{1,0:T(8,128)} custom-call(s32[1]{0:T(128)} %bitcast.59.core.which, bf16[1536,1024]{1,0:T(8,128)(2,1)} %pad_maximum_fusion.4.g_own, bf16[1536,1024]{1,0:T(8,128)(2,1)} %collective-permute-done.40.g_other, bf16[4,1408,512]{2,1,0:T(8,128)(2,1)} %all-to-all-done.2.w_dn.weights), custom_call_target="tpu_custom_call" | custom-call | tf_op jit(solution)/shard_map/hidden_raw/pallas_call | solution.py:340
  567.5 31.3 %feed_forward.1 = (bf16[1536,1408]{1,0:T(8,128)(2,1)}, bf16[1536,1408]{1,0:T(8,128)(2,1)}, bf16[1536,2816]{1,0:T(8,128)(2,1)}, f32[1536,1]{1,0:T(8,128)}) custom-call(s32[2]{0:T(128)} %pad_add_fusion.4.place, bf16[1536,1024]{1,0:T(8,128)(2,1)} %pad_maximum_fusion.3.x_own, bf16[1536,1024]{1,0:T(8,128)(2,1)} %collective-permute-done.33.x_other, ...), custom_call_target="tpu_custom_call" | custom-call | tf_op jit(solution)/shard_map/feed_forward/pallas_call | solution.py:394
  598.8 14.1 %rows_half.6 = bf16[1536,1024]{1,0:T(8,128)(2,1)} custom-call(s32[1]{0:T(128)S(6)} %sub.97.which, bf16[1536,2816]{1,0:T(8,128)(2,1)} %get-tuple-element.33.lhs, bf16[2048,2816]{1,0:T(8,128)(2,1)} %bitcast.72.w_gu.weights), custom_call_target="tpu_custom_call" | custom-call | tf_op jit(solution)/shard_map/rows_half/pallas_call | solution.py:458
  612.9 9.5 rows_half.4
  642.8 14.3 %rows_half.7 = bf16[1536,1024]{1,0:T(8,128)(2,1)} custom-call(s32[1]{0:T(128)} %bitcast.59.core.which, bf16[1536,2816]{1,0:T(8,128)(2,1)} %get-tuple-element.33.lhs, bf16[2048,2816]{1,0:T(8,128)(2,1)} %bitcast.72.w_gu.weights, bf16[1536,1024]{1,0:T(8,128)(2,1)} %collective-permute-done.50.rest_0_), custom_call_target="tpu_custom_call" | custom-call | tf_op jit(solution)/shard_map/rows_half/pallas_call | solution.py:458
  665.5 10.1 rows_half.5
  683.5 15.4 %collective-permute-done.52 = bf16[4,96,1024]{2,1,0:T(8,128)(2,1)} collective-permute-done((bf16[4,96,1024]{2,1,0:T(8,128)(2,1)}, bf16[4,96,1024]{2,1,0:T(8,128)(2,1)}, u32[]{:S(2)}, u32[]{:S(2)}) %collective-permute-start.52) | collective-permute-done | bytes 786464 | tf_op jit(solution)/shard_map/ppermute | solution.py:74
  706.2 22.8 %collective-permute-done.44 = bf16[4,96,1024]{2,1,0:T(8,128)(2,1)S(1)} collective-permute-done((bf16[4,96,1024]{2,1,0:T(8,128)(2,1)S(1)}, bf16[4,96,1024]{2,1,0:T(8,128)(2,1)S(1)}, u32[]{:S(2)}, u32[]{:S(2)}) %collective-permute-start.44) | collective-permute-done | bytes 786464 | tf_op jit(solution)/shard_map/ppermute | solution.py:74
  737.3 5.0 collective-permute-done.56
  743.4 7.4 collective-permute-done.47
  750.8 16.7 %collective-permute-done.48 = bf16[192,1024]{1,0:T(8,128)(2,1)S(1)} collective-permute-done((bf16[192,1024]{1,0:T(8,128)(2,1)S(1)}, bf16[192,1024]{1,0:T(8,128)(2,1)S(1)}, u32[]{:S(2)}, u32[]{:S(2)}) %collective-permute-start.48) | collective-permute-done | bytes 393248 | tf_op jit(solution)/shard_map/ppermute | solution.py:66
  771.2 8.3 collective-permute-start.67
  783.2 9.2 collective-permute-done.67
  792.4 15.8 %collective-permute-done.66 = bf16[2,96,1024]{2,1,0:T(8,128)(2,1)S(1)} collective-permute-done((bf16[2,96,1024]{2,1,0:T(8,128)(2,1)S(1)}, bf16[2,96,1024]{2,1,0:T(8,128)(2,1)S(1)}, u32[]{:S(2)}, u32[]{:S(2)}) %collective-permute-start.66) | collective-permute-done | bytes 393248 | tf_op jit(solution)/shard_map/ppermute | solution.py:66
  819.9 11.2 fusion.22
  831.1 50.2 %attention_bwd.1 = (bf16[768,1024]{1,0:T(8,128)(2,1)}, bf16[4,1024,512]{2,1,0:T(8,128)(2,1)}) custom-call(s32[4]{0:T(128)} %and_select_fusion.place, bf16[768,1024]{1,0:T(8,128)(2,1)} %get-tuple-element.35.q_in, bf16[768,1024]{1,0:T(8,128)(2,1)} %bitcast.369, bf16[4,1024,512]{2,1,0:T(8,128)(2,1)} %pad_maximum_fusion.2.kv, ...), custom_call_target="tpu_custom_call" | custom-call | tf_op jit(solution)/shard_map/attention_bwd/pallas_call | solution.py:291
  881.4 82.5 %reduce-scatter.5.cloned.1.call-done = bf16[1,1024,512]{2,1,0:T(8,128)(2,1)} async-done(((bf16[4,1024,512]{2,1,0:T(8,128)(2,1)}), bf16[1,1024,512]{2,1,0:T(8,128)(2,1)}) %reduce-scatter.5.cloned.1.call-update) | async-done | bytes 1048592 | tf_op jit(solution)/shard_map/reduce_scatter | solution.py:728
  966.5 5.9 convolution_convert_fusion.4
  972.7 10.2 convolution_convert_fusion.2
  991.1 8.7 copy.327
  999.8 8.6 convolution_convert_fusion.1
  1008.4 14.8 %convert_bitcast_fusion = bf16[4,1408,512]{1,2,0:T(8,128)(2,1)} fusion(bf16[1536,4,512]{0,2,1:T(8,128)(2,1)} %bitcast.360, bf16[1536,1408]{1,0:T(8,128)(2,1)} %get-tuple-element.38), kind=kOutput, calls=%fused_computation.5 | convolution fusion | flops 8861253632 | bytes 16384000 | tf_op jit(solution)/shard_map/rf,rsd->sfd/dot_general | solution.py:26
  1023.3 5.6 all-to-all-start.5
  1032.4 25.3 %convolution_convert_fusion = bf16[2048,2816]{1,0:T(8,128)(2,1)} fusion(bf16[1536,2816]{1,0:T(8,128)(2,1)} %get-tuple-element.33.lhs, bf16[1536,1024]{1,0:T(8,128)(2,1)S(1)} %get-tuple-element.58, bf16[1536,1024]{1,0:T(8,128)(2,1)S(1)} %get-tuple-element.57), kind=kOutput, calls=%fused_computation | convolution fusion | flops 17735090176 | bytes 26476544 | tf_op jit(solution)/shard_map/rd,rf->df/dot_general | solution.py:26
  1057.7 69.0 %all-to-all-done.5 = bf16[4,1408,512]{1,2,0:T(8,128)(2,1)} async-done(((bf16[4,1408,512]{1,2,0:T(8,128)(2,1)}), bf16[4,1408,512]{1,2,0:T(8,128)(2,1)}, u32[]{:S(2)}, u32[]{:S(2)}) %all-to-all-start.5) | async-done | bytes 5767200 | tf_op jit(solution)/shard_map/all_to_all | solution.py:38
  1126.6 6.6 all-to-all-start.4
  1155.1 10.0 collective-permute-done.72
  1165.1 32.9 %collective-permute-done.71 = bf16[256,1024]{1,0:T(8,128)(2,1)S(1)} collective-permute-done((bf16[256,1024]{1,0:T(8,128)(2,1)S(1)}, bf16[256,1024]{1,0:T(8,128)(2,1)S(1)}, u32[]{:S(2)}, u32[]{:S(2)}) %collective-permute-start.71) | collective-permute-done | bytes 524320 | tf_op jit(solution)/shard_map/ppermute | solution.py:66
  1200.8 112.2 %collective-permute-done.75 = f32[18,1024]{1,0:T(8,128)S(1)} collective-permute-done((f32[18,1024]{1,0:T(8,128)S(1)}, f32[18,1024]{1,0:T(8,128)S(1)}, u32[]{:S(2)}, u32[]{:S(2)}) %collective-permute-start.75) | collective-permute-done | bytes 73760 | tf_op jit(solution)/shard_map/ppermute | solution.py:45
  1314.6 5.6 collective-permute-done.76
  1321.7 8.4 copy.318
  1330.1 7.5 unpack_down.1
  1337.6 14.7 %unpack_gateup.1 = f32[2,512,2,2816]{3,2,1,0:T(2,128)} custom-call(bf16[2,2,512,2816]{3,2,1,0:T(8,128)(2,1)} %bitcast.155.src), custom_call_target="tpu_custom_call" | custom-call | tf_op jit(solution)/shard_map/unpack_gateup/pallas_call | solution.py:142
  1363.9 11.9 all-to-all-done.3
  (556 shorter events, 296.3 us)
Async XLA Ops:
  7.2 109.3 %all-gather.6.cloned.1.call-start = ((), (), s32[]{:S(2)}) async-start(), calls=%async_computation.11 | async-start | bytes 2621440 | tf_op jit(solution)/shard_map/all_gather | solution.py:526
  30.6 186.2 %all-gather.4.cloned.1.call-start = ((), (), s32[]{:S(2)}) async-start(), calls=%async_computation.10 | async-start | bytes 10485760 | tf_op jit(solution)/shard_map/all_gather | solution.py:529
  34.6 264.7 %all-gather.8.cloned.1.call-start = ((), (), s32[]{:S(2)}) async-start(), calls=%async_computation.12 | async-start | bytes 10485760 | tf_op jit(solution)/shard_map/all_gather | solution.py:530
  66.3 25.1 %collective-permute-start.5 = (bf16[256,1024]{1,0:T(8,128)(2,1)S(1)}, bf16[256,1024]{1,0:T(8,128)(2,1)}, u32[]{:S(2)}, u32[]{:S(2)}) collective-permute-start(bf16[256,1024]{1,0:T(8,128)(2,1)S(1)} %collective-permute-done.4), channel_id=1, source_target_pairs={{2,0},{4,2},{6,4},{3,1},{5,3},{7,5},{10,8},{12,10},{14,12},{11,9},... | collective-permute-start | bytes 1572872 | tf_op jit(solution)/shard_map/ppermute | solution.py:59
  67.6 25.0 %collective-permute-start.3 = (bf16[256,1024]{1,0:T(8,128)(2,1)S(1)}, bf16[256,1024]{1,0:T(8,128)(2,1)}, u32[]{:S(2)}, u32[]{:S(2)}) collective-permute-start(bf16[256,1024]{1,0:T(8,128)(2,1)S(1)} %collective-permute-done.2), channel_id=1, source_target_pairs={{0,2},{2,4},{4,6},{1,3},{3,5},{5,7},{8,10},{10,12},{12,14},{9,11},... | collective-permute-start | bytes 1572872 | tf_op jit(solution)/shard_map/ppermute | solution.py:58
  73.1 33.6 %collective-permute-start.9 = (s32[8,256]{1,0:T(8,128)S(1)}, s32[8,256]{1,0:T(8,128)S(1)}, u32[]{:S(2)}, u32[]{:S(2)}) collective-permute-start(s32[8,256]{1,0:T(8,128)S(1)} %get-tuple-element.126), channel_id=1, source_target_pairs={{2,0},{4,2},{6,4},{3,1},{5,3},{7,5},{10,8},{12,10},{14,12},{11,9},... | collective-permute-start | bytes 24584 | tf_op jit(solution)/shard_map/ppermute | solution.py:59
  74.4 33.6 %collective-permute-start.10 = (s32[8,256]{1,0:T(8,128)S(1)}, s32[8,256]{1,0:T(8,128)S(1)}, u32[]{:S(2)}, u32[]{:S(2)}) collective-permute-start(s32[8,256]{1,0:T(8,128)S(1)} %get-tuple-element.126), channel_id=1, source_target_pairs={{0,2},{2,4},{4,6},{1,3},{3,5},{5,7},{8,10},{10,12},{12,14},{9,11},... | collective-permute-start | bytes 24584 | tf_op jit(solution)/shard_map/ppermute | solution.py:58
  85.9 251.6 %all-to-all-start.2 = ((bf16[4,1408,512]{2,1,0:T(8,128)(2,1)}), bf16[4,1408,512]{2,1,0:T(8,128)(2,1)}, u32[]{:S(2)}, u32[]{:S(2)}) async-start(bf16[4,1408,512]{2,1,0:T(8,128)(2,1)} %bitcast.337), calls=%async_computation.2 | async-start | bytes 11534336 | tf_op jit(solution)/shard_map/all_to_all | solution.py:38
  106.7 30.7 %collective-permute-start.13 = (s32[8,256]{1,0:T(8,128)S(1)}, s32[8,256]{1,0:T(8,128)S(1)}, u32[]{:S(2)}, u32[]{:S(2)}) collective-permute-start(s32[8,256]{1,0:T(8,128)S(1)} %collective-permute-done.9), channel_id=1, source_target_pairs={{2,0},{4,2},{6,4},{3,1},{5,3},{7,5},{10,8},{12,10},{14,12},{11,9},... | collective-permute-start | bytes 24584 | tf_op jit(solution)/shard_map/ppermute | solution.py:59
  108.0 30.7 %collective-permute-start.11 = (s32[8,256]{1,0:T(8,128)S(1)}, s32[8,256]{1,0:T(8,128)S(1)}, u32[]{:S(2)}, u32[]{:S(2)}) collective-permute-start(s32[8,256]{1,0:T(8,128)S(1)} %collective-permute-done.10), channel_id=1, source_target_pairs={{0,2},{2,4},{4,6},{1,3},{3,5},{5,7},{8,10},{10,12},{12,14},{9,11},... | collective-permute-start | bytes 24584 | tf_op jit(solution)/shard_map/ppermute | solution.py:58
  130.4 28.3 %collective-permute-start.15 = (bf16[1024,512]{1,0:T(8,128)(2,1)S(1)}, bf16[1024,512]{1,0:T(8,128)(2,1)}, u32[]{:S(2)}, u32[]{:S(2)}) collective-permute-start(bf16[1024,512]{1,0:T(8,128)(2,1)S(1)} %bitcast.346), channel_id=1, source_target_pairs={{2,0},{4,2},{6,4},{3,1},{5,3},{7,5},{10,8},{12,10},{14,12},{11,9},... | collective-permute-start | bytes 3145736 | tf_op jit(solution)/shard_map/ppermute | solution.py:59
  131.7 28.5 %collective-permute-start.18 = (bf16[1024,512]{1,0:T(8,128)(2,1)S(1)}, bf16[1024,512]{1,0:T(8,128)(2,1)}, u32[]{:S(2)}, u32[]{:S(2)}) collective-permute-start(bf16[1024,512]{1,0:T(8,128)(2,1)S(1)} %bitcast.347), channel_id=1, source_target_pairs={{0,2},{2,4},{4,6},{1,3},{3,5},{5,7},{8,10},{10,12},{12,14},{9,11},... | collective-permute-start | bytes 3145736 | tf_op jit(solution)/shard_map/ppermute | solution.py:58
  137.4 20.0 %collective-permute-start.14 = (s32[8,256]{1,0:T(8,128)S(1)}, s32[8,256]{1,0:T(8,128)S(1)}, u32[]{:S(2)}, u32[]{:S(2)}) collective-permute-start(s32[8,256]{1,0:T(8,128)S(1)} %collective-permute-done.13), channel_id=1, source_target_pairs={{2,0},{4,2},{6,4},{3,1},{5,3},{7,5},{10,8},{12,10},{14,12},{11,9},... | collective-permute-start | bytes 24584 | tf_op jit(solution)/shard_map/ppermute | solution.py:59
  138.7 19.8 %collective-permute-start.12 = (s32[8,256]{1,0:T(8,128)S(1)}, s32[8,256]{1,0:T(8,128)S(1)}, u32[]{:S(2)}, u32[]{:S(2)}) collective-permute-start(s32[8,256]{1,0:T(8,128)S(1)} %collective-permute-done.11), channel_id=1, source_target_pairs={{0,2},{2,4},{4,6},{1,3},{3,5},{5,7},{8,10},{10,12},{12,14},{9,11},... | collective-permute-start | bytes 24584 | tf_op jit(solution)/shard_map/ppermute | solution.py:58
  158.7 26.7 %collective-permute-start.16 = (bf16[1024,512]{1,0:T(8,128)(2,1)}, bf16[1024,512]{1,0:T(8,128)(2,1)}, u32[]{:S(2)}, u32[]{:S(2)}) collective-permute-start(bf16[1024,512]{1,0:T(8,128)(2,1)} %collective-permute-done.15), channel_id=1, source_target_pairs={{2,0},{4,2},{6,4},{3,1},{5,3},{7,5},{10,8},{12,10},{14,12},{11,9},... | collective-permute-start | bytes 3145736 | tf_op jit(solution)/shard_map/ppermute | solution.py:59
  160.2 29.1 %collective-permute-start.19 = (bf16[1024,512]{1,0:T(8,128)(2,1)}, bf16[1024,512]{1,0:T(8,128)(2,1)}, u32[]{:S(2)}, u32[]{:S(2)}) collective-permute-start(bf16[1024,512]{1,0:T(8,128)(2,1)} %collective-permute-done.18), channel_id=1, source_target_pairs={{0,2},{2,4},{4,6},{1,3},{3,5},{5,7},{8,10},{10,12},{12,14},{9,11},... | collective-permute-start | bytes 3145736 | tf_op jit(solution)/shard_map/ppermute | solution.py:58
  185.4 25.3 %collective-permute-start.17 = (bf16[1024,512]{1,0:T(8,128)(2,1)}, bf16[1024,512]{1,0:T(8,128)(2,1)}, u32[]{:S(2)}, u32[]{:S(2)}) collective-permute-start(bf16[1024,512]{1,0:T(8,128)(2,1)} %collective-permute-done.16), channel_id=1, source_target_pairs={{2,0},{4,2},{6,4},{3,1},{5,3},{7,5},{10,8},{12,10},{14,12},{11,9},... | collective-permute-start | bytes 3145736 | tf_op jit(solution)/shard_map/ppermute | solution.py:59
  189.3 25.2 %collective-permute-start.20 = (bf16[1024,512]{1,0:T(8,128)(2,1)}, bf16[1024,512]{1,0:T(8,128)(2,1)S(1)}, u32[]{:S(2)}, u32[]{:S(2)}) collective-permute-start(bf16[1024,512]{1,0:T(8,128)(2,1)} %collective-permute-done.19), channel_id=1, source_target_pairs={{0,2},{2,4},{4,6},{1,3},{3,5},{5,7},{8,10},{10,12},{12,14},{9,11},... | collective-permute-start | bytes 3145736 | tf_op jit(solution)/shard_map/ppermute | solution.py:58
  305.0 41.4 %collective-permute-start.21 = (bf16[2,384,1024]{2,1,0:T(8,128)(2,1)}, bf16[2,384,1024]{2,1,0:T(8,128)(2,1)}, u32[]{:S(2)}, u32[]{:S(2)}) collective-permute-start(bf16[2,384,1024]{2,1,0:T(8,128)(2,1)} %fusion.23), channel_id=1, source_target_pairs={{0,1},{1,0},{2,3},{3,2},{4,5},{5,4},{6,7},{7,6},{8,9},{9,8},{10,11... | collective-permute-start | bytes 4718600 | tf_op jit(solution)/shard_map/ppermute | solution.py:34
  307.4 86.2 %collective-permute-start.36 = (bf16[2,96,1024]{2,1,0:T(8,128)(2,1)}, bf16[2,96,1024]{2,1,0:T(8,128)(2,1)}, u32[]{:S(2)}, u32[]{:S(2)}) collective-permute-start(bf16[2,96,1024]{2,1,0:T(8,128)(2,1)} %bitcast.79), channel_id=1, source_target_pairs={{0,2},{2,4},{4,6},{6,0},{1,3},{3,5},{5,7},{7,1},{8,10},{10,12},{12... | collective-permute-start | bytes 1179656 | tf_op jit(solution)/shard_map/ppermute | solution.py:66
  309.3 84.3 %collective-permute-start.35 = (bf16[2,96,1024]{2,1,0:T(8,128)(2,1)}, bf16[2,96,1024]{2,1,0:T(8,128)(2,1)}, u32[]{:S(2)}, u32[]{:S(2)}) collective-permute-start(bf16[2,96,1024]{2,1,0:T(8,128)(2,1)} %bitcast.77), channel_id=1, source_target_pairs={{0,4},{2,6},{4,0},{6,2},{1,5},{3,7},{5,1},{7,3},{8,12},{10,14},{12... | collective-permute-start | bytes 1179656 | tf_op jit(solution)/shard_map/ppermute | solution.py:66
  337.5 230.0 %all-to-all-start.1 = ((bf16[4,512,2816]{2,1,0:T(8,128)(2,1)}), bf16[4,512,2816]{2,1,0:T(8,128)(2,1)}, u32[]{:S(2)}, u32[]{:S(2)}) async-start(bf16[4,512,2816]{2,1,0:T(8,128)(2,1)} %bitcast.335), calls=%async_computation.1 | async-start | bytes 23068672 | tf_op jit(solution)/shard_map/all_to_all | solution.py:38
  343.9 620.1 %reduce-scatter.5.cloned.1.call-start = ((), (), s32[]{:S(2)}) async-start(), calls=%async_computation.13 | async-start | bytes 5242880 | tf_op jit(solution)/shard_map/reduce_scatter | solution.py:728
  353.3 36.1 %collective-permute-start.23 = (bf16[192,1024]{1,0:T(8,128)(2,1)}, bf16[192,1024]{1,0:T(8,128)(2,1)}, u32[]{:S(2)}, u32[]{:S(2)}) collective-permute-start(bf16[192,1024]{1,0:T(8,128)(2,1)} %bitcast.47), channel_id=1, source_target_pairs={{0,4},{2,6},{4,0},{6,2},{1,5},{3,7},{5,1},{7,3},{8,12},{10,14},{12... | collective-permute-start | bytes 1179656 | tf_op jit(solution)/shard_map/ppermute | solution.py:66
  353.9 35.6 %collective-permute-start.22 = (bf16[192,1024]{1,0:T(8,128)(2,1)S(1)}, bf16[192,1024]{1,0:T(8,128)(2,1)}, u32[]{:S(2)}, u32[]{:S(2)}) collective-permute-start(bf16[192,1024]{1,0:T(8,128)(2,1)S(1)} %bitcast.389), channel_id=1, source_target_pairs={{0,2},{2,4},{4,6},{6,0},{1,3},{3,5},{5,7},{7,1},{8,10},{10,12},{12... | collective-permute-start | bytes 1179656 | tf_op jit(solution)/shard_map/ppermute | solution.py:66
  363.8 29.8 %collective-permute-start.34 = (bf16[2,96,1024]{2,1,0:T(8,128)(2,1)}, bf16[2,96,1024]{2,1,0:T(8,128)(2,1)S(1)}, u32[]{:S(2)}, u32[]{:S(2)}) collective-permute-start(bf16[2,96,1024]{2,1,0:T(8,128)(2,1)} %bitcast.75), channel_id=1, source_target_pairs={{0,6},{2,0},{4,2},{6,4},{1,7},{3,1},{5,3},{7,5},{8,14},{10,8},{12,... | collective-permute-start | bytes 1179656 | tf_op jit(solution)/shard_map/ppermute | solution.py:66
  404.7 22.6 %collective-permute-start.28 = (bf16[2,96,1024]{2,1,0:T(8,128)(2,1)S(1)}, bf16[2,96,1024]{2,1,0:T(8,128)(2,1)S(1)}, u32[]{:S(2)}, u32[]{:S(2)}) collective-permute-start(bf16[2,96,1024]{2,1,0:T(8,128)(2,1)S(1)} %bitcast.386), channel_id=1, source_target_pairs={{0,4},{2,6},{4,0},{6,2},{1,5},{3,7},{5,1},{7,3},{8,12},{10,14},{12... | collective-permute-start | bytes 1179656 | tf_op jit(solution)/shard_map/ppermute | solution.py:66
  406.8 23.8 %collective-permute-start.27 = (bf16[2,96,1024]{2,1,0:T(8,128)(2,1)S(1)}, bf16[2,96,1024]{2,1,0:T(8,128)(2,1)S(1)}, u32[]{:S(2)}, u32[]{:S(2)}) collective-permute-start(bf16[2,96,1024]{2,1,0:T(8,128)(2,1)S(1)} %bitcast.383), channel_id=1, source_target_pairs={{0,6},{2,0},{4,2},{6,4},{1,7},{3,1},{5,3},{7,5},{8,14},{10,8},{12,... | collective-permute-start | bytes 1179656 | tf_op jit(solution)/shard_map/ppermute | solution.py:66
  409.9 79.1 %collective-permute-start.39 = (bf16[384,1024]{1,0:T(8,128)(2,1)S(1)}, bf16[384,1024]{1,0:T(8,128)(2,1)S(1)}, u32[]{:S(2)}, u32[]{:S(2)}) collective-permute-start(bf16[384,1024]{1,0:T(8,128)(2,1)S(1)} %bitcast.378), channel_id=1, source_target_pairs={{0,24},{8,16},{16,8},{24,0},{1,25},{9,17},{17,9},{25,1},{2,26},{10... | collective-permute-start | bytes 2359304 | tf_op jit(solution)/shard_map/ppermute | solution.py:74
  412.8 93.1 %collective-permute-start.37 = (bf16[384,1024]{1,0:T(8,128)(2,1)S(1)}, bf16[384,1024]{1,0:T(8,128)(2,1)S(1)}, u32[]{:S(2)}, u32[]{:S(2)}) collective-permute-start(bf16[384,1024]{1,0:T(8,128)(2,1)S(1)} %bitcast.379), channel_id=1, source_target_pairs={{0,8},{8,0},{16,24},{24,16},{1,9},{9,1},{17,25},{25,17},{2,10},{10... | collective-permute-start | bytes 2359304 | tf_op jit(solution)/shard_map/ppermute | solution.py:74
  414.1 91.7 %collective-permute-start.38 = (bf16[384,1024]{1,0:T(8,128)(2,1)S(1)}, bf16[384,1024]{1,0:T(8,128)(2,1)S(1)}, u32[]{:S(2)}, u32[]{:S(2)}) collective-permute-start(bf16[384,1024]{1,0:T(8,128)(2,1)S(1)} %bitcast.354), channel_id=1, source_target_pairs={{0,16},{8,24},{16,0},{24,8},{1,17},{9,25},{17,1},{25,9},{2,18},{10... | collective-permute-start | bytes 2359304 | tf_op jit(solution)/shard_map/ppermute | solution.py:74
  430.9 91.8 %collective-permute-start.32 = (bf16[384,1024]{1,0:T(8,128)(2,1)S(1)}, bf16[384,1024]{1,0:T(8,128)(2,1)S(1)}, u32[]{:S(2)}, u32[]{:S(2)}) collective-permute-start(bf16[384,1024]{1,0:T(8,128)(2,1)S(1)} %bitcast.380), channel_id=1, source_target_pairs={{0,24},{8,16},{16,8},{24,0},{1,25},{9,17},{17,9},{25,1},{2,26},{10... | collective-permute-start | bytes 2359304 | tf_op jit(solution)/shard_map/ppermute | solution.py:74
  433.8 103.8 %collective-permute-start.31 = (bf16[384,1024]{1,0:T(8,128)(2,1)S(1)}, bf16[384,1024]{1,0:T(8,128)(2,1)S(1)}, u32[]{:S(2)}, u32[]{:S(2)}) collective-permute-start(bf16[384,1024]{1,0:T(8,128)(2,1)S(1)} %bitcast.357), channel_id=1, source_target_pairs={{0,16},{8,24},{16,0},{24,8},{1,17},{9,25},{17,1},{25,9},{2,18},{10... | collective-permute-start | bytes 2359304 | tf_op jit(solution)/shard_map/ppermute | solution.py:74
  489.0 48.7 %collective-permute-start.30 = (bf16[384,1024]{1,0:T(8,128)(2,1)S(1)}, bf16[384,1024]{1,0:T(8,128)(2,1)S(1)}, u32[]{:S(2)}, u32[]{:S(2)}) collective-permute-start(bf16[384,1024]{1,0:T(8,128)(2,1)S(1)} %bitcast.381), channel_id=1, source_target_pairs={{0,8},{8,0},{16,24},{24,16},{1,9},{9,1},{17,25},{25,17},{2,10},{10... | collective-permute-start | bytes 2359304 | tf_op jit(solution)/shard_map/ppermute | solution.py:74
  508.0 44.4 %collective-permute-start.40 = (bf16[1536,1024]{1,0:T(8,128)(2,1)}, bf16[1536,1024]{1,0:T(8,128)(2,1)}, u32[]{:S(2)}, u32[]{:S(2)}) collective-permute-start(bf16[1536,1024]{1,0:T(8,128)(2,1)} %pad_maximum_fusion.4.g_own), channel_id=1, source_target_pairs={{0,1},{1,0},{2,3},{3,2},{4,5},{5,4},{6,7},{7,6},{8,9},{9,8},{10,11... | collective-permute-start | bytes 9437192 | tf_op jit(solution)/shard_map/ppermute | solution.py:34
  539.7 27.7 %collective-permute-start.33 = (bf16[1536,1024]{1,0:T(8,128)(2,1)}, bf16[1536,1024]{1,0:T(8,128)(2,1)}, u32[]{:S(2)}, u32[]{:S(2)}) collective-permute-start(bf16[1536,1024]{1,0:T(8,128)(2,1)} %pad_maximum_fusion.3.x_own), channel_id=1, source_target_pairs={{0,1},{1,0},{2,3},{3,2},{4,5},{5,4},{6,7},{7,6},{8,9},{9,8},{10,11... | collective-permute-start | bytes 9437192 | tf_op jit(solution)/shard_map/ppermute | solution.py:34
  612.8 30.0 %collective-permute-start.50 = (bf16[1536,1024]{1,0:T(8,128)(2,1)}, bf16[1536,1024]{1,0:T(8,128)(2,1)}, u32[]{:S(2)}, u32[]{:S(2)}) collective-permute-start(bf16[1536,1024]{1,0:T(8,128)(2,1)} %rows_half.6), channel_id=1, source_target_pairs={{0,1},{1,0},{2,3},{3,2},{4,5},{5,4},{6,7},{7,6},{8,9},{9,8},{10,11... | collective-permute-start | bytes 9437192 | tf_op jit(solution)/shard_map/ppermute | solution.py:34
  622.4 43.1 %collective-permute-start.43 = (bf16[1536,1024]{1,0:T(8,128)(2,1)}, bf16[1536,1024]{1,0:T(8,128)(2,1)}, u32[]{:S(2)}, u32[]{:S(2)}) collective-permute-start(bf16[1536,1024]{1,0:T(8,128)(2,1)} %rows_half.4), channel_id=1, source_target_pairs={{0,1},{1,0},{2,3},{3,2},{4,5},{5,4},{6,7},{7,6},{8,9},{9,8},{10,11... | collective-permute-start | bytes 9437192 | tf_op jit(solution)/shard_map/ppermute | solution.py:34
  660.7 21.7 %collective-permute-start.53 = (bf16[4,96,1024]{2,1,0:T(8,128)(2,1)}, bf16[4,96,1024]{2,1,0:T(8,128)(2,1)}, u32[]{:S(2)}, u32[]{:S(2)}) collective-permute-start(bf16[4,96,1024]{2,1,0:T(8,128)(2,1)} %bitcast.103), channel_id=1, source_target_pairs={{0,24},{8,16},{16,8},{24,0},{1,25},{9,17},{17,9},{25,1},{2,26},{10... | collective-permute-start | bytes 2359304 | tf_op jit(solution)/shard_map/ppermute | solution.py:74
  662.1 36.7 %collective-permute-start.52 = (bf16[4,96,1024]{2,1,0:T(8,128)(2,1)}, bf16[4,96,1024]{2,1,0:T(8,128)(2,1)}, u32[]{:S(2)}, u32[]{:S(2)}) collective-permute-start(bf16[4,96,1024]{2,1,0:T(8,128)(2,1)} %bitcast.102), channel_id=1, source_target_pairs={{0,8},{8,0},{16,24},{24,16},{1,9},{9,1},{17,25},{25,17},{2,10},{10... | collective-permute-start | bytes 2359304 | tf_op jit(solution)/shard_map/ppermute | solution.py:74
  664.5 36.1 %collective-permute-start.51 = (bf16[4,96,1024]{2,1,0:T(8,128)(2,1)}, bf16[4,96,1024]{2,1,0:T(8,128)(2,1)}, u32[]{:S(2)}, u32[]{:S(2)}) collective-permute-start(bf16[4,96,1024]{2,1,0:T(8,128)(2,1)} %bitcast.100), channel_id=1, source_target_pairs={{0,16},{8,24},{16,0},{24,8},{1,17},{9,25},{17,1},{25,9},{2,18},{10... | collective-permute-start | bytes 2359304 | tf_op jit(solution)/shard_map/ppermute | solution.py:74
  677.7 51.3 %collective-permute-start.44 = (bf16[4,96,1024]{2,1,0:T(8,128)(2,1)S(1)}, bf16[4,96,1024]{2,1,0:T(8,128)(2,1)S(1)}, u32[]{:S(2)}, u32[]{:S(2)}) collective-permute-start(bf16[4,96,1024]{2,1,0:T(8,128)(2,1)S(1)} %bitcast.377), channel_id=1, source_target_pairs={{0,16},{8,24},{16,0},{24,8},{1,17},{9,25},{17,1},{25,9},{2,18},{10... | collective-permute-start | bytes 2359304 | tf_op jit(solution)/shard_map/ppermute | solution.py:74
  678.8 53.9 %collective-permute-start.46 = (bf16[4,96,1024]{2,1,0:T(8,128)(2,1)S(1)}, bf16[4,96,1024]{2,1,0:T(8,128)(2,1)S(1)}, u32[]{:S(2)}, u32[]{:S(2)}) collective-permute-start(bf16[4,96,1024]{2,1,0:T(8,128)(2,1)S(1)} %bitcast.376), channel_id=1, source_target_pairs={{0,24},{8,16},{16,8},{24,0},{1,25},{9,17},{17,9},{25,1},{2,26},{10... | collective-permute-start | bytes 2359304 | tf_op jit(solution)/shard_map/ppermute | solution.py:74
  682.4 50.3 %collective-permute-start.45 = (bf16[4,96,1024]{2,1,0:T(8,128)(2,1)S(1)}, bf16[4,96,1024]{2,1,0:T(8,128)(2,1)S(1)}, u32[]{:S(2)}, u32[]{:S(2)}) collective-permute-start(bf16[4,96,1024]{2,1,0:T(8,128)(2,1)S(1)} %bitcast.375), channel_id=1, source_target_pairs={{0,8},{8,0},{16,24},{24,16},{1,9},{9,1},{17,25},{25,17},{2,10},{10... | collective-permute-start | bytes 2359304 | tf_op jit(solution)/shard_map/ppermute | solution.py:74
  702.1 31.8 %collective-permute-start.54 = (bf16[192,1024]{1,0:T(8,128)(2,1)S(1)}, bf16[192,1024]{1,0:T(8,128)(2,1)S(1)}, u32[]{:S(2)}, u32[]{:S(2)}) collective-permute-start(bf16[192,1024]{1,0:T(8,128)(2,1)S(1)} %pad_maximum_fusion.24), channel_id=1, source_target_pairs={{0,2},{2,4},{4,6},{6,0},{1,3},{3,5},{5,7},{7,1},{8,10},{10,12},{12... | collective-permute-start | bytes 1179656 | tf_op jit(solution)/shard_map/ppermute | solution.py:66
  704.2 33.1 %collective-permute-start.55 = (bf16[192,1024]{1,0:T(8,128)(2,1)S(1)}, bf16[192,1024]{1,0:T(8,128)(2,1)S(1)}, u32[]{:S(2)}, u32[]{:S(2)}) collective-permute-start(bf16[192,1024]{1,0:T(8,128)(2,1)S(1)} %pad_maximum_fusion.25), channel_id=1, source_target_pairs={{0,4},{2,6},{4,0},{6,2},{1,5},{3,7},{5,1},{7,3},{8,12},{10,14},{12... | collective-permute-start | bytes 1179656 | tf_op jit(solution)/shard_map/ppermute | solution.py:66
  733.2 17.6 %collective-permute-start.47 = (bf16[192,1024]{1,0:T(8,128)(2,1)S(1)}, bf16[192,1024]{1,0:T(8,128)(2,1)S(1)}, u32[]{:S(2)}, u32[]{:S(2)}) collective-permute-start(bf16[192,1024]{1,0:T(8,128)(2,1)S(1)} %pad_maximum_fusion.21), channel_id=1, source_target_pairs={{0,2},{2,4},{4,6},{6,0},{1,3},{3,5},{5,7},{7,1},{8,10},{10,12},{12... | collective-permute-start | bytes 1179656 | tf_op jit(solution)/shard_map/ppermute | solution.py:66
  733.3 34.2 %collective-permute-start.48 = (bf16[192,1024]{1,0:T(8,128)(2,1)S(1)}, bf16[192,1024]{1,0:T(8,128)(2,1)S(1)}, u32[]{:S(2)}, u32[]{:S(2)}) collective-permute-start(bf16[192,1024]{1,0:T(8,128)(2,1)S(1)} %pad_maximum_fusion.22), channel_id=1, source_target_pairs={{0,4},{2,6},{4,0},{6,2},{1,5},{3,7},{5,1},{7,3},{8,12},{10,14},{12... | collective-permute-start | bytes 1179656 | tf_op jit(solution)/shard_map/ppermute | solution.py:66
  733.9 33.6 %collective-permute-start.49 = (bf16[192,1024]{1,0:T(8,128)(2,1)S(1)}, bf16[192,1024]{1,0:T(8,128)(2,1)S(1)}, u32[]{:S(2)}, u32[]{:S(2)}) collective-permute-start(bf16[192,1024]{1,0:T(8,128)(2,1)S(1)} %pad_maximum_fusion.23), channel_id=1, source_target_pairs={{0,6},{2,0},{4,2},{6,4},{1,7},{3,1},{5,3},{7,5},{8,14},{10,8},{12,... | collective-permute-start | bytes 1179656 | tf_op jit(solution)/shard_map/ppermute | solution.py:66
  743.3 25.3 %collective-permute-start.64 = (f32[256,1]{0,1:T(1,128)S(1)}, f32[256,1]{0,1:T(1,128)S(1)}, u32[]{:S(2)}, u32[]{:S(2)}) collective-permute-start(f32[256,1]{0,1:T(1,128)S(1)} %bitcast.432), channel_id=1, source_target_pairs={{0,1},{1,0},{2,3},{3,2},{4,5},{5,4},{6,7},{7,6},{8,9},{9,8},{10,11... | collective-permute-start | bytes 3080 | tf_op jit(solution)/shard_map/ppermute | solution.py:34
  771.2 21.2 %collective-permute-start.67 = (bf16[2,96,1024]{2,1,0:T(8,128)(2,1)S(1)}, bf16[2,96,1024]{2,1,0:T(8,128)(2,1)S(1)}, u32[]{:S(2)}, u32[]{:S(2)}) collective-permute-start(bf16[2,96,1024]{2,1,0:T(8,128)(2,1)S(1)} %bitcast.395), channel_id=1, source_target_pairs={{0,2},{2,4},{4,6},{6,0},{1,3},{3,5},{5,7},{7,1},{8,10},{10,12},{12... | collective-permute-start | bytes 1179656 | tf_op jit(solution)/shard_map/ppermute | solution.py:66
  779.5 28.7 %collective-permute-start.66 = (bf16[2,96,1024]{2,1,0:T(8,128)(2,1)S(1)}, bf16[2,96,1024]{2,1,0:T(8,128)(2,1)S(1)}, u32[]{:S(2)}, u32[]{:S(2)}) collective-permute-start(bf16[2,96,1024]{2,1,0:T(8,128)(2,1)S(1)} %bitcast.393), channel_id=1, source_target_pairs={{0,4},{2,6},{4,0},{6,2},{1,5},{3,7},{5,1},{7,3},{8,12},{10,14},{12... | collective-permute-start | bytes 1179656 | tf_op jit(solution)/shard_map/ppermute | solution.py:66
  782.8 25.4 %collective-permute-start.65 = (bf16[2,96,1024]{2,1,0:T(8,128)(2,1)S(1)}, bf16[2,96,1024]{2,1,0:T(8,128)(2,1)S(1)}, u32[]{:S(2)}, u32[]{:S(2)}) collective-permute-start(bf16[2,96,1024]{2,1,0:T(8,128)(2,1)S(1)} %bitcast.391), channel_id=1, source_target_pairs={{0,6},{2,0},{4,2},{6,4},{1,7},{3,1},{5,3},{7,5},{8,14},{10,8},{12,... | collective-permute-start | bytes 1179656 | tf_op jit(solution)/shard_map/ppermute | solution.py:66
  881.3 473.4 %reduce-scatter.7.cloned.1.call-start = ((), (), s32[]{:S(2)}) async-start(), calls=%async_computation.14 | async-start | bytes 2621440 | tf_op jit(solution)/shard_map/reduce_scatter | solution.py:772
  972.4 406.4 %reduce-scatter.9.cloned.1.call-start = ((), (), s32[]{:S(2)}) async-start(), calls=%async_computation.15 | async-start | bytes 10485760 | tf_op jit(solution)/shard_map/reduce_scatter | solution.py:766
  982.9 400.1 %reduce-scatter.11.cloned.1.call-start = ((), (), s32[]{:S(2)}) async-start(), calls=%async_computation.16 | async-start | bytes 10485760 | tf_op jit(solution)/shard_map/reduce_scatter | solution.py:760
  1023.3 103.3 %all-to-all-start.5 = ((bf16[4,1408,512]{1,2,0:T(8,128)(2,1)}), bf16[4,1408,512]{1,2,0:T(8,128)(2,1)}, u32[]{:S(2)}, u32[]{:S(2)}) async-start(bf16[4,1408,512]{1,2,0:T(8,128)(2,1)} %convert_bitcast_fusion), calls=%async_computation.9 | async-start | bytes 11534336 | tf_op jit(solution)/shard_map/all_to_all | solution.py:38
  1126.6 211.0 %all-to-all-start.4 = ((bf16[4,512,2816]{2,1,0:T(8,128)(2,1)}), bf16[4,512,2816]{2,1,0:T(8,128)(2,1)}, u32[]{:S(2)}, u32[]{:S(2)}) async-start(bf16[4,512,2816]{2,1,0:T(8,128)(2,1)} %bitcast.342), calls=%async_computation.8 | async-start | bytes 23068672 | tf_op jit(solution)/shard_map/all_to_all | solution.py:38
  1152.7 45.3 %collective-permute-start.71 = (bf16[256,1024]{1,0:T(8,128)(2,1)S(1)}, bf16[256,1024]{1,0:T(8,128)(2,1)S(1)}, u32[]{:S(2)}, u32[]{:S(2)}) collective-permute-start(bf16[256,1024]{1,0:T(8,128)(2,1)S(1)} %get-tuple-element.73), channel_id=1, source_target_pairs={{0,4},{2,6},{4,0},{6,2},{1,5},{3,7},{5,1},{7,3},{8,12},{10,14},{12... | collective-permute-start | bytes 1572872 | tf_op jit(solution)/shard_map/ppermute | solution.py:66
  1152.7 45.3 %collective-permute-start.70 = (bf16[256,1024]{1,0:T(8,128)(2,1)S(1)}, bf16[256,1024]{1,0:T(8,128)(2,1)S(1)}, u32[]{:S(2)}, u32[]{:S(2)}) collective-permute-start(bf16[256,1024]{1,0:T(8,128)(2,1)S(1)} %get-tuple-element.71), channel_id=1, source_target_pairs={{0,2},{2,4},{4,6},{6,0},{1,3},{3,5},{5,7},{7,1},{8,10},{10,12},{12... | collective-permute-start | bytes 1572872 | tf_op jit(solution)/shard_map/ppermute | solution.py:66
  1198.8 114.2 %collective-permute-start.75 = (f32[18,1024]{1,0:T(8,128)S(1)}, f32[18,1024]{1,0:T(8,128)S(1)}, u32[]{:S(2)}, u32[]{:S(2)}) collective-permute-start(f32[18,1024]{1,0:T(8,128)S(1)} %pad_maximum_fusion.27), channel_id=1, source_target_pairs={{0,8},{8,0},{16,24},{24,16},{1,9},{9,1},{17,25},{25,17},{2,10},{10... | collective-permute-start | bytes 221192 | tf_op jit(solution)/shard_map/ppermute | solution.py:45
  1320.1 32.2 %collective-permute-start.77 = (f32[18,1024]{1,0:T(8,128)S(1)}, f32[18,1024]{1,0:T(8,128)S(1)}, u32[]{:S(2)}, u32[]{:S(2)}) collective-permute-start(f32[18,1024]{1,0:T(8,128)S(1)} %add.343), channel_id=1, source_target_pairs={{0,2},{2,0},{4,6},{6,4},{1,3},{3,1},{5,7},{7,5},{8,10},{10,8},{12,... | collective-permute-start | bytes 221192 | tf_op jit(solution)/shard_map/ppermute | solution.py:45
  1321.7 30.6 %collective-permute-start.74 = (f32[256,1]{0,1:T(1,128)S(1)}, f32[256,1]{0,1:T(1,128)S(1)}, u32[]{:S(2)}, u32[]{:S(2)}) collective-permute-start(f32[256,1]{0,1:T(1,128)S(1)} %bitcast.446), channel_id=1, source_target_pairs={{0,1},{1,0},{2,3},{3,2},{4,5},{5,4},{6,7},{7,6},{8,9},{9,8},{10,11... | collective-permute-start | bytes 3080 | tf_op jit(solution)/shard_map/ppermute | solution.py:34
  1356.7 19.1 %all-to-all-start.3 = ((bf16[4,128,2,2,128]{4,3,2,1,0:T(2,128)(2,1)}), bf16[4,128,2,2,128]{4,3,2,1,0:T(2,128)(2,1)S(1)}, u32[]{:S(2)}, u32[]{:S(2)}) async-start(bf16[4,128,2,2,128]{4,3,2,1,0:T(2,128)(2,1)} %reshape.734), calls=%async_computation.5 | async-start | bytes 1048576 | tf_op jit(solution)/shard_map/all_to_all | solution.py:38
  (116 other events, 2271.3 us)
Sparse Core Ops, SparseCore 0:
  30.7 34.4 all-gather.5
  67.6 141.7 all-gather.3
  211.8 87.4 all-gather.7
  881.5 82.4 reduce-scatter.4
  972.6 35.6 reduce-scatter.6
  1011.2 229.9 reduce-scatter.8
  1244.5 115.8 reduce-scatter.10

commit v3 on v2

--- a/solution.py
+++ b/solution.py
@@ -14,6 +14,7 @@
 F32 = jnp.float32
 BF16 = jnp.bfloat16
 LIMIT = 60 << 20
+WEIGHT = 0.01
 NT = (((1,), (1,)), ((), ()))
 TN = (((0,), (0,)), ((), ()))
 
@@ -51,10 +52,24 @@
     return values + swap(values)
 
 
-def relay(values, axis):
+def after(value, *done):
+    return lax.optimization_barrier((value,) + done)[0]
+
+
+def near_planes(values):
+    count = lax.axis_size("expert")
+    return [values] + [
+        lax.ppermute(values, "expert", [(i, (i - j) % count) for i in range(count)])
+        for j in range(1, count)
+    ]
+
+
+def relay(values, axis, *done):
     count = lax.axis_size(axis)
     up, down = [values], [values]
-    for _ in range(count - 1):
+    for step in range(count - 1):
+        if done and step == count - 2:
+            up[-1] = after(up[-1], *done)
         up.append(lax.ppermute(up[-1], axis, [(i, i + 1) for i in range(count - 1)]))
         down.append(lax.ppermute(down[-1], axis, [(i + 1, i) for i in range(count - 1)]))
     return [values] + [down[j] + up[count - j] for j in range(1, count)]
@@ -98,56 +113,59 @@
     return pltpu.CompilerParams(dimension_semantics=kinds, vmem_limit_bytes=LIMIT)
 
 
-def pack_kernel(ff, parts, src, out):
-    for part in range(parts):
-        for half in range(2):
-            out[part, 0, :, half * ff : (half + 1) * ff] = src[
-                0, :, half, part * ff : (part + 1) * ff
-            ].astype(BF16)
+def cost(flops, moved):
+    return pl.CostEstimate(
+        flops=int(flops * WEIGHT), bytes_accessed=int(moved * WEIGHT), transcendentals=0
+    )
+
+
+def pack_kernel(ff, parts, src, *outs):
+    for half in range(2):
+        for part in range(parts):
+            outs[half][part, 0] = src[0, :, half, part * ff : (part + 1) * ff].astype(BF16)
 
 
 def pack_gateup(weights, parts):
     local, depth, _, ff_core = weights.shape
     ff = ff_core // parts
     if ff % 128:
-        moved = weights.reshape(local, depth, 2, parts, ff).transpose(3, 0, 1, 2, 4)
-        return moved.astype(BF16).reshape(parts, local, depth, 2 * ff)
+        moved = weights.reshape(local, depth, 2, parts, ff).transpose(2, 3, 0, 1, 4).astype(BF16)
+        return moved[0], moved[1]
     rows = min(depth, 128)
     return pl.pallas_call(
         functools.partial(pack_kernel, ff, parts),
         grid=(local, depth // rows),
         in_specs=[pl.BlockSpec((1, rows, 2, ff_core), lambda l, r: (l, r, 0, 0))],
-        out_specs=pl.BlockSpec((parts, 1, rows, 2 * ff), lambda l, r: (0, l, r, 0)),
-        out_shape=jax.ShapeDtypeStruct((parts, local, depth, 2 * ff), BF16),
+        out_specs=[pl.BlockSpec((parts, 1, rows, ff), lambda l, r: (0, l, r, 0))] * 2,
+        out_shape=[jax.ShapeDtypeStruct((parts, local, depth, ff), BF16)] * 2,
         compiler_params=params("parallel", "parallel"),
+        cost_estimate=cost(0, weights.size * 6),
         name="pack_gateup",
     )(weights)
 
 
-def unpack_kernel(ff, parts, src, out):
-    for part in range(parts):
-        for half in range(2):
-            out[0, :, half, part * ff : (part + 1) * ff] = src[
-                part, 0, :, half * ff : (half + 1) * ff
-            ].astype(F32)
-
-
-def unpack_gateup(grads, parts):
-    _, local, depth, ff2 = grads.shape
-    ff = ff2 // 2
+def unpack_kernel(ff, parts, gate, up, out):
+    for half, src in enumerate((gate, up)):
+        for part in range(parts):
+            out[0, :, half, part * ff : (part + 1) * ff] = src[part, 0].astype(F32)
+
+
+def unpack_gateup(gate, up):
+    parts, local, depth, ff = gate.shape
     if ff % 128:
-        moved = grads.reshape(parts, local, depth, 2, ff).transpose(1, 2, 3, 0, 4)
+        moved = jnp.stack([gate, up], 0).transpose(2, 3, 0, 1, 4)
         return moved.astype(F32).reshape(local, depth, 2, parts * ff)
     rows = min(depth, 128)
     return pl.pallas_call(
         functools.partial(unpack_kernel, ff, parts),
         grid=(local, depth // rows),
-        in_specs=[pl.BlockSpec((parts, 1, rows, 2 * ff), lambda l, r: (0, l, r, 0))],
+        in_specs=[pl.BlockSpec((parts, 1, rows, ff), lambda l, r: (0, l, r, 0))] * 2,
         out_specs=pl.BlockSpec((1, rows, 2, parts * ff), lambda l, r: (l, r, 0, 0)),
         out_shape=jax.ShapeDtypeStruct((local, depth, 2, parts * ff), F32),
         compiler_params=params("parallel", "parallel"),
+        cost_estimate=cost(0, gate.size * 12),
         name="unpack_gateup",
-    )(grads)
+    )(gate, up)
 
 
 def cast_kernel(src, out):
@@ -164,6 +182,7 @@
         out_specs=pl.BlockSpec((1, 1, ff, depth), lambda p, l: (p, l, 0, 0)),
         out_shape=jax.ShapeDtypeStruct((parts, local, ff, depth), BF16),
         compiler_params=params("parallel", "parallel"),
+        cost_estimate=cost(0, weights.size * 6),
         name="pack_down",
     )(weights)
 
@@ -177,6 +196,7 @@
         out_specs=pl.BlockSpec((1, ff, depth), lambda p, l: (l, p, 0)),
         out_shape=jax.ShapeDtypeStruct((local, parts * ff, depth), F32),
         compiler_params=params("parallel", "parallel"),
+        cost_estimate=cost(0, grads.size * 6),
         name="unpack_down",
     )(grads)
 
@@ -235,14 +255,15 @@
         out_shape=[jax.ShapeDtypeStruct((rows, feats), BF16)] * 2,
         input_output_aliases=aliases,
         compiler_params=params("arbitrary", "arbitrary"),
+        cost_estimate=cost(40 * rows * seq * HD * group_heads, rows * feats * 4),
         name="attention_fwd",
     )(*operands)
 
 
 def att_bwd_kernel(
-    place, q_in, do_in, kv, cos, sin, key_cos, key_sin, row_pos, row_seg, key_seg,
-    dq_out, dkv_out, dk_sum, dv_sum,
+    place, q_in, do_in, kv, cos, sin, key_cos, key_sin, row_pos, row_seg, key_seg, *rest
 ):
+    dq_out, dkv_out, dk_sum, dv_sum = rest[-4:]
     step = pl.program_id(1)
     scale = 1.0 / math.sqrt(HD)
     query, grad_out = q_in[...], do_in[...]
@@ -276,50 +297,59 @@
 
 
 def att_backward(
-    place, query, grad_mixed, kv, cos, sin, key_cos, key_sin, row_pos, row_seg, key_seg
+    place, query, grad_mixed, kv, cos, sin, key_cos, key_sin, row_pos, row_seg, key_seg,
+    group, before,
 ):
     rows, feats = query.shape
-    planes, seq, wide = kv.shape
+    _, seq, wide = kv.shape
     group_heads = wide // (2 * HD)
     block = min(256, rows)
-    group = lambda h: h // group_heads
-    inner = lambda h: lax.rem(h, group_heads)
-    head = lambda h, i, place: (i, place[group(h)] * group_heads + inner(h))
+    head = lambda h, i, place: (i, place[group] * group_heads + h)
     row = lambda h, i, place: (i, 0)
     lane = lambda h, i, place: (0, i)
     whole = lambda h, i, place: (0, 0)
+    pair = lambda h, i, place: (0, 0, h)
+    in_specs = [
+        pl.BlockSpec((block, HD), head),
+        pl.BlockSpec((block, HD), head),
+        pl.BlockSpec((1, seq, 2 * HD), pair),
+        pl.BlockSpec((block, HD), row),
+        pl.BlockSpec((block, HD), row),
+        pl.BlockSpec((seq, HD), whole),
+        pl.BlockSpec((seq, HD), whole),
+        pl.BlockSpec((1, block), lane),
+        pl.BlockSpec((1, block), lane),
+        pl.BlockSpec((seq, 1), whole),
+    ]
+    operands = [
+        place, query, grad_mixed, kv, cos, sin, key_cos, key_sin, row_pos, row_seg, key_seg
+    ]
+    aliases = {}
+    if before is not None:
+        in_specs.append(pl.BlockSpec(memory_space=pl.ANY))
+        operands.append(before)
+        aliases = {11: 0}
     return pl.pallas_call(
         att_bwd_kernel,
         grid_spec=pltpu.PrefetchScalarGridSpec(
             num_scalar_prefetch=1,
-            grid=(planes * group_heads, rows // block),
-            in_specs=[
-                pl.BlockSpec((block, HD), head),
-                pl.BlockSpec((block, HD), head),
-                pl.BlockSpec((1, seq, 2 * HD), lambda h, i, place: (group(h), 0, inner(h))),
-                pl.BlockSpec((block, HD), row),
-                pl.BlockSpec((block, HD), row),
-                pl.BlockSpec((seq, HD), whole),
-                pl.BlockSpec((seq, HD), whole),
-                pl.BlockSpec((1, block), lane),
-                pl.BlockSpec((1, block), lane),
-                pl.BlockSpec((seq, 1), whole),
-            ],
+            grid=(group_heads, rows // block),
+            in_specs=in_specs,
             out_specs=[
                 pl.BlockSpec((block, HD), head),
-                pl.BlockSpec(
-                    (1, seq, 2 * HD), lambda h, i, place: (place[group(h)], 0, inner(h))
-                ),
+                pl.BlockSpec((1, seq, 2 * HD), pair),
             ],
             scratch_shapes=[pltpu.VMEM((seq, HD), F32)] * 2,
         ),
         out_shape=[
             jax.ShapeDtypeStruct((rows, feats), BF16),
-            jax.ShapeDtypeStruct((planes, seq, wide), BF16),
+            jax.ShapeDtypeStruct((1, seq, wide), BF16),
         ],
+        input_output_aliases=aliases,
         compiler_params=params("arbitrary", "arbitrary"),
+        cost_estimate=cost(60 * rows * seq * HD * group_heads, rows * feats * 4),
         name="attention_bwd",
-    )(place, query, grad_mixed, kv, cos, sin, key_cos, key_sin, row_pos, row_seg, key_seg)
+    )(*operands)
 
 
 def raw_kernel(core, g_own, g_other, w_dn, out):
@@ -353,14 +383,16 @@
         ),
         out_shape=jax.ShapeDtypeStruct((rows, ff), F32),
         compiler_params=params("arbitrary"),
+        cost_estimate=cost(2 * w_dn.size * rows, w_dn.size * 2 + rows * ff * 4),
         name="hidden_raw",
     )(core, g_own, g_other, w_dn)
 
 
-def ff_kernel(place, x_own, x_other, w_gu, raw, router, other, hid, hid_gated, duw, dgate):
+def ff_kernel(
+    place, x_own, x_other, w_gate, w_up, raw, router, other, hid, hid_gated, du, dw, dgate
+):
     core, expert = place[0], place[1]
     width = x_own.shape[1]
-    ff = raw.shape[1]
     mine = pl.ds(pl.multiple_of(core * width, width), width)
     theirs = pl.ds(pl.multiple_of((1 - core) * width, width), width)
 
@@ -372,8 +404,7 @@
     own_logit = jnp.sum(jnp.where(lanes == expert, logits, 0.0), 1, keepdims=True)
     other_logit = jnp.sum(jnp.where(lanes == other[...], logits, 0.0), 1, keepdims=True)
     gate = jax.nn.sigmoid(own_logit - other_logit)
-    both = product(w_gu)
-    gate_part, up_part = both[:, :ff], both[:, ff:]
+    gate_part, up_part = product(w_gate), product(w_up)
     sig = 1.0 / (1.0 + jnp.exp(-gate_part))
     silu = gate_part * sig
     hidden = silu * up_part
@@ -381,16 +412,17 @@
     hid_gated[...] = (hidden * gate).astype(BF16)
     dgate[...] = jnp.sum(hidden * raw[...], 1, keepdims=True)
     grad_hidden = raw[...] * gate
-    duw[:, :ff] = (grad_hidden * up_part * (sig * (1.0 + gate_part * (1.0 - sig)))).astype(BF16)
-    duw[:, ff:] = (grad_hidden * silu).astype(BF16)
-
-
-def feed_forward(place, x_own, x_other, w_gu, raw, router, other):
+    du[...] = (grad_hidden * up_part * (sig * (1.0 + gate_part * (1.0 - sig)))).astype(BF16)
+    dw[...] = (grad_hidden * silu).astype(BF16)
+
+
+def feed_forward(place, x_own, x_other, w_gate, w_up, raw, router, other):
     rows, width = x_own.shape
     ff = raw.shape[1]
     block = 256
     row = lambda i, c: (i, 0)
     whole = lambda i, c: (0, 0)
+    fixed = lambda array: pl.BlockSpec(array.shape, whole, pipeline_mode=pl.Buffered(1))
     return pl.pallas_call(
         ff_kernel,
         grid_spec=pltpu.PrefetchScalarGridSpec(
@@ -399,64 +431,56 @@
             in_specs=[
                 pl.BlockSpec((block, width), row),
                 pl.BlockSpec((block, width), row),
-                pl.BlockSpec(w_gu.shape, whole, pipeline_mode=pl.Buffered(1)),
+                fixed(w_gate),
+                fixed(w_up),
                 pl.BlockSpec((block, ff), row),
-                pl.BlockSpec(router.shape, whole, pipeline_mode=pl.Buffered(1)),
+                fixed(router),
                 pl.BlockSpec((block, 1), row),
             ],
-            out_specs=[
-                pl.BlockSpec((block, ff), row),
-                pl.BlockSpec((block, ff), row),
-                pl.BlockSpec((block, 2 * ff), row),
-                pl.BlockSpec((block, 1), row),
-            ],
+            out_specs=[pl.BlockSpec((block, ff), row)] * 4 + [pl.BlockSpec((block, 1), row)],
         ),
-        out_shape=[
-            jax.ShapeDtypeStruct((rows, ff), BF16),
-            jax.ShapeDtypeStruct((rows, ff), BF16),
-            jax.ShapeDtypeStruct((rows, 2 * ff), BF16),
-            jax.ShapeDtypeStruct((rows, 1), F32),
-        ],
+        out_shape=[jax.ShapeDtypeStruct((rows, ff), BF16)] * 4
+        + [jax.ShapeDtypeStruct((rows, 1), F32)],
         compiler_params=params("arbitrary"),
+        cost_estimate=cost(5 * w_gate.size * rows, w_gate.size * 4 + rows * ff * 12),
         name="feed_forward",
-    )(place, x_own, x_other, w_gu, raw, router, other)
-
-
-def rows_kernel(transposed, which, lhs, weights, *rest):
-    out = rest[-1]
-    if transposed:
-        total = gdot(lhs[...], weights[...], NT)
-    else:
-        total = jnp.concatenate(
-            [dot(lhs[...], weights[i]) for i in range(weights.shape[0])], 1
-        )
-    if len(rest) > 1:
-        total = total + rest[0][...].astype(F32)
+    )(place, x_own, x_other, w_gate, w_up, raw, router, other)
+
+
+def rows_kernel(count, which, *refs):
+    out = refs[-1]
+    total = None
+    for lhs, weights in zip(refs[:count], refs[count : 2 * count]):
+        if len(weights.shape) == 2:
+            part = gdot(lhs[...], weights[...], NT)
+        else:
+            part = jnp.concatenate(
+                [dot(lhs[...], weights[i]) for i in range(weights.shape[0])], 1
+            )
+        total = part if total is None else total + part
+    if len(refs) > 2 * count + 1:
+        total = total + refs[2 * count][...].astype(F32)
     out[...] = total.astype(BF16)
 
 
 def rows_half(which, lhs, weights, width, add=None):
-    rows, inner = lhs.shape
-    transposed = weights.ndim == 2
+    rows = lhs[0].shape[0]
     block = 256
     row = lambda i, c: (i, 0)
-    if transposed:
-        w_spec = pl.BlockSpec(
-            (width, inner), lambda i, c: (c[0], 0), pipeline_mode=pl.Buffered(1)
-        )
-    else:
-        w_spec = pl.BlockSpec(
-            (weights.shape[0] // 2,) + weights.shape[1:],
-            lambda i, c: (c[0], 0, 0),
-            pipeline_mode=pl.Buffered(1),
-        )
-    in_specs = [pl.BlockSpec((block, inner), row), w_spec]
-    operands = [which, lhs, weights]
+    in_specs = [pl.BlockSpec((block, array.shape[1]), row) for array in lhs]
+    for array in weights:
+        if array.ndim == 2:
+            shape, index = (width, array.shape[1]), lambda i, c: (c[0], 0)
+        else:
+            shape = (array.shape[0] // 2,) + array.shape[1:]
+            index = lambda i, c: (c[0], 0, 0)
+        in_specs.append(pl.BlockSpec(shape, index, pipeline_mode=pl.Buffered(1)))
+    operands = [which, *lhs, *weights]
     if add is not None:
         in_specs.append(pl.BlockSpec((block, width), row))
         operands.append(add)
     return pl.pallas_call(
-        functools.partial(rows_kernel, transposed),
+        functools.partial(rows_kernel, len(lhs)),
         grid_spec=pltpu.PrefetchScalarGridSpec(
             num_scalar_prefetch=1,
             grid=(rows // block,),
@@ -465,8 +489,84 @@
         ),
         out_shape=jax.ShapeDtypeStruct((rows, width), BF16),
         compiler_params=params("arbitrary"),
+        cost_estimate=cost(sum(array.size for array in weights) * rows, rows * width * 4),
         name="rows_half",
     )(*operands)
+
+
+def gu_outer_kernel(core, x_own, x_other, duw, out):
+    half = pl.num_programs(0) // 2
+    mine = (pl.program_id(0) // half) == core[0]
+
+    @pl.when(mine)
+    def _():
+        out[0] = gdot(x_own[...], duw[...], TN).astype(BF16)
+
+    @pl.when(jnp.logical_not(mine))
+    def _():
+        out[0] = gdot(x_other[...], duw[...], TN).astype(BF16)
+
+
+def gu_outer(core, x_own, x_other, duw, columns):
+    rows, width = x_own.shape
+    half = columns // 2
+    depth = width // half
+    part = lambda s, c: (0, lax.rem(s, half))
+    return pl.pallas_call(
+        gu_outer_kernel,
+        grid_spec=pltpu.PrefetchScalarGridSpec(
+            num_scalar_prefetch=1,
+            grid=(columns,),
+            in_specs=[
+                pl.BlockSpec((rows, depth), part),
+                pl.BlockSpec((rows, depth), part),
+                pl.BlockSpec(duw.shape, lambda s, c: (0, 0), pipeline_mode=pl.Buffered(1)),
+            ],
+            out_specs=pl.BlockSpec((1, depth, duw.shape[1]), lambda s, c: (s, 0, 0)),
+        ),
+        out_shape=jax.ShapeDtypeStruct((columns, depth, duw.shape[1]), BF16),
+        compiler_params=params("arbitrary"),
+        cost_estimate=cost(2 * rows * 2 * width * duw.shape[1], rows * width * 8),
+        name="grad_gateup",
+    )(core, x_own, x_other, duw)
+
+
+def dn_outer_kernel(core, hid, g_own, g_other, out):
+    half = pl.num_programs(0) // 2
+    mine = (pl.program_id(0) // half) == core[0]
+
+    @pl.when(mine)
+    def _():
+        out[0] = gdot(hid[...], g_own[...], TN).astype(BF16)
+
+    @pl.when(jnp.logical_not(mine))
+    def _():
+        out[0] = gdot(hid[...], g_other[...], TN).astype(BF16)
+
+
+def dn_outer(core, hid, g_own, g_other, columns):
+    rows, width = g_own.shape
+    half = columns // 2
+    depth = width // half
+    ff = hid.shape[1]
+    part = lambda s, c: (0, lax.rem(s, half))
+    return pl.pallas_call(
+        dn_outer_kernel,
+        grid_spec=pltpu.PrefetchScalarGridSpec(
+            num_scalar_prefetch=1,
+            grid=(columns,),
+            in_specs=[
+                pl.BlockSpec(hid.shape, lambda s, c: (0, 0), pipeline_mode=pl.Buffered(1)),
+                pl.BlockSpec((rows, depth), part),
+                pl.BlockSpec((rows, depth), part),
+            ],
+            out_specs=pl.BlockSpec((1, ff, depth), lambda s, c: (s, 0, 0)),
+        ),
+        out_shape=jax.ShapeDtypeStruct((columns, ff, depth), BF16),
+        compiler_params=params("arbitrary"),
+        cost_estimate=cost(2 * rows * 2 * width * ff, rows * width * 8),
+        name="grad_down",
+    )(core, hid, g_own, g_other)
 
 
 def shards(
@@ -521,17 +621,25 @@
         twice = jnp.concatenate([blocks, blocks], 0)
         return lax.dynamic_slice_in_dim(twice, plane, planes, 0)
 
+    def relative_down(blocks):
+        twice = jnp.concatenate([blocks[::-1], blocks[::-1]], 0)
+        return lax.dynamic_slice_in_dim(twice, planes - 1 - plane, planes, 0)
+
     kv_send = w_kv.astype(BF16).reshape(w_kv.shape[0], 2, planes, part_heads, HD)
-    kv_send = a2a(kv_send.transpose(2, 0, 3, 1, 4), "expert")
+    near_tokens = near_planes(tokens)
+    kv_send = absolute(jnp.stack(shift(list(relative_down(kv_send.transpose(2, 0, 3, 1, 4))), -1), 0))
     w_kv_part = lax.all_gather(kv_send, "dp", axis=0, tiled=True).reshape(
         full_width, 2 * kv_part
     )
-    whole_query = lax.all_gather(w_query.astype(BF16), "dp", axis=1, tiled=True)
+    whole_query = lax.all_gather(
+        after(w_query.astype(BF16), kv_send), "dp", axis=1, tiled=True
+    )
     whole_output = lax.all_gather(w_output.astype(BF16), "dp", axis=2, tiled=True)
     down_send = pack_down(w_down, ff_parts).reshape(columns, ff, depth)
+    gate_send, up_send = pack_gateup(w_gateup, ff_parts)
     w_dn = a2a(down_send, "dp")
-    gu_send = pack_gateup(w_gateup, ff_parts).reshape(columns, depth, 2 * ff)
-    w_gu = a2a(gu_send, "dp").reshape(full_width, 2 * ff)
+    w_gate = a2a(gate_send.reshape(columns, depth, ff), "dp").reshape(full_width, ff)
+    w_up = a2a(up_send.reshape(columns, depth, ff), "dp").reshape(full_width, ff)
 
     ints = jnp.concatenate(
         [
@@ -542,7 +650,7 @@
         ],
         0,
     )
-    near_ints = jnp.stack(relay(ints, "expert"), 0)[None]
+    near_ints = jnp.stack(near_planes(ints), 0)[None]
     step = 1
     while step < columns:
         pairs = [(i, i ^ step) for i in range(columns)]
@@ -550,7 +658,8 @@
         step *= 2
 
     residual = tokens.astype(F32)
-    seq_res = jnp.concatenate(relay(tokens, "expert"), 0).astype(F32)
+    near_tokens[-1] = after(near_tokens[-1], down_send, gate_send, up_send)
+    seq_res = jnp.concatenate(near_tokens, 0).astype(F32)
 
     def rms_scale(values):
         return lax.rsqrt(
@@ -581,7 +690,7 @@
     keys = keys * cos_near[:, None] + turned * sin_near[:, None]
     kv_mine = jnp.stack([keys.astype(BF16), kv_raw[:, :, 1].astype(BF16)], 2)
     kv_mine = absolute(kv_mine.reshape(planes, count, 2 * kv_part)).reshape(seq, 2 * kv_part)
-    kv_near = relay(kv_mine, "expert")
+    kv_near = relay(kv_mine, "expert", w_dn)
 
     seq_ints = near_ints[0]
     own_att = jnp.arange(local_att, dtype=jnp.int32) + plane * local_att
@@ -613,15 +722,19 @@
     seq_seg = absolute(seq_ints[:, 0]).reshape(seq)
     att_rows = planes * local_att * cap
 
-    def to_expert(rows_half):
-        held = shift(list(rows_half.reshape(planes, local_mlp, cap, width)), -1)
+    def to_plane(rows_half):
+        return shift(list(rows_half.reshape(planes, local_mlp, cap, width)), -1)
+
+    def to_expert(held, early=(), late=()):
+        held[-1] = after(held[-1], *early)
         held = jnp.stack(held, 1)
         sent = [held[k % local_mlp].reshape(planes * cap, width) for k in range(columns)]
-        own = jnp.concatenate(cross(sent), 0)
+        got = cross(sent)
+        got[-1] = after(got[-1], *late)
+        own = jnp.concatenate(got, 0)
         return own, swap(own)
 
-    g_own, g_other = to_expert(dot(flat_mlp, cotangent).astype(BF16))
-    raw = hidden_raw(core_at, g_own, g_other, w_dn)
+    g_held = to_plane(dot(flat_mlp, after(cotangent, kv_near[1], kv_near[-1])).astype(BF16))
 
     def gates_of(half_rows, router, routes):
         part = lax.dynamic_slice_in_dim(router, core * width, width, 0).astype(BF16)
@@ -646,6 +759,7 @@
             row_pos[:, None], row_seg[:, None], seq_seg[None], j, before,
         )
     mixed_rows, query_rows = before
+    mixed_rows = after(mixed_rows, w_gate)
     mixed_owner = mixed_rows.reshape(local_att, planes * cap, feats)
 
     def halves(values, axis):
@@ -655,6 +769,8 @@
 
     out_mine, out_theirs = halves(whole_output, 2)
     given = swap(ein("lrf,lfd->lrd", mixed_owner, out_theirs).astype(BF16))
+    g_own, g_other = to_expert(g_held, (), (given,))
+    raw = hidden_raw(core_at, g_own, g_other, w_dn)
     branch_a = ein("lrf,lfd->lrd", mixed_owner, out_mine) + given.astype(F32)
     branch_a = branch_a.astype(BF16).reshape(local_att, planes, cap, width)
     home_a = jnp.concatenate(
@@ -666,28 +782,52 @@
     scale_b = rms_scale(middle)
     rows_b_half = (middle * scale_b * norm_mlp).astype(BF16)
     gates_b, named_b, router_b = gates_of(rows_b_half, router_mlp, ints[3:5])
-    x_own, x_other = to_expert(dot(flat_mlp, rows_b_half).astype(BF16))
+    x_own, x_other = to_expert(
+        to_plane(dot(flat_mlp, rows_b_half).astype(BF16)), (raw,), (w_up,)
+    )
     router_wide = jnp.pad(router_mlp.astype(BF16), ((0, 0), (0, HD - n_mlp)))
     place = jnp.stack([core, mlp_expert]).astype(jnp.int32)
-    hidden, hidden_gated, grad_both, row_dgate = feed_forward(
-        place, x_own, x_other, w_gu, raw, router_wide, row_other
-    )
-
-    def mlp_home(rows):
+    hidden, hidden_gated, grad_gate, grad_up, row_dgate = feed_forward(
+        place, x_own, x_other, w_gate, w_up, raw, router_wide, row_other
+    )
+
+    def over_parts(rows, *done):
         tail = rows.shape[1:]
         got = cross(list(rows.reshape((columns, planes, cap) + tail)))
+        there = got[1:]
+        got[-1] = after(got[-1], *done)
         sums = []
         for near in range(local_mlp):
             parts = [got[k].astype(F32) for k in range(near, columns, local_mlp)]
             sums.append(functools.reduce(jnp.add, parts).astype(rows.dtype))
-        back = shift(
-            [jnp.concatenate([part[j] for part in sums], 0) for j in range(planes)], 1
-        )
-        return jnp.concatenate(back, 0)
-
-    dgate_home = mlp_home(core_sum(row_dgate[:, 0]))
-    given = swap(rows_half(other_at, grad_both, w_gu, width))
-    home_db = mlp_home(rows_half(core_at, grad_both, w_gu, width, given))
+        return [jnp.concatenate([part[j] for part in sums], 0) for j in range(planes)], there
+
+    def mlp_home(blocks, *done):
+        back = shift(blocks, 1)
+        there = back[1:]
+        back[-1] = after(back[-1], *done)
+        return jnp.concatenate(back, 0), there
+
+    dgate_blocks, dgate_there = over_parts(core_sum(row_dgate[:, 0]))
+    dgate_home, dgate_back = mlp_home(dgate_blocks)
+    branch_theirs = rows_half(other_at, (hidden,), (w_dn,), width)
+    given = swap(branch_theirs)
+    grad_wgate = gu_outer(core_at, x_own, x_other, after(grad_gate, branch_theirs), columns)
+    branch_b = rows_half(core_at, (after(hidden, grad_wgate),), (w_dn,), width, given)
+    branch_blocks, branch_there = over_parts(after(branch_b, *dgate_there))
+    home_b, branch_back = mlp_home(branch_blocks)
+    grad_pair = (after(grad_gate, branch_b), grad_up)
+    given = swap(rows_half(other_at, grad_pair, (w_gate, w_up), width))
+    db_rows = rows_half(core_at, grad_pair, (w_gate, w_up), width, given)
+    grad_wup = gu_outer(core_at, x_own, x_other, after(grad_up, db_rows, *dgate_back), columns)
+    grad_wdn = dn_outer(core_at, after(hidden_gated, grad_wup), g_own, g_other, columns)
+    db_blocks, db_there = over_parts(
+        after(db_rows, *branch_there), grad_wdn, *branch_back
+    )
+    home_db, _ = mlp_home(db_blocks)
+    got_gate = a2a(after(grad_wgate, *db_there), "dp")
+    got_up = a2a(grad_wup, "dp")
+    got_dn = a2a(grad_wdn, "dp")
 
     def gates_back(gates, grad_gates, named):
         chosen = gates * (grad_gates - jnp.sum(gates * grad_gates, 0, keepdims=True))
@@ -714,81 +854,76 @@
     grad_logit_a = gates_back(gates_a, grad_gates_a, named_a)
     grad_taken_a = (gates_a[:, :, None] * grad_middle[None]).astype(BF16)
     sent_a = ein("jst,jtd->sd", pick_att, grad_taken_a).astype(BF16)
+    sent_a = after(sent_a, got_gate)
     got_a = shift(list(sent_a.reshape(planes, local_att, cap, width)), -1)
+    got_a[-1] = after(got_a[-1], got_up)
     held_grad_a = both_halves(
         jnp.stack(got_a, 1).reshape(local_att, planes * cap, width), core
     )
     grad_mixed = ein("lrd,lfd->lrf", held_grad_a, whole_output).astype(BF16)
-    grad_query, grad_kv_seq = att_backward(
-        source_planes, query_rows, grad_mixed.reshape(att_rows, feats),
-        jnp.stack(kv_near, 0), cos_rows, sin_rows, cos_seq, sin_seq,
-        row_pos[None], row_seg[None], seq_seg[:, None],
-    )
+    grad_wo = ein("lrf,lrd->lfd", mixed_owner, held_grad_a).astype(BF16)
+    grad_woutput = lax.psum_scatter(grad_wo, "dp", scatter_dimension=2, tiled=True).astype(F32)
+    grad_query = None
+    sent_kv = [None] * planes
+    for j in [planes // 2] + [j for j in range(1, planes) if j != planes // 2] + [0]:
+        if j == 1:
+            grad_query = after(grad_query, grad_wo)
+        grad_query, grad_kv_group = att_backward(
+            source_planes, query_rows, grad_mixed.reshape(att_rows, feats), kv_near[j][None],
+            cos_rows, sin_rows, cos_seq, sin_seq, row_pos[None], row_seg[None],
+            seq_seg[:, None], j, grad_query,
+        )
+        sent_kv[j] = grad_kv_group[0]
     grad_query = grad_query.reshape(local_att, planes * cap, feats)
-    grad_kv = lax.psum_scatter(grad_kv_seq, "expert", scatter_dimension=0, tiled=True)
+    got_kv = shift(sent_kv, 1)
+    grad_wq = ein(
+        "lrd,lrf->ldf", after(held_a, got_kv[planes // 2], got_dn), grad_query
+    ).astype(BF16)
+    taken_b = ein("jst,sd->jtd", pick_mlp, home_b)
+    output = (middle + jnp.sum(gates_b[:, :, None] * taken_b, 0)).astype(BF16)
+    got_kv[0] = after(got_kv[0], grad_wq, grad_woutput)
+    grad_kv = functools.reduce(jnp.add, [part.astype(F32) for part in got_kv]).astype(BF16)
     grad_kv = relative(grad_kv.reshape(planes, count, 2 * kv_part)).reshape(seq, 2 * kv_part)
+    grad_wquery = lax.psum_scatter(
+        after(grad_wq, grad_kv), "dp", scatter_dimension=1, tiled=True
+    ).astype(F32)
     query_mine, query_theirs = halves(whole_query, 1)
     kvw_mine, kvw_theirs = halves(w_kv_part, 0)
 
-    def grad_seq(query_half, kv_half):
-        rows = ein("lrf,ldf->lrd", grad_query, query_half).astype(BF16)
+    def grad_seq(query_half, kv_half, done):
+        rows = ein("lrf,ldf->lrd", after(grad_query, done), query_half).astype(BF16)
         rows = ein("slct,lscd->std", spread, rows.reshape(local_att, planes, cap, width))
         return rows.reshape(seq, width) + ein("tf,df->td", grad_kv, kv_half)
 
-    given = swap(grad_seq(query_theirs, kvw_theirs).astype(BF16))
-    grad_seq_a = (grad_seq(query_mine, kvw_mine) + given.astype(F32)).astype(BF16)
+    given = swap(grad_seq(query_theirs, kvw_theirs, got_kv[1]).astype(BF16))
+    grad_seq_a = (grad_seq(query_mine, kvw_mine, got_kv[-1]) + given.astype(F32)).astype(BF16)
+    grad_wgateup = unpack_gateup(
+        after(got_gate, grad_kv).reshape(ff_parts, local_mlp, depth, ff),
+        got_up.reshape(ff_parts, local_mlp, depth, ff),
+    )
+    grad_wdown = unpack_down(got_dn.reshape(ff_parts, local_mlp, ff, depth))
+    grad_kv_w = lax.psum_scatter(
+        ein("td,tf->df", seq_a, grad_kv).astype(BF16), "dp", scatter_dimension=0, tiled=True
+    )
+    grad_kv_w = a2a(
+        grad_kv_w.reshape(planes, w_kv.shape[0], part_heads, 2, HD), "expert"
+    )
+    grad_wkv = grad_kv_w.transpose(1, 3, 0, 2, 4).astype(F32).reshape(w_kv.shape)
     back_a = shift(list(grad_seq_a.reshape(planes, count, width)), 1)
+    back_a[0] = after(back_a[0], grad_wgateup, grad_wdown)
     grad_rows_a = functools.reduce(jnp.add, [part.astype(F32) for part in back_a])
     grad_normed_a = grad_rows_a + ein("et,de->td", grad_logit_a, router_a)
     grad_router_a = ein("et,td->ed", grad_logit_a, rows_a_half)
     grad_in_norm, grad_gain_a = normalize_back(residual, norm_attn, scale_a, grad_normed_a)
     grad_tokens = grad_middle + grad_in_norm
 
-    def absolute_halves(own, other):
-        first = jnp.where(core == 0, own, other)
-        second = jnp.where(core == 0, other, own)
-        return jnp.concatenate([first, second], -1)
-
-    x_rows = absolute_halves(x_own, x_other)
-    g_rows = absolute_halves(g_own, g_other)
-    grad_gu = ein("rd,rf->df", x_rows, grad_both).astype(BF16)
-    got_gu = a2a(grad_gu.reshape(columns, depth, 2 * ff), "dp")
-    grad_wgateup = unpack_gateup(got_gu.reshape(ff_parts, local_mlp, depth, 2 * ff), ff_parts)
-    grad_dn = ein("rf,rsd->sfd", hidden_gated, g_rows.reshape(-1, columns, depth)).astype(BF16)
-    got_dn = a2a(grad_dn, "dp")
-    grad_wdown = unpack_down(got_dn.reshape(ff_parts, local_mlp, ff, depth))
-    grad_woutput = lax.psum_scatter(
-        ein("lrf,lrd->lfd", mixed_owner, held_grad_a).astype(BF16),
-        "dp",
-        scatter_dimension=2,
-        tiled=True,
-    ).astype(F32)
-    grad_wquery = lax.psum_scatter(
-        ein("lrd,lrf->ldf", held_a, grad_query).astype(BF16),
-        "dp",
-        scatter_dimension=1,
-        tiled=True,
-    ).astype(F32)
-    grad_kv_w = lax.psum_scatter(
-        ein("td,tf->df", seq_a, grad_kv).astype(BF16), "dp", scatter_dimension=0, tiled=True
-    )
-    grad_kv_w = a2a(
-        grad_kv_w.reshape(planes, w_kv.shape[0], part_heads, 2, HD), "expert"
-    )
-    grad_wkv = grad_kv_w.transpose(1, 3, 0, 2, 4).astype(F32).reshape(w_kv.shape)
-
-    given = swap(rows_half(other_at, hidden, w_dn, width))
-    home_b = mlp_home(rows_half(core_at, hidden, w_dn, width, given))
-    taken_b = ein("jst,sd->jtd", pick_mlp, home_b)
-    output = middle + jnp.sum(gates_b[:, :, None] * taken_b, 0)
-
     small = jnp.concatenate(
         [grad_router_a, grad_router_b, grad_gain_a[None], grad_gain_b[None]], 0
     )
     small = total_over(total_over(small, "dp"), "expert")
     routers = both_halves(small[: n_att + n_mlp], core)
     return (
-        output.astype(BF16),
+        output,
         grad_tokens,
         small[n_att + n_mlp],
         small[n_att + n_mlp + 1],

time: 1410 us -> 1200 us (0.85)
  waiting for transfers between devices: 673 us -> 507 us
  Pallas kernels: 235 us -> 291 us
  matrix products: 123 us -> 79.5 us
  starting transfers between devices: 172 us -> 147 us
  blocking collectives: 20.6 us -> 0 us
    ppermute x4, waiting for transfers between devices: 118 us -> 13.6 us  [total_over(): lax.ppermute(values, axis, [(i, i ^ step) for i in range(count)])]
    ppermute x9 -> x3, waiting for transfers between devices: 54.6 us -> 2.9 us  [relay(): lax.ppermute(down[-1], axis, [(i + 1, i) for i in range(count - 1)])]
    pallas_call x4 -> x7, Pallas kernels: 48 us -> 94.8 us  [the longest x4 50.4 us: rows_half(): pl.pallas_call(functools.partial(rows_kernel, len(lhs)), grid_spec=pltpu....]
    reduce_scatter x3 -> x2, waiting for transfers between devices: 82.5 us -> 37.2 us  [the longest x1 22 us: shards(): lax.psum_scatter(grad_wo, 'dp', scatter_dimension=2, tiled=True).astype(F32)]
    dot_general x26 -> x24, matrix products: 119 us -> 75.4 us  [ein(): return jnp.einsum(spec, lhs, rhs, preferred_element_type=F32)]
    all_gather x1, waiting for transfers between devices: 0.01 us -> 38.9 us  [shards(): lax.all_gather(after(w_query.astype(BF16), kv_send), 'dp', axis=1, tiled=...]
    ppermute x9 -> x3, starting transfers between devices: 44.3 us -> 12.2 us  [relay(): lax.ppermute(up[-1], axis, [(i, i + 1) for i in range(count - 1)])]
    ppermute x15, waiting for transfers between devices: 144 us -> 113 us  [cross(): lax.ppermute(blocks[k], 'dp', [(i, i ^ k) for i in range(count)])]
  transfers between devices with their start and end apart: 92 -> 93, of which waited for: 43 -> 57; matrix products, arithmetic and copies ran while one was open for 17% -> 16% of each run, Pallas kernels for 10% -> 19%
where the time goes in v3:
time: 1200 us; the launch traced here: 1190 us
  waiting for transfers between devices  507 us (42%)
  Pallas kernels  291 us (24%)
  starting transfers between devices  147 us (12%)
  other arithmetic  86.7 us (7%)
  matrix products  79.5 us (7%)
  local copies, waits for them, and re-layouts  61.4 us (5%)
  between operations  16.4 us (1%)
    ppermute x30, waiting for transfers between devices, shift(): lax.ppermute(blocks[j], 'expert', [(i, (i + sign * j) % count) for i in r...  139 us
    ppermute x15, waiting for transfers between devices, cross(): lax.ppermute(blocks[k], 'dp', [(i, i ^ k) for i in range(count)])  113 us
    dot_general x24, matrix products, ein(): return jnp.einsum(spec, lhs, rhs, preferred_element_type=F32)  75.4 us
    all_to_all x7, waiting for transfers between devices, a2a(): return lax.all_to_all(values, axis, split_axis=0, concat_axis=0, tiled=True)  65.3 us
    pallas_call x4, Pallas kernels, att_backward(): pl.pallas_call(att_bwd_kernel, grid_spec=pltpu.PrefetchScalarGridSpec(num...  58.9 us
    pallas_call x4, Pallas kernels, rows_half(): pl.pallas_call(functools.partial(rows_kernel, len(lhs)), grid_spec=pltpu....  50.4 us
    ppermute x30, starting transfers between devices, shift(): lax.ppermute(blocks[j], 'expert', [(i, (i + sign * j) % count) for i in r...  49.4 us
    all_gather x1, waiting for transfers between devices, shards(): lax.all_gather(w_output.astype(BF16), 'dp', axis=2, tiled=True)  44.6 us
  transfers between devices with their start and end apart: 93, of which 57 were waited for; matrix products, arithmetic and copies ran while one was open for 16% of the time, Pallas kernels for 19%

profile of v3, /device:TPU:0, one launch (start us, length us, event | category | flops | bytes accessed | tf_op | source)
XLA Modules:
  0.0 1188.7 jit_solution(14033913924203790352)
XLA Ops:
  18.0 7.3 collective-permute-done.10
  42.3 6.9 pack_down.1
  54.4 25.9 %pack_gateup.1 = (bf16[2,2,512,1408]{3,2,1,0:T(8,128)(2,1)}, bf16[2,2,512,1408]{3,2,1,0:T(8,128)(2,1)}) custom-call(f32[2,512,2,2816]{3,2,1,0:T(2,128)} %src.3), custom_call_target="tpu_custom_call" | custom-call | bytes 346030 | tf_op jit(solution)/shard_map/pack_gateup/pallas_call | solution.py:135
  91.1 5.6 fusion.84
  128.9 5.3 all-to-all-done.w_dn.refs_1_
  139.4 8.3 collective-permute-done.15
  147.8 5.5 collective-permute-start.16
  158.8 16.2 %collective-permute-done.16 = bf16[1024,512]{1,0:T(8,128)(2,1)} collective-permute-done((bf16[1024,512]{1,0:T(8,128)(2,1)}, bf16[1024,512]{1,0:T(8,128)(2,1)}, u32[]{:S(2)}, u32[]{:S(2)}) %collective-permute-start.16) | collective-permute-done | bytes 1048608 | tf_op jit(solution)/shard_map/ppermute | solution.py:73
  192.8 8.3 collective-permute-done.17
  214.3 38.9 %all-gather.4.cloned.1.call-done = bf16[2,2048,1024]{2,1,0:T(8,128)(2,1)} async-done(((bf16[2,512,1024]{2,1,0:T(8,128)(2,1)}), bf16[2,2048,1024]{2,1,0:T(8,128)(2,1)}) %all-gather.4.cloned.1.call-update) | async-done | bytes 8388624 | tf_op jit(solution)/shard_map/all_gather | solution.py:634
  253.2 9.4 fusion.144
  262.7 9.1 attention_fwd.4
  271.7 8.8 attention_fwd.5
  280.5 8.8 attention_fwd.6
  289.3 8.8 attention_fwd.7
  298.2 44.6 %all-gather.8.cloned.1.call-done = bf16[2,1024,2048]{2,1,0:T(8,128)(2,1)} async-done(((bf16[2,1024,512]{2,1,0:T(8,128)(2,1)}), bf16[2,1024,2048]{2,1,0:T(8,128)(2,1)}) %all-gather.8.cloned.1.call-update) | async-done | bytes 8388624 | tf_op jit(solution)/shard_map/all_gather | solution.py:637
  342.8 5.6 fusion.19
  361.1 11.4 collective-permute-done.32
  372.5 16.9 %collective-permute-done.30 = bf16[384,1024]{1,0:T(8,128)(2,1)} collective-permute-done((bf16[384,1024]{1,0:T(8,128)(2,1)}, bf16[384,1024]{1,0:T(8,128)(2,1)}, u32[]{:S(2)}, u32[]{:S(2)}) %collective-permute-start.30) | collective-permute-done | bytes 786464 | tf_op jit(solution)/shard_map/ppermute | solution.py:89
  391.6 5.5 add_convert_fusion
  403.7 8.8 collective-permute-done.19
  412.6 15.5 %collective-permute-done.20 = bf16[192,1024]{1,0:T(8,128)(2,1)} collective-permute-done((bf16[192,1024]{1,0:T(8,128)(2,1)}, bf16[192,1024]{1,0:T(8,128)(2,1)}, u32[]{:S(2)}, u32[]{:S(2)}) %collective-permute-start.20) | collective-permute-done | bytes 393248 | tf_op jit(solution)/shard_map/ppermute | solution.py:81
  436.0 8.9 collective-permute-start.26
  446.6 15.1 %hidden_raw.1.raw = f32[1536,1408]{1,0:T(8,128)} custom-call(s32[1]{0:T(128)} %bitcast.68.core.which, bf16[1536,1024]{1,0:T(8,128)(2,1)} %copy-done.2, bf16[1536,1024]{1,0:T(8,128)(2,1)} %collective-permute-done.33.g_other, bf16[4,1408,512]{2,1,0:T(8,128)(2,1)} %all-to-all-done.w_dn.refs_1_), custom_call_target="tpu_custom_call" | custom-call | flops 88583696 | bytes 144179 | tf_op jit(solution)/shard_map/hidden_raw/pallas_call | solution.py:370
  464.0 16.8 %collective-permute-done.25 = bf16[2,96,1024]{2,1,0:T(8,128)(2,1)} collective-permute-done((bf16[2,96,1024]{2,1,0:T(8,128)(2,1)}, bf16[2,96,1024]{2,1,0:T(8,128)(2,1)}, u32[]{:S(2)}, u32[]{:S(2)}) %collective-permute-start.25) | collective-permute-done | bytes 393248 | tf_op jit(solution)/shard_map/ppermute | solution.py:81
  486.0 17.9 %collective-permute-done.36 = bf16[384,1024]{1,0:T(8,128)(2,1)S(1)} collective-permute-done((bf16[384,1024]{1,0:T(8,128)(2,1)S(1)}, bf16[384,1024]{1,0:T(8,128)(2,1)S(1)}, u32[]{:S(2)}, u32[]{:S(2)}) %collective-permute-start.36) | collective-permute-done | bytes 786464 | tf_op jit(solution)/shard_map/ppermute | solution.py:89
  503.9 15.9 %collective-permute-done.34 = bf16[384,1024]{1,0:T(8,128)(2,1)S(1)} collective-permute-done((bf16[384,1024]{1,0:T(8,128)(2,1)S(1)}, bf16[384,1024]{1,0:T(8,128)(2,1)S(1)}, u32[]{:S(2)}, u32[]{:S(2)}) %collective-permute-start.34) | collective-permute-done | bytes 786464 | tf_op jit(solution)/shard_map/ppermute | solution.py:89
  535.0 32.0 %feed_forward.1 = (bf16[1536,1408]{1,0:T(8,128)(2,1)}, bf16[1536,1408]{1,0:T(8,128)(2,1)}, bf16[1536,1408]{1,0:T(8,128)(2,1)}, bf16[1536,1408]{1,0:T(8,128)(2,1)}, f32[1536,1]{1,0:T(8,128)}) custom-call(s32[2]{0:T(128)} %pad_add_fusion.4.place, bf16[1536,1024]{1,0:T(8,128)(2,1)} %copy-done.1, bf16[1536,1024]{1,0:T(8,128)(2,1)} %collective-permute-done.37.x_other, ...), custom_call_target="tpu_custom_call" | custom-call | flops 221459248 | bytes 374865 | tf_op jit(solution)/shard_map/feed_forward/pallas_call | solution.py:426
  567.0 9.5 rows_half.4
  576.5 15.0 %grad_gateup.2 = bf16[4,512,1408]{2,1,0:T(8,128)(2,1)} custom-call(s32[1]{0:T(128)} %bitcast.68.core.which, bf16[1536,1024]{1,0:T(8,128)(2,1)} %copy-done.1, bf16[1536,1024]{1,0:T(8,128)(2,1)} %collective-permute-done.37.x_other, bf16[1536,1408]{1,0:T(8,128)(2,1)} %get-tuple-element.84.duw.refs_0_), custom_call_target="tpu_custom_call" | custom-call | flops 88583696 | bytes 125829 | tf_op jit(solution)/shard_map/grad_gateup/pallas_call | solution.py:515
  593.2 10.1 rows_half.5
  603.3 15.4 %rows_half.6 = bf16[1536,1024]{1,0:T(8,128)(2,1)} custom-call(s32[1]{0:T(128)S(6)} %sub.102.which, bf16[1536,1408]{1,0:T(8,128)(2,1)} %get-tuple-element.84.duw.refs_0_, bf16[1536,1408]{1,0:T(8,128)(2,1)} %get-tuple-element.88.refs_1_.duw, bf16[2048,1408]{1,0:T(8,128)(2,1)} %bitcast.51.w_gate.refs_2_, bf16[2048,1408]{1,0:T(8,128)(2,1)} %bitcast.91.w_up.refs_3_), custom_call_target="tpu_custom_call" | custom-call | flops 88583696 | bytes 62914 | tf_op jit(solution)/shard_map/rows_half/pallas_call | solution.py:482
  636.2 15.4 %rows_half.7 = bf16[1536,1024]{1,0:T(8,128)(2,1)} custom-call(s32[1]{0:T(128)} %bitcast.68.core.which, bf16[1536,1408]{1,0:T(8,128)(2,1)} %get-tuple-element.84.duw.refs_0_, bf16[1536,1408]{1,0:T(8,128)(2,1)} %get-tuple-element.88.refs_1_.duw, bf16[2048,1408]{1,0:T(8,128)(2,1)} %bitcast.51.w_gate.refs_2_, bf16[2048,1408]{1,0:T(8,128)(2,1)} %bitcast.91.w_up.refs_3_, ...), custom_call_target="tpu_custom_call" | custom-call | flops 88583696 | bytes 62914 | tf_op jit(solution)/shard_map/rows_half/pallas_call | solution.py:482
  654.7 14.5 %collective-permute-done.47 = bf16[4,96,1024]{2,1,0:T(8,128)(2,1)} collective-permute-done((bf16[4,96,1024]{2,1,0:T(8,128)(2,1)}, bf16[4,96,1024]{2,1,0:T(8,128)(2,1)}, u32[]{:S(2)}, u32[]{:S(2)}) %collective-permute-start.47) | collective-permute-done | bytes 786464 | tf_op jit(solution)/shard_map/ppermute | solution.py:89
  675.1 15.9 %collective-permute-done.52 = bf16[4,96,1024]{2,1,0:T(8,128)(2,1)S(1)} collective-permute-done((bf16[4,96,1024]{2,1,0:T(8,128)(2,1)S(1)}, bf16[4,96,1024]{2,1,0:T(8,128)(2,1)S(1)}, u32[]{:S(2)}, u32[]{:S(2)}) %collective-permute-start.52) | collective-permute-done | bytes 786464 | tf_op jit(solution)/shard_map/ppermute | solution.py:89
  694.1 12.4 %collective-permute-done.54 = bf16[4,96,1024]{2,1,0:T(8,128)(2,1)} collective-permute-done((bf16[4,96,1024]{2,1,0:T(8,128)(2,1)S(1)}, bf16[4,96,1024]{2,1,0:T(8,128)(2,1)}, u32[]{:S(2)}, u32[]{:S(2)}) %collective-permute-start.54) | collective-permute-done | bytes 786464 | tf_op jit(solution)/shard_map/ppermute | solution.py:89
  730.9 7.0 collective-permute-done.48
  738.7 14.9 %grad_gateup.3 = bf16[4,512,1408]{2,1,0:T(8,128)(2,1)} custom-call(s32[1]{0:T(128)} %bitcast.68.core.which, bf16[1536,1024]{1,0:T(8,128)(2,1)} %copy-done.1, bf16[1536,1024]{1,0:T(8,128)(2,1)} %collective-permute-done.37.x_other, bf16[1536,1408]{1,0:T(8,128)(2,1)} %get-tuple-element.88.refs_1_.duw), custom_call_target="tpu_custom_call" | custom-call | flops 88583696 | bytes 125829 | tf_op jit(solution)/shard_map/grad_gateup/pallas_call | solution.py:515
  753.6 18.9 %all-to-all-done.3 = bf16[4,512,1408]{2,1,0:T(8,128)(2,1)} async-done(((bf16[4,512,1408]{2,1,0:T(8,128)(2,1)}), bf16[4,512,1408]{2,1,0:T(8,128)(2,1)}, u32[]{:S(2)}, u32[]{:S(2)}) %all-to-all-start.3) | async-done | bytes 5767200 | tf_op jit(solution)/shard_map/all_to_all | solution.py:39
  781.3 14.6 %grad_down.1 = bf16[4,1408,512]{2,1,0:T(8,128)(2,1)} custom-call(s32[1]{0:T(128)} %bitcast.68.core.which, bf16[1536,1408]{1,0:T(8,128)(2,1)} %get-tuple-element.89.hid, bf16[1536,1024]{1,0:T(8,128)(2,1)} %copy-done.2, bf16[1536,1024]{1,0:T(8,128)(2,1)} %collective-permute-done.33.g_other), custom_call_target="tpu_custom_call" | custom-call | flops 88583696 | bytes 125829 | tf_op jit(solution)/shard_map/grad_down/pallas_call | solution.py:553
  800.4 9.6 collective-permute-done.60
  810.0 14.5 %collective-permute-done.58 = bf16[192,1024]{1,0:T(8,128)(2,1)S(1)} collective-permute-done((bf16[192,1024]{1,0:T(8,128)(2,1)S(1)}, bf16[192,1024]{1,0:T(8,128)(2,1)S(1)}, u32[]{:S(2)}, u32[]{:S(2)}) %collective-permute-start.58) | collective-permute-done | bytes 393248 | tf_op jit(solution)/shard_map/ppermute | solution.py:81
  824.5 6.7 collective-permute-done.59
  844.0 8.0 collective-permute-done.64
  852.1 8.1 collective-permute-done.62
  860.1 16.9 %collective-permute-done.63 = bf16[2,96,1024]{2,1,0:T(8,128)(2,1)} collective-permute-done((bf16[2,96,1024]{2,1,0:T(8,128)(2,1)S(1)}, bf16[2,96,1024]{2,1,0:T(8,128)(2,1)}, u32[]{:S(2)}, u32[]{:S(2)}) %collective-permute-start.63) | collective-permute-done | bytes 393248 | tf_op jit(solution)/shard_map/ppermute | solution.py:81
  883.9 6.8 convolution_convert_fusion.1
  890.8 5.3 all-to-all-start.5
  900.8 8.9 fusion.18
  909.7 14.7 %attention_bwd.4 = (bf16[768,1024]{1,0:T(8,128)(2,1)}, bf16[1,1024,512]{2,1,0:T(8,128)(2,1)}) custom-call(s32[4]{0:T(128)} %and_select_fusion.place, bf16[768,1024]{1,0:T(8,128)(2,1)} %get-tuple-element.91.q_in, bf16[768,1024]{1,0:T(8,128)(2,1)} %bitcast.355, bf16[1,1024,512]{2,1,0:T(8,128)(2,1)} %add_bitcast_fusion.kv, f32[768,128]{1,0:T(8,128)} %pad_maximum_fusion.17.cos, ...), custom_call_target="tpu_custom_call" | custom-call | flops 120795952 | bytes 31457 | tf_op jit(solution)/shard_map/attention_bwd/pallas_call | solution.py:332
  924.4 14.7 %attention_bwd.5 = (bf16[768,1024]{1,0:T(8,128)(2,1)}, bf16[1,1024,512]{2,1,0:T(8,128)(2,1)}) custom-call(s32[4]{0:T(128)} %and_select_fusion.place, bf16[768,1024]{1,0:T(8,128)(2,1)} %get-tuple-element.91.q_in, bf16[768,1024]{1,0:T(8,128)(2,1)} %bitcast.356, bf16[1,1024,512]{2,1,0:T(8,128)(2,1)} %bitcast.375, ...), custom_call_target="tpu_custom_call", output_to_operand_aliasing={{0}: (11, {})} | custom-call | flops 120795952 | bytes 31457 | tf_op jit(solution)/shard_map/attention_bwd/pallas_call | solution.py:332
  939.1 14.7 %attention_bwd.6 = (bf16[768,1024]{1,0:T(8,128)(2,1)}, bf16[1,1024,512]{2,1,0:T(8,128)(2,1)}) custom-call(s32[4]{0:T(128)} %and_select_fusion.place, bf16[768,1024]{1,0:T(8,128)(2,1)} %get-tuple-element.91.q_in, bf16[768,1024]{1,0:T(8,128)(2,1)} %bitcast.357, bf16[1,1024,512]{2,1,0:T(8,128)(2,1)} %bitcast.377, ...), custom_call_target="tpu_custom_call", output_to_operand_aliasing={{0}: (11, {})} | custom-call | flops 120795952 | bytes 31457 | tf_op jit(solution)/shard_map/attention_bwd/pallas_call | solution.py:332
  957.6 14.8 %attention_bwd.7 = (bf16[768,1024]{1,0:T(8,128)(2,1)}, bf16[1,1024,512]{2,1,0:T(8,128)(2,1)}) custom-call(s32[4]{0:T(128)} %and_select_fusion.place, bf16[768,1024]{1,0:T(8,128)(2,1)} %get-tuple-element.91.q_in, bf16[768,1024]{1,0:T(8,128)(2,1)} %bitcast.358, bf16[1,1024,512]{2,1,0:T(8,128)(2,1)} %bitcast.373, ...), custom_call_target="tpu_custom_call", output_to_operand_aliasing={{0}: (11, {})} | custom-call | flops 120795952 | bytes 31457 | tf_op jit(solution)/shard_map/attention_bwd/pallas_call | solution.py:332
  972.4 33.5 %all-to-all-done.5 = bf16[4,1408,512]{2,1,0:T(8,128)(2,1)} async-done(((bf16[4,1408,512]{2,1,0:T(8,128)(2,1)}), bf16[4,1408,512]{2,1,0:T(8,128)(2,1)}, u32[]{:S(2)}, u32[]{:S(2)}) %all-to-all-start.5) | async-done | bytes 5767200 | tf_op jit(solution)/shard_map/all_to_all | solution.py:39
  1005.9 10.4 convolution_convert_fusion
  1016.2 22.0 %reduce-scatter.4.cloned.1.call-done = bf16[2,1024,512]{2,1,0:T(8,128)(2,1)} async-done(((bf16[2,1024,2048]{2,1,0:T(8,128)(2,1)}), bf16[2,1024,512]{2,1,0:T(8,128)(2,1)}) %reduce-scatter.4.cloned.1.call-update) | async-done | bytes 2097168 | tf_op jit(solution)/shard_map/reduce_scatter | solution.py:865
  1074.7 7.4 unpack_down.1
  1082.1 14.3 %unpack_gateup.1 = f32[2,512,2,2816]{3,2,1,0:T(2,128)} custom-call(bf16[2,2,512,1408]{3,2,1,0:T(8,128)(2,1)} %bitcast.156.gate, bf16[2,2,512,1408]{3,2,1,0:T(8,128)(2,1)} %bitcast.157.up), custom_call_target="tpu_custom_call" | custom-call | bytes 346030 | tf_op jit(solution)/shard_map/unpack_gateup/pallas_call | solution.py:159
  1096.5 10.2 collective-permute-done.71
  1111.1 6.2 collective-permute-done.75
  1118.6 6.0 collective-permute-done.76
  1124.6 11.6 collective-permute-start.77
  1151.4 7.6 all-to-all-done.6
  1162.1 15.3 %reduce-scatter.8.cloned.1.call-done = bf16[2,512,1024]{2,1,0:T(8,128)(2,1)} async-done(((bf16[2,2048,1024]{2,1,0:T(8,128)(2,1)}), bf16[2,512,1024]{2,1,0:T(8,128)(2,1)}) %reduce-scatter.8.cloned.1.call-update) | async-done | bytes 2097168 | tf_op jit(solution)/shard_map/reduce_scatter | solution.py:887
  (556 shorter events, 332.7 us)
Async XLA Ops:
  7.2 98.8 %all-gather.6.cloned.1.call-start = ((), (), s32[]{:S(2)}) async-start(), calls=%async_computation.11 | async-start | bytes 2621440 | tf_op jit(solution)/shard_map/all_gather | solution.py:631
  26.5 226.7 %all-gather.4.cloned.1.call-start = ((), (), s32[]{:S(2)}) async-start(), calls=%async_computation.10 | async-start | bytes 10485760 | tf_op jit(solution)/shard_map/all_gather | solution.py:634
  30.4 312.3 %all-gather.8.cloned.1.call-start = ((), (), s32[]{:S(2)}) async-start(), calls=%async_computation.12 | async-start | bytes 10485760 | tf_op jit(solution)/shard_map/all_gather | solution.py:637
  35.4 44.9 %collective-permute-start.2 = (bf16[256,1024]{1,0:T(8,128)(2,1)S(1)}, bf16[256,1024]{1,0:T(8,128)(2,1)S(1)}, u32[]{:S(2)}, u32[]{:S(2)}) collective-permute-start(bf16[256,1024]{1,0:T(8,128)(2,1)S(1)} %copy-done.21), channel_id=1, source_target_pairs={{0,2},{2,4},{4,6},{6,0},{1,3},{3,5},{5,7},{7,1},{8,10},{10,12},{12... | collective-permute-start | bytes 1572872 | tf_op jit(solution)/shard_map/ppermute | solution.py:62
  36.1 46.4 %collective-permute-start = (bf16[256,1024]{1,0:T(8,128)(2,1)S(1)}, bf16[256,1024]{1,0:T(8,128)(2,1)S(1)}, u32[]{:S(2)}, u32[]{:S(2)}) collective-permute-start(bf16[256,1024]{1,0:T(8,128)(2,1)S(1)} %copy-done.21), channel_id=1, source_target_pairs={{0,6},{2,0},{4,2},{6,4},{1,7},{3,1},{5,3},{7,5},{8,14},{10,8},{12,... | collective-permute-start | bytes 1572872 | tf_op jit(solution)/shard_map/ppermute | solution.py:62
  39.2 45.2 %collective-permute-start.1 = (bf16[256,1024]{1,0:T(8,128)(2,1)S(1)}, bf16[256,1024]{1,0:T(8,128)(2,1)S(1)}, u32[]{:S(2)}, u32[]{:S(2)}) collective-permute-start(bf16[256,1024]{1,0:T(8,128)(2,1)S(1)} %copy-done.21), channel_id=1, source_target_pairs={{0,4},{2,6},{4,0},{6,2},{1,5},{3,7},{5,1},{7,3},{8,12},{10,14},{12... | collective-permute-start | bytes 1572872 | tf_op jit(solution)/shard_map/ppermute | solution.py:62
  40.2 88.6 %collective-permute-start.6 = (s32[8,256]{1,0:T(8,128)S(1)}, s32[8,256]{1,0:T(8,128)S(1)}, u32[]{:S(2)}, u32[]{:S(2)}) collective-permute-start(s32[8,256]{1,0:T(8,128)S(1)} %get-tuple-element.198), channel_id=1, source_target_pairs={{0,6},{2,0},{4,2},{6,4},{1,7},{3,1},{5,3},{7,5},{8,14},{10,8},{12,... | collective-permute-start | bytes 24584 | tf_op jit(solution)/shard_map/ppermute | solution.py:62
  41.1 87.8 %collective-permute-start.7 = (s32[8,256]{1,0:T(8,128)S(1)}, s32[8,256]{1,0:T(8,128)S(1)}, u32[]{:S(2)}, u32[]{:S(2)}) collective-permute-start(s32[8,256]{1,0:T(8,128)S(1)} %get-tuple-element.198), channel_id=1, source_target_pairs={{0,4},{2,6},{4,0},{6,2},{1,5},{3,7},{5,1},{7,3},{8,12},{10,14},{12... | collective-permute-start | bytes 24584 | tf_op jit(solution)/shard_map/ppermute | solution.py:62
  49.3 84.9 %all-to-all-start = ((bf16[4,1408,512]{2,1,0:T(8,128)(2,1)}), bf16[4,1408,512]{2,1,0:T(8,128)(2,1)}, u32[]{:S(2)}, u32[]{:S(2)}) async-start(bf16[4,1408,512]{2,1,0:T(8,128)(2,1)} %bitcast.359), calls=%async_computation | async-start | bytes 11534336 | tf_op jit(solution)/shard_map/all_to_all | solution.py:39
  80.3 48.6 %collective-permute-start.8 = (s32[8,256]{1,0:T(8,128)S(1)}, s32[8,256]{1,0:T(8,128)S(1)}, u32[]{:S(2)}, u32[]{:S(2)}) collective-permute-start(s32[8,256]{1,0:T(8,128)S(1)} %get-tuple-element.198), channel_id=1, source_target_pairs={{0,2},{2,4},{4,6},{6,0},{1,3},{3,5},{5,7},{7,1},{8,10},{10,12},{12... | collective-permute-start | bytes 24584 | tf_op jit(solution)/shard_map/ppermute | solution.py:62
  123.2 24.5 %collective-permute-start.15 = (bf16[1024,512]{1,0:T(8,128)(2,1)S(1)}, bf16[1024,512]{1,0:T(8,128)(2,1)}, u32[]{:S(2)}, u32[]{:S(2)}) collective-permute-start(bf16[1024,512]{1,0:T(8,128)(2,1)S(1)} %bitcast.370), channel_id=1, source_target_pairs={{0,2},{2,4},{4,6},{1,3},{3,5},{5,7},{8,10},{10,12},{12,14},{9,11},... | collective-permute-start | bytes 3145736 | tf_op jit(solution)/shard_map/ppermute | solution.py:73
  125.5 27.7 %collective-permute-start.12 = (bf16[1024,512]{1,0:T(8,128)(2,1)S(1)}, bf16[1024,512]{1,0:T(8,128)(2,1)}, u32[]{:S(2)}, u32[]{:S(2)}) collective-permute-start(bf16[1024,512]{1,0:T(8,128)(2,1)S(1)} %bitcast.371), channel_id=1, source_target_pairs={{2,0},{4,2},{6,4},{3,1},{5,3},{7,5},{10,8},{12,10},{14,12},{11,9},... | collective-permute-start | bytes 3145736 | tf_op jit(solution)/shard_map/ppermute | solution.py:74
  134.2 164.0 %all-to-all-start.1 = ((bf16[4,512,1408]{2,1,0:T(8,128)(2,1)}), bf16[4,512,1408]{2,1,0:T(8,128)(2,1)}, u32[]{:S(2)}, u32[]{:S(2)}) async-start(bf16[4,512,1408]{2,1,0:T(8,128)(2,1)} %bitcast.387), calls=%async_computation.1 | async-start | bytes 11534336 | tf_op jit(solution)/shard_map/all_to_all | solution.py:39
  147.8 27.2 %collective-permute-start.16 = (bf16[1024,512]{1,0:T(8,128)(2,1)}, bf16[1024,512]{1,0:T(8,128)(2,1)}, u32[]{:S(2)}, u32[]{:S(2)}) collective-permute-start(bf16[1024,512]{1,0:T(8,128)(2,1)} %collective-permute-done.15), channel_id=1, source_target_pairs={{0,2},{2,4},{4,6},{1,3},{3,5},{5,7},{8,10},{10,12},{12,14},{9,11},... | collective-permute-start | bytes 3145736 | tf_op jit(solution)/shard_map/ppermute | solution.py:73
  153.2 26.8 %collective-permute-start.13 = (bf16[1024,512]{1,0:T(8,128)(2,1)}, bf16[1024,512]{1,0:T(8,128)(2,1)}, u32[]{:S(2)}, u32[]{:S(2)}) collective-permute-start(bf16[1024,512]{1,0:T(8,128)(2,1)} %collective-permute-done.12), channel_id=1, source_target_pairs={{2,0},{4,2},{6,4},{3,1},{5,3},{7,5},{10,8},{12,10},{14,12},{11,9},... | collective-permute-start | bytes 3145736 | tf_op jit(solution)/shard_map/ppermute | solution.py:74
  174.9 26.2 %collective-permute-start.17 = (bf16[1024,512]{1,0:T(8,128)(2,1)}, bf16[1024,512]{1,0:T(8,128)(2,1)S(1)}, u32[]{:S(2)}, u32[]{:S(2)}) collective-permute-start(bf16[1024,512]{1,0:T(8,128)(2,1)} %collective-permute-done.16), channel_id=1, source_target_pairs={{0,2},{2,4},{4,6},{1,3},{3,5},{5,7},{8,10},{10,12},{12,14},{9,11},... | collective-permute-start | bytes 3145736 | tf_op jit(solution)/shard_map/ppermute | solution.py:73
  180.0 25.9 %collective-permute-start.14 = (bf16[1024,512]{1,0:T(8,128)(2,1)}, bf16[1024,512]{1,0:T(8,128)(2,1)}, u32[]{:S(2)}, u32[]{:S(2)}) collective-permute-start(bf16[1024,512]{1,0:T(8,128)(2,1)} %collective-permute-done.13), channel_id=1, source_target_pairs={{2,0},{4,2},{6,4},{3,1},{5,3},{7,5},{10,8},{12,10},{14,12},{11,9},... | collective-permute-start | bytes 3145736 | tf_op jit(solution)/shard_map/ppermute | solution.py:74
  210.3 138.1 %collective-permute-start.27 = (bf16[2,96,1024]{2,1,0:T(8,128)(2,1)}, bf16[2,96,1024]{2,1,0:T(8,128)(2,1)}, u32[]{:S(2)}, u32[]{:S(2)}) collective-permute-start(bf16[2,96,1024]{2,1,0:T(8,128)(2,1)} %bitcast.79), channel_id=1, source_target_pairs={{0,6},{2,0},{4,2},{6,4},{1,7},{3,1},{5,3},{7,5},{8,14},{10,8},{12,... | collective-permute-start | bytes 1179656 | tf_op jit(solution)/shard_map/ppermute | solution.py:81
  212.1 136.3 %collective-permute-start.28 = (bf16[2,96,1024]{2,1,0:T(8,128)(2,1)S(1)}, bf16[2,96,1024]{2,1,0:T(8,128)(2,1)}, u32[]{:S(2)}, u32[]{:S(2)}) collective-permute-start(bf16[2,96,1024]{2,1,0:T(8,128)(2,1)S(1)} %bitcast.410), channel_id=1, source_target_pairs={{0,4},{2,6},{4,0},{6,2},{1,5},{3,7},{5,1},{7,3},{8,12},{10,14},{12... | collective-permute-start | bytes 1179656 | tf_op jit(solution)/shard_map/ppermute | solution.py:81
  212.2 136.2 %collective-permute-start.29 = (bf16[2,96,1024]{2,1,0:T(8,128)(2,1)}, bf16[2,96,1024]{2,1,0:T(8,128)(2,1)}, u32[]{:S(2)}, u32[]{:S(2)}) collective-permute-start(bf16[2,96,1024]{2,1,0:T(8,128)(2,1)} %bitcast.83), channel_id=1, source_target_pairs={{0,2},{2,4},{4,6},{6,0},{1,3},{3,5},{5,7},{7,1},{8,10},{10,12},{12... | collective-permute-start | bytes 1179656 | tf_op jit(solution)/shard_map/ppermute | solution.py:81
  348.4 24.1 %collective-permute-start.18 = (bf16[2,384,1024]{2,1,0:T(8,128)(2,1)}, bf16[2,384,1024]{2,1,0:T(8,128)(2,1)}, u32[]{:S(2)}, u32[]{:S(2)}) collective-permute-start(bf16[2,384,1024]{2,1,0:T(8,128)(2,1)} %fusion.19), channel_id=1, source_target_pairs={{0,1},{1,0},{2,3},{3,2},{4,5},{5,4},{6,7},{7,6},{8,9},{9,8},{10,11... | collective-permute-start | bytes 4718600 | tf_op jit(solution)/shard_map/ppermute | solution.py:35
  350.9 21.6 %collective-permute-start.32 = (bf16[384,1024]{1,0:T(8,128)(2,1)}, bf16[384,1024]{1,0:T(8,128)(2,1)}, u32[]{:S(2)}, u32[]{:S(2)}) collective-permute-start(bf16[384,1024]{1,0:T(8,128)(2,1)} %bitcast.86), channel_id=1, source_target_pairs={{0,24},{8,16},{16,8},{24,0},{1,25},{9,17},{17,9},{25,1},{2,26},{10... | collective-permute-start | bytes 2359304 | tf_op jit(solution)/shard_map/ppermute | solution.py:89
  352.4 37.0 %collective-permute-start.30 = (bf16[384,1024]{1,0:T(8,128)(2,1)}, bf16[384,1024]{1,0:T(8,128)(2,1)}, u32[]{:S(2)}, u32[]{:S(2)}) collective-permute-start(bf16[384,1024]{1,0:T(8,128)(2,1)} %bitcast.86), channel_id=1, source_target_pairs={{0,8},{8,0},{16,24},{24,16},{1,9},{9,1},{17,25},{25,17},{2,10},{10... | collective-permute-start | bytes 2359304 | tf_op jit(solution)/shard_map/ppermute | solution.py:89
  353.8 35.6 %collective-permute-start.31 = (bf16[384,1024]{1,0:T(8,128)(2,1)S(1)}, bf16[384,1024]{1,0:T(8,128)(2,1)}, u32[]{:S(2)}, u32[]{:S(2)}) collective-permute-start(bf16[384,1024]{1,0:T(8,128)(2,1)S(1)} %bitcast.395), channel_id=1, source_target_pairs={{0,16},{8,24},{16,0},{24,8},{1,17},{9,25},{17,1},{25,9},{2,18},{10... | collective-permute-start | bytes 2359304 | tf_op jit(solution)/shard_map/ppermute | solution.py:89
  354.4 131.6 %all-to-all-start.2 = ((bf16[4,512,1408]{2,1,0:T(8,128)(2,1)}), bf16[4,512,1408]{2,1,0:T(8,128)(2,1)}, u32[]{:S(2)}, u32[]{:S(2)}) async-start(bf16[4,512,1408]{2,1,0:T(8,128)(2,1)} %bitcast.386), calls=%async_computation.2 | async-start | bytes 11534336 | tf_op jit(solution)/shard_map/all_to_all | solution.py:39
  391.5 55.1 %collective-permute-start.33 = (bf16[1536,1024]{1,0:T(8,128)(2,1)S(1)}, bf16[1536,1024]{1,0:T(8,128)(2,1)}, u32[]{:S(2)}, u32[]{:S(2)}) collective-permute-start(bf16[1536,1024]{1,0:T(8,128)(2,1)S(1)} %pad_maximum_fusion.1.g_own), channel_id=1, source_target_pairs={{0,1},{1,0},{2,3},{3,2},{4,5},{5,4},{6,7},{7,6},{8,9},{9,8},{10,11... | collective-permute-start | bytes 9437192 | tf_op jit(solution)/shard_map/ppermute | solution.py:35
  398.3 14.3 %collective-permute-start.19 = (bf16[192,1024]{1,0:T(8,128)(2,1)}, bf16[192,1024]{1,0:T(8,128)(2,1)}, u32[]{:S(2)}, u32[]{:S(2)}) collective-permute-start(bf16[192,1024]{1,0:T(8,128)(2,1)} %bitcast.55), channel_id=1, source_target_pairs={{0,2},{2,4},{4,6},{6,0},{1,3},{3,5},{5,7},{7,1},{8,10},{10,12},{12... | collective-permute-start | bytes 1179656 | tf_op jit(solution)/shard_map/ppermute | solution.py:81
  399.8 28.3 %collective-permute-start.20 = (bf16[192,1024]{1,0:T(8,128)(2,1)}, bf16[192,1024]{1,0:T(8,128)(2,1)}, u32[]{:S(2)}, u32[]{:S(2)}) collective-permute-start(bf16[192,1024]{1,0:T(8,128)(2,1)} %bitcast.56), channel_id=1, source_target_pairs={{0,4},{2,6},{4,0},{6,2},{1,5},{3,7},{5,1},{7,3},{8,12},{10,14},{12... | collective-permute-start | bytes 1179656 | tf_op jit(solution)/shard_map/ppermute | solution.py:81
  402.2 25.9 %collective-permute-start.21 = (bf16[192,1024]{1,0:T(8,128)(2,1)}, bf16[192,1024]{1,0:T(8,128)(2,1)}, u32[]{:S(2)}, u32[]{:S(2)}) collective-permute-start(bf16[192,1024]{1,0:T(8,128)(2,1)} %bitcast.57), channel_id=1, source_target_pairs={{0,6},{2,0},{4,2},{6,4},{1,7},{3,1},{5,3},{7,5},{8,14},{10,8},{12,... | collective-permute-start | bytes 1179656 | tf_op jit(solution)/shard_map/ppermute | solution.py:81
  436.0 25.7 %collective-permute-start.26 = (bf16[2,96,1024]{2,1,0:T(8,128)(2,1)}, bf16[2,96,1024]{2,1,0:T(8,128)(2,1)}, u32[]{:S(2)}, u32[]{:S(2)}) collective-permute-start(bf16[2,96,1024]{2,1,0:T(8,128)(2,1)} %bitcast.76), channel_id=1, source_target_pairs={{0,2},{2,4},{4,6},{6,0},{1,3},{3,5},{5,7},{7,1},{8,10},{10,12},{12... | collective-permute-start | bytes 1179656 | tf_op jit(solution)/shard_map/ppermute | solution.py:81
  444.9 19.1 %collective-permute-start.24 = (bf16[2,96,1024]{2,1,0:T(8,128)(2,1)}, bf16[2,96,1024]{2,1,0:T(8,128)(2,1)}, u32[]{:S(2)}, u32[]{:S(2)}) collective-permute-start(bf16[2,96,1024]{2,1,0:T(8,128)(2,1)} %bitcast.72), channel_id=1, source_target_pairs={{0,6},{2,0},{4,2},{6,4},{1,7},{3,1},{5,3},{7,5},{8,14},{10,8},{12,... | collective-permute-start | bytes 1179656 | tf_op jit(solution)/shard_map/ppermute | solution.py:81
  446.0 34.8 %collective-permute-start.25 = (bf16[2,96,1024]{2,1,0:T(8,128)(2,1)}, bf16[2,96,1024]{2,1,0:T(8,128)(2,1)}, u32[]{:S(2)}, u32[]{:S(2)}) collective-permute-start(bf16[2,96,1024]{2,1,0:T(8,128)(2,1)} %bitcast.74), channel_id=1, source_target_pairs={{0,4},{2,6},{4,0},{6,2},{1,5},{3,7},{5,1},{7,3},{8,12},{10,14},{12... | collective-permute-start | bytes 1179656 | tf_op jit(solution)/shard_map/ppermute | solution.py:81
  482.5 21.4 %collective-permute-start.36 = (bf16[384,1024]{1,0:T(8,128)(2,1)S(1)}, bf16[384,1024]{1,0:T(8,128)(2,1)S(1)}, u32[]{:S(2)}, u32[]{:S(2)}) collective-permute-start(bf16[384,1024]{1,0:T(8,128)(2,1)S(1)} %bitcast.408), channel_id=1, source_target_pairs={{0,24},{8,16},{16,8},{24,0},{1,25},{9,17},{17,9},{25,1},{2,26},{10... | collective-permute-start | bytes 2359304 | tf_op jit(solution)/shard_map/ppermute | solution.py:89
  483.7 36.1 %collective-permute-start.34 = (bf16[384,1024]{1,0:T(8,128)(2,1)S(1)}, bf16[384,1024]{1,0:T(8,128)(2,1)S(1)}, u32[]{:S(2)}, u32[]{:S(2)}) collective-permute-start(bf16[384,1024]{1,0:T(8,128)(2,1)S(1)} %bitcast.409), channel_id=1, source_target_pairs={{0,8},{8,0},{16,24},{24,16},{1,9},{9,1},{17,25},{25,17},{2,10},{10... | collective-permute-start | bytes 2359304 | tf_op jit(solution)/shard_map/ppermute | solution.py:89
  485.5 35.2 %collective-permute-start.35 = (bf16[384,1024]{1,0:T(8,128)(2,1)S(1)}, bf16[384,1024]{1,0:T(8,128)(2,1)}, u32[]{:S(2)}, u32[]{:S(2)}) collective-permute-start(bf16[384,1024]{1,0:T(8,128)(2,1)S(1)} %bitcast.397), channel_id=1, source_target_pairs={{0,16},{8,24},{16,0},{24,8},{1,17},{9,25},{17,1},{25,9},{2,18},{10... | collective-permute-start | bytes 2359304 | tf_op jit(solution)/shard_map/ppermute | solution.py:89
  576.5 15.0 %collective-permute-start.40 = (bf16[1536,1024]{1,0:T(8,128)(2,1)}, bf16[1536,1024]{1,0:T(8,128)(2,1)S(1)}, u32[]{:S(2)}, u32[]{:S(2)}) collective-permute-start(bf16[1536,1024]{1,0:T(8,128)(2,1)} %rows_half.4), channel_id=1, source_target_pairs={{0,1},{1,0},{2,3},{3,2},{4,5},{5,4},{6,7},{7,6},{8,9},{9,8},{10,11... | collective-permute-start | bytes 9437192 | tf_op jit(solution)/shard_map/ppermute | solution.py:35
  618.6 17.6 %collective-permute-start.51 = (bf16[1536,1024]{1,0:T(8,128)(2,1)}, bf16[1536,1024]{1,0:T(8,128)(2,1)}, u32[]{:S(2)}, u32[]{:S(2)}) collective-permute-start(bf16[1536,1024]{1,0:T(8,128)(2,1)} %rows_half.6), channel_id=1, source_target_pairs={{0,1},{1,0},{2,3},{3,2},{4,5},{5,4},{6,7},{7,6},{8,9},{9,8},{10,11... | collective-permute-start | bytes 9437192 | tf_op jit(solution)/shard_map/ppermute | solution.py:35
  632.7 19.8 %collective-permute-start.45 = (bf16[4,96,1024]{2,1,0:T(8,128)(2,1)}, bf16[4,96,1024]{2,1,0:T(8,128)(2,1)S(1)}, u32[]{:S(2)}, u32[]{:S(2)}) collective-permute-start(bf16[4,96,1024]{2,1,0:T(8,128)(2,1)} %bitcast.95), channel_id=1, source_target_pairs={{0,16},{8,24},{16,0},{24,8},{1,17},{9,25},{17,1},{25,9},{2,18},{10... | collective-permute-start | bytes 2359304 | tf_op jit(solution)/shard_map/ppermute | solution.py:89
  634.0 20.7 %collective-permute-start.46 = (bf16[4,96,1024]{2,1,0:T(8,128)(2,1)}, bf16[4,96,1024]{2,1,0:T(8,128)(2,1)S(1)}, u32[]{:S(2)}, u32[]{:S(2)}) collective-permute-start(bf16[4,96,1024]{2,1,0:T(8,128)(2,1)} %bitcast.97), channel_id=1, source_target_pairs={{0,8},{8,0},{16,24},{24,16},{1,9},{9,1},{17,25},{25,17},{2,10},{10... | collective-permute-start | bytes 2359304 | tf_op jit(solution)/shard_map/ppermute | solution.py:89
  635.0 34.2 %collective-permute-start.47 = (bf16[4,96,1024]{2,1,0:T(8,128)(2,1)}, bf16[4,96,1024]{2,1,0:T(8,128)(2,1)}, u32[]{:S(2)}, u32[]{:S(2)}) collective-permute-start(bf16[4,96,1024]{2,1,0:T(8,128)(2,1)} %bitcast.98), channel_id=1, source_target_pairs={{0,24},{8,16},{16,8},{24,0},{1,25},{9,17},{17,9},{25,1},{2,26},{10... | collective-permute-start | bytes 2359304 | tf_op jit(solution)/shard_map/ppermute | solution.py:89
  671.4 19.6 %collective-permute-start.52 = (bf16[4,96,1024]{2,1,0:T(8,128)(2,1)S(1)}, bf16[4,96,1024]{2,1,0:T(8,128)(2,1)S(1)}, u32[]{:S(2)}, u32[]{:S(2)}) collective-permute-start(bf16[4,96,1024]{2,1,0:T(8,128)(2,1)S(1)} %bitcast.407), channel_id=1, source_target_pairs={{0,16},{8,24},{16,0},{24,8},{1,17},{9,25},{17,1},{25,9},{2,18},{10... | collective-permute-start | bytes 2359304 | tf_op jit(solution)/shard_map/ppermute | solution.py:89
  672.7 20.5 %collective-permute-start.53 = (bf16[4,96,1024]{2,1,0:T(8,128)(2,1)S(1)}, bf16[4,96,1024]{2,1,0:T(8,128)(2,1)S(1)}, u32[]{:S(2)}, u32[]{:S(2)}) collective-permute-start(bf16[4,96,1024]{2,1,0:T(8,128)(2,1)S(1)} %bitcast.406), channel_id=1, source_target_pairs={{0,8},{8,0},{16,24},{24,16},{1,9},{9,1},{17,25},{25,17},{2,10},{10... | collective-permute-start | bytes 2359304 | tf_op jit(solution)/shard_map/ppermute | solution.py:89
  673.7 32.7 %collective-permute-start.54 = (bf16[4,96,1024]{2,1,0:T(8,128)(2,1)S(1)}, bf16[4,96,1024]{2,1,0:T(8,128)(2,1)}, u32[]{:S(2)}, u32[]{:S(2)}) collective-permute-start(bf16[4,96,1024]{2,1,0:T(8,128)(2,1)S(1)} %bitcast.405), channel_id=1, source_target_pairs={{0,24},{8,16},{16,8},{24,0},{1,25},{9,17},{17,9},{25,1},{2,26},{10... | collective-permute-start | bytes 2359304 | tf_op jit(solution)/shard_map/ppermute | solution.py:89
  706.5 66.1 %all-to-all-start.3 = ((bf16[4,512,1408]{2,1,0:T(8,128)(2,1)}), bf16[4,512,1408]{2,1,0:T(8,128)(2,1)}, u32[]{:S(2)}, u32[]{:S(2)}) async-start(bf16[4,512,1408]{2,1,0:T(8,128)(2,1)} %grad_gateup.2), calls=%async_computation.3 | async-start | bytes 11534336 | tf_op jit(solution)/shard_map/all_to_all | solution.py:39
  723.8 14.0 %collective-permute-start.48 = (bf16[192,1024]{1,0:T(8,128)(2,1)S(1)}, bf16[192,1024]{1,0:T(8,128)(2,1)S(1)}, u32[]{:S(2)}, u32[]{:S(2)}) collective-permute-start(bf16[192,1024]{1,0:T(8,128)(2,1)S(1)} %pad_maximum_fusion.19), channel_id=1, source_target_pairs={{0,2},{2,4},{4,6},{6,0},{1,3},{3,5},{5,7},{7,1},{8,10},{10,12},{12... | collective-permute-start | bytes 1179656 | tf_op jit(solution)/shard_map/ppermute | solution.py:81
  725.4 52.4 %collective-permute-start.49 = (bf16[192,1024]{1,0:T(8,128)(2,1)}, bf16[192,1024]{1,0:T(8,128)(2,1)}, u32[]{:S(2)}, u32[]{:S(2)}) collective-permute-start(bf16[192,1024]{1,0:T(8,128)(2,1)} %pad_maximum_fusion.20), channel_id=1, source_target_pairs={{0,4},{2,6},{4,0},{6,2},{1,5},{3,7},{5,1},{7,3},{8,12},{10,14},{12... | collective-permute-start | bytes 1179656 | tf_op jit(solution)/shard_map/ppermute | solution.py:81
  728.2 51.4 %collective-permute-start.50 = (bf16[192,1024]{1,0:T(8,128)(2,1)}, bf16[192,1024]{1,0:T(8,128)(2,1)}, u32[]{:S(2)}, u32[]{:S(2)}) collective-permute-start(bf16[192,1024]{1,0:T(8,128)(2,1)} %pad_maximum_fusion.21), channel_id=1, source_target_pairs={{0,6},{2,0},{4,2},{6,4},{1,7},{3,1},{5,3},{7,5},{8,14},{10,8},{12,... | collective-permute-start | bytes 1179656 | tf_op jit(solution)/shard_map/ppermute | solution.py:81
  772.5 71.5 %all-to-all-start.4 = ((bf16[4,512,1408]{2,1,0:T(8,128)(2,1)}), bf16[4,512,1408]{2,1,0:T(8,128)(2,1)}, u32[]{:S(2)}, u32[]{:S(2)}) async-start(bf16[4,512,1408]{2,1,0:T(8,128)(2,1)} %grad_gateup.3), calls=%async_computation.4 | async-start | bytes 11534336 | tf_op jit(solution)/shard_map/all_to_all | solution.py:39
  777.7 260.5 %reduce-scatter.4.cloned.1.call-start = ((), (), s32[]{:S(2)}) async-start(), calls=%async_computation.13 | async-start | bytes 10485760 | tf_op jit(solution)/shard_map/reduce_scatter | solution.py:865
  799.3 31.9 %collective-permute-start.59 = (bf16[192,1024]{1,0:T(8,128)(2,1)S(1)}, bf16[192,1024]{1,0:T(8,128)(2,1)S(1)}, u32[]{:S(2)}, u32[]{:S(2)}) collective-permute-start(bf16[192,1024]{1,0:T(8,128)(2,1)S(1)} %pad_maximum_fusion.23), channel_id=1, source_target_pairs={{0,4},{2,6},{4,0},{6,2},{1,5},{3,7},{5,1},{7,3},{8,12},{10,14},{12... | collective-permute-start | bytes 1179656 | tf_op jit(solution)/shard_map/ppermute | solution.py:81
  799.5 25.1 %collective-permute-start.58 = (bf16[192,1024]{1,0:T(8,128)(2,1)S(1)}, bf16[192,1024]{1,0:T(8,128)(2,1)S(1)}, u32[]{:S(2)}, u32[]{:S(2)}) collective-permute-start(bf16[192,1024]{1,0:T(8,128)(2,1)S(1)} %pad_maximum_fusion.22), channel_id=1, source_target_pairs={{0,2},{2,4},{4,6},{6,0},{1,3},{3,5},{5,7},{7,1},{8,10},{10,12},{12... | collective-permute-start | bytes 1179656 | tf_op jit(solution)/shard_map/ppermute | solution.py:81
  840.0 20.1 %collective-permute-start.62 = (bf16[2,96,1024]{2,1,0:T(8,128)(2,1)S(1)}, bf16[2,96,1024]{2,1,0:T(8,128)(2,1)}, u32[]{:S(2)}, u32[]{:S(2)}) collective-permute-start(bf16[2,96,1024]{2,1,0:T(8,128)(2,1)S(1)} %bitcast.414), channel_id=1, source_target_pairs={{0,6},{2,0},{4,2},{6,4},{1,7},{3,1},{5,3},{7,5},{8,14},{10,8},{12,... | collective-permute-start | bytes 1179656 | tf_op jit(solution)/shard_map/ppermute | solution.py:81
  841.9 35.1 %collective-permute-start.63 = (bf16[2,96,1024]{2,1,0:T(8,128)(2,1)S(1)}, bf16[2,96,1024]{2,1,0:T(8,128)(2,1)}, u32[]{:S(2)}, u32[]{:S(2)}) collective-permute-start(bf16[2,96,1024]{2,1,0:T(8,128)(2,1)S(1)} %bitcast.412), channel_id=1, source_target_pairs={{0,4},{2,6},{4,0},{6,2},{1,5},{3,7},{5,1},{7,3},{8,12},{10,14},{12... | collective-permute-start | bytes 1179656 | tf_op jit(solution)/shard_map/ppermute | solution.py:81
  890.8 115.1 %all-to-all-start.5 = ((bf16[4,1408,512]{2,1,0:T(8,128)(2,1)}), bf16[4,1408,512]{2,1,0:T(8,128)(2,1)}, u32[]{:S(2)}, u32[]{:S(2)}) async-start(bf16[4,1408,512]{2,1,0:T(8,128)(2,1)} %grad_down.1), calls=%async_computation.5 | async-start | bytes 11534336 | tf_op jit(solution)/shard_map/all_to_all | solution.py:39
  896.1 243.8 %reduce-scatter.6.cloned.1.call-start = ((), (), s32[]{:S(2)}) async-start(), calls=%async_computation.14 | async-start | bytes 2621440 | tf_op jit(solution)/shard_map/reduce_scatter | solution.py:905
  924.4 81.5 %collective-permute-start.67 = (bf16[1024,512]{1,0:T(8,128)(2,1)}, bf16[1024,512]{1,0:T(8,128)(2,1)S(1)}, u32[]{:S(2)}, u32[]{:S(2)}) collective-permute-start(bf16[1024,512]{1,0:T(8,128)(2,1)} %bitcast.472), channel_id=1, source_target_pairs={{0,4},{2,6},{4,0},{6,2},{1,5},{3,7},{5,1},{7,3},{8,12},{10,14},{12... | collective-permute-start | bytes 3145736 | tf_op jit(solution)/shard_map/ppermute | solution.py:81
  953.8 88.7 %collective-permute-start.66 = (bf16[1024,512]{1,0:T(8,128)(2,1)}, bf16[1024,512]{1,0:T(8,128)(2,1)}, u32[]{:S(2)}, u32[]{:S(2)}) collective-permute-start(bf16[1024,512]{1,0:T(8,128)(2,1)} %bitcast.471), channel_id=1, source_target_pairs={{0,6},{2,0},{4,2},{6,4},{1,7},{3,1},{5,3},{7,5},{8,14},{10,8},{12,... | collective-permute-start | bytes 3145736 | tf_op jit(solution)/shard_map/ppermute | solution.py:81
  956.8 85.7 %collective-permute-start.68 = (bf16[1024,512]{1,0:T(8,128)(2,1)}, bf16[1024,512]{1,0:T(8,128)(2,1)}, u32[]{:S(2)}, u32[]{:S(2)}) collective-permute-start(bf16[1024,512]{1,0:T(8,128)(2,1)} %bitcast.470), channel_id=1, source_target_pairs={{0,2},{2,4},{4,6},{6,0},{1,3},{3,5},{5,7},{7,1},{8,10},{10,12},{12... | collective-permute-start | bytes 3145736 | tf_op jit(solution)/shard_map/ppermute | solution.py:81
  1050.5 126.8 %reduce-scatter.8.cloned.1.call-start = ((), (), s32[]{:S(2)}) async-start(), calls=%async_computation.15 | async-start | bytes 10485760 | tf_op jit(solution)/shard_map/reduce_scatter | solution.py:887
  1068.1 28.3 %collective-permute-start.70 = (bf16[256,1024]{1,0:T(8,128)(2,1)S(1)}, bf16[256,1024]{1,0:T(8,128)(2,1)}, u32[]{:S(2)}, u32[]{:S(2)}) collective-permute-start(bf16[256,1024]{1,0:T(8,128)(2,1)S(1)} %get-tuple-element.142), channel_id=1, source_target_pairs={{0,2},{2,4},{4,6},{6,0},{1,3},{3,5},{5,7},{7,1},{8,10},{10,12},{12... | collective-permute-start | bytes 1572872 | tf_op jit(solution)/shard_map/ppermute | solution.py:81
  1069.6 37.1 %collective-permute-start.71 = (bf16[256,1024]{1,0:T(8,128)(2,1)S(1)}, bf16[256,1024]{1,0:T(8,128)(2,1)}, u32[]{:S(2)}, u32[]{:S(2)}) collective-permute-start(bf16[256,1024]{1,0:T(8,128)(2,1)S(1)} %get-tuple-element.141), channel_id=1, source_target_pairs={{0,4},{2,6},{4,0},{6,2},{1,5},{3,7},{5,1},{7,3},{8,12},{10,14},{12... | collective-permute-start | bytes 1572872 | tf_op jit(solution)/shard_map/ppermute | solution.py:81
  1072.0 34.7 %collective-permute-start.72 = (bf16[256,1024]{1,0:T(8,128)(2,1)S(1)}, bf16[256,1024]{1,0:T(8,128)(2,1)}, u32[]{:S(2)}, u32[]{:S(2)}) collective-permute-start(bf16[256,1024]{1,0:T(8,128)(2,1)S(1)} %get-tuple-element.140), channel_id=1, source_target_pairs={{0,6},{2,0},{4,2},{6,4},{1,7},{3,1},{5,3},{7,5},{8,14},{10,8},{12,... | collective-permute-start | bytes 1572872 | tf_op jit(solution)/shard_map/ppermute | solution.py:81
  1124.6 14.2 %collective-permute-start.77 = (f32[18,1024]{1,0:T(8,128)S(1)}, f32[18,1024]{1,0:T(8,128)S(1)}, u32[]{:S(2)}, u32[]{:S(2)}) collective-permute-start(f32[18,1024]{1,0:T(8,128)S(1)} %add.336), channel_id=1, source_target_pairs={{0,2},{2,0},{4,6},{6,4},{1,3},{3,1},{5,7},{7,5},{8,10},{10,8},{12,... | collective-permute-start | bytes 221192 | tf_op jit(solution)/shard_map/ppermute | solution.py:46
  1141.9 17.1 %all-to-all-start.6 = ((bf16[4,128,2,2,128]{4,3,2,1,0:T(2,128)(2,1)}), bf16[4,128,2,2,128]{4,3,2,1,0:T(2,128)(2,1)S(1)}, u32[]{:S(2)}, u32[]{:S(2)}) async-start(bf16[4,128,2,2,128]{4,3,2,1,0:T(2,128)(2,1)} %reshape.745), calls=%async_computation.8 | async-start | bytes 1048576 | tf_op jit(solution)/shard_map/all_to_all | solution.py:39
  (115 other events, 1700.4 us)
Sparse Core Ops, SparseCore 0:
  26.7 72.4 all-gather.5
  101.6 151.6 all-gather.3
  255.1 87.6 all-gather.7
  890.9 147.3 reduce-scatter.3
  1050.6 35.1 reduce-scatter.5
  1088.8 88.5 reduce-scatter.7

commit v4 on v3

--- a/solution.py
+++ b/solution.py
@@ -754,6 +754,8 @@
     before = None
     order = [0, planes // 2] + [j for j in range(1, planes) if j != planes // 2]
     for j in order:
+        if j == order[-2]:
+            kv_near[j] = after(kv_near[j], *g_held[1:])
         before = att_forward(
             source_planes, query_raw, kv_near[j][None], cos_rows, sin_rows,
             row_pos[:, None], row_seg[:, None], seq_seg[None], j, before,
@@ -769,13 +771,12 @@
 
     out_mine, out_theirs = halves(whole_output, 2)
     given = swap(ein("lrf,lfd->lrd", mixed_owner, out_theirs).astype(BF16))
-    g_own, g_other = to_expert(g_held, (), (given,))
-    raw = hidden_raw(core_at, g_own, g_other, w_dn)
     branch_a = ein("lrf,lfd->lrd", mixed_owner, out_mine) + given.astype(F32)
     branch_a = branch_a.astype(BF16).reshape(local_att, planes, cap, width)
-    home_a = jnp.concatenate(
-        shift([branch_a[:, j].reshape(local_att * cap, width) for j in range(planes)], 1), 0
-    )
+    home_a = shift([branch_a[:, j].reshape(local_att * cap, width) for j in range(planes)], 1)
+    g_own, g_other = to_expert(g_held, (), tuple(home_a[1:]))
+    raw = hidden_raw(core_at, g_own, g_other, w_dn)
+    home_a = jnp.concatenate(home_a, 0)
     taken_a = ein("jst,sd->jtd", pick_att, home_a)
     middle = residual + jnp.sum(gates_a[:, :, None] * taken_a, 0)
 
@@ -794,8 +795,9 @@
     def over_parts(rows, *done):
         tail = rows.shape[1:]
         got = cross(list(rows.reshape((columns, planes, cap) + tail)))
+        if done:
+            got = list(lax.optimization_barrier(tuple(got) + done)[:columns])
         there = got[1:]
-        got[-1] = after(got[-1], *done)
         sums = []
         for near in range(local_mlp):
             parts = [got[k].astype(F32) for k in range(near, columns, local_mlp)]
@@ -813,17 +815,15 @@
     branch_theirs = rows_half(other_at, (hidden,), (w_dn,), width)
     given = swap(branch_theirs)
     grad_wgate = gu_outer(core_at, x_own, x_other, after(grad_gate, branch_theirs), columns)
-    branch_b = rows_half(core_at, (after(hidden, grad_wgate),), (w_dn,), width, given)
-    branch_blocks, branch_there = over_parts(after(branch_b, *dgate_there))
-    home_b, branch_back = mlp_home(branch_blocks)
-    grad_pair = (after(grad_gate, branch_b), grad_up)
+    branch_b = rows_half(core_at, (after(hidden, grad_wgate, *dgate_there),), (w_dn,), width, given)
+    grad_pair = (after(grad_gate, branch_b, *dgate_back), grad_up)
     given = swap(rows_half(other_at, grad_pair, (w_gate, w_up), width))
     db_rows = rows_half(core_at, grad_pair, (w_gate, w_up), width, given)
-    grad_wup = gu_outer(core_at, x_own, x_other, after(grad_up, db_rows, *dgate_back), columns)
+    grad_wup = gu_outer(core_at, x_own, x_other, after(grad_up, db_rows), columns)
+    branch_blocks, _ = over_parts(branch_b, grad_wup)
+    home_b, branch_back = mlp_home(branch_blocks)
     grad_wdn = dn_outer(core_at, after(hidden_gated, grad_wup), g_own, g_other, columns)
-    db_blocks, db_there = over_parts(
-        after(db_rows, *branch_there), grad_wdn, *branch_back
-    )
+    db_blocks, db_there = over_parts(db_rows, grad_wdn, *branch_back)
     home_db, _ = mlp_home(db_blocks)
     got_gate = a2a(after(grad_wgate, *db_there), "dp")
     got_up = a2a(grad_wup, "dp")
@@ -854,9 +854,8 @@
     grad_logit_a = gates_back(gates_a, grad_gates_a, named_a)
     grad_taken_a = (gates_a[:, :, None] * grad_middle[None]).astype(BF16)
     sent_a = ein("jst,jtd->sd", pick_att, grad_taken_a).astype(BF16)
-    sent_a = after(sent_a, got_gate)
     got_a = shift(list(sent_a.reshape(planes, local_att, cap, width)), -1)
-    got_a[-1] = after(got_a[-1], got_up)
+    got_a[-1] = after(got_a[-1], got_gate)
     held_grad_a = both_halves(
         jnp.stack(got_a, 1).reshape(local_att, planes * cap, width), core
     )
@@ -877,7 +876,7 @@
     grad_query = grad_query.reshape(local_att, planes * cap, feats)
     got_kv = shift(sent_kv, 1)
     grad_wq = ein(
-        "lrd,lrf->ldf", after(held_a, got_kv[planes // 2], got_dn), grad_query
+        "lrd,lrf->ldf", after(held_a, got_kv[planes // 2], got_up), grad_query
     ).astype(BF16)
     taken_b = ein("jst,sd->jtd", pick_mlp, home_b)
     output = (middle + jnp.sum(gates_b[:, :, None] * taken_b, 0)).astype(BF16)
@@ -885,7 +884,7 @@
     grad_kv = functools.reduce(jnp.add, [part.astype(F32) for part in got_kv]).astype(BF16)
     grad_kv = relative(grad_kv.reshape(planes, count, 2 * kv_part)).reshape(seq, 2 * kv_part)
     grad_wquery = lax.psum_scatter(
-        after(grad_wq, grad_kv), "dp", scatter_dimension=1, tiled=True
+        grad_wq, "dp", scatter_dimension=1, tiled=True
     ).astype(F32)
     query_mine, query_theirs = halves(whole_query, 1)
     kvw_mine, kvw_theirs = halves(w_kv_part, 0)
@@ -902,9 +901,10 @@
         got_up.reshape(ff_parts, local_mlp, depth, ff),
     )
     grad_wdown = unpack_down(got_dn.reshape(ff_parts, local_mlp, ff, depth))
-    grad_kv_w = lax.psum_scatter(
-        ein("td,tf->df", seq_a, grad_kv).astype(BF16), "dp", scatter_dimension=0, tiled=True
-    )
+    grad_kv_w = a2a(ein("td,tf->df", seq_a, grad_kv).astype(BF16), "dp")
+    grad_kv_w = jnp.sum(
+        grad_kv_w.reshape(columns, full_width // columns, 2 * kv_part).astype(F32), 0
+    ).astype(BF16)
     grad_kv_w = a2a(
         grad_kv_w.reshape(planes, w_kv.shape[0], part_heads, 2, HD), "expert"
     )

time: 1200 us -> 1160 us (0.967)
  waiting for transfers between devices: 507 us -> 445 us
  starting transfers between devices: 147 us -> 166 us
    ppermute x15, waiting for transfers between devices: 113 us -> 31.9 us  [cross(): lax.ppermute(blocks[k], 'dp', [(i, i ^ k) for i in range(count)])]
    all_gather x1, waiting for transfers between devices: 38.9 us -> 5.04 us  [shards(): lax.all_gather(after(w_query.astype(BF16), kv_send), 'dp', axis=1, tiled=...]
    all_to_all x7 -> x8, waiting for transfers between devices: 65.3 us -> 91.9 us  [a2a(): return lax.all_to_all(values, axis, split_axis=0, concat_axis=0, tiled=True)]
    ppermute x30, starting transfers between devices: 49.4 us -> 69.9 us  [shift(): lax.ppermute(blocks[j], 'expert', [(i, (i + sign * j) % count) for i in r...]
    reduce_scatter x2 -> x1, waiting for transfers between devices: 15.3 us -> 24.9 us  [shards(): lax.psum_scatter(grad_wq, 'dp', scatter_dimension=1, tiled=True).astype(F32)]
    all_to_all x7 -> x8, starting transfers between devices: 35.9 us -> 40.8 us  [a2a(): return lax.all_to_all(values, axis, split_axis=0, concat_axis=0, tiled=True)]
  transfers between devices with their start and end apart: 93 -> 93, of which waited for: 57 -> 46; matrix products, arithmetic and copies ran while one was open for 16% -> 17% of each run, Pallas kernels for 19% -> 20%
where the time goes in v4:
time: 1160 us; the launch traced here: 1150 us
  waiting for transfers between devices  445 us (38%)
  Pallas kernels  291 us (25%)
  starting transfers between devices  166 us (14%)
  other arithmetic  89.3 us (8%)
  matrix products  85.9 us (7%)
  local copies, waits for them, and re-layouts  53.8 us (5%)
  between operations  16 us (1%)
    ppermute x30, waiting for transfers between devices, shift(): lax.ppermute(blocks[j], 'expert', [(i, (i + sign * j) % count) for i in r...  149 us
    all_to_all x8, waiting for transfers between devices, a2a(): return lax.all_to_all(values, axis, split_axis=0, concat_axis=0, tiled=True)  91.9 us
    dot_general x24, matrix products, ein(): return jnp.einsum(spec, lhs, rhs, preferred_element_type=F32)  81.8 us
    ppermute x30, starting transfers between devices, shift(): lax.ppermute(blocks[j], 'expert', [(i, (i + sign * j) % count) for i in r...  69.9 us
    pallas_call x4, Pallas kernels, att_backward(): pl.pallas_call(att_bwd_kernel, grid_spec=pltpu.PrefetchScalarGridSpec(num...  59.1 us
    pallas_call x4, Pallas kernels, rows_half(): pl.pallas_call(functools.partial(rows_kernel, len(lhs)), grid_spec=pltpu....  50.2 us
    all_gather x1, waiting for transfers between devices, shards(): lax.all_gather(w_output.astype(BF16), 'dp', axis=2, tiled=True)  45.3 us
    all_to_all x8, starting transfers between devices, a2a(): return lax.all_to_all(values, axis, split_axis=0, concat_axis=0, tiled=True)  40.8 us
  transfers between devices with their start and end apart: 93, of which 46 were waited for; matrix products, arithmetic and copies ran while one was open for 17% of the time, Pallas kernels for 20%

profile of v4, /device:TPU:0, one launch (start us, length us, event | category | flops | bytes accessed | tf_op | source)
XLA Modules:
  0.0 1146.7 jit_solution(7981766781401787005)
XLA Ops:
  9.0 5.1 collective-permute-start.9
  18.0 7.3 collective-permute-done.10
  40.0 25.8 %pack_gateup.1 = (bf16[2,2,512,1408]{3,2,1,0:T(8,128)(2,1)}, bf16[2,2,512,1408]{3,2,1,0:T(8,128)(2,1)}) custom-call(f32[2,512,2,2816]{3,2,1,0:T(2,128)} %src.3), custom_call_target="tpu_custom_call" | custom-call | bytes 346030 | tf_op jit(solution)/shard_map/pack_gateup/pallas_call | solution.py:135
  65.8 7.2 pack_down.1
  73.0 11.1 collective-permute-done.1
  84.9 5.1 all-to-all-start
  98.0 5.6 fusion.82
  132.8 18.1 %collective-permute-done.15 = bf16[1024,512]{1,0:T(8,128)(2,1)S(1)} collective-permute-done((bf16[1024,512]{1,0:T(8,128)(2,1)S(1)}, bf16[1024,512]{1,0:T(8,128)(2,1)S(1)}, u32[]{:S(2)}, u32[]{:S(2)}) %collective-permute-start.15) | collective-permute-done | bytes 1048608 | tf_op jit(solution)/shard_map/ppermute | solution.py:73
  150.9 5.4 collective-permute-start.16
  157.6 19.4 %all-to-all-done.w_dn.refs_1_ = bf16[4,1408,512]{2,1,0:T(8,128)(2,1)} async-done(((bf16[4,1408,512]{2,1,0:T(8,128)(2,1)}), bf16[4,1408,512]{2,1,0:T(8,128)(2,1)}, u32[]{:S(2)}, u32[]{:S(2)}) %all-to-all-start) | async-done | bytes 5767200 | tf_op jit(solution)/shard_map/all_to_all | solution.py:39
  177.0 5.2 all-to-all-start.1
  197.0 12.5 %collective-permute-done.17 = bf16[1024,512]{1,0:T(8,128)(2,1)} collective-permute-done((bf16[1024,512]{1,0:T(8,128)(2,1)}, bf16[1024,512]{1,0:T(8,128)(2,1)}, u32[]{:S(2)}, u32[]{:S(2)}) %collective-permute-start.17) | collective-permute-done | bytes 1048608 | tf_op jit(solution)/shard_map/ppermute | solution.py:73
  220.6 11.6 %collective-permute-start.20 = (bf16[2,96,1024]{2,1,0:T(8,128)(2,1)S(1)}, bf16[2,96,1024]{2,1,0:T(8,128)(2,1)}, u32[]{:S(2)}, u32[]{:S(2)}) collective-permute-start(bf16[2,96,1024]{2,1,0:T(8,128)(2,1)S(1)} %bitcast.410), channel_id=1, source_target_pairs={{0,2},{2,4},{4,6},{6,0},{1,3},{3,5},{5,7},{7,1},{8,10},{10,12},{12... | collective-permute-start | bytes 1179656 | tf_op jit(solution)/shard_map/ppermute | solution.py:81
  237.3 16.2 %collective-permute-done.19 = bf16[2,96,1024]{2,1,0:T(8,128)(2,1)} collective-permute-done((bf16[2,96,1024]{2,1,0:T(8,128)(2,1)S(1)}, bf16[2,96,1024]{2,1,0:T(8,128)(2,1)}, u32[]{:S(2)}, u32[]{:S(2)}) %collective-permute-start.19) | collective-permute-done | bytes 393248 | tf_op jit(solution)/shard_map/ppermute | solution.py:81
  253.5 5.0 all-gather.4.cloned.1.call-done
  258.5 8.5 fusion.142
  267.0 9.1 attention_fwd.4
  276.1 8.8 attention_fwd.5
  284.9 8.8 attention_fwd.6
  293.8 8.8 attention_fwd.7
  302.6 45.3 %all-gather.8.cloned.1.call-done = bf16[2,1024,2048]{2,1,0:T(8,128)(2,1)} async-done(((bf16[2,1024,512]{2,1,0:T(8,128)(2,1)}), bf16[2,1024,2048]{2,1,0:T(8,128)(2,1)}) %all-gather.8.cloned.1.call-update) | async-done | bytes 8388624 | tf_op jit(solution)/shard_map/all_gather | solution.py:637
  347.8 5.6 fusion.19
  368.7 8.7 collective-permute-done.32
  380.8 13.5 %collective-permute-done.23 = bf16[192,1024]{1,0:T(8,128)(2,1)S(1)} collective-permute-done((bf16[192,1024]{1,0:T(8,128)(2,1)S(1)}, bf16[192,1024]{1,0:T(8,128)(2,1)S(1)}, u32[]{:S(2)}, u32[]{:S(2)}) %collective-permute-start.23) | collective-permute-done | bytes 393248 | tf_op jit(solution)/shard_map/ppermute | solution.py:81
  399.5 5.1 all-to-all-start.2
  416.5 7.1 collective-permute-start.29
  425.6 15.1 %hidden_raw.1.raw = f32[1536,1408]{1,0:T(8,128)} custom-call(s32[1]{0:T(128)} %bitcast.71.core.which, bf16[1536,1024]{1,0:T(8,128)(2,1)} %copy-done.2, bf16[1536,1024]{1,0:T(8,128)(2,1)} %collective-permute-done.33.g_other, bf16[4,1408,512]{2,1,0:T(8,128)(2,1)} %all-to-all-done.w_dn.refs_1_), custom_call_target="tpu_custom_call" | custom-call | flops 88583696 | bytes 144179 | tf_op jit(solution)/shard_map/hidden_raw/pallas_call | solution.py:370
  443.0 16.8 %collective-permute-done.28 = bf16[2,96,1024]{2,1,0:T(8,128)(2,1)} collective-permute-done((bf16[2,96,1024]{2,1,0:T(8,128)(2,1)}, bf16[2,96,1024]{2,1,0:T(8,128)(2,1)}, u32[]{:S(2)}, u32[]{:S(2)}) %collective-permute-start.28) | collective-permute-done | bytes 393248 | tf_op jit(solution)/shard_map/ppermute | solution.py:81
  464.9 19.2 %all-to-all-done.2 = bf16[4,512,1408]{2,1,0:T(8,128)(2,1)} async-done(((bf16[4,512,1408]{2,1,0:T(8,128)(2,1)}), bf16[4,512,1408]{2,1,0:T(8,128)(2,1)}, u32[]{:S(2)}, u32[]{:S(2)}) %all-to-all-start.2) | async-done | bytes 5767200 | tf_op jit(solution)/shard_map/all_to_all | solution.py:39
  488.0 13.9 %collective-permute-done.34 = bf16[384,1024]{1,0:T(8,128)(2,1)S(1)} collective-permute-done((bf16[384,1024]{1,0:T(8,128)(2,1)S(1)}, bf16[384,1024]{1,0:T(8,128)(2,1)S(1)}, u32[]{:S(2)}, u32[]{:S(2)}) %collective-permute-start.34) | collective-permute-done | bytes 786464 | tf_op jit(solution)/shard_map/ppermute | solution.py:89
  517.0 32.1 %feed_forward.1 = (bf16[1536,1408]{1,0:T(8,128)(2,1)}, bf16[1536,1408]{1,0:T(8,128)(2,1)}, bf16[1536,1408]{1,0:T(8,128)(2,1)}, bf16[1536,1408]{1,0:T(8,128)(2,1)}, f32[1536,1]{1,0:T(8,128)}) custom-call(s32[2]{0:T(128)} %pad_add_fusion.4.place, bf16[1536,1024]{1,0:T(8,128)(2,1)} %copy-done.1, bf16[1536,1024]{1,0:T(8,128)(2,1)} %collective-permute-done.37.x_other, ...), custom_call_target="tpu_custom_call" | custom-call | flops 221459248 | bytes 374865 | tf_op jit(solution)/shard_map/feed_forward/pallas_call | solution.py:426
  549.1 9.5 rows_half.4
  568.0 14.9 %grad_gateup.2 = bf16[4,512,1408]{2,1,0:T(8,128)(2,1)} custom-call(s32[1]{0:T(128)} %bitcast.71.core.which, bf16[1536,1024]{1,0:T(8,128)(2,1)} %copy-done.1, bf16[1536,1024]{1,0:T(8,128)(2,1)} %collective-permute-done.37.x_other, bf16[1536,1408]{1,0:T(8,128)(2,1)} %get-tuple-element.89.duw.refs_0_), custom_call_target="tpu_custom_call" | custom-call | flops 88583696 | bytes 125829 | tf_op jit(solution)/shard_map/grad_gateup/pallas_call | solution.py:515
  583.2 8.3 collective-permute-start.50
  594.8 10.1 rows_half.5
  605.0 15.2 %rows_half.6 = bf16[1536,1024]{1,0:T(8,128)(2,1)} custom-call(s32[1]{0:T(128)S(6)} %sub.102.which, bf16[1536,1408]{1,0:T(8,128)(2,1)} %get-tuple-element.89.duw.refs_0_, bf16[1536,1408]{1,0:T(8,128)(2,1)} %get-tuple-element.90.refs_1_.duw, bf16[2048,1408]{1,0:T(8,128)(2,1)} %bitcast.60.w_gate.refs_2_, bf16[2048,1408]{1,0:T(8,128)(2,1)} %bitcast.91.w_up.refs_3_), custom_call_target="tpu_custom_call" | custom-call | flops 88583696 | bytes 62914 | tf_op jit(solution)/shard_map/rows_half/pallas_call | solution.py:482
  632.9 15.4 %rows_half.7 = bf16[1536,1024]{1,0:T(8,128)(2,1)} custom-call(s32[1]{0:T(128)} %bitcast.71.core.which, bf16[1536,1408]{1,0:T(8,128)(2,1)} %get-tuple-element.89.duw.refs_0_, bf16[1536,1408]{1,0:T(8,128)(2,1)} %get-tuple-element.90.refs_1_.duw, bf16[2048,1408]{1,0:T(8,128)(2,1)} %bitcast.60.w_gate.refs_2_, bf16[2048,1408]{1,0:T(8,128)(2,1)} %bitcast.91.w_up.refs_3_, ...), custom_call_target="tpu_custom_call" | custom-call | flops 88583696 | bytes 62914 | tf_op jit(solution)/shard_map/rows_half/pallas_call | solution.py:482
  648.3 15.0 %grad_gateup.3 = bf16[4,512,1408]{2,1,0:T(8,128)(2,1)} custom-call(s32[1]{0:T(128)} %bitcast.71.core.which, bf16[1536,1024]{1,0:T(8,128)(2,1)} %copy-done.1, bf16[1536,1024]{1,0:T(8,128)(2,1)} %collective-permute-done.37.x_other, bf16[1536,1408]{1,0:T(8,128)(2,1)} %get-tuple-element.90.refs_1_.duw), custom_call_target="tpu_custom_call" | custom-call | flops 88583696 | bytes 125829 | tf_op jit(solution)/shard_map/grad_gateup/pallas_call | solution.py:515
  684.7 14.2 %grad_down.1 = bf16[4,1408,512]{2,1,0:T(8,128)(2,1)} custom-call(s32[1]{0:T(128)} %bitcast.71.core.which, bf16[1536,1408]{1,0:T(8,128)(2,1)} %get-tuple-element.96.hid, bf16[1536,1024]{1,0:T(8,128)(2,1)} %copy-done.2, bf16[1536,1024]{1,0:T(8,128)(2,1)} %collective-permute-done.33.g_other), custom_call_target="tpu_custom_call" | custom-call | flops 88583696 | bytes 125829 | tf_op jit(solution)/shard_map/grad_down/pallas_call | solution.py:553
  700.4 7.5 collective-permute-done.53
  709.9 5.2 all-to-all-start.3
  725.7 7.4 collective-permute-done.60
  733.1 14.4 %collective-permute-done.58 = bf16[192,1024]{1,0:T(8,128)(2,1)S(1)} collective-permute-done((bf16[192,1024]{1,0:T(8,128)(2,1)S(1)}, bf16[192,1024]{1,0:T(8,128)(2,1)S(1)}, u32[]{:S(2)}, u32[]{:S(2)}) %collective-permute-start.58) | collective-permute-done | bytes 393248 | tf_op jit(solution)/shard_map/ppermute | solution.py:81
  747.5 7.2 collective-permute-done.59
  765.1 8.7 collective-permute-done.64
  781.1 17.0 %collective-permute-done.63 = bf16[2,96,1024]{2,1,0:T(8,128)(2,1)S(1)} collective-permute-done((bf16[2,96,1024]{2,1,0:T(8,128)(2,1)S(1)}, bf16[2,96,1024]{2,1,0:T(8,128)(2,1)S(1)}, u32[]{:S(2)}, u32[]{:S(2)}) %collective-permute-start.63) | collective-permute-done | bytes 393248 | tf_op jit(solution)/shard_map/ppermute | solution.py:81
  803.9 6.8 convolution_convert_fusion.1
  810.8 5.3 all-to-all-start.4
  821.0 9.0 fusion.18
  830.0 14.9 %attention_bwd.4 = (bf16[768,1024]{1,0:T(8,128)(2,1)}, bf16[1,1024,512]{2,1,0:T(8,128)(2,1)}) custom-call(s32[4]{0:T(128)} %and_select_fusion.place, bf16[768,1024]{1,0:T(8,128)(2,1)} %get-tuple-element.101.q_in, bf16[768,1024]{1,0:T(8,128)(2,1)} %bitcast.355, bf16[1,1024,512]{2,1,0:T(8,128)(2,1)} %add_bitcast_fusion.kv, f32[768,128]{1,0:T(8,128)} %pad_maximum_fusion.17.cos, ...), custom_call_target="tpu_custom_call" | custom-call | flops 120795952 | bytes 31457 | tf_op jit(solution)/shard_map/attention_bwd/pallas_call | solution.py:332
  844.9 14.7 %attention_bwd.5 = (bf16[768,1024]{1,0:T(8,128)(2,1)}, bf16[1,1024,512]{2,1,0:T(8,128)(2,1)}) custom-call(s32[4]{0:T(128)} %and_select_fusion.place, bf16[768,1024]{1,0:T(8,128)(2,1)} %get-tuple-element.101.q_in, bf16[768,1024]{1,0:T(8,128)(2,1)} %bitcast.356, bf16[1,1024,512]{2,1,0:T(8,128)(2,1)} %bitcast.375, ...), custom_call_target="tpu_custom_call", output_to_operand_aliasing={{0}: (11, {})} | custom-call | flops 120795952 | bytes 31457 | tf_op jit(solution)/shard_map/attention_bwd/pallas_call | solution.py:332
  859.6 14.7 %attention_bwd.6 = (bf16[768,1024]{1,0:T(8,128)(2,1)}, bf16[1,1024,512]{2,1,0:T(8,128)(2,1)}) custom-call(s32[4]{0:T(128)} %and_select_fusion.place, bf16[768,1024]{1,0:T(8,128)(2,1)} %get-tuple-element.101.q_in, bf16[768,1024]{1,0:T(8,128)(2,1)} %bitcast.357, bf16[1,1024,512]{2,1,0:T(8,128)(2,1)} %bitcast.377, ...), custom_call_target="tpu_custom_call", output_to_operand_aliasing={{0}: (11, {})} | custom-call | flops 120795952 | bytes 31457 | tf_op jit(solution)/shard_map/attention_bwd/pallas_call | solution.py:332
  874.3 14.8 %attention_bwd.7 = (bf16[768,1024]{1,0:T(8,128)(2,1)}, bf16[1,1024,512]{2,1,0:T(8,128)(2,1)}) custom-call(s32[4]{0:T(128)} %and_select_fusion.place, bf16[768,1024]{1,0:T(8,128)(2,1)} %get-tuple-element.101.q_in, bf16[768,1024]{1,0:T(8,128)(2,1)} %bitcast.358, bf16[1,1024,512]{2,1,0:T(8,128)(2,1)} %bitcast.373, ...), custom_call_target="tpu_custom_call", output_to_operand_aliasing={{0}: (11, {})} | custom-call | flops 120795952 | bytes 31457 | tf_op jit(solution)/shard_map/attention_bwd/pallas_call | solution.py:332
  889.2 36.6 %all-to-all-done.4 = bf16[4,512,1408]{2,1,0:T(8,128)(2,1)} async-done(((bf16[4,512,1408]{2,1,0:T(8,128)(2,1)}), bf16[4,512,1408]{2,1,0:T(8,128)(2,1)}, u32[]{:S(2)}, u32[]{:S(2)}) %all-to-all-start.4) | async-done | bytes 5767200 | tf_op jit(solution)/shard_map/all_to_all | solution.py:39
  925.8 10.7 convolution_convert_fusion
  936.6 5.3 all-to-all-start.5
  945.6 19.2 %collective-permute-done.68 = bf16[1024,512]{1,0:T(8,128)(2,1)} collective-permute-done((bf16[1024,512]{1,0:T(8,128)(2,1)}, bf16[1024,512]{1,0:T(8,128)(2,1)}, u32[]{:S(2)}, u32[]{:S(2)}) %collective-permute-start.68) | collective-permute-done | bytes 1048608 | tf_op jit(solution)/shard_map/ppermute | solution.py:81
  971.6 28.4 %reduce-scatter.3.cloned.1.call-done = bf16[2,1024,512]{2,1,0:T(8,128)(2,1)} async-done(((bf16[2,1024,2048]{2,1,0:T(8,128)(2,1)}), bf16[2,1024,512]{2,1,0:T(8,128)(2,1)}) %reduce-scatter.3.cloned.1.call-update) | async-done | bytes 2097168 | tf_op jit(solution)/shard_map/reduce_scatter | solution.py:864
  1015.5 5.3 fusion.22
  1043.4 7.4 unpack_down.1
  1050.8 14.2 %unpack_gateup.1 = f32[2,512,2,2816]{3,2,1,0:T(2,128)} custom-call(bf16[2,2,512,1408]{3,2,1,0:T(8,128)(2,1)} %bitcast.156.gate, bf16[2,2,512,1408]{3,2,1,0:T(8,128)(2,1)} %bitcast.157.up), custom_call_target="tpu_custom_call" | custom-call | bytes 346030 | tf_op jit(solution)/shard_map/unpack_gateup/pallas_call | solution.py:159
  1065.0 12.9 %all-to-all-done.6 = bf16[4,512,512]{2,1,0:T(8,128)(2,1)} async-done(((bf16[4,512,512]{2,1,0:T(8,128)(2,1)}), bf16[4,512,512]{2,1,0:T(8,128)(2,1)}, u32[]{:S(2)}, u32[]{:S(2)}) %all-to-all-start.6) | async-done | bytes 2097184 | tf_op jit(solution)/shard_map/all_to_all | solution.py:39
  1081.1 4.9 all-to-all-start.7
  1095.4 24.9 %reduce-scatter.5.cloned.1.call-done = bf16[2,512,1024]{2,1,0:T(8,128)(2,1)} async-done(((bf16[2,2048,1024]{2,1,0:T(8,128)(2,1)}), bf16[2,512,1024]{2,1,0:T(8,128)(2,1)}) %reduce-scatter.5.cloned.1.call-update) | async-done | bytes 2097168 | tf_op jit(solution)/shard_map/reduce_scatter | solution.py:886
  (577 shorter events, 323.6 us)
Async XLA Ops:
  7.2 105.3 %all-gather.6.cloned.1.call-start = ((), (), s32[]{:S(2)}) async-start(), calls=%async_computation.11 | async-start | bytes 2621440 | tf_op jit(solution)/shard_map/all_gather | solution.py:631
  26.5 232.0 %all-gather.4.cloned.1.call-start = ((), (), s32[]{:S(2)}) async-start(), calls=%async_computation.10 | async-start | bytes 10485760 | tf_op jit(solution)/shard_map/all_gather | solution.py:634
  30.4 317.4 %all-gather.8.cloned.1.call-start = ((), (), s32[]{:S(2)}) async-start(), calls=%async_computation.12 | async-start | bytes 10485760 | tf_op jit(solution)/shard_map/all_gather | solution.py:637
  35.3 37.6 %collective-permute-start.2 = (bf16[256,1024]{1,0:T(8,128)(2,1)S(1)}, bf16[256,1024]{1,0:T(8,128)(2,1)S(1)}, u32[]{:S(2)}, u32[]{:S(2)}) collective-permute-start(bf16[256,1024]{1,0:T(8,128)(2,1)S(1)} %copy-done.26), channel_id=1, source_target_pairs={{0,2},{2,4},{4,6},{6,0},{1,3},{3,5},{5,7},{7,1},{8,10},{10,12},{12... | collective-permute-start | bytes 1572872 | tf_op jit(solution)/shard_map/ppermute | solution.py:62
  36.0 37.0 %collective-permute-start = (bf16[256,1024]{1,0:T(8,128)(2,1)S(1)}, bf16[256,1024]{1,0:T(8,128)(2,1)S(1)}, u32[]{:S(2)}, u32[]{:S(2)}) collective-permute-start(bf16[256,1024]{1,0:T(8,128)(2,1)S(1)} %copy-done.26), channel_id=1, source_target_pairs={{0,6},{2,0},{4,2},{6,4},{1,7},{3,1},{5,3},{7,5},{8,14},{10,8},{12,... | collective-permute-start | bytes 1572872 | tf_op jit(solution)/shard_map/ppermute | solution.py:62
  39.2 44.9 %collective-permute-start.1 = (bf16[256,1024]{1,0:T(8,128)(2,1)S(1)}, bf16[256,1024]{1,0:T(8,128)(2,1)S(1)}, u32[]{:S(2)}, u32[]{:S(2)}) collective-permute-start(bf16[256,1024]{1,0:T(8,128)(2,1)S(1)} %copy-done.26), channel_id=1, source_target_pairs={{0,4},{2,6},{4,0},{6,2},{1,5},{3,7},{5,1},{7,3},{8,12},{10,14},{12... | collective-permute-start | bytes 1572872 | tf_op jit(solution)/shard_map/ppermute | solution.py:62
  84.9 92.1 %all-to-all-start = ((bf16[4,1408,512]{2,1,0:T(8,128)(2,1)}), bf16[4,1408,512]{2,1,0:T(8,128)(2,1)}, u32[]{:S(2)}, u32[]{:S(2)}) async-start(bf16[4,1408,512]{2,1,0:T(8,128)(2,1)} %bitcast.359), calls=%async_computation | async-start | bytes 11534336 | tf_op jit(solution)/shard_map/all_to_all | solution.py:39
  95.4 37.3 %collective-permute-start.6 = (s32[8,256]{1,0:T(8,128)S(1)}, s32[8,256]{1,0:T(8,128)S(1)}, u32[]{:S(2)}, u32[]{:S(2)}) collective-permute-start(s32[8,256]{1,0:T(8,128)S(1)} %get-tuple-element.261), channel_id=1, source_target_pairs={{0,6},{2,0},{4,2},{6,4},{1,7},{3,1},{5,3},{7,5},{8,14},{10,8},{12,... | collective-permute-start | bytes 24584 | tf_op jit(solution)/shard_map/ppermute | solution.py:62
  97.0 35.8 %collective-permute-start.7 = (s32[8,256]{1,0:T(8,128)S(1)}, s32[8,256]{1,0:T(8,128)S(1)}, u32[]{:S(2)}, u32[]{:S(2)}) collective-permute-start(s32[8,256]{1,0:T(8,128)S(1)} %get-tuple-element.261), channel_id=1, source_target_pairs={{0,4},{2,6},{4,0},{6,2},{1,5},{3,7},{5,1},{7,3},{8,12},{10,14},{12... | collective-permute-start | bytes 24584 | tf_op jit(solution)/shard_map/ppermute | solution.py:62
  97.0 35.8 %collective-permute-start.8 = (s32[8,256]{1,0:T(8,128)S(1)}, s32[8,256]{1,0:T(8,128)S(1)}, u32[]{:S(2)}, u32[]{:S(2)}) collective-permute-start(s32[8,256]{1,0:T(8,128)S(1)} %get-tuple-element.261), channel_id=1, source_target_pairs={{0,2},{2,4},{4,6},{6,0},{1,3},{3,5},{5,7},{7,1},{8,10},{10,12},{12... | collective-permute-start | bytes 24584 | tf_op jit(solution)/shard_map/ppermute | solution.py:62
  124.3 26.6 %collective-permute-start.15 = (bf16[1024,512]{1,0:T(8,128)(2,1)S(1)}, bf16[1024,512]{1,0:T(8,128)(2,1)S(1)}, u32[]{:S(2)}, u32[]{:S(2)}) collective-permute-start(bf16[1024,512]{1,0:T(8,128)(2,1)S(1)} %bitcast.370), channel_id=1, source_target_pairs={{0,2},{2,4},{4,6},{1,3},{3,5},{5,7},{8,10},{10,12},{12,14},{9,11},... | collective-permute-start | bytes 3145736 | tf_op jit(solution)/shard_map/ppermute | solution.py:73
  129.1 27.2 %collective-permute-start.12 = (bf16[1024,512]{1,0:T(8,128)(2,1)S(1)}, bf16[1024,512]{1,0:T(8,128)(2,1)}, u32[]{:S(2)}, u32[]{:S(2)}) collective-permute-start(bf16[1024,512]{1,0:T(8,128)(2,1)S(1)} %bitcast.371), channel_id=1, source_target_pairs={{2,0},{4,2},{6,4},{3,1},{5,3},{7,5},{10,8},{12,10},{14,12},{11,9},... | collective-permute-start | bytes 3145736 | tf_op jit(solution)/shard_map/ppermute | solution.py:74
  150.9 32.8 %collective-permute-start.16 = (bf16[1024,512]{1,0:T(8,128)(2,1)S(1)}, bf16[1024,512]{1,0:T(8,128)(2,1)}, u32[]{:S(2)}, u32[]{:S(2)}) collective-permute-start(bf16[1024,512]{1,0:T(8,128)(2,1)S(1)} %collective-permute-done.15), channel_id=1, source_target_pairs={{0,2},{2,4},{4,6},{1,3},{3,5},{5,7},{8,10},{10,12},{12,14},{9,11},... | collective-permute-start | bytes 3145736 | tf_op jit(solution)/shard_map/ppermute | solution.py:73
  156.3 31.8 %collective-permute-start.13 = (bf16[1024,512]{1,0:T(8,128)(2,1)}, bf16[1024,512]{1,0:T(8,128)(2,1)}, u32[]{:S(2)}, u32[]{:S(2)}) collective-permute-start(bf16[1024,512]{1,0:T(8,128)(2,1)} %collective-permute-done.12), channel_id=1, source_target_pairs={{2,0},{4,2},{6,4},{3,1},{5,3},{7,5},{10,8},{12,10},{14,12},{11,9},... | collective-permute-start | bytes 3145736 | tf_op jit(solution)/shard_map/ppermute | solution.py:74
  177.0 125.5 %all-to-all-start.1 = ((bf16[4,512,1408]{2,1,0:T(8,128)(2,1)}), bf16[4,512,1408]{2,1,0:T(8,128)(2,1)}, u32[]{:S(2)}, u32[]{:S(2)}) async-start(bf16[4,512,1408]{2,1,0:T(8,128)(2,1)} %bitcast.387), calls=%async_computation.1 | async-start | bytes 11534336 | tf_op jit(solution)/shard_map/all_to_all | solution.py:39
  183.7 25.8 %collective-permute-start.17 = (bf16[1024,512]{1,0:T(8,128)(2,1)}, bf16[1024,512]{1,0:T(8,128)(2,1)}, u32[]{:S(2)}, u32[]{:S(2)}) collective-permute-start(bf16[1024,512]{1,0:T(8,128)(2,1)} %collective-permute-done.16), channel_id=1, source_target_pairs={{0,2},{2,4},{4,6},{1,3},{3,5},{5,7},{8,10},{10,12},{12,14},{9,11},... | collective-permute-start | bytes 3145736 | tf_op jit(solution)/shard_map/ppermute | solution.py:73
  188.1 26.5 %collective-permute-start.14 = (bf16[1024,512]{1,0:T(8,128)(2,1)}, bf16[1024,512]{1,0:T(8,128)(2,1)}, u32[]{:S(2)}, u32[]{:S(2)}) collective-permute-start(bf16[1024,512]{1,0:T(8,128)(2,1)} %collective-permute-done.13), channel_id=1, source_target_pairs={{2,0},{4,2},{6,4},{3,1},{5,3},{7,5},{10,8},{12,10},{14,12},{11,9},... | collective-permute-start | bytes 3145736 | tf_op jit(solution)/shard_map/ppermute | solution.py:74
  218.6 18.7 %collective-permute-start.18 = (bf16[2,96,1024]{2,1,0:T(8,128)(2,1)S(1)}, bf16[2,96,1024]{2,1,0:T(8,128)(2,1)}, u32[]{:S(2)}, u32[]{:S(2)}) collective-permute-start(bf16[2,96,1024]{2,1,0:T(8,128)(2,1)S(1)} %bitcast.417), channel_id=1, source_target_pairs={{0,6},{2,0},{4,2},{6,4},{1,7},{3,1},{5,3},{7,5},{8,14},{10,8},{12,... | collective-permute-start | bytes 1179656 | tf_op jit(solution)/shard_map/ppermute | solution.py:81
  220.6 32.8 %collective-permute-start.19 = (bf16[2,96,1024]{2,1,0:T(8,128)(2,1)S(1)}, bf16[2,96,1024]{2,1,0:T(8,128)(2,1)}, u32[]{:S(2)}, u32[]{:S(2)}) collective-permute-start(bf16[2,96,1024]{2,1,0:T(8,128)(2,1)S(1)} %bitcast.413), channel_id=1, source_target_pairs={{0,4},{2,6},{4,0},{6,2},{1,5},{3,7},{5,1},{7,3},{8,12},{10,14},{12... | collective-permute-start | bytes 1179656 | tf_op jit(solution)/shard_map/ppermute | solution.py:81
  220.6 32.8 %collective-permute-start.20 = (bf16[2,96,1024]{2,1,0:T(8,128)(2,1)S(1)}, bf16[2,96,1024]{2,1,0:T(8,128)(2,1)}, u32[]{:S(2)}, u32[]{:S(2)}) collective-permute-start(bf16[2,96,1024]{2,1,0:T(8,128)(2,1)S(1)} %bitcast.410), channel_id=1, source_target_pairs={{0,2},{2,4},{4,6},{6,0},{1,3},{3,5},{5,7},{7,1},{8,10},{10,12},{12... | collective-permute-start | bytes 1179656 | tf_op jit(solution)/shard_map/ppermute | solution.py:81
  356.0 21.5 %collective-permute-start.32 = (bf16[384,1024]{1,0:T(8,128)(2,1)}, bf16[384,1024]{1,0:T(8,128)(2,1)S(1)}, u32[]{:S(2)}, u32[]{:S(2)}) collective-permute-start(bf16[384,1024]{1,0:T(8,128)(2,1)} %bitcast.86), channel_id=1, source_target_pairs={{0,24},{8,16},{16,8},{24,0},{1,25},{9,17},{17,9},{25,1},{2,26},{10... | collective-permute-start | bytes 2359304 | tf_op jit(solution)/shard_map/ppermute | solution.py:89
  357.4 38.7 %collective-permute-start.30 = (bf16[384,1024]{1,0:T(8,128)(2,1)}, bf16[384,1024]{1,0:T(8,128)(2,1)S(1)}, u32[]{:S(2)}, u32[]{:S(2)}) collective-permute-start(bf16[384,1024]{1,0:T(8,128)(2,1)} %bitcast.86), channel_id=1, source_target_pairs={{0,8},{8,0},{16,24},{24,16},{1,9},{9,1},{17,25},{25,17},{2,10},{10... | collective-permute-start | bytes 2359304 | tf_op jit(solution)/shard_map/ppermute | solution.py:89
  358.9 37.3 %collective-permute-start.31 = (bf16[384,1024]{1,0:T(8,128)(2,1)S(1)}, bf16[384,1024]{1,0:T(8,128)(2,1)S(1)}, u32[]{:S(2)}, u32[]{:S(2)}) collective-permute-start(bf16[384,1024]{1,0:T(8,128)(2,1)S(1)} %bitcast.395), channel_id=1, source_target_pairs={{0,16},{8,24},{16,0},{24,8},{1,17},{9,25},{17,1},{25,9},{2,18},{10... | collective-permute-start | bytes 2359304 | tf_op jit(solution)/shard_map/ppermute | solution.py:89
  366.3 28.0 %collective-permute-start.23 = (bf16[192,1024]{1,0:T(8,128)(2,1)S(1)}, bf16[192,1024]{1,0:T(8,128)(2,1)S(1)}, u32[]{:S(2)}, u32[]{:S(2)}) collective-permute-start(bf16[192,1024]{1,0:T(8,128)(2,1)S(1)} %bitcast.418), channel_id=1, source_target_pairs={{0,4},{2,6},{4,0},{6,2},{1,5},{3,7},{5,1},{7,3},{8,12},{10,14},{12... | collective-permute-start | bytes 1179656 | tf_op jit(solution)/shard_map/ppermute | solution.py:81
  377.4 18.7 %collective-permute-start.24 = (bf16[192,1024]{1,0:T(8,128)(2,1)S(1)}, bf16[192,1024]{1,0:T(8,128)(2,1)S(1)}, u32[]{:S(2)}, u32[]{:S(2)}) collective-permute-start(bf16[192,1024]{1,0:T(8,128)(2,1)S(1)} %bitcast.414), channel_id=1, source_target_pairs={{0,6},{2,0},{4,2},{6,4},{1,7},{3,1},{5,3},{7,5},{8,14},{10,8},{12,... | collective-permute-start | bytes 1179656 | tf_op jit(solution)/shard_map/ppermute | solution.py:81
  397.8 27.8 %collective-permute-start.33 = (bf16[1536,1024]{1,0:T(8,128)(2,1)S(1)}, bf16[1536,1024]{1,0:T(8,128)(2,1)}, u32[]{:S(2)}, u32[]{:S(2)}) collective-permute-start(bf16[1536,1024]{1,0:T(8,128)(2,1)S(1)} %pad_maximum_fusion.1.g_own), channel_id=1, source_target_pairs={{0,1},{1,0},{2,3},{3,2},{4,5},{5,4},{6,7},{7,6},{8,9},{9,8},{10,11... | collective-permute-start | bytes 9437192 | tf_op jit(solution)/shard_map/ppermute | solution.py:35
  399.5 84.6 %all-to-all-start.2 = ((bf16[4,512,1408]{2,1,0:T(8,128)(2,1)}), bf16[4,512,1408]{2,1,0:T(8,128)(2,1)}, u32[]{:S(2)}, u32[]{:S(2)}) async-start(bf16[4,512,1408]{2,1,0:T(8,128)(2,1)} %bitcast.386), calls=%async_computation.2 | async-start | bytes 11534336 | tf_op jit(solution)/shard_map/all_to_all | solution.py:39
  416.5 24.3 %collective-permute-start.29 = (bf16[2,96,1024]{2,1,0:T(8,128)(2,1)}, bf16[2,96,1024]{2,1,0:T(8,128)(2,1)}, u32[]{:S(2)}, u32[]{:S(2)}) collective-permute-start(bf16[2,96,1024]{2,1,0:T(8,128)(2,1)} %bitcast.79), channel_id=1, source_target_pairs={{0,2},{2,4},{4,6},{6,0},{1,3},{3,5},{5,7},{7,1},{8,10},{10,12},{12... | collective-permute-start | bytes 1179656 | tf_op jit(solution)/shard_map/ppermute | solution.py:81
  423.6 19.4 %collective-permute-start.27 = (bf16[2,96,1024]{2,1,0:T(8,128)(2,1)}, bf16[2,96,1024]{2,1,0:T(8,128)(2,1)}, u32[]{:S(2)}, u32[]{:S(2)}) collective-permute-start(bf16[2,96,1024]{2,1,0:T(8,128)(2,1)} %bitcast.75), channel_id=1, source_target_pairs={{0,6},{2,0},{4,2},{6,4},{1,7},{3,1},{5,3},{7,5},{8,14},{10,8},{12,... | collective-permute-start | bytes 1179656 | tf_op jit(solution)/shard_map/ppermute | solution.py:81
  425.1 34.7 %collective-permute-start.28 = (bf16[2,96,1024]{2,1,0:T(8,128)(2,1)}, bf16[2,96,1024]{2,1,0:T(8,128)(2,1)}, u32[]{:S(2)}, u32[]{:S(2)}) collective-permute-start(bf16[2,96,1024]{2,1,0:T(8,128)(2,1)} %bitcast.77), channel_id=1, source_target_pairs={{0,4},{2,6},{4,0},{6,2},{1,5},{3,7},{5,1},{7,3},{8,12},{10,14},{12... | collective-permute-start | bytes 1179656 | tf_op jit(solution)/shard_map/ppermute | solution.py:81
  461.4 26.6 %collective-permute-start.36 = (bf16[384,1024]{1,0:T(8,128)(2,1)S(1)}, bf16[384,1024]{1,0:T(8,128)(2,1)S(1)}, u32[]{:S(2)}, u32[]{:S(2)}) collective-permute-start(bf16[384,1024]{1,0:T(8,128)(2,1)S(1)} %bitcast.407), channel_id=1, source_target_pairs={{0,24},{8,16},{16,8},{24,0},{1,25},{9,17},{17,9},{25,1},{2,26},{10... | collective-permute-start | bytes 2359304 | tf_op jit(solution)/shard_map/ppermute | solution.py:89
  464.3 37.6 %collective-permute-start.34 = (bf16[384,1024]{1,0:T(8,128)(2,1)S(1)}, bf16[384,1024]{1,0:T(8,128)(2,1)S(1)}, u32[]{:S(2)}, u32[]{:S(2)}) collective-permute-start(bf16[384,1024]{1,0:T(8,128)(2,1)S(1)} %bitcast.408), channel_id=1, source_target_pairs={{0,8},{8,0},{16,24},{24,16},{1,9},{9,1},{17,25},{25,17},{2,10},{10... | collective-permute-start | bytes 2359304 | tf_op jit(solution)/shard_map/ppermute | solution.py:89
  464.9 37.9 %collective-permute-start.35 = (bf16[384,1024]{1,0:T(8,128)(2,1)S(1)}, bf16[384,1024]{1,0:T(8,128)(2,1)}, u32[]{:S(2)}, u32[]{:S(2)}) collective-permute-start(bf16[384,1024]{1,0:T(8,128)(2,1)S(1)} %bitcast.398), channel_id=1, source_target_pairs={{0,16},{8,24},{16,0},{24,8},{1,17},{9,25},{17,1},{25,9},{2,18},{10... | collective-permute-start | bytes 2359304 | tf_op jit(solution)/shard_map/ppermute | solution.py:89
  558.6 34.6 %collective-permute-start.44 = (bf16[1536,1024]{1,0:T(8,128)(2,1)}, bf16[1536,1024]{1,0:T(8,128)(2,1)S(1)}, u32[]{:S(2)}, u32[]{:S(2)}) collective-permute-start(bf16[1536,1024]{1,0:T(8,128)(2,1)} %rows_half.4), channel_id=1, source_target_pairs={{0,1},{1,0},{2,3},{3,2},{4,5},{5,4},{6,7},{7,6},{8,9},{9,8},{10,11... | collective-permute-start | bytes 9437192 | tf_op jit(solution)/shard_map/ppermute | solution.py:35
  564.4 18.7 %collective-permute-start.41 = (f32[4,96]{1,0:T(4,128)S(1)}, f32[4,96]{1,0:T(4,128)S(1)}, u32[]{:S(2)}, u32[]{:S(2)}) collective-permute-start(f32[4,96]{1,0:T(4,128)S(1)} %unstack.194), channel_id=1, source_target_pairs={{0,8},{8,0},{16,24},{24,16},{1,9},{9,1},{17,25},{25,17},{2,10},{10... | collective-permute-start | bytes 4616 | tf_op jit(solution)/shard_map/ppermute | solution.py:89
  565.5 17.6 %collective-permute-start.42 = (f32[4,96]{1,0:T(4,128)S(1)}, f32[4,96]{1,0:T(4,128)S(1)}, u32[]{:S(2)}, u32[]{:S(2)}) collective-permute-start(f32[4,96]{1,0:T(4,128)S(1)} %unstack.196), channel_id=1, source_target_pairs={{0,16},{8,24},{16,0},{24,8},{1,17},{9,25},{17,1},{25,9},{2,18},{10... | collective-permute-start | bytes 4616 | tf_op jit(solution)/shard_map/ppermute | solution.py:89
  583.2 21.7 %collective-permute-start.50 = (f32[192]{0:T(256)S(1)}, f32[192]{0:T(256)S(1)}, u32[]{:S(2)}, u32[]{:S(2)}) collective-permute-start(f32[192]{0:T(256)S(1)} %pad_maximum_fusion.29), channel_id=1, source_target_pairs={{0,6},{2,0},{4,2},{6,4},{1,7},{3,1},{5,3},{7,5},{8,14},{10,8},{12,... | collective-permute-start | bytes 2312 | tf_op jit(solution)/shard_map/ppermute | solution.py:81
  629.0 34.4 %collective-permute-start.45 = (bf16[4,96,1024]{2,1,0:T(8,128)(2,1)}, bf16[4,96,1024]{2,1,0:T(8,128)(2,1)S(1)}, u32[]{:S(2)}, u32[]{:S(2)}) collective-permute-start(bf16[4,96,1024]{2,1,0:T(8,128)(2,1)} %bitcast.95), channel_id=1, source_target_pairs={{0,8},{8,0},{16,24},{24,16},{1,9},{9,1},{17,25},{25,17},{2,10},{10... | collective-permute-start | bytes 2359304 | tf_op jit(solution)/shard_map/ppermute | solution.py:89
  630.0 35.5 %collective-permute-start.46 = (bf16[4,96,1024]{2,1,0:T(8,128)(2,1)}, bf16[4,96,1024]{2,1,0:T(8,128)(2,1)}, u32[]{:S(2)}, u32[]{:S(2)}) collective-permute-start(bf16[4,96,1024]{2,1,0:T(8,128)(2,1)} %bitcast.96), channel_id=1, source_target_pairs={{0,16},{8,24},{16,0},{24,8},{1,17},{9,25},{17,1},{25,9},{2,18},{10... | collective-permute-start | bytes 2359304 | tf_op jit(solution)/shard_map/ppermute | solution.py:89
  631.5 35.2 %collective-permute-start.47 = (bf16[4,96,1024]{2,1,0:T(8,128)(2,1)}, bf16[4,96,1024]{2,1,0:T(8,128)(2,1)}, u32[]{:S(2)}, u32[]{:S(2)}) collective-permute-start(bf16[4,96,1024]{2,1,0:T(8,128)(2,1)} %bitcast.97), channel_id=1, source_target_pairs={{0,24},{8,16},{16,8},{24,0},{1,25},{9,17},{17,9},{25,1},{2,26},{10... | collective-permute-start | bytes 2359304 | tf_op jit(solution)/shard_map/ppermute | solution.py:89
  673.6 34.3 %collective-permute-start.55 = (bf16[4,96,1024]{2,1,0:T(8,128)(2,1)}, bf16[4,96,1024]{2,1,0:T(8,128)(2,1)}, u32[]{:S(2)}, u32[]{:S(2)}) collective-permute-start(bf16[4,96,1024]{2,1,0:T(8,128)(2,1)} %bitcast.114), channel_id=1, source_target_pairs={{0,8},{8,0},{16,24},{24,16},{1,9},{9,1},{17,25},{25,17},{2,10},{10... | collective-permute-start | bytes 2359304 | tf_op jit(solution)/shard_map/ppermute | solution.py:89
  674.6 35.4 %collective-permute-start.56 = (bf16[4,96,1024]{2,1,0:T(8,128)(2,1)}, bf16[4,96,1024]{2,1,0:T(8,128)(2,1)}, u32[]{:S(2)}, u32[]{:S(2)}) collective-permute-start(bf16[4,96,1024]{2,1,0:T(8,128)(2,1)} %bitcast.115), channel_id=1, source_target_pairs={{0,16},{8,24},{16,0},{24,8},{1,17},{9,25},{17,1},{25,9},{2,18},{10... | collective-permute-start | bytes 2359304 | tf_op jit(solution)/shard_map/ppermute | solution.py:89
  675.9 34.0 %collective-permute-start.57 = (bf16[4,96,1024]{2,1,0:T(8,128)(2,1)}, bf16[4,96,1024]{2,1,0:T(8,128)(2,1)}, u32[]{:S(2)}, u32[]{:S(2)}) collective-permute-start(bf16[4,96,1024]{2,1,0:T(8,128)(2,1)} %bitcast.116), channel_id=1, source_target_pairs={{0,24},{8,16},{16,8},{24,0},{1,25},{9,17},{17,9},{25,1},{2,26},{10... | collective-permute-start | bytes 2359304 | tf_op jit(solution)/shard_map/ppermute | solution.py:89
  677.8 22.5 %collective-permute-start.54 = (bf16[192,1024]{1,0:T(8,128)(2,1)}, bf16[192,1024]{1,0:T(8,128)(2,1)}, u32[]{:S(2)}, u32[]{:S(2)}) collective-permute-start(bf16[192,1024]{1,0:T(8,128)(2,1)} %pad_maximum_fusion.21), channel_id=1, source_target_pairs={{0,6},{2,0},{4,2},{6,4},{1,7},{3,1},{5,3},{7,5},{8,14},{10,8},{12,... | collective-permute-start | bytes 1179656 | tf_op jit(solution)/shard_map/ppermute | solution.py:81
  684.0 23.8 %collective-permute-start.53 = (bf16[192,1024]{1,0:T(8,128)(2,1)}, bf16[192,1024]{1,0:T(8,128)(2,1)S(1)}, u32[]{:S(2)}, u32[]{:S(2)}) collective-permute-start(bf16[192,1024]{1,0:T(8,128)(2,1)} %pad_maximum_fusion.20), channel_id=1, source_target_pairs={{0,4},{2,6},{4,0},{6,2},{1,5},{3,7},{5,1},{7,3},{8,12},{10,14},{12... | collective-permute-start | bytes 1179656 | tf_op jit(solution)/shard_map/ppermute | solution.py:81
  709.9 67.4 %all-to-all-start.3 = ((bf16[4,512,1408]{2,1,0:T(8,128)(2,1)}), bf16[4,512,1408]{2,1,0:T(8,128)(2,1)}, u32[]{:S(2)}, u32[]{:S(2)}) async-start(bf16[4,512,1408]{2,1,0:T(8,128)(2,1)} %grad_gateup.2), calls=%async_computation.3 | async-start | bytes 11534336 | tf_op jit(solution)/shard_map/all_to_all | solution.py:39
  715.1 284.9 %reduce-scatter.3.cloned.1.call-start = ((), (), s32[]{:S(2)}) async-start(), calls=%async_computation.13 | async-start | bytes 10485760 | tf_op jit(solution)/shard_map/reduce_scatter | solution.py:864
  723.6 31.2 %collective-permute-start.59 = (bf16[192,1024]{1,0:T(8,128)(2,1)S(1)}, bf16[192,1024]{1,0:T(8,128)(2,1)S(1)}, u32[]{:S(2)}, u32[]{:S(2)}) collective-permute-start(bf16[192,1024]{1,0:T(8,128)(2,1)S(1)} %pad_maximum_fusion.23), channel_id=1, source_target_pairs={{0,4},{2,6},{4,0},{6,2},{1,5},{3,7},{5,1},{7,3},{8,12},{10,14},{12... | collective-permute-start | bytes 1179656 | tf_op jit(solution)/shard_map/ppermute | solution.py:81
  723.7 23.8 %collective-permute-start.58 = (bf16[192,1024]{1,0:T(8,128)(2,1)S(1)}, bf16[192,1024]{1,0:T(8,128)(2,1)S(1)}, u32[]{:S(2)}, u32[]{:S(2)}) collective-permute-start(bf16[192,1024]{1,0:T(8,128)(2,1)S(1)} %pad_maximum_fusion.22), channel_id=1, source_target_pairs={{0,2},{2,4},{4,6},{6,0},{1,3},{3,5},{5,7},{7,1},{8,10},{10,12},{12... | collective-permute-start | bytes 1179656 | tf_op jit(solution)/shard_map/ppermute | solution.py:81
  761.2 19.9 %collective-permute-start.62 = (bf16[2,96,1024]{2,1,0:T(8,128)(2,1)S(1)}, bf16[2,96,1024]{2,1,0:T(8,128)(2,1)S(1)}, u32[]{:S(2)}, u32[]{:S(2)}) collective-permute-start(bf16[2,96,1024]{2,1,0:T(8,128)(2,1)S(1)} %bitcast.415), channel_id=1, source_target_pairs={{0,6},{2,0},{4,2},{6,4},{1,7},{3,1},{5,3},{7,5},{8,14},{10,8},{12,... | collective-permute-start | bytes 1179656 | tf_op jit(solution)/shard_map/ppermute | solution.py:81
  763.8 34.3 %collective-permute-start.63 = (bf16[2,96,1024]{2,1,0:T(8,128)(2,1)S(1)}, bf16[2,96,1024]{2,1,0:T(8,128)(2,1)S(1)}, u32[]{:S(2)}, u32[]{:S(2)}) collective-permute-start(bf16[2,96,1024]{2,1,0:T(8,128)(2,1)S(1)} %bitcast.411), channel_id=1, source_target_pairs={{0,4},{2,6},{4,0},{6,2},{1,5},{3,7},{5,1},{7,3},{8,12},{10,14},{12... | collective-permute-start | bytes 1179656 | tf_op jit(solution)/shard_map/ppermute | solution.py:81
  810.8 115.0 %all-to-all-start.4 = ((bf16[4,512,1408]{2,1,0:T(8,128)(2,1)}), bf16[4,512,1408]{2,1,0:T(8,128)(2,1)}, u32[]{:S(2)}, u32[]{:S(2)}) async-start(bf16[4,512,1408]{2,1,0:T(8,128)(2,1)} %grad_gateup.3), calls=%async_computation.4 | async-start | bytes 11534336 | tf_op jit(solution)/shard_map/all_to_all | solution.py:39
  816.1 304.2 %reduce-scatter.5.cloned.1.call-start = ((), (), s32[]{:S(2)}) async-start(), calls=%async_computation.14 | async-start | bytes 10485760 | tf_op jit(solution)/shard_map/reduce_scatter | solution.py:886
  844.9 80.9 %collective-permute-start.67 = (bf16[1024,512]{1,0:T(8,128)(2,1)}, bf16[1024,512]{1,0:T(8,128)(2,1)S(1)}, u32[]{:S(2)}, u32[]{:S(2)}) collective-permute-start(bf16[1024,512]{1,0:T(8,128)(2,1)} %bitcast.477), channel_id=1, source_target_pairs={{0,4},{2,6},{4,0},{6,2},{1,5},{3,7},{5,1},{7,3},{8,12},{10,14},{12... | collective-permute-start | bytes 3145736 | tf_op jit(solution)/shard_map/ppermute | solution.py:81
  936.5 28.3 %collective-permute-start.68 = (bf16[1024,512]{1,0:T(8,128)(2,1)}, bf16[1024,512]{1,0:T(8,128)(2,1)}, u32[]{:S(2)}, u32[]{:S(2)}) collective-permute-start(bf16[1024,512]{1,0:T(8,128)(2,1)} %bitcast.476), channel_id=1, source_target_pairs={{0,2},{2,4},{4,6},{6,0},{1,3},{3,5},{5,7},{7,1},{8,10},{10,12},{12... | collective-permute-start | bytes 3145736 | tf_op jit(solution)/shard_map/ppermute | solution.py:81
  936.6 88.4 %all-to-all-start.5 = ((bf16[4,1408,512]{2,1,0:T(8,128)(2,1)}), bf16[4,1408,512]{2,1,0:T(8,128)(2,1)}, u32[]{:S(2)}, u32[]{:S(2)}) async-start(bf16[4,1408,512]{2,1,0:T(8,128)(2,1)} %grad_down.1), calls=%async_computation.6 | async-start | bytes 11534336 | tf_op jit(solution)/shard_map/all_to_all | solution.py:39
  941.9 62.4 %collective-permute-start.66 = (bf16[1024,512]{1,0:T(8,128)(2,1)}, bf16[1024,512]{1,0:T(8,128)(2,1)}, u32[]{:S(2)}, u32[]{:S(2)}) collective-permute-start(bf16[1024,512]{1,0:T(8,128)(2,1)} %bitcast.475), channel_id=1, source_target_pairs={{0,6},{2,0},{4,2},{6,4},{1,7},{3,1},{5,3},{7,5},{8,14},{10,8},{12,... | collective-permute-start | bytes 3145736 | tf_op jit(solution)/shard_map/ppermute | solution.py:81
  1011.3 19.1 %collective-permute-start.69 = (bf16[1024,1024]{1,0:T(8,128)(2,1)}, bf16[1024,1024]{1,0:T(8,128)(2,1)}, u32[]{:S(2)}, u32[]{:S(2)}) collective-permute-start(bf16[1024,1024]{1,0:T(8,128)(2,1)} %fusion.3), channel_id=1, source_target_pairs={{0,1},{1,0},{2,3},{3,2},{4,5},{5,4},{6,7},{7,6},{8,9},{9,8},{10,11... | collective-permute-start | bytes 6291464 | tf_op jit(solution)/shard_map/ppermute | solution.py:35
  1024.9 53.0 %all-to-all-start.6 = ((bf16[4,512,512]{2,1,0:T(8,128)(2,1)}), bf16[4,512,512]{2,1,0:T(8,128)(2,1)}, u32[]{:S(2)}, u32[]{:S(2)}) async-start(bf16[4,512,512]{2,1,0:T(8,128)(2,1)} %bitcast.401), calls=%async_computation.7 | async-start | bytes 4194304 | tf_op jit(solution)/shard_map/all_to_all | solution.py:39
  1036.2 49.8 %collective-permute-start.70 = (bf16[256,1024]{1,0:T(8,128)(2,1)}, bf16[256,1024]{1,0:T(8,128)(2,1)}, u32[]{:S(2)}, u32[]{:S(2)}) collective-permute-start(bf16[256,1024]{1,0:T(8,128)(2,1)} %get-tuple-element.205), channel_id=1, source_target_pairs={{0,2},{2,4},{4,6},{6,0},{1,3},{3,5},{5,7},{7,1},{8,10},{10,12},{12... | collective-permute-start | bytes 1572872 | tf_op jit(solution)/shard_map/ppermute | solution.py:81
  1039.4 46.6 %collective-permute-start.71 = (bf16[256,1024]{1,0:T(8,128)(2,1)}, bf16[256,1024]{1,0:T(8,128)(2,1)}, u32[]{:S(2)}, u32[]{:S(2)}) collective-permute-start(bf16[256,1024]{1,0:T(8,128)(2,1)} %get-tuple-element.204), channel_id=1, source_target_pairs={{0,4},{2,6},{4,0},{6,2},{1,5},{3,7},{5,1},{7,3},{8,12},{10,14},{12... | collective-permute-start | bytes 1572872 | tf_op jit(solution)/shard_map/ppermute | solution.py:81
  1040.2 45.8 %collective-permute-start.72 = (bf16[256,1024]{1,0:T(8,128)(2,1)}, bf16[256,1024]{1,0:T(8,128)(2,1)}, u32[]{:S(2)}, u32[]{:S(2)}) collective-permute-start(bf16[256,1024]{1,0:T(8,128)(2,1)} %get-tuple-element.203), channel_id=1, source_target_pairs={{0,6},{2,0},{4,2},{6,4},{1,7},{3,1},{5,3},{7,5},{8,14},{10,8},{12,... | collective-permute-start | bytes 1572872 | tf_op jit(solution)/shard_map/ppermute | solution.py:81
  1081.1 44.8 %all-to-all-start.7 = ((bf16[4,128,2,2,128]{4,3,2,1,0:T(2,128)(2,1)}), bf16[4,128,2,2,128]{4,3,2,1,0:T(2,128)(2,1)S(1)}, u32[]{:S(2)}, u32[]{:S(2)}) async-start(bf16[4,128,2,2,128]{4,3,2,1,0:T(2,128)(2,1)} %reshape.745), calls=%async_computation.8 | async-start | bytes 1048576 | tf_op jit(solution)/shard_map/all_to_all | solution.py:39
  1094.4 29.9 %collective-permute-start.76 = (f32[18,1024]{1,0:T(8,128)S(1)}, f32[18,1024]{1,0:T(8,128)S(1)}, u32[]{:S(2)}, u32[]{:S(2)}) collective-permute-start(f32[18,1024]{1,0:T(8,128)S(1)} %fusion.126), channel_id=1, source_target_pairs={{0,16},{8,24},{16,0},{24,8},{1,17},{9,25},{17,1},{25,9},{2,18},{10... | collective-permute-start | bytes 221192 | tf_op jit(solution)/shard_map/ppermute | solution.py:46
  (126 other events, 1698.0 us)
Sparse Core Ops, SparseCore 0:
  26.7 35.5 all-gather.5
  64.7 193.7 all-gather.3
  260.9 86.8 all-gather.7
  810.8 189.0 reduce-scatter.2
  1003.2 117.0 reduce-scatter.4

commit v5 on v4

--- a/solution.py
+++ b/solution.py
@@ -144,28 +144,44 @@
     )(weights)
 
 
-def unpack_kernel(ff, parts, gate, up, out):
-    for half, src in enumerate((gate, up)):
-        for part in range(parts):
-            out[0, :, half, part * ff : (part + 1) * ff] = src[part, 0].astype(F32)
-
-
-def unpack_gateup(gate, up):
-    parts, local, depth, ff = gate.shape
+def unpack_kernel(ff, parts, early, gate, up_early, up_late, out):
+    first = pl.program_id(1) < early
+    for part in range(parts):
+        where = slice(part * ff, (part + 1) * ff)
+        out[0, :, 0, where] = gate[part, 0].astype(F32)
+
+        @pl.when(first)
+        def _():
+            out[0, :, 1, where] = up_early[part, 0].astype(F32)
+
+        @pl.when(jnp.logical_not(first))
+        def _():
+            out[0, :, 1, where] = up_late[part, 0].astype(F32)
+
+
+def unpack_gateup(sooner, later):
+    parts, local, half, ff = later.shape
+    depth = 2 * half
     if ff % 128:
-        moved = jnp.stack([gate, up], 0).transpose(2, 3, 0, 1, 4)
-        return moved.astype(F32).reshape(local, depth, 2, parts * ff)
-    rows = min(depth, 128)
-    return pl.pallas_call(
-        functools.partial(unpack_kernel, ff, parts),
-        grid=(local, depth // rows),
-        in_specs=[pl.BlockSpec((parts, 1, rows, ff), lambda l, r: (0, l, r, 0))] * 2,
+        both = jnp.concatenate([sooner, later], 2).reshape(parts, local, 2, depth, ff)
+        return both.transpose(1, 3, 2, 0, 4).astype(F32).reshape(local, depth, 2, parts * ff)
+    rows = min(half, 128)
+    early = half // rows
+    block = (parts, 1, rows, ff)
+    return pl.pallas_call(
+        functools.partial(unpack_kernel, ff, parts, early),
+        grid=(local, 2 * early),
+        in_specs=[
+            pl.BlockSpec(block, lambda l, r: (0, l, r, 0)),
+            pl.BlockSpec(block, lambda l, r: (0, l, 2 * early + jnp.minimum(r, early - 1), 0)),
+            pl.BlockSpec(block, lambda l, r: (0, l, jnp.maximum(r - early, 0), 0)),
+        ],
         out_specs=pl.BlockSpec((1, rows, 2, parts * ff), lambda l, r: (l, r, 0, 0)),
         out_shape=jax.ShapeDtypeStruct((local, depth, 2, parts * ff), F32),
         compiler_params=params("parallel", "parallel"),
-        cost_estimate=cost(0, gate.size * 12),
+        cost_estimate=cost(0, later.size * 48),
         name="unpack_gateup",
-    )(gate, up)
+    )(sooner, sooner, later)
 
 
 def cast_kernel(src, out):
@@ -494,41 +510,51 @@
     )(*operands)
 
 
-def gu_outer_kernel(core, x_own, x_other, duw, out):
+def gu_outer_kernel(sooner, core, x_own, x_other, *refs):
+    out = refs[-1]
     half = pl.num_programs(0) // 2
+    depth = x_own.shape[1]
     mine = (pl.program_id(0) // half) == core[0]
+
+    def fill(rows):
+        if sooner:
+            du, dw = refs[0], refs[1]
+            out[0, :depth] = gdot(rows[...], du[...], TN).astype(BF16)
+            out[0, depth:] = gdot(rows[:, : depth // 2], dw[...], TN).astype(BF16)
+        else:
+            out[0] = gdot(rows[:, depth // 2 :], refs[0][...], TN).astype(BF16)
 
     @pl.when(mine)
     def _():
-        out[0] = gdot(x_own[...], duw[...], TN).astype(BF16)
+        fill(x_own)
 
     @pl.when(jnp.logical_not(mine))
     def _():
-        out[0] = gdot(x_other[...], duw[...], TN).astype(BF16)
-
-
-def gu_outer(core, x_own, x_other, duw, columns):
+        fill(x_other)
+
+
+def gu_outer(core, x_own, x_other, hidden_grads, columns):
     rows, width = x_own.shape
     half = columns // 2
     depth = width // half
+    ff = hidden_grads[0].shape[1]
+    sooner = len(hidden_grads) == 2
+    height = 3 * depth // 2 if sooner else depth // 2
     part = lambda s, c: (0, lax.rem(s, half))
-    return pl.pallas_call(
-        gu_outer_kernel,
+    fixed = pl.BlockSpec((rows, ff), lambda s, c: (0, 0), pipeline_mode=pl.Buffered(1))
+    return pl.pallas_call(
+        functools.partial(gu_outer_kernel, sooner),
         grid_spec=pltpu.PrefetchScalarGridSpec(
             num_scalar_prefetch=1,
             grid=(columns,),
-            in_specs=[
-                pl.BlockSpec((rows, depth), part),
-                pl.BlockSpec((rows, depth), part),
-                pl.BlockSpec(duw.shape, lambda s, c: (0, 0), pipeline_mode=pl.Buffered(1)),
-            ],
-            out_specs=pl.BlockSpec((1, depth, duw.shape[1]), lambda s, c: (s, 0, 0)),
+            in_specs=[pl.BlockSpec((rows, depth), part)] * 2 + [fixed] * len(hidden_grads),
+            out_specs=pl.BlockSpec((1, height, ff), lambda s, c: (s, 0, 0)),
         ),
-        out_shape=jax.ShapeDtypeStruct((columns, depth, duw.shape[1]), BF16),
+        out_shape=jax.ShapeDtypeStruct((columns, height, ff), BF16),
         compiler_params=params("arbitrary"),
-        cost_estimate=cost(2 * rows * 2 * width * duw.shape[1], rows * width * 8),
+        cost_estimate=cost(2 * rows * columns * height * ff, rows * width * 8),
         name="grad_gateup",
-    )(core, x_own, x_other, duw)
+    )(core, x_own, x_other, *hidden_grads)
 
 
 def dn_outer_kernel(core, hid, g_own, g_other, out):
@@ -774,8 +800,6 @@
     branch_a = ein("lrf,lfd->lrd", mixed_owner, out_mine) + given.astype(F32)
     branch_a = branch_a.astype(BF16).reshape(local_att, planes, cap, width)
     home_a = shift([branch_a[:, j].reshape(local_att * cap, width) for j in range(planes)], 1)
-    g_own, g_other = to_expert(g_held, (), tuple(home_a[1:]))
-    raw = hidden_raw(core_at, g_own, g_other, w_dn)
     home_a = jnp.concatenate(home_a, 0)
     taken_a = ein("jst,sd->jtd", pick_att, home_a)
     middle = residual + jnp.sum(gates_a[:, :, None] * taken_a, 0)
@@ -783,9 +807,10 @@
     scale_b = rms_scale(middle)
     rows_b_half = (middle * scale_b * norm_mlp).astype(BF16)
     gates_b, named_b, router_b = gates_of(rows_b_half, router_mlp, ints[3:5])
-    x_own, x_other = to_expert(
-        to_plane(dot(flat_mlp, rows_b_half).astype(BF16)), (raw,), (w_up,)
-    )
+    x_held = to_plane(dot(flat_mlp, rows_b_half).astype(BF16))
+    g_own, g_other = to_expert(g_held, (), tuple(x_held[1:]))
+    raw = hidden_raw(core_at, g_own, g_other, w_dn)
+    x_own, x_other = to_expert(x_held, (w_up,), (raw,))
     router_wide = jnp.pad(router_mlp.astype(BF16), ((0, 0), (0, HD - n_mlp)))
     place = jnp.stack([core, mlp_expert]).astype(jnp.int32)
     hidden, hidden_gated, grad_gate, grad_up, row_dgate = feed_forward(
@@ -814,12 +839,14 @@
     dgate_home, dgate_back = mlp_home(dgate_blocks)
     branch_theirs = rows_half(other_at, (hidden,), (w_dn,), width)
     given = swap(branch_theirs)
-    grad_wgate = gu_outer(core_at, x_own, x_other, after(grad_gate, branch_theirs), columns)
+    grad_wgate = gu_outer(
+        core_at, x_own, x_other, (after(grad_gate, branch_theirs), grad_up), columns
+    )
     branch_b = rows_half(core_at, (after(hidden, grad_wgate, *dgate_there),), (w_dn,), width, given)
     grad_pair = (after(grad_gate, branch_b, *dgate_back), grad_up)
     given = swap(rows_half(other_at, grad_pair, (w_gate, w_up), width))
     db_rows = rows_half(core_at, grad_pair, (w_gate, w_up), width, given)
-    grad_wup = gu_outer(core_at, x_own, x_other, after(grad_up, db_rows), columns)
+    grad_wup = gu_outer(core_at, x_own, x_other, (after(grad_up, db_rows),), columns)
     branch_blocks, _ = over_parts(branch_b, grad_wup)
     home_b, branch_back = mlp_home(branch_blocks)
     grad_wdn = dn_outer(core_at, after(hidden_gated, grad_wup), g_own, g_other, columns)
@@ -883,9 +910,7 @@
     got_kv[0] = after(got_kv[0], grad_wq, grad_woutput)
     grad_kv = functools.reduce(jnp.add, [part.astype(F32) for part in got_kv]).astype(BF16)
     grad_kv = relative(grad_kv.reshape(planes, count, 2 * kv_part)).reshape(seq, 2 * kv_part)
-    grad_wquery = lax.psum_scatter(
-        grad_wq, "dp", scatter_dimension=1, tiled=True
-    ).astype(F32)
+    grad_wquery = lax.psum_scatter(grad_wq, "dp", scatter_dimension=1, tiled=True)
     query_mine, query_theirs = halves(whole_query, 1)
     kvw_mine, kvw_theirs = halves(w_kv_part, 0)
 
@@ -897,8 +922,8 @@
     given = swap(grad_seq(query_theirs, kvw_theirs, got_kv[1]).astype(BF16))
     grad_seq_a = (grad_seq(query_mine, kvw_mine, got_kv[-1]) + given.astype(F32)).astype(BF16)
     grad_wgateup = unpack_gateup(
-        after(got_gate, grad_kv).reshape(ff_parts, local_mlp, depth, ff),
-        got_up.reshape(ff_parts, local_mlp, depth, ff),
+        after(got_gate, grad_kv).reshape(ff_parts, local_mlp, 3 * depth // 2, ff),
+        got_up.reshape(ff_parts, local_mlp, depth // 2, ff),
     )
     grad_wdown = unpack_down(got_dn.reshape(ff_parts, local_mlp, ff, depth))
     grad_kv_w = a2a(ein("td,tf->df", seq_a, grad_kv).astype(BF16), "dp")
@@ -921,6 +946,7 @@
         [grad_router_a, grad_router_b, grad_gain_a[None], grad_gain_b[None]], 0
     )
     small = total_over(total_over(small, "dp"), "expert")
+    grad_wquery = after(grad_wquery, small).astype(F32)
     routers = both_halves(small[: n_att + n_mlp], core)
     return (
         output,

time: 1160 us -> 1110 us (0.957)
  waiting for transfers between devices: 445 us -> 396 us
    all_to_all x8, waiting for transfers between devices: 91.9 us -> 51.8 us  [a2a(): return lax.all_to_all(values, axis, split_axis=0, concat_axis=0, tiled=True)]
    ppermute x15, waiting for transfers between devices: 31.9 us -> 53.8 us  [cross(): lax.ppermute(blocks[k], 'dp', [(i, i ^ k) for i in range(count)])]
    reduce_scatter x1, waiting for transfers between devices: 24.9 us -> 4.63 us  [shards(): lax.psum_scatter(grad_wq, 'dp', scatter_dimension=1, tiled=True)]
  transfers between devices with their start and end apart: 93 -> 93, of which waited for: 46 -> 42; matrix products, arithmetic and copies ran while one was open for 17% -> 17% of each run, Pallas kernels for 20% -> 22%
where the time goes in v5:
time: 1110 us; the launch traced here: 1100 us
  waiting for transfers between devices  396 us (36%)
  Pallas kernels  293 us (26%)
  starting transfers between devices  168 us (15%)
  matrix products  85.6 us (8%)
  other arithmetic  85.4 us (8%)
  local copies, waits for them, and re-layouts  55.1 us (5%)
  between operations  15.9 us (1%)
    ppermute x30, waiting for transfers between devices, shift(): lax.ppermute(blocks[j], 'expert', [(i, (i + sign * j) % count) for i in r...  140 us
    dot_general x24, matrix products, ein(): return jnp.einsum(spec, lhs, rhs, preferred_element_type=F32)  81.4 us
    ppermute x30, starting transfers between devices, shift(): lax.ppermute(blocks[j], 'expert', [(i, (i + sign * j) % count) for i in r...  70.5 us
    pallas_call x4, Pallas kernels, att_backward(): pl.pallas_call(att_bwd_kernel, grid_spec=pltpu.PrefetchScalarGridSpec(num...  58.8 us
    ppermute x15, waiting for transfers between devices, cross(): lax.ppermute(blocks[k], 'dp', [(i, i ^ k) for i in range(count)])  53.8 us
    all_to_all x8, waiting for transfers between devices, a2a(): return lax.all_to_all(values, axis, split_axis=0, concat_axis=0, tiled=True)  51.8 us
    pallas_call x4, Pallas kernels, rows_half(): pl.pallas_call(functools.partial(rows_kernel, len(lhs)), grid_spec=pltpu....  50.1 us
    all_gather x1, waiting for transfers between devices, shards(): lax.all_gather(w_output.astype(BF16), 'dp', axis=2, tiled=True)  43.9 us
  transfers between devices with their start and end apart: 93, of which 42 were waited for; matrix products, arithmetic and copies ran while one was open for 17% of the time, Pallas kernels for 22%

profile of v5, /device:TPU:0, one launch (start us, length us, event | category | flops | bytes accessed | tf_op | source)
XLA Modules:
  0.0 1098.9 jit_solution(13584211274422984022)
XLA Ops:
  9.0 5.1 collective-permute-start.9
  18.0 7.3 collective-permute-done.10
  40.0 25.8 %pack_gateup.1 = (bf16[2,2,512,1408]{3,2,1,0:T(8,128)(2,1)}, bf16[2,2,512,1408]{3,2,1,0:T(8,128)(2,1)}) custom-call(f32[2,512,2,2816]{3,2,1,0:T(2,128)} %src.3), custom_call_target="tpu_custom_call" | custom-call | bytes 346030 | tf_op jit(solution)/shard_map/pack_gateup/pallas_call | solution.py:135
  65.8 7.2 pack_down.1
  73.0 11.1 %collective-permute-done.1 = bf16[256,1024]{1,0:T(8,128)(2,1)S(1)} collective-permute-done((bf16[256,1024]{1,0:T(8,128)(2,1)S(1)}, bf16[256,1024]{1,0:T(8,128)(2,1)S(1)}, u32[]{:S(2)}, u32[]{:S(2)}) %collective-permute-start.1) | collective-permute-done | bytes 524320 | tf_op jit(solution)/shard_map/ppermute | solution.py:62
  84.9 5.1 all-to-all-start
  97.9 5.6 fusion.82
  129.0 5.7 collective-permute-start.15
  137.8 17.9 %collective-permute-done.15 = bf16[1024,512]{1,0:T(8,128)(2,1)} collective-permute-done((bf16[1024,512]{1,0:T(8,128)(2,1)S(1)}, bf16[1024,512]{1,0:T(8,128)(2,1)}, u32[]{:S(2)}, u32[]{:S(2)}) %collective-permute-start.15) | collective-permute-done | bytes 1048608 | tf_op jit(solution)/shard_map/ppermute | solution.py:73
  155.7 5.5 collective-permute-start.16
  162.5 14.5 %all-to-all-done.w_dn.refs_1_ = bf16[4,1408,512]{2,1,0:T(8,128)(2,1)} async-done(((bf16[4,1408,512]{2,1,0:T(8,128)(2,1)}), bf16[4,1408,512]{2,1,0:T(8,128)(2,1)}, u32[]{:S(2)}, u32[]{:S(2)}) %all-to-all-start) | async-done | bytes 5767200 | tf_op jit(solution)/shard_map/all_to_all | solution.py:39
  177.0 5.2 all-to-all-start.1
  197.0 12.5 %collective-permute-done.17 = bf16[1024,512]{1,0:T(8,128)(2,1)} collective-permute-done((bf16[1024,512]{1,0:T(8,128)(2,1)}, bf16[1024,512]{1,0:T(8,128)(2,1)}, u32[]{:S(2)}, u32[]{:S(2)}) %collective-permute-start.17) | collective-permute-done | bytes 1048608 | tf_op jit(solution)/shard_map/ppermute | solution.py:73
  229.8 23.2 %collective-permute-done.19 = bf16[2,96,1024]{2,1,0:T(8,128)(2,1)} collective-permute-done((bf16[2,96,1024]{2,1,0:T(8,128)(2,1)S(1)}, bf16[2,96,1024]{2,1,0:T(8,128)(2,1)}, u32[]{:S(2)}, u32[]{:S(2)}) %collective-permute-start.19) | collective-permute-done | bytes 393248 | tf_op jit(solution)/shard_map/ppermute | solution.py:81
  253.0 5.5 all-gather.4.cloned.1.call-done
  258.5 9.5 fusion.142
  268.0 9.0 attention_fwd.4
  277.0 8.8 attention_fwd.5
  285.8 8.8 attention_fwd.6
  294.6 8.8 attention_fwd.7
  303.4 43.9 %all-gather.8.cloned.1.call-done = bf16[2,1024,2048]{2,1,0:T(8,128)(2,1)} async-done(((bf16[2,1024,512]{2,1,0:T(8,128)(2,1)}), bf16[2,1024,2048]{2,1,0:T(8,128)(2,1)}) %all-gather.8.cloned.1.call-update) | async-done | bytes 8388624 | tf_op jit(solution)/shard_map/all_gather | solution.py:663
  347.3 5.6 fusion.19
  352.9 5.3 all-to-all-start.2
  372.6 7.0 collective-permute-done.22
  379.6 16.1 %collective-permute-done.23 = bf16[192,1024]{1,0:T(8,128)(2,1)S(1)} collective-permute-done((bf16[192,1024]{1,0:T(8,128)(2,1)S(1)}, bf16[192,1024]{1,0:T(8,128)(2,1)S(1)}, u32[]{:S(2)}, u32[]{:S(2)}) %collective-permute-start.23) | collective-permute-done | bytes 393248 | tf_op jit(solution)/shard_map/ppermute | solution.py:81
  404.4 9.8 collective-permute-start.27
  414.9 26.5 %collective-permute-done.35 = bf16[384,1024]{1,0:T(8,128)(2,1)S(1)} collective-permute-done((bf16[384,1024]{1,0:T(8,128)(2,1)S(1)}, bf16[384,1024]{1,0:T(8,128)(2,1)S(1)}, u32[]{:S(2)}, u32[]{:S(2)}) %collective-permute-start.35) | collective-permute-done | bytes 786464 | tf_op jit(solution)/shard_map/ppermute | solution.py:89
  442.9 10.7 collective-permute-done.29
  464.9 15.1 %hidden_raw.1.raw = f32[1536,1408]{1,0:T(8,128)} custom-call(s32[1]{0:T(128)} %bitcast.71.core.which, bf16[1536,1024]{1,0:T(8,128)(2,1)} %copy-done.2, bf16[1536,1024]{1,0:T(8,128)(2,1)} %collective-permute-done.36.g_other, bf16[4,1408,512]{2,1,0:T(8,128)(2,1)} %all-to-all-done.w_dn.refs_1_), custom_call_target="tpu_custom_call" | custom-call | flops 88583696 | bytes 144179 | tf_op jit(solution)/shard_map/hidden_raw/pallas_call | solution.py:386
  483.2 15.5 %collective-permute-done.30 = bf16[384,1024]{1,0:T(8,128)(2,1)} collective-permute-done((bf16[384,1024]{1,0:T(8,128)(2,1)}, bf16[384,1024]{1,0:T(8,128)(2,1)}, u32[]{:S(2)}, u32[]{:S(2)}) %collective-permute-start.30) | collective-permute-done | bytes 786464 | tf_op jit(solution)/shard_map/ppermute | solution.py:89
  512.1 32.0 %feed_forward.1 = (bf16[1536,1408]{1,0:T(8,128)(2,1)}, bf16[1536,1408]{1,0:T(8,128)(2,1)}, bf16[1536,1408]{1,0:T(8,128)(2,1)}, bf16[1536,1408]{1,0:T(8,128)(2,1)}, f32[1536,1]{1,0:T(8,128)}) custom-call(s32[2]{0:T(128)} %pad_add_fusion.4.place, bf16[1536,1024]{1,0:T(8,128)(2,1)} %copy-done.1, bf16[1536,1024]{1,0:T(8,128)(2,1)} %collective-permute-done.37.x_other, ...), custom_call_target="tpu_custom_call" | custom-call | flops 221459248 | bytes 374865 | tf_op jit(solution)/shard_map/feed_forward/pallas_call | solution.py:442
  544.1 9.5 rows_half.4
  563.0 21.7 %grad_gateup.2 = bf16[4,768,1408]{2,1,0:T(8,128)(2,1)} custom-call(s32[1]{0:T(128)} %bitcast.71.core.which, bf16[1536,1024]{1,0:T(8,128)(2,1)} %copy-done.1, bf16[1536,1024]{1,0:T(8,128)(2,1)} %collective-permute-done.37.x_other, bf16[1536,1408]{1,0:T(8,128)(2,1)} %get-tuple-element.90.refs_0_, bf16[1536,1408]{1,0:T(8,128)(2,1)} %get-tuple-element.91.refs_1_.refs_0_), custom_call_target="tpu_custom_call" | custom-call | flops 132875552 | bytes 125829 | tf_op jit(solution)/shard_map/grad_gateup/pallas_call | solution.py:545
  591.2 10.0 rows_half.5
  601.3 15.2 %rows_half.6 = bf16[1536,1024]{1,0:T(8,128)(2,1)} custom-call(s32[1]{0:T(128)S(6)} %sub.102.which, bf16[1536,1408]{1,0:T(8,128)(2,1)} %get-tuple-element.90.refs_0_, bf16[1536,1408]{1,0:T(8,128)(2,1)} %get-tuple-element.91.refs_1_.refs_0_, bf16[2048,1408]{1,0:T(8,128)(2,1)} %bitcast.60.w_gate.refs_2_, bf16[2048,1408]{1,0:T(8,128)(2,1)} %bitcast.81.w_up.refs_3_), custom_call_target="tpu_custom_call" | custom-call | flops 88583696 | bytes 62914 | tf_op jit(solution)/shard_map/rows_half/pallas_call | solution.py:498
  622.5 15.4 %rows_half.7 = bf16[1536,1024]{1,0:T(8,128)(2,1)} custom-call(s32[1]{0:T(128)} %bitcast.71.core.which, bf16[1536,1408]{1,0:T(8,128)(2,1)} %get-tuple-element.90.refs_0_, bf16[1536,1408]{1,0:T(8,128)(2,1)} %get-tuple-element.91.refs_1_.refs_0_, bf16[2048,1408]{1,0:T(8,128)(2,1)} %bitcast.60.w_gate.refs_2_, bf16[2048,1408]{1,0:T(8,128)(2,1)} %bitcast.81.w_up.refs_3_, ...), custom_call_target="tpu_custom_call" | custom-call | flops 88583696 | bytes 62914 | tf_op jit(solution)/shard_map/rows_half/pallas_call | solution.py:498
  637.9 10.8 grad_gateup.3
  650.4 5.3 collective-permute-done.46
  672.1 18.9 %collective-permute-start.52 = (bf16[192,1024]{1,0:T(8,128)(2,1)}, bf16[192,1024]{1,0:T(8,128)(2,1)S(1)}, u32[]{:S(2)}, u32[]{:S(2)}) collective-permute-start(bf16[192,1024]{1,0:T(8,128)(2,1)} %pad_maximum_fusion.19), channel_id=1, source_target_pairs={{0,2},{2,4},{4,6},{6,0},{1,3},{3,5},{5,7},{7,1},{8,10},{10,12},{12... | collective-permute-start | bytes 1179656 | tf_op jit(solution)/shard_map/ppermute | solution.py:81
  691.2 14.2 %grad_down.1 = bf16[4,1408,512]{2,1,0:T(8,128)(2,1)} custom-call(s32[1]{0:T(128)} %bitcast.71.core.which, bf16[1536,1408]{1,0:T(8,128)(2,1)} %get-tuple-element.97.hid, bf16[1536,1024]{1,0:T(8,128)(2,1)} %copy-done.2, bf16[1536,1024]{1,0:T(8,128)(2,1)} %collective-permute-done.36.g_other), custom_call_target="tpu_custom_call" | custom-call | flops 88583696 | bytes 125829 | tf_op jit(solution)/shard_map/grad_down/pallas_call | solution.py:579
  706.6 5.7 all-to-all-start.3
  721.9 9.2 collective-permute-done.60
  731.1 15.4 %collective-permute-done.58 = bf16[192,1024]{1,0:T(8,128)(2,1)S(1)} collective-permute-done((bf16[192,1024]{1,0:T(8,128)(2,1)S(1)}, bf16[192,1024]{1,0:T(8,128)(2,1)S(1)}, u32[]{:S(2)}, u32[]{:S(2)}) %collective-permute-start.58) | collective-permute-done | bytes 393248 | tf_op jit(solution)/shard_map/ppermute | solution.py:81
  746.5 9.3 collective-permute-done.59
  765.2 9.8 collective-permute-done.64
  775.0 23.1 %all-to-all-done.3 = bf16[4,768,1408]{2,1,0:T(8,128)(2,1)} async-done(((bf16[4,768,1408]{2,1,0:T(8,128)(2,1)}), bf16[4,768,1408]{2,1,0:T(8,128)(2,1)}, u32[]{:S(2)}, u32[]{:S(2)}) %all-to-all-start.3) | async-done | bytes 8650784 | tf_op jit(solution)/shard_map/all_to_all | solution.py:39
  805.5 6.8 convolution_convert_fusion.1
  823.8 8.9 fusion.18
  832.8 14.7 %attention_bwd.4 = (bf16[768,1024]{1,0:T(8,128)(2,1)}, bf16[1,1024,512]{2,1,0:T(8,128)(2,1)}) custom-call(s32[4]{0:T(128)} %and_select_fusion.place, bf16[768,1024]{1,0:T(8,128)(2,1)} %get-tuple-element.102.q_in, bf16[768,1024]{1,0:T(8,128)(2,1)} %bitcast.355, bf16[1,1024,512]{2,1,0:T(8,128)(2,1)} %add_bitcast_fusion.kv, f32[768,128]{1,0:T(8,128)} %pad_maximum_fusion.17.cos, ...), custom_call_target="tpu_custom_call" | custom-call | flops 120795952 | bytes 31457 | tf_op jit(solution)/shard_map/attention_bwd/pallas_call | solution.py:348
  847.5 14.7 %attention_bwd.5 = (bf16[768,1024]{1,0:T(8,128)(2,1)}, bf16[1,1024,512]{2,1,0:T(8,128)(2,1)}) custom-call(s32[4]{0:T(128)} %and_select_fusion.place, bf16[768,1024]{1,0:T(8,128)(2,1)} %get-tuple-element.102.q_in, bf16[768,1024]{1,0:T(8,128)(2,1)} %bitcast.356, bf16[1,1024,512]{2,1,0:T(8,128)(2,1)} %bitcast.376, ...), custom_call_target="tpu_custom_call", output_to_operand_aliasing={{0}: (11, {})} | custom-call | flops 120795952 | bytes 31457 | tf_op jit(solution)/shard_map/attention_bwd/pallas_call | solution.py:348
  862.2 14.7 %attention_bwd.6 = (bf16[768,1024]{1,0:T(8,128)(2,1)}, bf16[1,1024,512]{2,1,0:T(8,128)(2,1)}) custom-call(s32[4]{0:T(128)} %and_select_fusion.place, bf16[768,1024]{1,0:T(8,128)(2,1)} %get-tuple-element.102.q_in, bf16[768,1024]{1,0:T(8,128)(2,1)} %bitcast.357, bf16[1,1024,512]{2,1,0:T(8,128)(2,1)} %bitcast.378, ...), custom_call_target="tpu_custom_call", output_to_operand_aliasing={{0}: (11, {})} | custom-call | flops 120795952 | bytes 31457 | tf_op jit(solution)/shard_map/attention_bwd/pallas_call | solution.py:348
  876.9 14.7 %attention_bwd.7 = (bf16[768,1024]{1,0:T(8,128)(2,1)}, bf16[1,1024,512]{2,1,0:T(8,128)(2,1)}) custom-call(s32[4]{0:T(128)} %and_select_fusion.place, bf16[768,1024]{1,0:T(8,128)(2,1)} %get-tuple-element.102.q_in, bf16[768,1024]{1,0:T(8,128)(2,1)} %bitcast.358, bf16[1,1024,512]{2,1,0:T(8,128)(2,1)} %bitcast.374, ...), custom_call_target="tpu_custom_call", output_to_operand_aliasing={{0}: (11, {})} | custom-call | flops 120795952 | bytes 31457 | tf_op jit(solution)/shard_map/attention_bwd/pallas_call | solution.py:348
  894.3 10.3 convolution_convert_fusion
  904.7 5.3 all-to-all-start.5
  913.9 18.9 %collective-permute-done.68 = bf16[1024,512]{1,0:T(8,128)(2,1)S(1)} collective-permute-done((bf16[1024,512]{1,0:T(8,128)(2,1)}, bf16[1024,512]{1,0:T(8,128)(2,1)S(1)}, u32[]{:S(2)}, u32[]{:S(2)}) %collective-permute-start.68) | collective-permute-done | bytes 1048608 | tf_op jit(solution)/shard_map/ppermute | solution.py:81
  940.1 27.1 %reduce-scatter.3.cloned.1.call-done = bf16[2,1024,512]{2,1,0:T(8,128)(2,1)} async-done(((bf16[2,1024,2048]{2,1,0:T(8,128)(2,1)}), bf16[2,1024,512]{2,1,0:T(8,128)(2,1)}) %reduce-scatter.3.cloned.1.call-update) | async-done | bytes 2097168 | tf_op jit(solution)/shard_map/reduce_scatter | solution.py:891
  982.7 5.3 fusion.22
  993.4 4.6 all-to-all-start.6
  1011.5 7.4 unpack_down.1
  1019.0 14.6 %unpack_gateup.1 = f32[2,512,2,2816]{3,2,1,0:T(2,128)} custom-call(bf16[2,2,768,1408]{3,2,1,0:T(8,128)(2,1)} %bitcast.156.gate.up_early, bf16[2,2,768,1408]{3,2,1,0:T(8,128)(2,1)} %bitcast.156.gate.up_early, bf16[2,2,256,1408]{3,2,1,0:T(8,128)(2,1)} %bitcast.370), custom_call_target="tpu_custom_call" | custom-call | bytes 692060 | tf_op jit(solution)/shard_map/unpack_gateup/pallas_call | solution.py:171
  1033.6 12.5 %all-to-all-done.6 = bf16[4,512,512]{2,1,0:T(8,128)(2,1)} async-done(((bf16[4,512,512]{2,1,0:T(8,128)(2,1)}), bf16[4,512,512]{2,1,0:T(8,128)(2,1)}, u32[]{:S(2)}, u32[]{:S(2)}) %all-to-all-start.6) | async-done | bytes 2097184 | tf_op jit(solution)/shard_map/all_to_all | solution.py:39
  1049.2 4.6 all-to-all-start.7
  1063.2 5.6 collective-permute-done.76
  1082.8 4.6 reduce-scatter.5.cloned.1.call-done
  (549 shorter events, 304.4 us)
Async XLA Ops:
  7.2 107.8 %all-gather.6.cloned.1.call-start = ((), (), s32[]{:S(2)}) async-start(), calls=%async_computation.11 | async-start | bytes 2621440 | tf_op jit(solution)/shard_map/all_gather | solution.py:657
  26.5 232.0 %all-gather.4.cloned.1.call-start = ((), (), s32[]{:S(2)}) async-start(), calls=%async_computation.10 | async-start | bytes 10485760 | tf_op jit(solution)/shard_map/all_gather | solution.py:660
  30.4 316.8 %all-gather.8.cloned.1.call-start = ((), (), s32[]{:S(2)}) async-start(), calls=%async_computation.12 | async-start | bytes 10485760 | tf_op jit(solution)/shard_map/all_gather | solution.py:663
  35.4 37.6 %collective-permute-start.2 = (bf16[256,1024]{1,0:T(8,128)(2,1)S(1)}, bf16[256,1024]{1,0:T(8,128)(2,1)S(1)}, u32[]{:S(2)}, u32[]{:S(2)}) collective-permute-start(bf16[256,1024]{1,0:T(8,128)(2,1)S(1)} %copy-done.28), channel_id=1, source_target_pairs={{0,2},{2,4},{4,6},{6,0},{1,3},{3,5},{5,7},{7,1},{8,10},{10,12},{12... | collective-permute-start | bytes 1572872 | tf_op jit(solution)/shard_map/ppermute | solution.py:62
  36.1 36.9 %collective-permute-start = (bf16[256,1024]{1,0:T(8,128)(2,1)S(1)}, bf16[256,1024]{1,0:T(8,128)(2,1)S(1)}, u32[]{:S(2)}, u32[]{:S(2)}) collective-permute-start(bf16[256,1024]{1,0:T(8,128)(2,1)S(1)} %copy-done.28), channel_id=1, source_target_pairs={{0,6},{2,0},{4,2},{6,4},{1,7},{3,1},{5,3},{7,5},{8,14},{10,8},{12,... | collective-permute-start | bytes 1572872 | tf_op jit(solution)/shard_map/ppermute | solution.py:62
  39.2 44.9 %collective-permute-start.1 = (bf16[256,1024]{1,0:T(8,128)(2,1)S(1)}, bf16[256,1024]{1,0:T(8,128)(2,1)S(1)}, u32[]{:S(2)}, u32[]{:S(2)}) collective-permute-start(bf16[256,1024]{1,0:T(8,128)(2,1)S(1)} %copy-done.28), channel_id=1, source_target_pairs={{0,4},{2,6},{4,0},{6,2},{1,5},{3,7},{5,1},{7,3},{8,12},{10,14},{12... | collective-permute-start | bytes 1572872 | tf_op jit(solution)/shard_map/ppermute | solution.py:62
  84.9 92.1 %all-to-all-start = ((bf16[4,1408,512]{2,1,0:T(8,128)(2,1)}), bf16[4,1408,512]{2,1,0:T(8,128)(2,1)}, u32[]{:S(2)}, u32[]{:S(2)}) async-start(bf16[4,1408,512]{2,1,0:T(8,128)(2,1)} %bitcast.359), calls=%async_computation | async-start | bytes 11534336 | tf_op jit(solution)/shard_map/all_to_all | solution.py:39
  94.8 16.4 %collective-permute-start.5 = (bf16[1024,1024]{1,0:T(8,128)(2,1)S(1)}, bf16[1024,1024]{1,0:T(8,128)(2,1)}, u32[]{:S(2)}, u32[]{:S(2)}) collective-permute-start(bf16[1024,1024]{1,0:T(8,128)(2,1)S(1)} %fusion.2), channel_id=1, source_target_pairs={{0,1},{1,0},{2,3},{3,2},{4,5},{5,4},{6,7},{7,6},{8,9},{9,8},{10,11... | collective-permute-start | bytes 6291464 | tf_op jit(solution)/shard_map/ppermute | solution.py:35
  95.4 42.3 %collective-permute-start.6 = (s32[8,256]{1,0:T(8,128)S(1)}, s32[8,256]{1,0:T(8,128)S(1)}, u32[]{:S(2)}, u32[]{:S(2)}) collective-permute-start(s32[8,256]{1,0:T(8,128)S(1)} %get-tuple-element.263), channel_id=1, source_target_pairs={{0,6},{2,0},{4,2},{6,4},{1,7},{3,1},{5,3},{7,5},{8,14},{10,8},{12,... | collective-permute-start | bytes 24584 | tf_op jit(solution)/shard_map/ppermute | solution.py:62
  97.0 40.7 %collective-permute-start.7 = (s32[8,256]{1,0:T(8,128)S(1)}, s32[8,256]{1,0:T(8,128)S(1)}, u32[]{:S(2)}, u32[]{:S(2)}) collective-permute-start(s32[8,256]{1,0:T(8,128)S(1)} %get-tuple-element.263), channel_id=1, source_target_pairs={{0,4},{2,6},{4,0},{6,2},{1,5},{3,7},{5,1},{7,3},{8,12},{10,14},{12... | collective-permute-start | bytes 24584 | tf_op jit(solution)/shard_map/ppermute | solution.py:62
  97.0 40.7 %collective-permute-start.8 = (s32[8,256]{1,0:T(8,128)S(1)}, s32[8,256]{1,0:T(8,128)S(1)}, u32[]{:S(2)}, u32[]{:S(2)}) collective-permute-start(s32[8,256]{1,0:T(8,128)S(1)} %get-tuple-element.263), channel_id=1, source_target_pairs={{0,2},{2,4},{4,6},{6,0},{1,3},{3,5},{5,7},{7,1},{8,10},{10,12},{12... | collective-permute-start | bytes 24584 | tf_op jit(solution)/shard_map/ppermute | solution.py:62
  129.0 26.6 %collective-permute-start.15 = (bf16[1024,512]{1,0:T(8,128)(2,1)S(1)}, bf16[1024,512]{1,0:T(8,128)(2,1)}, u32[]{:S(2)}, u32[]{:S(2)}) collective-permute-start(bf16[1024,512]{1,0:T(8,128)(2,1)S(1)} %bitcast.371), channel_id=1, source_target_pairs={{0,2},{2,4},{4,6},{1,3},{3,5},{5,7},{8,10},{10,12},{12,14},{9,11},... | collective-permute-start | bytes 3145736 | tf_op jit(solution)/shard_map/ppermute | solution.py:73
  134.8 26.4 %collective-permute-start.12 = (bf16[1024,512]{1,0:T(8,128)(2,1)S(1)}, bf16[1024,512]{1,0:T(8,128)(2,1)}, u32[]{:S(2)}, u32[]{:S(2)}) collective-permute-start(bf16[1024,512]{1,0:T(8,128)(2,1)S(1)} %bitcast.372), channel_id=1, source_target_pairs={{2,0},{4,2},{6,4},{3,1},{5,3},{7,5},{10,8},{12,10},{14,12},{11,9},... | collective-permute-start | bytes 3145736 | tf_op jit(solution)/shard_map/ppermute | solution.py:74
  155.7 28.0 %collective-permute-start.16 = (bf16[1024,512]{1,0:T(8,128)(2,1)}, bf16[1024,512]{1,0:T(8,128)(2,1)}, u32[]{:S(2)}, u32[]{:S(2)}) collective-permute-start(bf16[1024,512]{1,0:T(8,128)(2,1)} %collective-permute-done.15), channel_id=1, source_target_pairs={{0,2},{2,4},{4,6},{1,3},{3,5},{5,7},{8,10},{10,12},{12,14},{9,11},... | collective-permute-start | bytes 3145736 | tf_op jit(solution)/shard_map/ppermute | solution.py:73
  161.2 26.9 %collective-permute-start.13 = (bf16[1024,512]{1,0:T(8,128)(2,1)}, bf16[1024,512]{1,0:T(8,128)(2,1)}, u32[]{:S(2)}, u32[]{:S(2)}) collective-permute-start(bf16[1024,512]{1,0:T(8,128)(2,1)} %collective-permute-done.12), channel_id=1, source_target_pairs={{2,0},{4,2},{6,4},{3,1},{5,3},{7,5},{10,8},{12,10},{14,12},{11,9},... | collective-permute-start | bytes 3145736 | tf_op jit(solution)/shard_map/ppermute | solution.py:74
  177.0 126.3 %all-to-all-start.1 = ((bf16[4,512,1408]{2,1,0:T(8,128)(2,1)}), bf16[4,512,1408]{2,1,0:T(8,128)(2,1)}, u32[]{:S(2)}, u32[]{:S(2)}) async-start(bf16[4,512,1408]{2,1,0:T(8,128)(2,1)} %bitcast.388), calls=%async_computation.1 | async-start | bytes 11534336 | tf_op jit(solution)/shard_map/all_to_all | solution.py:39
  183.6 25.8 %collective-permute-start.17 = (bf16[1024,512]{1,0:T(8,128)(2,1)}, bf16[1024,512]{1,0:T(8,128)(2,1)}, u32[]{:S(2)}, u32[]{:S(2)}) collective-permute-start(bf16[1024,512]{1,0:T(8,128)(2,1)} %collective-permute-done.16), channel_id=1, source_target_pairs={{0,2},{2,4},{4,6},{1,3},{3,5},{5,7},{8,10},{10,12},{12,14},{9,11},... | collective-permute-start | bytes 3145736 | tf_op jit(solution)/shard_map/ppermute | solution.py:73
  188.1 26.5 %collective-permute-start.14 = (bf16[1024,512]{1,0:T(8,128)(2,1)}, bf16[1024,512]{1,0:T(8,128)(2,1)}, u32[]{:S(2)}, u32[]{:S(2)}) collective-permute-start(bf16[1024,512]{1,0:T(8,128)(2,1)} %collective-permute-done.13), channel_id=1, source_target_pairs={{2,0},{4,2},{6,4},{3,1},{5,3},{7,5},{10,8},{12,10},{14,12},{11,9},... | collective-permute-start | bytes 3145736 | tf_op jit(solution)/shard_map/ppermute | solution.py:74
  220.2 32.8 %collective-permute-start.19 = (bf16[2,96,1024]{2,1,0:T(8,128)(2,1)S(1)}, bf16[2,96,1024]{2,1,0:T(8,128)(2,1)}, u32[]{:S(2)}, u32[]{:S(2)}) collective-permute-start(bf16[2,96,1024]{2,1,0:T(8,128)(2,1)S(1)} %bitcast.418), channel_id=1, source_target_pairs={{0,4},{2,6},{4,0},{6,2},{1,5},{3,7},{5,1},{7,3},{8,12},{10,14},{12... | collective-permute-start | bytes 1179656 | tf_op jit(solution)/shard_map/ppermute | solution.py:81
  220.2 32.8 %collective-permute-start.20 = (bf16[2,96,1024]{2,1,0:T(8,128)(2,1)S(1)}, bf16[2,96,1024]{2,1,0:T(8,128)(2,1)}, u32[]{:S(2)}, u32[]{:S(2)}) collective-permute-start(bf16[2,96,1024]{2,1,0:T(8,128)(2,1)S(1)} %bitcast.414), channel_id=1, source_target_pairs={{0,2},{2,4},{4,6},{6,0},{1,3},{3,5},{5,7},{7,1},{8,10},{10,12},{12... | collective-permute-start | bytes 1179656 | tf_op jit(solution)/shard_map/ppermute | solution.py:81
  352.9 104.6 %all-to-all-start.2 = ((bf16[4,512,1408]{2,1,0:T(8,128)(2,1)}), bf16[4,512,1408]{2,1,0:T(8,128)(2,1)}, u32[]{:S(2)}, u32[]{:S(2)}) async-start(bf16[4,512,1408]{2,1,0:T(8,128)(2,1)} %bitcast.387), calls=%async_computation.2 | async-start | bytes 11534336 | tf_op jit(solution)/shard_map/all_to_all | solution.py:39
  365.7 14.0 %collective-permute-start.22 = (bf16[192,1024]{1,0:T(8,128)(2,1)S(1)}, bf16[192,1024]{1,0:T(8,128)(2,1)S(1)}, u32[]{:S(2)}, u32[]{:S(2)}) collective-permute-start(bf16[192,1024]{1,0:T(8,128)(2,1)S(1)} %bitcast.420), channel_id=1, source_target_pairs={{0,2},{2,4},{4,6},{6,0},{1,3},{3,5},{5,7},{7,1},{8,10},{10,12},{12... | collective-permute-start | bytes 1179656 | tf_op jit(solution)/shard_map/ppermute | solution.py:81
  367.2 28.5 %collective-permute-start.23 = (bf16[192,1024]{1,0:T(8,128)(2,1)S(1)}, bf16[192,1024]{1,0:T(8,128)(2,1)S(1)}, u32[]{:S(2)}, u32[]{:S(2)}) collective-permute-start(bf16[192,1024]{1,0:T(8,128)(2,1)S(1)} %bitcast.415), channel_id=1, source_target_pairs={{0,4},{2,6},{4,0},{6,2},{1,5},{3,7},{5,1},{7,3},{8,12},{10,14},{12... | collective-permute-start | bytes 1179656 | tf_op jit(solution)/shard_map/ppermute | solution.py:81
  369.6 26.1 %collective-permute-start.24 = (bf16[192,1024]{1,0:T(8,128)(2,1)S(1)}, bf16[192,1024]{1,0:T(8,128)(2,1)S(1)}, u32[]{:S(2)}, u32[]{:S(2)}) collective-permute-start(bf16[192,1024]{1,0:T(8,128)(2,1)S(1)} %bitcast.413), channel_id=1, source_target_pairs={{0,6},{2,0},{4,2},{6,4},{1,7},{3,1},{5,3},{7,5},{8,14},{10,8},{12,... | collective-permute-start | bytes 1179656 | tf_op jit(solution)/shard_map/ppermute | solution.py:81
  398.6 42.9 %collective-permute-start.35 = (bf16[384,1024]{1,0:T(8,128)(2,1)S(1)}, bf16[384,1024]{1,0:T(8,128)(2,1)S(1)}, u32[]{:S(2)}, u32[]{:S(2)}) collective-permute-start(bf16[384,1024]{1,0:T(8,128)(2,1)S(1)} %bitcast.406), channel_id=1, source_target_pairs={{0,24},{8,16},{16,8},{24,0},{1,25},{9,17},{17,9},{25,1},{2,26},{10... | collective-permute-start | bytes 2359304 | tf_op jit(solution)/shard_map/ppermute | solution.py:89
  401.4 55.6 %collective-permute-start.33 = (bf16[384,1024]{1,0:T(8,128)(2,1)S(1)}, bf16[384,1024]{1,0:T(8,128)(2,1)S(1)}, u32[]{:S(2)}, u32[]{:S(2)}) collective-permute-start(bf16[384,1024]{1,0:T(8,128)(2,1)S(1)} %bitcast.407), channel_id=1, source_target_pairs={{0,8},{8,0},{16,24},{24,16},{1,9},{9,1},{17,25},{25,17},{2,10},{10... | collective-permute-start | bytes 2359304 | tf_op jit(solution)/shard_map/ppermute | solution.py:89
  401.9 55.1 %collective-permute-start.34 = (bf16[384,1024]{1,0:T(8,128)(2,1)S(1)}, bf16[384,1024]{1,0:T(8,128)(2,1)S(1)}, u32[]{:S(2)}, u32[]{:S(2)}) collective-permute-start(bf16[384,1024]{1,0:T(8,128)(2,1)S(1)} %bitcast.396), channel_id=1, source_target_pairs={{0,16},{8,24},{16,0},{24,8},{1,17},{9,25},{17,1},{25,9},{2,18},{10... | collective-permute-start | bytes 2359304 | tf_op jit(solution)/shard_map/ppermute | solution.py:89
  404.4 38.5 %collective-permute-start.27 = (bf16[2,96,1024]{2,1,0:T(8,128)(2,1)S(1)}, bf16[2,96,1024]{2,1,0:T(8,128)(2,1)S(1)}, u32[]{:S(2)}, u32[]{:S(2)}) collective-permute-start(bf16[2,96,1024]{2,1,0:T(8,128)(2,1)S(1)} %bitcast.425), channel_id=1, source_target_pairs={{0,6},{2,0},{4,2},{6,4},{1,7},{3,1},{5,3},{7,5},{8,14},{10,8},{12,... | collective-permute-start | bytes 1179656 | tf_op jit(solution)/shard_map/ppermute | solution.py:81
  414.2 28.7 %collective-permute-start.28 = (bf16[2,96,1024]{2,1,0:T(8,128)(2,1)S(1)}, bf16[2,96,1024]{2,1,0:T(8,128)(2,1)S(1)}, u32[]{:S(2)}, u32[]{:S(2)}) collective-permute-start(bf16[2,96,1024]{2,1,0:T(8,128)(2,1)S(1)} %bitcast.423), channel_id=1, source_target_pairs={{0,4},{2,6},{4,0},{6,2},{1,5},{3,7},{5,1},{7,3},{8,12},{10,14},{12... | collective-permute-start | bytes 1179656 | tf_op jit(solution)/shard_map/ppermute | solution.py:81
  461.4 21.7 %collective-permute-start.32 = (bf16[384,1024]{1,0:T(8,128)(2,1)}, bf16[384,1024]{1,0:T(8,128)(2,1)}, u32[]{:S(2)}, u32[]{:S(2)}) collective-permute-start(bf16[384,1024]{1,0:T(8,128)(2,1)} %bitcast.84), channel_id=1, source_target_pairs={{0,24},{8,16},{16,8},{24,0},{1,25},{9,17},{17,9},{25,1},{2,26},{10... | collective-permute-start | bytes 2359304 | tf_op jit(solution)/shard_map/ppermute | solution.py:89
  462.9 35.8 %collective-permute-start.30 = (bf16[384,1024]{1,0:T(8,128)(2,1)}, bf16[384,1024]{1,0:T(8,128)(2,1)}, u32[]{:S(2)}, u32[]{:S(2)}) collective-permute-start(bf16[384,1024]{1,0:T(8,128)(2,1)} %bitcast.84), channel_id=1, source_target_pairs={{0,8},{8,0},{16,24},{24,16},{1,9},{9,1},{17,25},{25,17},{2,10},{10... | collective-permute-start | bytes 2359304 | tf_op jit(solution)/shard_map/ppermute | solution.py:89
  464.4 34.3 %collective-permute-start.31 = (bf16[384,1024]{1,0:T(8,128)(2,1)}, bf16[384,1024]{1,0:T(8,128)(2,1)}, u32[]{:S(2)}, u32[]{:S(2)}) collective-permute-start(bf16[384,1024]{1,0:T(8,128)(2,1)} %bitcast.83), channel_id=1, source_target_pairs={{0,16},{8,24},{16,0},{24,8},{1,17},{9,25},{17,1},{25,9},{2,18},{10... | collective-permute-start | bytes 2359304 | tf_op jit(solution)/shard_map/ppermute | solution.py:89
  553.6 36.0 %collective-permute-start.44 = (bf16[1536,1024]{1,0:T(8,128)(2,1)}, bf16[1536,1024]{1,0:T(8,128)(2,1)S(1)}, u32[]{:S(2)}, u32[]{:S(2)}) collective-permute-start(bf16[1536,1024]{1,0:T(8,128)(2,1)} %rows_half.4), channel_id=1, source_target_pairs={{0,1},{1,0},{2,3},{3,2},{4,5},{5,4},{6,7},{7,6},{8,9},{9,8},{10,11... | collective-permute-start | bytes 9437192 | tf_op jit(solution)/shard_map/ppermute | solution.py:35
  559.4 25.5 %collective-permute-start.41 = (f32[4,96]{1,0:T(4,128)S(1)}, f32[4,96]{1,0:T(4,128)S(1)}, u32[]{:S(2)}, u32[]{:S(2)}) collective-permute-start(f32[4,96]{1,0:T(4,128)S(1)} %unstack.194), channel_id=1, source_target_pairs={{0,8},{8,0},{16,24},{24,16},{1,9},{9,1},{17,25},{25,17},{2,10},{10... | collective-permute-start | bytes 4616 | tf_op jit(solution)/shard_map/ppermute | solution.py:89
  560.4 24.5 %collective-permute-start.42 = (f32[4,96]{1,0:T(4,128)S(1)}, f32[4,96]{1,0:T(4,128)S(1)}, u32[]{:S(2)}, u32[]{:S(2)}) collective-permute-start(f32[4,96]{1,0:T(4,128)S(1)} %unstack.196), channel_id=1, source_target_pairs={{0,16},{8,24},{16,0},{24,8},{1,17},{9,25},{17,1},{25,9},{2,18},{10... | collective-permute-start | bytes 4616 | tf_op jit(solution)/shard_map/ppermute | solution.py:89
  561.4 23.5 %collective-permute-start.43 = (f32[4,96]{1,0:T(4,128)S(1)}, f32[4,96]{1,0:T(4,128)S(1)}, u32[]{:S(2)}, u32[]{:S(2)}) collective-permute-start(f32[4,96]{1,0:T(4,128)S(1)} %unstack.198), channel_id=1, source_target_pairs={{0,24},{8,16},{16,8},{24,0},{1,25},{9,17},{17,9},{25,1},{2,26},{10... | collective-permute-start | bytes 4616 | tf_op jit(solution)/shard_map/ppermute | solution.py:89
  585.0 16.3 %collective-permute-start.50 = (f32[192]{0:T(256)S(1)}, f32[192]{0:T(256)S(1)}, u32[]{:S(2)}, u32[]{:S(2)}) collective-permute-start(f32[192]{0:T(256)S(1)} %pad_maximum_fusion.29), channel_id=1, source_target_pairs={{0,6},{2,0},{4,2},{6,4},{1,7},{3,1},{5,3},{7,5},{8,14},{10,8},{12,... | collective-permute-start | bytes 2312 | tf_op jit(solution)/shard_map/ppermute | solution.py:81
  618.0 32.4 %collective-permute-start.45 = (bf16[4,96,1024]{2,1,0:T(8,128)(2,1)}, bf16[4,96,1024]{2,1,0:T(8,128)(2,1)}, u32[]{:S(2)}, u32[]{:S(2)}) collective-permute-start(bf16[4,96,1024]{2,1,0:T(8,128)(2,1)} %bitcast.95), channel_id=1, source_target_pairs={{0,8},{8,0},{16,24},{24,16},{1,9},{9,1},{17,25},{25,17},{2,10},{10... | collective-permute-start | bytes 2359304 | tf_op jit(solution)/shard_map/ppermute | solution.py:89
  618.9 36.8 %collective-permute-start.46 = (bf16[4,96,1024]{2,1,0:T(8,128)(2,1)}, bf16[4,96,1024]{2,1,0:T(8,128)(2,1)}, u32[]{:S(2)}, u32[]{:S(2)}) collective-permute-start(bf16[4,96,1024]{2,1,0:T(8,128)(2,1)} %bitcast.96), channel_id=1, source_target_pairs={{0,16},{8,24},{16,0},{24,8},{1,17},{9,25},{17,1},{25,9},{2,18},{10... | collective-permute-start | bytes 2359304 | tf_op jit(solution)/shard_map/ppermute | solution.py:89
  619.8 35.9 %collective-permute-start.47 = (bf16[4,96,1024]{2,1,0:T(8,128)(2,1)}, bf16[4,96,1024]{2,1,0:T(8,128)(2,1)}, u32[]{:S(2)}, u32[]{:S(2)}) collective-permute-start(bf16[4,96,1024]{2,1,0:T(8,128)(2,1)} %bitcast.97), channel_id=1, source_target_pairs={{0,24},{8,16},{16,8},{24,0},{1,25},{9,17},{17,9},{25,1},{2,26},{10... | collective-permute-start | bytes 2359304 | tf_op jit(solution)/shard_map/ppermute | solution.py:89
  661.8 43.7 %collective-permute-start.55 = (bf16[4,96,1024]{2,1,0:T(8,128)(2,1)}, bf16[4,96,1024]{2,1,0:T(8,128)(2,1)}, u32[]{:S(2)}, u32[]{:S(2)}) collective-permute-start(bf16[4,96,1024]{2,1,0:T(8,128)(2,1)} %bitcast.114), channel_id=1, source_target_pairs={{0,8},{8,0},{16,24},{24,16},{1,9},{9,1},{17,25},{25,17},{2,10},{10... | collective-permute-start | bytes 2359304 | tf_op jit(solution)/shard_map/ppermute | solution.py:89
  662.9 42.6 %collective-permute-start.56 = (bf16[4,96,1024]{2,1,0:T(8,128)(2,1)}, bf16[4,96,1024]{2,1,0:T(8,128)(2,1)S(1)}, u32[]{:S(2)}, u32[]{:S(2)}) collective-permute-start(bf16[4,96,1024]{2,1,0:T(8,128)(2,1)} %bitcast.115), channel_id=1, source_target_pairs={{0,16},{8,24},{16,0},{24,8},{1,17},{9,25},{17,1},{25,9},{2,18},{10... | collective-permute-start | bytes 2359304 | tf_op jit(solution)/shard_map/ppermute | solution.py:89
  663.6 41.9 %collective-permute-start.57 = (bf16[4,96,1024]{2,1,0:T(8,128)(2,1)}, bf16[4,96,1024]{2,1,0:T(8,128)(2,1)}, u32[]{:S(2)}, u32[]{:S(2)}) collective-permute-start(bf16[4,96,1024]{2,1,0:T(8,128)(2,1)} %bitcast.116), channel_id=1, source_target_pairs={{0,24},{8,16},{16,8},{24,0},{1,25},{9,17},{17,9},{25,1},{2,26},{10... | collective-permute-start | bytes 2359304 | tf_op jit(solution)/shard_map/ppermute | solution.py:89
  666.0 39.4 %collective-permute-start.53 = (bf16[192,1024]{1,0:T(8,128)(2,1)}, bf16[192,1024]{1,0:T(8,128)(2,1)S(1)}, u32[]{:S(2)}, u32[]{:S(2)}) collective-permute-start(bf16[192,1024]{1,0:T(8,128)(2,1)} %pad_maximum_fusion.20), channel_id=1, source_target_pairs={{0,4},{2,6},{4,0},{6,2},{1,5},{3,7},{5,1},{7,3},{8,12},{10,14},{12... | collective-permute-start | bytes 1179656 | tf_op jit(solution)/shard_map/ppermute | solution.py:81
  672.1 33.3 %collective-permute-start.52 = (bf16[192,1024]{1,0:T(8,128)(2,1)}, bf16[192,1024]{1,0:T(8,128)(2,1)S(1)}, u32[]{:S(2)}, u32[]{:S(2)}) collective-permute-start(bf16[192,1024]{1,0:T(8,128)(2,1)} %pad_maximum_fusion.19), channel_id=1, source_target_pairs={{0,2},{2,4},{4,6},{6,0},{1,3},{3,5},{5,7},{7,1},{8,10},{10,12},{12... | collective-permute-start | bytes 1179656 | tf_op jit(solution)/shard_map/ppermute | solution.py:81
  706.6 91.5 %all-to-all-start.3 = ((bf16[4,768,1408]{2,1,0:T(8,128)(2,1)}), bf16[4,768,1408]{2,1,0:T(8,128)(2,1)}, u32[]{:S(2)}, u32[]{:S(2)}) async-start(bf16[4,768,1408]{2,1,0:T(8,128)(2,1)} %grad_gateup.2), calls=%async_computation.3 | async-start | bytes 17301504 | tf_op jit(solution)/shard_map/all_to_all | solution.py:39
  712.3 254.9 %reduce-scatter.3.cloned.1.call-start = ((), (), s32[]{:S(2)}) async-start(), calls=%async_computation.13 | async-start | bytes 10485760 | tf_op jit(solution)/shard_map/reduce_scatter | solution.py:891
  719.7 36.1 %collective-permute-start.59 = (bf16[192,1024]{1,0:T(8,128)(2,1)S(1)}, bf16[192,1024]{1,0:T(8,128)(2,1)S(1)}, u32[]{:S(2)}, u32[]{:S(2)}) collective-permute-start(bf16[192,1024]{1,0:T(8,128)(2,1)S(1)} %pad_maximum_fusion.23), channel_id=1, source_target_pairs={{0,4},{2,6},{4,0},{6,2},{1,5},{3,7},{5,1},{7,3},{8,12},{10,14},{12... | collective-permute-start | bytes 1179656 | tf_op jit(solution)/shard_map/ppermute | solution.py:81
  721.2 25.2 %collective-permute-start.58 = (bf16[192,1024]{1,0:T(8,128)(2,1)S(1)}, bf16[192,1024]{1,0:T(8,128)(2,1)S(1)}, u32[]{:S(2)}, u32[]{:S(2)}) collective-permute-start(bf16[192,1024]{1,0:T(8,128)(2,1)S(1)} %pad_maximum_fusion.22), channel_id=1, source_target_pairs={{0,2},{2,4},{4,6},{6,0},{1,3},{3,5},{5,7},{7,1},{8,10},{10,12},{12... | collective-permute-start | bytes 1179656 | tf_op jit(solution)/shard_map/ppermute | solution.py:81
  761.2 13.8 %collective-permute-start.64 = (bf16[2,96,1024]{2,1,0:T(8,128)(2,1)S(1)}, bf16[2,96,1024]{2,1,0:T(8,128)(2,1)S(1)}, u32[]{:S(2)}, u32[]{:S(2)}) collective-permute-start(bf16[2,96,1024]{2,1,0:T(8,128)(2,1)S(1)} %bitcast.426), channel_id=1, source_target_pairs={{0,2},{2,4},{4,6},{6,0},{1,3},{3,5},{5,7},{7,1},{8,10},{10,12},{12... | collective-permute-start | bytes 1179656 | tf_op jit(solution)/shard_map/ppermute | solution.py:81
  761.3 36.9 %collective-permute-start.62 = (bf16[2,96,1024]{2,1,0:T(8,128)(2,1)}, bf16[2,96,1024]{2,1,0:T(8,128)(2,1)S(1)}, u32[]{:S(2)}, u32[]{:S(2)}) collective-permute-start(bf16[2,96,1024]{2,1,0:T(8,128)(2,1)} %bitcast.133), channel_id=1, source_target_pairs={{0,6},{2,0},{4,2},{6,4},{1,7},{3,1},{5,3},{7,5},{8,14},{10,8},{12,... | collective-permute-start | bytes 1179656 | tf_op jit(solution)/shard_map/ppermute | solution.py:81
  765.1 34.7 %collective-permute-start.63 = (bf16[2,96,1024]{2,1,0:T(8,128)(2,1)S(1)}, bf16[2,96,1024]{2,1,0:T(8,128)(2,1)S(1)}, u32[]{:S(2)}, u32[]{:S(2)}) collective-permute-start(bf16[2,96,1024]{2,1,0:T(8,128)(2,1)S(1)} %bitcast.416), channel_id=1, source_target_pairs={{0,4},{2,6},{4,0},{6,2},{1,5},{3,7},{5,1},{7,3},{8,12},{10,14},{12... | collective-permute-start | bytes 1179656 | tf_op jit(solution)/shard_map/ppermute | solution.py:81
  812.4 79.2 %all-to-all-start.4 = ((bf16[4,256,1408]{2,1,0:T(8,128)(2,1)}), bf16[4,256,1408]{2,1,0:T(8,128)(2,1)S(1)}, u32[]{:S(2)}, u32[]{:S(2)}) async-start(bf16[4,256,1408]{2,1,0:T(8,128)(2,1)} %grad_gateup.3), calls=%async_computation.4 | async-start | bytes 5767168 | tf_op jit(solution)/shard_map/all_to_all | solution.py:39
  816.5 270.9 %reduce-scatter.5.cloned.1.call-start = ((), (), s32[]{:S(2)}) async-start(), calls=%async_computation.14 | async-start | bytes 10485760 | tf_op jit(solution)/shard_map/reduce_scatter | solution.py:913
  847.5 46.8 %collective-permute-start.67 = (bf16[1024,512]{1,0:T(8,128)(2,1)}, bf16[1024,512]{1,0:T(8,128)(2,1)}, u32[]{:S(2)}, u32[]{:S(2)}) collective-permute-start(bf16[1024,512]{1,0:T(8,128)(2,1)} %bitcast.482), channel_id=1, source_target_pairs={{0,4},{2,6},{4,0},{6,2},{1,5},{3,7},{5,1},{7,3},{8,12},{10,14},{12... | collective-permute-start | bytes 3145736 | tf_op jit(solution)/shard_map/ppermute | solution.py:81
  904.6 28.1 %collective-permute-start.68 = (bf16[1024,512]{1,0:T(8,128)(2,1)}, bf16[1024,512]{1,0:T(8,128)(2,1)S(1)}, u32[]{:S(2)}, u32[]{:S(2)}) collective-permute-start(bf16[1024,512]{1,0:T(8,128)(2,1)} %bitcast.481), channel_id=1, source_target_pairs={{0,2},{2,4},{4,6},{6,0},{1,3},{3,5},{5,7},{7,1},{8,10},{10,12},{12... | collective-permute-start | bytes 3145736 | tf_op jit(solution)/shard_map/ppermute | solution.py:81
  904.7 88.7 %all-to-all-start.5 = ((bf16[4,1408,512]{2,1,0:T(8,128)(2,1)}), bf16[4,1408,512]{2,1,0:T(8,128)(2,1)}, u32[]{:S(2)}, u32[]{:S(2)}) async-start(bf16[4,1408,512]{2,1,0:T(8,128)(2,1)} %grad_down.1), calls=%async_computation.6 | async-start | bytes 11534336 | tf_op jit(solution)/shard_map/all_to_all | solution.py:39
  910.0 61.5 %collective-permute-start.66 = (bf16[1024,512]{1,0:T(8,128)(2,1)}, bf16[1024,512]{1,0:T(8,128)(2,1)}, u32[]{:S(2)}, u32[]{:S(2)}) collective-permute-start(bf16[1024,512]{1,0:T(8,128)(2,1)} %bitcast.480), channel_id=1, source_target_pairs={{0,6},{2,0},{4,2},{6,4},{1,7},{3,1},{5,3},{7,5},{8,14},{10,8},{12,... | collective-permute-start | bytes 3145736 | tf_op jit(solution)/shard_map/ppermute | solution.py:81
  978.5 20.4 %collective-permute-start.69 = (bf16[1024,1024]{1,0:T(8,128)(2,1)}, bf16[1024,1024]{1,0:T(8,128)(2,1)}, u32[]{:S(2)}, u32[]{:S(2)}) collective-permute-start(bf16[1024,1024]{1,0:T(8,128)(2,1)} %fusion.3), channel_id=1, source_target_pairs={{0,1},{1,0},{2,3},{3,2},{4,5},{5,4},{6,7},{7,6},{8,9},{9,8},{10,11... | collective-permute-start | bytes 6291464 | tf_op jit(solution)/shard_map/ppermute | solution.py:35
  993.4 52.7 %all-to-all-start.6 = ((bf16[4,512,512]{2,1,0:T(8,128)(2,1)}), bf16[4,512,512]{2,1,0:T(8,128)(2,1)}, u32[]{:S(2)}, u32[]{:S(2)}) async-start(bf16[4,512,512]{2,1,0:T(8,128)(2,1)} %bitcast.400), calls=%async_computation.7 | async-start | bytes 4194304 | tf_op jit(solution)/shard_map/all_to_all | solution.py:39
  1004.7 49.2 %collective-permute-start.70 = (bf16[256,1024]{1,0:T(8,128)(2,1)}, bf16[256,1024]{1,0:T(8,128)(2,1)}, u32[]{:S(2)}, u32[]{:S(2)}) collective-permute-start(bf16[256,1024]{1,0:T(8,128)(2,1)} %get-tuple-element.207), channel_id=1, source_target_pairs={{0,2},{2,4},{4,6},{6,0},{1,3},{3,5},{5,7},{7,1},{8,10},{10,12},{12... | collective-permute-start | bytes 1572872 | tf_op jit(solution)/shard_map/ppermute | solution.py:81
  1006.2 47.6 %collective-permute-start.71 = (bf16[256,1024]{1,0:T(8,128)(2,1)}, bf16[256,1024]{1,0:T(8,128)(2,1)}, u32[]{:S(2)}, u32[]{:S(2)}) collective-permute-start(bf16[256,1024]{1,0:T(8,128)(2,1)} %get-tuple-element.206), channel_id=1, source_target_pairs={{0,4},{2,6},{4,0},{6,2},{1,5},{3,7},{5,1},{7,3},{8,12},{10,14},{12... | collective-permute-start | bytes 1572872 | tf_op jit(solution)/shard_map/ppermute | solution.py:81
  1008.5 45.3 %collective-permute-start.72 = (bf16[256,1024]{1,0:T(8,128)(2,1)}, bf16[256,1024]{1,0:T(8,128)(2,1)}, u32[]{:S(2)}, u32[]{:S(2)}) collective-permute-start(bf16[256,1024]{1,0:T(8,128)(2,1)} %get-tuple-element.205), channel_id=1, source_target_pairs={{0,6},{2,0},{4,2},{6,4},{1,7},{3,1},{5,3},{7,5},{8,14},{10,8},{12,... | collective-permute-start | bytes 1572872 | tf_op jit(solution)/shard_map/ppermute | solution.py:81
  1049.2 22.1 %all-to-all-start.7 = ((bf16[4,128,2,2,128]{4,3,2,1,0:T(2,128)(2,1)}), bf16[4,128,2,2,128]{4,3,2,1,0:T(2,128)(2,1)S(1)}, u32[]{:S(2)}, u32[]{:S(2)}) async-start(bf16[4,128,2,2,128]{4,3,2,1,0:T(2,128)(2,1)} %reshape.745), calls=%async_computation.8 | async-start | bytes 1048576 | tf_op jit(solution)/shard_map/all_to_all | solution.py:39
  (112 other events, 1566.7 us)
Sparse Core Ops, SparseCore 0:
  26.7 35.5 all-gather.5
  64.7 193.8 all-gather.3
  260.4 86.8 all-gather.7
  812.5 154.5 reduce-scatter.2
  970.4 117.0 reduce-scatter.4
